TPU v7x, 128 devices: a whole 4x4x4 slice. The times are simulated.
128 devices in a mesh: energy: 16 (over y, x_hi, core), layer: 8 (over x_lo, z).
Axes of the slice: x: 4 (x_hi: 2, x_lo: 2; x = x_hi * 2 + x_lo), y: 4, z: 4, core: 2. Of those that a mesh axis runs over, the one named last changes fastest.
Arguments:
- green_blocks: bfloat16 [64, 8, 2, 384, 384], P('energy', 'layer'), may hold values from -6 to 6
- offsets: int32 [4], replicated, may hold values from -4 to 4, as said below
- occupation: float32 [4], replicated, may hold values from 0.1 to 2
- coupling: int32 [8, 4], P('layer'), may hold values from 0 to 3
- vertex: bfloat16 [4, 2, 384, 384], replicated, may hold values from -0.15625 to 0.15625
- magnon_free: bfloat16 [4, 2, 384, 384], replicated, may hold values from -0.0034179688 to 0.0034179688
Outputs:
- sigma: bfloat16 [64, 8, 2, 384, 384], P('energy', 'layer')
Inputs may be any that keep to these rules, and one draw needn't show every extreme that they name: `offsets`: each offset is a nonzero whole number; one equals 4 and one equals -4.
All inputs are finite; a program needn't handle non-finite values.
Results may differ from a plain program's by a relative error of at most 0.0056.
Values may be sent and summed in bfloat16 or wider, within the bound.
No kernel may reach another device: no remote copies, remote signals or barrier semaphores. Data moves between devices by JAX's collectives and lax.ppermute only.
A program may use at most 192 MiB of HBM per device.

v0:
```python
import jax
import jax.numpy as jnp
from jax import lax
from jax.sharding import PartitionSpec as P


def padded_2(block, sides, width):
    for axis, dim in sides:
        count = lax.axis_size(axis)
        forward = [(i, i + 1) for i in range(count - 1)]
        backward = [(target, source) for source, target in forward]
        low = lax.ppermute(
            lax.slice_in_dim(block, block.shape[dim] - width, None, axis=dim), axis, forward
        )
        high = lax.ppermute(lax.slice_in_dim(block, 0, width, axis=dim), axis, backward)
        block = jnp.concatenate([low, block, high], axis=dim)
    return block


def complex_mul(pattern, left_real, left_imag, right_real, right_imag):

    def product(first, second):
        return jnp.einsum(pattern, first, second, preferred_element_type=jnp.float32)

    return (
        product(left_real, right_real) - product(left_imag, right_imag),
        product(left_real, right_imag) + product(left_imag, right_real),
    )


def per_device(green_blocks, offsets, occupation, coupling, vertex, magnon_free):
    count = green_blocks.shape[0]
    padded = padded_2(green_blocks, (("energy", 0),), count)
    local_index = jnp.arange(count, dtype=jnp.int32)[:, None]
    below = jnp.take(padded, local_index + count - offsets[None, :], axis=0)
    above = jnp.take(padded, local_index + count + offsets[None, :], axis=0)
    below_wide = below.astype(jnp.float32)
    above_wide = above.astype(jnp.float32)
    chosen = vertex[coupling]
    weights = occupation[None, :, None, None, None, None]
    mixed = (weights * below_wide + (weights + 1.0) * above_wide).astype(jnp.bfloat16)
    half_real, half_imag = complex_mul(
        "gkab,ekgbc->ekgac", chosen[:, :, 0], chosen[:, :, 1], mixed[:, :, :, 0], mixed[:, :, :, 1]
    )
    half_real = half_real.astype(jnp.bfloat16)
    half_imag = half_imag.astype(jnp.bfloat16)
    born_real, born_imag = complex_mul(
        "ekgab,gkcb->egac", half_real, half_imag, chosen[:, :, 0], -chosen[:, :, 1]
    )
    own_wide = green_blocks.astype(jnp.float32)[:, None]
    flipped = jnp.swapaxes(above_wide, -1, -2)
    polar_real = jnp.sum(
        own_wide[:, :, :, 0] * flipped[:, :, :, 0] - own_wide[:, :, :, 1] * flipped[:, :, :, 1],
        axis=(0, 2),
    )
    polar_imag = jnp.sum(
        own_wide[:, :, :, 0] * flipped[:, :, :, 1] + own_wide[:, :, :, 1] * flipped[:, :, :, 0],
        axis=(0, 2),
    )
    partial_polar = jnp.stack([polar_real, polar_imag], axis=1)
    polar_full = lax.psum(partial_polar, ("energy", "layer")).astype(jnp.bfloat16)
    full_real, full_imag = complex_mul(
        "kab,kbc->kac", polar_full[:, 0], polar_full[:, 1], magnon_free[:, 0], magnon_free[:, 1]
    )
    magnon = jnp.stack([full_real, full_imag], axis=1).astype(jnp.bfloat16)
    magnon_wide = magnon.astype(jnp.float32)
    summed = below_wide + above_wide
    hadamard_real = jnp.sum(
        magnon_wide[None, :, None, 0] * summed[:, :, :, 0]
        - magnon_wide[None, :, None, 1] * summed[:, :, :, 1],
        axis=1,
    )
    hadamard_imag = jnp.sum(
        magnon_wide[None, :, None, 0] * summed[:, :, :, 1]
        + magnon_wide[None, :, None, 1] * summed[:, :, :, 0],
        axis=1,
    )
    return jnp.stack([born_real + hadamard_real, born_imag + hadamard_imag], axis=2).astype(
        jnp.bfloat16
    )


def solution(mesh):
    placed = (P("energy", "layer", None, None, None), P(), P(), P("layer", None), P(), P())
    return jax.shard_map(
        per_device,
        mesh=mesh,
        in_specs=placed,
        out_specs=P("energy", "layer", None, None, None),
        check_vma=False,
    )
```

profile of v0, /device:TPU:0, one launch (start us, length us, event | category | flops | bytes accessed | tf_op | source)
XLA Modules:
  0.0 323.6 jit_solution(7075733603432876331)
XLA Ops:
  0.0 0.0 copy-start
  0.0 2.8 collective-permute-start
  2.8 1.3 collective-permute-start.1
  4.1 0.7 compare_select_fusion
  4.9 0.1 reshape.295
  4.9 0.7 compare_and_fusion
  5.7 0.1 copy.21
  5.8 0.1 reshape.290
  5.9 0.1 copy.19
  6.0 0.7 fusion.38
  6.6 2.3 gather_fusion
  8.9 2.1 copy.49
  11.0 0.3 copy-done.8
  11.3 0.3 bitcast_convert_fusion
  11.7 2.6 slice_bitcast_fusion.17
  14.2 0.0 collective-permute-done
  14.2 0.0 collective-permute-done.1
  14.2 5.9 %maximum_bitcast_fusion = bf16[12,2,384,384]{3,2,1,0:T(8,128)(2,1)} fusion(bf16[4,1,2,384,384]{4,3,2,1,0:T(8,128)(2,1)} %collective-permute-done.1, bf16[4,1,2,384,384]{4,3,2,1,0:T(8,128)(2,1)S(1)} %copy-done.8, bf16[4,1,2,384,384]{4,3,2,1,0:T(8,128)(2,1)} %collective-permute-done), kind=kLoop, calls=%fused_computation.21 | loop fusion | flops 7077888 | bytes 14155776 | tf_op jit(solution)/shard_map/jit(_take)/Arg_0.3 | solution.py:35
  20.2 8.6 %gather_fusion.2 = bf16[16,2,384,384]{3,2,1,0:T(8,128)(2,1)} fusion(bf16[12,2,384,384]{3,2,1,0:T(8,128)(2,1)} %maximum_bitcast_fusion, s32[1024]{0:T(1024)S(1)} %pad_clamp_fusion), kind=kCustom, calls=%fused_computation.1.clone | custom fusion | bytes 18874432 | tf_op jit(solution)/shard_map/jit(_take)/gather | solution.py:36
  28.8 12.7 %copy.22 = bf16[4,4,1,2,384,384]{4,5,0,1,3,2:T(8,128)(2,1)} copy(bf16[4,4,1,2,384,384]{5,4,3,1,0,2:T(8,128)(2,1)} %bitcast.213) | data formatting | bytes 18874368 | tf_op jit(solution)/shard_map/jit(_take)/gather | solution.py:36
  41.5 11.5 %convert_bitcast_fusion = f32[4,4,1,2,384,384]{5,4,0,1,3,2:T(8,128)} fusion(bf16[4,4,1,2,384,384]{4,5,0,1,3,2:T(8,128)(2,1)} %copy.22, pred[4,4]{0,1:T(4,128)(4,1)S(1)} %copy.21), kind=kLoop, calls=%fused_computation.4 | loop fusion | flops 9437184 | bytes 28311568 | tf_op jit(solution)/shard_map/transpose | solution.py:51
  53.0 9.3 %subtract_reduce_fusion.1 = (f32[4,384,384]{2,1,0:T(8,128)S(1)}, f32[4,384,384]{2,1,0:T(8,128)S(1)}) fusion(f32[4,4,1,2,384,384]{5,4,0,1,3,2:T(8,128)} %convert_bitcast_fusion, f32[4,384,384]{2,1,0:T(8,128)} %get-tuple-element.15, f32[4,384,384]{2,1,0:T(8,128)} %get-tuple-element.14), kind=kLoop, calls=%fused_computation.16 | loop fusion | flops 17694720 | bytes 28311552 | tf_op jit(solution)/shard_map/reduce_sum | solution.py:52
  62.3 2.5 pad_maximum_fusion
  64.8 150.0 %all-reduce.1 = bf16[4,2,384,384]{3,2,0,1:T(8,128)(2,1)} all-reduce(f32[4,2,384,384]{3,2,0,1:T(8,128)} %pad_maximum_fusion), channel_id=1, replica_groups=mesh['energy'=16,'layer'=8] {'energy','layer'}, use_global_device_ids=true, to_apply=%region_2.4 | all-reduce | flops 1179648 | bytes 7077888 | tf_op jit(solution)/shard_map/psum | solution.py:61
  214.8 4.0 %fusion.25 = f32[4,384,384]{2,1,0:T(8,128)} fusion(bf16[4,2,384,384]{3,2,0,1:T(8,128)(2,1)} %all-reduce.1, bf16[4,2,384,384]{3,2,1,0:T(8,128)(2,1)} %param.13), kind=kOutput, calls=%fused_computation.63 | convolution fusion | flops 452984832 | bytes 4718592 | tf_op jit(solution)/shard_map/kab,kbc->kac/dot_general | solution.py:23
  218.8 2.3 fusion.21
  221.2 8.6 %gather_fusion.1 = bf16[16,2,384,384]{3,2,1,0:T(8,128)(2,1)} fusion(bf16[12,2,384,384]{3,2,1,0:T(8,128)(2,1)} %maximum_bitcast_fusion, s32[1024]{0:T(1024)S(1)} %pad_clamp_fusion.1), kind=kCustom, calls=%fused_computation.clone | custom fusion | bytes 18874432 | tf_op jit(solution)/shard_map/jit(_take)/gather | solution.py:35
  229.8 12.7 %copy.20 = bf16[4,4,1,2,384,384]{4,5,0,1,3,2:T(8,128)(2,1)} copy(bf16[4,4,1,2,384,384]{5,4,3,1,0,2:T(8,128)(2,1)} %bitcast.212) | data formatting | bytes 18874368 | tf_op jit(solution)/shard_map/jit(_take)/gather | solution.py:35
  242.5 14.5 %fusion.1 = (bf16[4,4,1,2,384,384]{4,5,0,1,3,2:T(8,128)(2,1)S(1)}, f32[4,4,1,2,384,384]{4,5,0,1,3,2:T(8,128)}) fusion(f32[4]{0:T(128)S(1)} %broadcast_add_fusion, f32[4]{0:T(128)S(1)} %copy-done.13, bf16[4,4,1,2,384,384]{4,5,0,1,3,2:T(8,128)(2,1)} %copy.20, pred[4,4]{0,1:T(4,128)(4,1)S(1)} %copy.19, bf16[4,4,1,2,384,384]{4,5,0,1,3,2:T(8,128)(2,1)} %copy.22, ...), kind=kLoop, calls=%fused_computation.8 | loop fusion | flops 42467328 | bytes 47185984 | tf_op jit(solution)/shard_map/convert_element_type | solution.py:41
  257.0 6.0 %fusion.5 = f32[4,4,384,384]{3,2,1,0:T(8,128)} fusion(bf16[4,4,1,2,384,384]{4,5,0,1,3,2:T(8,128)(2,1)S(1)} %get-tuple-element.10, bf16[1,4,2,384,384]{4,3,1,2,0:T(8,128)(2,1)S(1)} %bitcast.214), kind=kOutput, calls=%fused_computation.28 | convolution fusion | flops 1811939328 | bytes 15335424 | tf_op jit(solution)/shard_map/gkab,ekgbc->ekgac/dot_general | solution.py:23
  263.0 5.4 %fusion.4 = f32[4,4,384,384]{3,2,1,0:T(8,128)} fusion(bf16[4,4,1,2,384,384]{4,5,0,1,3,2:T(8,128)(2,1)S(1)} %get-tuple-element.10, bf16[1,4,2,384,384]{4,3,1,2,0:T(8,128)(2,1)S(1)} %bitcast.215), kind=kOutput, calls=%fused_computation.27 | convolution fusion | flops 1811939328 | bytes 15335424 | tf_op jit(solution)/shard_map/gkab,ekgbc->ekgac/dot_general | solution.py:23
  268.5 6.9 %fusion.2 = bf16[4,4,384,384]{2,3,0,1:T(8,128)(2,1)} fusion(f32[4,4,384,384]{3,2,1,0:T(8,128)} %fusion.5, bf16[4,4,1,2,384,384]{4,5,0,1,3,2:T(8,128)(2,1)S(1)} %get-tuple-element.10, bf16[1,4,2,384,384]{4,3,1,2,0:T(8,128)(2,1)S(1)} %bitcast.216), kind=kOutput, calls=%fused_computation.22 | convolution fusion | flops 1816657920 | bytes 20054016 | tf_op jit(solution)/shard_map/gkab,ekgbc->ekgac/dot_general | solution.py:23
  275.4 5.9 %fusion.33 = f32[384,4,384,1]{2,0,1,3:T(8,128)} fusion(bf16[4,4,384,384]{2,3,0,1:T(8,128)(2,1)} %fusion.2, bf16[1,4,2,384,384]{4,3,1,2,0:T(8,128)(2,1)S(1)} %bitcast.217), kind=kOutput, calls=%fused_computation.72 | convolution fusion | flops 1811939328 | bytes 8257536 | tf_op jit(solution)/shard_map/ekgab,gkcb->egac/dot_general | solution.py:23
  281.3 3.5 %fusion.18 = f32[384,4,384,1]{2,0,1,3:T(8,128)} fusion(bf16[4,4,384,384]{2,3,0,1:T(8,128)(2,1)S(1)} %copy-done.5, bf16[1,4,2,384,384]{4,3,1,2,0:T(8,128)(2,1)S(1)} %bitcast.218), kind=kOutput, calls=%fused_computation.56 | convolution fusion | flops 1813708800 | bytes 8257536 | tf_op jit(solution)/shard_map/ekgab,gkcb->egac/dot_general | solution.py:23
  284.8 0.9 fusion.16
  285.7 0.8 copy-done.9
  286.4 0.9 fusion.17
  287.3 0.3 maximum_convert_fusion
  287.7 2.6 slice_bitcast_fusion.15
  290.2 3.1 copy.27
  293.3 3.0 copy.28
  296.4 8.3 %fusion.3 = bf16[4,4,384,384]{2,3,0,1:T(8,128)(2,1)S(1)} fusion(f32[4,4,384,384]{3,2,1,0:T(8,128)} %fusion.4, bf16[4,4,1,2,384,384]{4,5,0,1,3,2:T(8,128)(2,1)} %copy-done.2, bf16[1,4,2,384,384]{4,3,1,2,0:T(8,128)(2,1)S(1)} %bitcast.219), kind=kOutput, calls=%fused_computation.23 | convolution fusion | flops 1816657920 | bytes 20054016 | tf_op jit(solution)/shard_map/gkab,ekgbc->ekgac/dot_general | solution.py:23
  304.7 8.7 %subtract_reduce_fusion = (f32[4,384,384]{1,2,0:T(8,128)S(1)}, f32[4,384,384]{1,2,0:T(8,128)S(1)}) fusion(f32[4,4,1,2,384,384]{4,5,0,1,3,2:T(8,128)} %get-tuple-element.11, f32[4,384,384]{1,2,0:T(8,128)S(1)} %copy-done.7, f32[4,384,384]{1,2,0:T(8,128)S(1)} %copy-done.6), kind=kLoop, calls=%fused_computation.14 | loop fusion | flops 17694720 | bytes 28311552 | tf_op jit(solution)/shard_map/reduce_sum | solution.py:68
  313.4 2.1 fusion.14
  315.5 2.1 fusion.15
  317.6 0.0 copy-start.1
  317.6 1.7 pad_maximum_fusion.1
  319.3 4.3 %copy.31 = bf16[4,1,2,384,384]{4,3,2,1,0:T(8,128)(2,1)} copy(bf16[4,1,2,384,384]{3,4,0,2,1:T(8,128)(2,1)} %pad_maximum_fusion.1) | data formatting | bytes 4718592 | tf_op jit(solution)/shard_map/stack | solution.py:78
  (33 shorter events, 0.1 us)
Async XLA Ops:
  0.0 6.6 %copy-start = (bf16[4,2,384,384]{3,2,1,0:T(8,128)(2,1)S(1)}, bf16[4,2,384,384]{3,2,1,0:T(8,128)(2,1)}, u32[]{:S(2)}) copy-start(bf16[4,2,384,384]{3,2,1,0:T(8,128)(2,1)} %param.12) | copy-start | bytes 7077892
  0.0 14.2 %collective-permute-start = (bf16[4,1,2,384,384]{4,3,2,1,0:T(8,128)(2,1)}, bf16[4,1,2,384,384]{4,3,2,1,0:T(8,128)(2,1)}, u32[]{:S(2)}, u32[]{:S(2)}) collective-permute-start(bf16[4,1,2,384,384]{4,3,2,1,0:T(8,128)(2,1)} %param.8), channel_id=1, source_target_pairs={{0,8},{8,16},{16,24},{24,32},{32,40},{40,48},{48,56},{56,64},{64,7... | collective-permute-start | bytes 7077896 | tf_op jit(solution)/shard_map/ppermute | solution.py:12
  2.8 11.4 %collective-permute-start.1 = (bf16[4,1,2,384,384]{4,3,2,1,0:T(8,128)(2,1)}, bf16[4,1,2,384,384]{4,3,2,1,0:T(8,128)(2,1)}, u32[]{:S(2)}, u32[]{:S(2)}) collective-permute-start(bf16[4,1,2,384,384]{4,3,2,1,0:T(8,128)(2,1)} %param.8), channel_id=1, source_target_pairs={{8,0},{16,8},{24,16},{32,24},{40,32},{48,40},{56,48},{64,56},{72,6... | collective-permute-start | bytes 7077896 | tf_op jit(solution)/shard_map/ppermute | solution.py:15
  8.9 2.1 copy-start.13
  8.9 2.4 copy-start.8
  214.8 4.1 %copy-start.3 = (bf16[4,2,384,384]{3,2,0,1:T(8,128)(2,1)S(1)}, bf16[4,2,384,384]{3,2,0,1:T(8,128)(2,1)}, u32[]{:S(2)}) copy-start(bf16[4,2,384,384]{3,2,0,1:T(8,128)(2,1)} %all-reduce.1) | copy-start | bytes 7077892
  214.8 4.1 %copy-start.11 = (bf16[4,2,384,384]{3,2,1,0:T(8,128)(2,1)S(1)}, bf16[4,2,384,384]{3,2,1,0:T(8,128)(2,1)}, u32[]{:S(2)}) copy-start(bf16[4,2,384,384]{3,2,1,0:T(8,128)(2,1)} %param.13) | copy-start | bytes 7077892
  257.0 11.4 %copy-start.2 = (bf16[4,4,1,2,384,384]{4,5,0,1,3,2:T(8,128)(2,1)}, bf16[4,4,1,2,384,384]{4,5,0,1,3,2:T(8,128)(2,1)S(1)}, u32[]{:S(2)}) copy-start(bf16[4,4,1,2,384,384]{4,5,0,1,3,2:T(8,128)(2,1)S(1)} %get-tuple-element.10) | copy-start | bytes 28311556
  275.4 5.9 %copy-start.5 = (bf16[4,4,384,384]{2,3,0,1:T(8,128)(2,1)S(1)}, bf16[4,4,384,384]{2,3,0,1:T(8,128)(2,1)}, u32[]{:S(2)}) copy-start(bf16[4,4,384,384]{2,3,0,1:T(8,128)(2,1)} %fusion.2) | copy-start | bytes 14155780
  281.3 3.5 %copy-start.4 = (bf16[4,2,384,384]{3,2,0,1:T(8,128)(2,1)S(1)}, bf16[4,2,384,384]{3,2,0,1:T(8,128)(2,1)}, u32[]{:S(2)}) copy-start(bf16[4,2,384,384]{3,2,0,1:T(8,128)(2,1)} %all-reduce.1) | copy-start | bytes 7077892
  281.3 3.5 %copy-start.10 = (f32[4,384,384]{2,1,0:T(8,128)S(1)}, f32[4,384,384]{2,1,0:T(8,128)}, u32[]{:S(2)}) copy-start(f32[4,384,384]{2,1,0:T(8,128)} %fusion.25) | copy-start | bytes 7077892
  281.3 3.5 %copy-start.12 = (bf16[4,2,384,384]{3,2,1,0:T(8,128)(2,1)S(1)}, bf16[4,2,384,384]{3,2,1,0:T(8,128)(2,1)}, u32[]{:S(2)}) copy-start(bf16[4,2,384,384]{3,2,1,0:T(8,128)(2,1)} %param.13) | copy-start | bytes 7077892
  284.8 1.7 copy-start.9
  296.4 8.3 %copy-start.6 = (f32[4,384,384]{1,2,0:T(8,128)S(1)}, f32[4,384,384]{1,2,0:T(8,128)}, u32[]{:S(2)}) copy-start(f32[4,384,384]{1,2,0:T(8,128)} %copy.27) | copy-start | bytes 7077892
  296.4 8.3 %copy-start.7 = (f32[4,384,384]{1,2,0:T(8,128)S(1)}, f32[4,384,384]{1,2,0:T(8,128)}, u32[]{:S(2)}) copy-start(f32[4,384,384]{1,2,0:T(8,128)} %copy.28) | copy-start | bytes 7077892
  304.7 8.7 %copy-start.14 = (f32[384,4,384,1]{2,0,1,3:T(8,128)S(1)}, f32[384,4,384,1]{2,0,1,3:T(8,128)}, u32[]{:S(2)}) copy-start(f32[384,4,384,1]{2,0,1,3:T(8,128)} %fusion.33) | copy-start | bytes 7077892
  313.4 2.1 copy-start.15
  317.6 6.0 %copy-start.1 = (bf16[4,2,384,384]{3,2,1,0:T(8,128)(2,1)S(1)}, bf16[4,2,384,384]{3,2,1,0:T(8,128)(2,1)}, u32[]{:S(2)}) copy-start(bf16[4,2,384,384]{3,2,1,0:T(8,128)(2,1)} %param.12) | copy-start | bytes 7077892
where the time goes:
time: 325 us; the launch traced here: 324 us
  blocking collectives  150 us (46%)
  local copies, waits for them, and re-layouts  64 us (20%)
  other arithmetic  56.9 us (18%)
  matrix products  48.3 us (15%)
  starting transfers between devices  4.11 us (1%)
    psum x1, blocking collectives, per_device(): lax.psum(partial_polar, ('energy', 'layer')).astype(jnp.bfloat16)  150 us
    dot_general x12, matrix products, product(): jnp.einsum(pattern, first, second, preferred_element_type=jnp.float32)  48.3 us
    gather x2, local copies, waits for them, and re-layouts, per_device(): below = jnp.take(padded, local_index + count - offsets[None, :], axis=0)  21.3 us
    gather x2, local copies, waits for them, and re-layouts, per_device(): above = jnp.take(padded, local_index + count + offsets[None, :], axis=0)  21.3 us
    convert_element_type x1, other arithmetic, per_device(): (weights * below_wide + (weights + 1.0) * above_wide).astype(jnp.bfloat16)  14.5 us
    transpose x1, other arithmetic, per_device(): flipped = jnp.swapaxes(above_wide, -1, -2)  11.5 us
    reduce_sum x1, other arithmetic, per_device(): jnp.sum(own_wide[:, :, :, 0] * flipped[:, :, :, 0] - own_wide[:, :, :, 1]...  9.32 us
    reduce_sum x1, other arithmetic, per_device(): jnp.sum(magnon_wide[None, :, None, 0] * summed[:, :, :, 0] - magnon_wide[...  8.71 us
  transfers between devices with their start and end apart: 2, of which 0 were waited for; matrix products, arithmetic and copies ran while one was open for 3% of the time, Pallas kernels for 0%

commit v1 on v0

v1 whole, which is shorter than its diff:
```python
import jax
import jax.numpy as jnp
from jax import lax
from jax.experimental import pallas as pl
from jax.experimental.pallas import tpu as pltpu
from jax.sharding import Mesh
from jax.sharding import PartitionSpec as P


NB = 384
HALF = NB // 2
BANDS = 64
ROWS = 56
FLAT = BANDS * ROWS
F32 = jnp.float32
BF16 = jnp.bfloat16
SWAP = [(0, 1), (1, 0)]
OTHERS = ("y", "xh", "xl", "z")
ENERGY = ("y", "xh", "core")
LAYER = ("xl", "z")
ANY = pl.BlockSpec(memory_space=pl.ANY)
SMEM = pl.BlockSpec(memory_space=pltpu.SMEM)


def first_index(offsets, value):
    return jnp.where(
        offsets[0] == value, 0, jnp.where(offsets[1] == value, 1, jnp.where(offsets[2] == value, 2, 3))
    )


def offset_roles(offsets):
    top = first_index(offsets, 4)
    bottom = first_index(offsets, -4)
    low = jnp.minimum(top, bottom)
    high = jnp.maximum(top, bottom)
    first = jnp.where(low != 0, 0, jnp.where(high != 1, 1, 2))
    last = jnp.where(high != 3, 3, jnp.where(low != 2, 2, 1))
    return top, bottom, first, last


def spans(offsets, first, last):
    return (jnp.int32(4), jnp.abs(offsets[first]), jnp.abs(offsets[last]))


def polar_body(place, offsets, own, mate, near, send, keep, slots, turned, sems):
    core = place[0]
    copies = [
        pltpu.make_async_copy(own, slots.at[pl.ds(2, 4)], sems.at[0]),
        pltpu.make_async_copy(
            mate.at[pl.ds(2 * core, 2)], slots.at[pl.ds(6 - 6 * core, 2)], sems.at[1]
        ),
        pltpu.make_async_copy(near, slots.at[pl.ds(6 * core, 2)], sems.at[2]),
    ]
    for copy in copies:
        copy.start()
    for copy in copies:
        copy.wait()

    @pl.loop(0, 10)
    def _(step):
        slot = step // 2
        part = step % 2
        turned[slot, part] = slots[slot + 3, part].astype(F32).T

    _, _, first, last = offset_roles(offsets)
    for index, span in enumerate(spans(offsets, first, last)):
        base = jnp.clip(4 - span, 0, 2)
        for target, half in ((send, 1 - core), (keep, core)):

            @pl.loop(0, HALF // 16)
            def _(block):
                rows = pl.ds(pl.multiple_of(half * HALF + block * 16, 16), 16)
                real = jnp.zeros((16, NB), F32)
                imag = jnp.zeros((16, NB), F32)
                for step in range(4):
                    left = base + step
                    right = left + span - 3
                    ar = slots[left, 0, rows, :].astype(F32)
                    ai = slots[left, 1, rows, :].astype(F32)
                    br = turned[right, 0, rows, :]
                    bi = turned[right, 1, rows, :]
                    real += ar * br - ai * bi
                    imag += ar * bi + ai * br
                for part, value in enumerate((real, imag)):
                    for panel in range(3):
                        start = ((index * 2 + part) * 3 + panel) * HALF
                        target[pl.ds(pl.multiple_of(start + block * 16, 16), 16), :] = value[
                            :, panel * 128 : (panel + 1) * 128
                        ].astype(target.dtype)

    tail = pl.ds(18 * HALF, FLAT - 18 * HALF)
    send[tail, :] = jnp.zeros((FLAT - 18 * HALF, 128), BF16)
    keep[tail, :] = jnp.zeros((FLAT - 18 * HALF, 128), F32)


def polar_call(place, offsets, own, mate, near):
    return pl.pallas_call(
        polar_body,
        out_shape=(
            jax.ShapeDtypeStruct((FLAT, 128), BF16),
            jax.ShapeDtypeStruct((FLAT, 128), F32),
        ),
        in_specs=[SMEM, SMEM, ANY, ANY, ANY],
        out_specs=(
            pl.BlockSpec(memory_space=pltpu.VMEM),
            pl.BlockSpec(memory_space=pltpu.VMEM),
        ),
        scratch_shapes=[
            pltpu.VMEM((8, 2, NB, NB), BF16),
            pltpu.VMEM((5, 2, NB, NB), F32),
            pltpu.SemaphoreType.DMA((3,)),
        ],
        compiler_params=pltpu.CompilerParams(vmem_limit_bytes=24 << 20),
        cost_estimate=pl.CostEstimate(flops=20_000_000, bytes_accessed=9_000_000, transcendentals=0),
        name="polar",
    )(place, offsets, own, mate, near)


def window_copies(core, own, mate, near, far, slots, sems):
    copies = [
        pltpu.make_async_copy(own, slots.at[pl.ds(4, 4)], sems.at[0]),
        pltpu.make_async_copy(mate, slots.at[pl.ds(8 - 8 * core, 4)], sems.at[1]),
        pltpu.make_async_copy(near, slots.at[pl.ds(2 + 6 * core, 2)], sems.at[2]),
    ]
    if far is not None:
        copies.append(pltpu.make_async_copy(far, slots.at[pl.ds(10 * core, 2)], sems.at[3]))
    return copies


def born_body(early, *refs):
    if early:
        (place, offsets, occupation, coupling, own, mate, near, vertex, out, *rest) = refs
        far = None
    else:
        (place, offsets, occupation, coupling, own, mate, near, far, vertex, out, *rest) = refs
    slots, mixed, wide, stack, side, total, sems = rest
    core = place[0]
    copies = window_copies(core, own, mate, near, far, slots, sems)
    for copy in copies:
        copy.start()
    for copy in copies:
        copy.wait()
    energy = 2 * (1 - core) if early else 2 * core

    @pl.loop(0, 4)
    def _(k):
        which = coupling[0, k]
        vr = vertex[which, 0]
        vi = vertex[which, 1]
        wide[:NB, :NB] = vr
        wide[:NB, NB:] = -vi
        wide[NB:, :NB] = vi
        wide[NB:, NB:] = vr
        side[:NB, :NB] = vr
        side[:NB, NB:] = vi
        side[NB:, :NB] = -vi
        side[NB:, NB:] = vr
        span = offsets[k]
        weight = occupation[k]
        for item in range(2):
            at = energy + 4 + item
            for part in range(2):
                low = slots[at - span, part].astype(F32)
                high = slots[at + span, part].astype(F32)
                value = weight * low + (weight + 1.0) * high
                mixed[part * NB : (part + 1) * NB, item * NB : (item + 1) * NB] = value.astype(BF16)
        half = jnp.dot(wide[...], mixed[...], preferred_element_type=F32).astype(BF16)
        for item in range(2):
            for part in range(2):
                stack[item * NB : (item + 1) * NB, part * NB : (part + 1) * NB] = half[
                    part * NB : (part + 1) * NB, item * NB : (item + 1) * NB
                ]
        term = lax.dot_general(
            stack[...], side[...], (((1,), (1,)), ((), ())), preferred_element_type=F32
        )

        @pl.when(k == 0)
        def _():
            total[...] = term

        @pl.when(k > 0)
        def _():
            total[...] += term

    out[...] = total[...]


def born_call(early, place, offsets, occupation, coupling, arrays, vertex):
    size = 2 * NB
    return pl.pallas_call(
        lambda *refs: born_body(early, *refs),
        out_shape=jax.ShapeDtypeStruct((size, size), F32),
        in_specs=[SMEM] * 4 + [ANY] * len(arrays) + [pl.BlockSpec(memory_space=pltpu.VMEM)],
        out_specs=pl.BlockSpec(memory_space=pltpu.VMEM),
        scratch_shapes=[
            pltpu.VMEM((12, 2, NB, NB), BF16),
            pltpu.VMEM((size, size), BF16),
            pltpu.VMEM((size, size), BF16),
            pltpu.VMEM((size, size), BF16),
            pltpu.VMEM((size, size), BF16),
            pltpu.VMEM((size, size), F32),
            pltpu.SemaphoreType.DMA((4,)),
        ],
        compiler_params=pltpu.CompilerParams(vmem_limit_bytes=32 << 20),
        cost_estimate=pl.CostEstimate(
            flops=16 * size**3, bytes_accessed=12_000_000, transcendentals=0
        ),
        name="born_early" if early else "born_late",
    )(place, offsets, occupation, coupling, *arrays, vertex)


def final_body(
    place, offsets, mine, other, free, own, mate, near, far, early, late, out,
    slots, joined, flipped, table, magnon, sems,
):
    core = place[0]
    copies = window_copies(core, own, mate, near, far, slots, sems)
    for copy in copies:
        copy.start()
    for source, half in ((mine, core), (other, 1 - core)):
        rows = pl.ds(pl.multiple_of(half * HALF, HALF), HALF)
        for index in range(3):
            for part in range(2):
                for panel in range(3):
                    start = ((index * 2 + part) * 3 + panel) * HALF
                    joined[index, rows, part * NB + panel * 128 : part * NB + (panel + 1) * 128] = source[
                        start : start + HALF, :
                    ]

    def turn(index, target):
        for part in range(2):
            columns = slice(part * NB, (part + 1) * NB)
            target[:, columns] = joined[index, :, columns].astype(F32).T.astype(BF16)

    def product(left, k):
        fr = free[k, 0]
        fi = free[k, 1]
        table[:NB, :NB] = fr
        table[:NB, NB:] = fi
        table[NB:, :NB] = -fi
        table[NB:, NB:] = fr
        value = jnp.dot(left[...], table[...], preferred_element_type=F32)
        return value.astype(BF16).astype(F32)

    top, bottom, first, last = offset_roles(offsets)
    turn(0, flipped)
    magnon[0] = product(joined.at[0], top)
    magnon[0] += product(flipped, bottom)
    for index, k in ((1, first), (2, last)):

        @pl.when(offsets[k] < 0)
        def _():
            turn(index, flipped)

        @pl.when(offsets[k] > 0)
        def _():
            flipped[...] = joined[index]

        magnon[index] = product(flipped, k)

    for copy in copies:
        copy.wait()
    reach = spans(offsets, first, last)
    for source, energy in ((early, 2 * (1 - core)), (late, 2 * core)):
        for item in range(2):

            @pl.loop(0, NB // 16)
            def _(block):
                rows = pl.ds(pl.multiple_of(block * 16, 16), 16)
                begin = pl.ds(pl.multiple_of(item * NB + block * 16, 16), 16)
                real = source[begin, :NB]
                imag = source[begin, NB:]
                at = energy + 4 + item
                for index in range(3):
                    down = at - reach[index]
                    up = at + reach[index]
                    sr = slots[down, 0, rows, :].astype(F32) + slots[up, 0, rows, :].astype(F32)
                    si = slots[down, 1, rows, :].astype(F32) + slots[up, 1, rows, :].astype(F32)
                    mr = magnon[index, rows, :NB]
                    mi = magnon[index, rows, NB:]
                    real += mr * sr - mi * si
                    imag += mr * si + mi * sr
                out[energy + item, 0, 0, rows, :] = real.astype(BF16)
                out[energy + item, 0, 1, rows, :] = imag.astype(BF16)


def final_call(place, offsets, mine, other, free, own, mate, near, far, early, late):
    vmem = pl.BlockSpec(memory_space=pltpu.VMEM)
    return pl.pallas_call(
        final_body,
        out_shape=jax.ShapeDtypeStruct((4, 1, 2, NB, NB), BF16),
        in_specs=[SMEM, SMEM, vmem, vmem, vmem, ANY, ANY, ANY, ANY, vmem, vmem],
        out_specs=vmem,
        scratch_shapes=[
            pltpu.VMEM((12, 2, NB, NB), BF16),
            pltpu.VMEM((3, NB, 2 * NB), BF16),
            pltpu.VMEM((NB, 2 * NB), BF16),
            pltpu.VMEM((2 * NB, 2 * NB), BF16),
            pltpu.VMEM((3, NB, 2 * NB), F32),
            pltpu.SemaphoreType.DMA((4,)),
        ],
        compiler_params=pltpu.CompilerParams(vmem_limit_bytes=40 << 20),
        cost_estimate=pl.CostEstimate(
            flops=2_000_000_000, bytes_accessed=18_000_000, transcendentals=0
        ),
        name="final",
    )(place, offsets, mine, other, free, own, mate, near, far, early, late)


def per_device(green_blocks, offsets, occupation, coupling, vertex, magnon_free):
    count = lax.axis_size(ENERGY)
    core = lax.axis_index("core").astype(jnp.int32)
    place = core[None]
    own = green_blocks.reshape(4, 2, NB, NB)
    across = [(i, i + 1) for i in range(1, count - 1, 2)]
    across += [(target, source) for source, target in across]
    near = lax.ppermute(lax.dynamic_slice_in_dim(own, 2 * core, 2, 0), ENERGY, across)
    mate = lax.ppermute(own, "core", SWAP)
    far = lax.ppermute(lax.dynamic_slice_in_dim(own, 2 - 2 * core, 2, 0), ENERGY, across)
    send, keep = polar_call(place, offsets, own, mate, near)
    pair = keep + lax.ppermute(send, "core", SWAP).astype(F32)
    bands = lax.all_to_all(pair.astype(BF16).reshape(BANDS, ROWS, 128), OTHERS, 0, 0, tiled=True)
    polar = jnp.sum(bands.astype(F32), axis=0).astype(BF16)
    early = born_call(True, place, offsets, occupation, coupling, (own, mate, near), vertex)
    mine = lax.all_to_all(
        jnp.broadcast_to(polar[None], (BANDS, ROWS, 128)), OTHERS, 0, 0, tiled=True
    ).reshape(FLAT, 128)
    late = born_call(False, place, offsets, occupation, coupling, (own, mate, near, far), vertex)
    other = lax.ppermute(mine, "core", SWAP)
    return final_call(place, offsets, mine, other, magnon_free, own, mate, near, far, early, late)


def solution(mesh):
    fine = Mesh(mesh.devices.reshape(4, 2, 2, 2, 4), ("y", "xh", "core", "xl", "z"))
    blocks = P(ENERGY, LAYER, None, None, None)
    placed = (blocks, P(), P(), P(LAYER, None), P(), P())
    return jax.shard_map(
        per_device, mesh=fine, in_specs=placed, out_specs=blocks, check_vma=False
    )
```

time: 325 us -> 161 us (0.50)
  the two profiles are of different devices: /device:TPU:0 before, /device:TPU:93 now
where the time goes in v1:
time: 161 us; the launch traced here: 160 us
  starting transfers between devices  70.5 us (44%)
  Pallas kernels  46.7 us (29%)
  blocking collectives  22 us (14%)
  waiting for transfers between devices  10.8 us (7%)
  local copies, waits for them, and re-layouts  7.89 us (5%)
  other arithmetic  2.21 us (1%)
    ppermute x1, starting transfers between devices, per_device(): pair = keep + lax.ppermute(send, 'core', SWAP).astype(F32)  29.4 us
    pallas_call x2, Pallas kernels, born_call(): pl.pallas_call(lambda *refs: born_body(early, *refs), out_shape=jax.Shape...  28.1 us
    ppermute x1, starting transfers between devices, per_device(): other = lax.ppermute(mine, 'core', SWAP)  27 us
    all_to_all x1, blocking collectives, per_device(): lax.all_to_all(pair.astype(BF16).reshape(BANDS, ROWS, 128), OTHERS, 0, 0,...  22 us
    pallas_call x1, Pallas kernels, final_call(): pl.pallas_call(final_body, out_shape=jax.ShapeDtypeStruct((4, 1, 2, NB, N...  11.8 us
    all_to_all x1, starting transfers between devices, per_device(): lax.all_to_all(jnp.broadcast_to(polar[None], (BANDS, ROWS, 128)), OTHERS,...  10.9 us
    all_to_all x1, waiting for transfers between devices, per_device(): lax.all_to_all(jnp.broadcast_to(polar[None], (BANDS, ROWS, 128)), OTHERS,...  8 us
    pallas_call x1, Pallas kernels, polar_call(): pl.pallas_call(polar_body, out_shape=(jax.ShapeDtypeStruct((FLAT, 128), B...  6.86 us
  transfers between devices with their start and end apart: 6, of which 3 were waited for; matrix products, arithmetic and copies ran while one was open for 2% of the time, Pallas kernels for 17%

profile of v1, /device:TPU:93, one launch (start us, length us, event | category | flops | bytes accessed | tf_op | source)
XLA Modules:
  0.0 160.3 jit_solution(4654380546939276430)
XLA Ops:
  0.0 0.7 collective-permute-start
  0.7 0.0 copy-start
  0.7 0.0 copy-start.3
  0.7 3.0 %dynamic-slice_bitcast_fusion = (bf16[2,2,384,384]{3,2,1,0:T(8,128)(2,1)}, bf16[2,2,384,384]{3,2,1,0:T(8,128)(2,1)S(1)}) fusion(bf16[4,1,2,384,384]{4,3,2,1,0:T(8,128)(2,1)} %param.6, s32[]{:T(128)S(6)} %select_n.7, s32[]{:T(128)S(6)} %select_n.6), kind=kLoop, calls=%fused_computation.1 | loop fusion | bytes 4718600 | tf_op jit(solution)/shard_map/dynamic_slice | solution.py:319
  3.7 0.7 collective-permute-start.1
  4.4 0.0 collective-permute-done.1.near.refs_6_
  4.4 0.7 collective-permute-done.mate.refs_5_
  5.2 0.0 copy-done
  5.2 0.0 copy-done.3
  5.2 6.9 %polar.1 = (bf16[3584,128]{1,0:T(8,128)(2,1)S(1)}, f32[3584,128]{1,0:T(8,128)S(1)}) custom-call(s32[1]{0:T(128)} %bitcast.place.refs_0_, s32[4]{0:T(128)S(1)} %copy-done.3, bf16[4,2,384,384]{3,2,1,0:T(8,128)(2,1)S(1)} %bitcast.9, bf16[4,2,384,384]{3,2,1,0:T(8,128)(2,1)} %collective-permute-done.mate.refs_5_, ...), custom_call_target="tpu_custom_call" | custom-call | flops 20000000 | bytes 9000000 | tf_op jit(solution)/shard_map/polar/pallas_call | solution.py:97
  12.1 29.4 %collective-permute-start.2 = (bf16[3584,128]{1,0:T(8,128)(2,1)S(1)}, bf16[3584,128]{1,0:T(8,128)(2,1)S(1)}, u32[]{:S(2)}, u32[]{:S(2)}) collective-permute-start(bf16[3584,128]{1,0:T(8,128)(2,1)S(1)} %get-tuple-element.8), channel_id=1, source_target_pairs={{0,8},{8,0},{1,9},{9,1},{2,10},{10,2},{3,11},{11,3},{4,12},{12,4},... | collective-permute-start | bytes 2752520 | tf_op jit(solution)/shard_map/ppermute | solution.py:321
  41.5 2.1 %collective-permute-done.2 = bf16[3584,128]{1,0:T(8,128)(2,1)S(1)} collective-permute-done((bf16[3584,128]{1,0:T(8,128)(2,1)S(1)}, bf16[3584,128]{1,0:T(8,128)(2,1)S(1)}, u32[]{:S(2)}, u32[]{:S(2)}) %collective-permute-start.2) | collective-permute-done | bytes 917536 | tf_op jit(solution)/shard_map/ppermute | solution.py:321
  43.6 0.2 add_convert_fusion
  43.8 22.0 %all_to_all.10 = bf16[64,56,128]{2,1,0:T(8,128)(2,1)} all-to-all(bf16[64,56,128]{2,1,0:T(8,128)(2,1)S(1)} %bitcast.13), channel_id=1, replica_groups=mesh['y'=4,'xh'=2,'core'=2,'xl'=2,'z'=4] {'y','xh','xl','z'}, dimensions={0} | all-to-all | bytes 1835008 | tf_op jit(solution)/shard_map/all_to_all | solution.py:322
  65.8 0.0 copy-start.6
  65.8 0.0 copy-start.7
  65.8 2.0 %reduce_sum.12 = bf16[56,128]{1,0:T(8,128)(2,1)} reduce(bf16[64,56,128]{2,1,0:T(8,128)(2,1)} %all_to_all.10, bf16[]{:T(256)} %constant.17.clone.1), dimensions={0}, to_apply=%region_0.0 | reduce | flops 451584 | bytes 931842 | tf_op jit(solution)/shard_map/reduce_sum | solution.py:323
  67.8 1.8 %broadcast_in_dim.10 = bf16[64,56,128]{2,1,0:T(8,128)(2,1)} broadcast(bf16[56,128]{1,0:T(8,128)(2,1)} %reduce_sum.12), dimensions={1,2} | broadcast | bytes 931840 | tf_op jit(solution)/shard_map/broadcast_in_dim | solution.py:326
  69.6 10.9 %all-to-all-start.1 = ((bf16[64,56,128]{2,1,0:T(8,128)(2,1)}), bf16[64,56,128]{2,1,0:T(8,128)(2,1)}, u32[]{:S(2)}, u32[]{:S(2)}) async-start(bf16[64,56,128]{2,1,0:T(8,128)(2,1)} %broadcast_in_dim.10), calls=%async_computation.1 | async-start | bytes 1835008 | tf_op jit(solution)/shard_map/all_to_all | solution.py:325
  80.5 1.7 %collective-permute-start.4 = (bf16[2,2,384,384]{3,2,1,0:T(8,128)(2,1)}, bf16[2,2,384,384]{3,2,1,0:T(8,128)(2,1)}, u32[]{:S(2)}, u32[]{:S(2)}) collective-permute-start(bf16[2,2,384,384]{3,2,1,0:T(8,128)(2,1)} %get-tuple-element.9), channel_id=1, source_target_pairs={{8,16},{24,32},{40,48},{56,64},{72,80},{88,96},{104,112},{16,8},{3... | collective-permute-start | bytes 3538952 | tf_op jit(solution)/shard_map/ppermute | solution.py:319
  82.2 8.0 %all-to-all-done.1 = bf16[64,56,128]{2,1,0:T(8,128)(2,1)} async-done(((bf16[64,56,128]{2,1,0:T(8,128)(2,1)}), bf16[64,56,128]{2,1,0:T(8,128)(2,1)}, u32[]{:S(2)}, u32[]{:S(2)}) %all-to-all-start.1) | async-done | bytes 917536 | tf_op jit(solution)/shard_map/all_to_all | solution.py:325
  90.3 27.0 %collective-permute-start.3 = (bf16[3584,128]{1,0:T(8,128)(2,1)}, bf16[3584,128]{1,0:T(8,128)(2,1)S(1)}, u32[]{:S(2)}, u32[]{:S(2)}) collective-permute-start(bf16[3584,128]{1,0:T(8,128)(2,1)} %bitcast.4.mine), channel_id=1, source_target_pairs={{0,8},{8,0},{1,9},{9,1},{2,10},{10,2},{3,11},{11,3},{4,12},{12,4},... | collective-permute-start | bytes 2752520 | tf_op jit(solution)/shard_map/ppermute | solution.py:329
  117.3 0.0 copy-done.6
  117.3 0.0 copy-done.7
  117.3 0.0 copy-start.4
  117.3 1.7 %copy-done.4 = bf16[4,2,384,384]{3,2,1,0:T(8,128)(2,1)S(1)} copy-done((bf16[4,2,384,384]{3,2,1,0:T(8,128)(2,1)S(1)}, bf16[4,2,384,384]{3,2,1,0:T(8,128)(2,1)}, u32[]{:S(2)}) %copy-start.4) | copy-done | bytes 2359320
  119.0 0.0 copy-start.5
  119.0 13.9 %born_early.1.early = f32[768,768]{1,0:T(8,128)S(1)} custom-call(s32[1]{0:T(128)} %bitcast.place.refs_0_, s32[4]{0:T(128)S(1)} %copy-done.3, f32[4]{0:T(128)S(1)} %copy-done.6, s32[1,4]{1,0:T(1,128)S(1)} %copy-done.7, bf16[4,2,384,384]{3,2,1,0:T(8,128)(2,1)S(1)} %bitcast.10, bf16[4,2,384,384]{3,2,1,0:T(8,128)(2,1)} %collective-permute-done.mate.refs_5_, ...), custom_call_target="tpu_custom_call" | custom-call | flops 7247757312 | bytes 12000000 | tf_op jit(solution)/shard_map/born_early/pallas_call | solution.py:190
  132.8 0.0 copy-start.1
  132.8 0.0 collective-permute-done.4.refs_7_.far
  132.9 0.0 copy-done.5
  132.9 14.2 %born_late.1.late = f32[768,768]{1,0:T(8,128)S(1)} custom-call(s32[1]{0:T(128)} %bitcast.place.refs_0_, s32[4]{0:T(128)S(1)} %copy-done.3, f32[4]{0:T(128)S(1)} %copy-done.6, s32[1,4]{1,0:T(1,128)S(1)} %copy-done.7, bf16[4,2,384,384]{3,2,1,0:T(8,128)(2,1)S(1)} %bitcast.11, bf16[4,2,384,384]{3,2,1,0:T(8,128)(2,1)} %collective-permute-done.mate.refs_5_, ...), custom_call_target="tpu_custom_call" | custom-call | flops 7247757312 | bytes 12000000 | tf_op jit(solution)/shard_map/born_late/pallas_call | solution.py:190
  147.1 0.0 copy-start.2
  147.1 1.4 copy-done.2
  148.5 0.0 collective-permute-done.3.other
  148.5 0.0 copy-done.1
  148.5 11.8 %final.1 = bf16[4,1,2,384,384]{4,3,2,1,0:T(8,128)(2,1)} custom-call(s32[1]{0:T(128)} %bitcast.place.refs_0_, s32[4]{0:T(128)S(1)} %copy-done.3, bf16[3584,128]{1,0:T(8,128)(2,1)} %bitcast.4.mine, bf16[3584,128]{1,0:T(8,128)(2,1)S(1)} %collective-permute-done.3.other, bf16[4,2,384,384]{3,2,1,0:T(8,128)(2,1)S(1)} %copy-done.1, ...), custom_call_target="tpu_custom_call" | custom-call | flops 2000000000 | bytes 18000000 | tf_op jit(solution)/shard_map/final/pallas_call | solution.py:289
Async XLA Ops:
  0.0 5.2 %collective-permute-start = (bf16[4,2,384,384]{3,2,1,0:T(8,128)(2,1)}, bf16[4,2,384,384]{3,2,1,0:T(8,128)(2,1)}, u32[]{:S(2)}, u32[]{:S(2)}) collective-permute-start(bf16[4,2,384,384]{3,2,1,0:T(8,128)(2,1)} %bitcast.8), channel_id=1, source_target_pairs={{0,8},{8,0},{1,9},{9,1},{2,10},{10,2},{3,11},{11,3},{4,12},{12,4},... | collective-permute-start | bytes 7077896 | tf_op jit(solution)/shard_map/ppermute | solution.py:318
  0.7 4.5 %copy-start = (bf16[4,1,2,384,384]{4,3,2,1,0:T(8,128)(2,1)S(1)}, bf16[4,1,2,384,384]{4,3,2,1,0:T(8,128)(2,1)}, u32[]{:S(2)}) copy-start(bf16[4,1,2,384,384]{4,3,2,1,0:T(8,128)(2,1)} %param.6) | copy-start | bytes 7077892
  0.7 4.5 %copy-start.3 = (s32[4]{0:T(128)S(1)}, s32[4]{0:T(128)}, u32[]{:S(2)}) copy-start(s32[4]{0:T(128)} %offsets.3) | copy-start | bytes 52
  3.7 0.7 collective-permute-start.1
  12.1 31.5 %collective-permute-start.2 = (bf16[3584,128]{1,0:T(8,128)(2,1)S(1)}, bf16[3584,128]{1,0:T(8,128)(2,1)S(1)}, u32[]{:S(2)}, u32[]{:S(2)}) collective-permute-start(bf16[3584,128]{1,0:T(8,128)(2,1)S(1)} %get-tuple-element.8), channel_id=1, source_target_pairs={{0,8},{8,0},{1,9},{9,1},{2,10},{10,2},{3,11},{11,3},{4,12},{12,4},... | collective-permute-start | bytes 2752520 | tf_op jit(solution)/shard_map/ppermute | solution.py:321
  65.8 51.5 %copy-start.6 = (f32[4]{0:T(128)S(1)}, f32[4]{0:T(128)}, u32[]{:S(2)}) copy-start(f32[4]{0:T(128)} %refs_2_.3) | copy-start | bytes 52
  65.8 51.5 %copy-start.7 = (s32[1,4]{1,0:T(1,128)S(1)}, s32[1,4]{1,0:T(1,128)}, u32[]{:S(2)}) copy-start(s32[1,4]{1,0:T(1,128)} %refs_3_.3) | copy-start | bytes 52
  69.6 20.7 %all-to-all-start.1 = ((bf16[64,56,128]{2,1,0:T(8,128)(2,1)}), bf16[64,56,128]{2,1,0:T(8,128)(2,1)}, u32[]{:S(2)}, u32[]{:S(2)}) async-start(bf16[64,56,128]{2,1,0:T(8,128)(2,1)} %broadcast_in_dim.10), calls=%async_computation.1 | async-start | bytes 1835008 | tf_op jit(solution)/shard_map/all_to_all | solution.py:325
  80.5 52.3 %collective-permute-start.4 = (bf16[2,2,384,384]{3,2,1,0:T(8,128)(2,1)}, bf16[2,2,384,384]{3,2,1,0:T(8,128)(2,1)}, u32[]{:S(2)}, u32[]{:S(2)}) collective-permute-start(bf16[2,2,384,384]{3,2,1,0:T(8,128)(2,1)} %get-tuple-element.9), channel_id=1, source_target_pairs={{8,16},{24,32},{40,48},{56,64},{72,80},{88,96},{104,112},{16,8},{3... | collective-permute-start | bytes 3538952 | tf_op jit(solution)/shard_map/ppermute | solution.py:319
  90.3 58.2 %collective-permute-start.3 = (bf16[3584,128]{1,0:T(8,128)(2,1)}, bf16[3584,128]{1,0:T(8,128)(2,1)S(1)}, u32[]{:S(2)}, u32[]{:S(2)}) collective-permute-start(bf16[3584,128]{1,0:T(8,128)(2,1)} %bitcast.4.mine), channel_id=1, source_target_pairs={{0,8},{8,0},{1,9},{9,1},{2,10},{10,2},{3,11},{11,3},{4,12},{12,4},... | collective-permute-start | bytes 2752520 | tf_op jit(solution)/shard_map/ppermute | solution.py:329
  117.3 1.7 %copy-start.4 = (bf16[4,2,384,384]{3,2,1,0:T(8,128)(2,1)S(1)}, bf16[4,2,384,384]{3,2,1,0:T(8,128)(2,1)}, u32[]{:S(2)}) copy-start(bf16[4,2,384,384]{3,2,1,0:T(8,128)(2,1)} %refs_8_.1) | copy-start | bytes 7077892
  119.0 13.9 %copy-start.5 = (bf16[4,2,384,384]{3,2,1,0:T(8,128)(2,1)S(1)}, bf16[4,2,384,384]{3,2,1,0:T(8,128)(2,1)}, u32[]{:S(2)}) copy-start(bf16[4,2,384,384]{3,2,1,0:T(8,128)(2,1)} %refs_8_.1) | copy-start | bytes 7077892
  132.8 15.7 %copy-start.1 = (bf16[4,2,384,384]{3,2,1,0:T(8,128)(2,1)S(1)}, bf16[4,2,384,384]{3,2,1,0:T(8,128)(2,1)}, u32[]{:S(2)}) copy-start(bf16[4,2,384,384]{3,2,1,0:T(8,128)(2,1)} %free.1) | copy-start | bytes 7077892
  147.1 1.4 copy-start.2

commit v2 on v1

v2 whole, which is shorter than its diff:
```python
import jax
import jax.numpy as jnp
from jax import lax
from jax.experimental import pallas as pl
from jax.experimental.pallas import tpu as pltpu
from jax.sharding import Mesh
from jax.sharding import PartitionSpec as P


NB = 384
HALF = NB // 2
BANDS = 64
ROWS = 56
FLAT = BANDS * ROWS
FULL = 60 << 20
F32 = jnp.float32
BF16 = jnp.bfloat16
SWAP = [(0, 1), (1, 0)]
OTHERS = ("y", "xh", "xl", "z")
ENERGY = ("y", "xh", "core")
LAYER = ("xl", "z")
ANY = pl.BlockSpec(memory_space=pl.ANY)
SMEM = pl.BlockSpec(memory_space=pltpu.SMEM)
VMEM = pl.BlockSpec(memory_space=pltpu.VMEM)


def first_index(offsets, value):
    return jnp.where(
        offsets[0] == value, 0, jnp.where(offsets[1] == value, 1, jnp.where(offsets[2] == value, 2, 3))
    )


def offset_roles(offsets):
    top = first_index(offsets, 4)
    bottom = first_index(offsets, -4)
    low = jnp.minimum(top, bottom)
    high = jnp.maximum(top, bottom)
    first = jnp.where(low != 0, 0, jnp.where(high != 1, 1, 2))
    last = jnp.where(high != 3, 3, jnp.where(low != 2, 2, 1))
    return top, bottom, first, last


def spans(offsets, first, last):
    return (jnp.int32(4), jnp.abs(offsets[first]), jnp.abs(offsets[last]))


def cut_body(place, base, sign, own, out, sem):
    copy = pltpu.make_async_copy(own.at[pl.ds(base + sign * place[0], 2)], out, sem)
    copy.start()
    copy.wait()


def cut_call(place, own, base, sign):
    return pl.pallas_call(
        lambda place, own, out, sem: cut_body(place, base, sign, own, out, sem),
        out_shape=jax.ShapeDtypeStruct((2, 2, NB, NB), BF16),
        in_specs=[SMEM, ANY],
        out_specs=VMEM,
        scratch_shapes=[pltpu.SemaphoreType.DMA],
        compiler_params=pltpu.CompilerParams(vmem_limit_bytes=4 << 20),
        cost_estimate=pl.CostEstimate(flops=0, bytes_accessed=2_400_000, transcendentals=0),
    )(place, own)


def polar_pairs(core, near, slots, turned, offsets, each):
    _, _, first, last = offset_roles(offsets)
    for index, span in enumerate(spans(offsets, first, last)):
        base = jnp.clip(4 - span, 0, 2)
        split = jnp.where(core == 0, jnp.maximum(base, 2), jnp.maximum(base, 6 - span))
        outer = (core == 0) == near
        begin = jnp.where(outer, base, split)
        end = jnp.where(outer, split, base + 4)
        if index == 0:
            back = jnp.bool_(False)
        else:
            back = offsets[first if index == 1 else last] < 0
        plain = jnp.where(back, span, 0)
        cross = jnp.where(back, 0, span)

        def block_sum(rows, real, imag):
            def step(s, carry):
                real, imag = carry
                ar = slots[s + plain + 2, 0, rows, :].astype(F32)
                ai = slots[s + plain + 2, 1, rows, :].astype(F32)
                br = turned[s + cross, 0, rows, :]
                bi = turned[s + cross, 1, rows, :]
                return real + (ar * br - ai * bi), imag + (ar * bi + ai * br)

            return lax.fori_loop(begin, end, step, (real, imag))

        each(index, block_sum)


def prepare_body(place, offsets, own, mate, slots, turned, partial, sems):
    core = place[0]
    copies = [
        pltpu.make_async_copy(own, slots.at[pl.ds(4, 4)], sems.at[0]),
        pltpu.make_async_copy(mate, slots.at[pl.ds(8 - 8 * core, 4)], sems.at[1]),
    ]
    for copy in copies:
        copy.start()
    for copy in copies:
        copy.wait()

    @pl.loop(0, 12)
    def _(step):
        slot = step // 2 + 2 - 2 * core
        part = step % 2
        turned[slot, part] = slots[slot + 2, part].astype(F32).T

    def each(index, block_sum):
        @pl.loop(0, NB // 16)
        def _(block):
            rows = pl.ds(pl.multiple_of(block * 16, 16), 16)
            zero = jnp.zeros((16, NB), F32)
            real, imag = block_sum(rows, zero, zero)
            partial[index, 0, rows, :] = real
            partial[index, 1, rows, :] = imag

    polar_pairs(core, False, slots, turned, offsets, each)


def prepare_call(place, offsets, own, mate):
    return pl.pallas_call(
        prepare_body,
        out_shape=(
            jax.ShapeDtypeStruct((12, 2, NB, NB), BF16),
            jax.ShapeDtypeStruct((8, 2, NB, NB), F32),
            jax.ShapeDtypeStruct((3, 2, NB, NB), F32),
        ),
        in_specs=[SMEM, SMEM, ANY, ANY],
        out_specs=(VMEM, VMEM, VMEM),
        scratch_shapes=[pltpu.SemaphoreType.DMA((2,))],
        compiler_params=pltpu.CompilerParams(vmem_limit_bytes=4 << 20),
        cost_estimate=pl.CostEstimate(flops=20_000_000, bytes_accessed=9_000_000, transcendentals=0),
        name="prepare",
    )(place, offsets, own, mate)


def polar_body(place, offsets, near, slots_in, turned_in, partial, slots, turned, send, keep, sem):
    core = place[0]
    copy = pltpu.make_async_copy(near, slots.at[pl.ds(2 + 6 * core, 2)], sem)
    copy.start()
    copy.wait()
    for item in range(2):
        slot = 6 * core + item
        for part in range(2):
            turned[slot, part] = slots[slot + 2, part].astype(F32).T

    def each(index, block_sum):
        for target, half in ((send, 1 - core), (keep, core)):

            @pl.loop(0, HALF // 16)
            def _(block):
                rows = pl.ds(pl.multiple_of(half * HALF + block * 16, 16), 16)
                pair = block_sum(rows, partial[index, 0, rows, :], partial[index, 1, rows, :])
                for part, value in enumerate(pair):
                    for panel in range(3):
                        start = ((index * 2 + part) * 3 + panel) * HALF
                        target[pl.ds(pl.multiple_of(start + block * 16, 16), 16), :] = value[
                            :, panel * 128 : (panel + 1) * 128
                        ].astype(target.dtype)

    polar_pairs(core, True, slots, turned, offsets, each)
    tail = pl.ds(18 * HALF, FLAT - 18 * HALF)
    send[tail, :] = jnp.zeros((FLAT - 18 * HALF, 128), BF16)
    keep[tail, :] = jnp.zeros((FLAT - 18 * HALF, 128), F32)


def polar_call(place, offsets, near, slots, turned, partial):
    return pl.pallas_call(
        polar_body,
        out_shape=(
            jax.ShapeDtypeStruct(slots.shape, BF16),
            jax.ShapeDtypeStruct(turned.shape, F32),
            jax.ShapeDtypeStruct((FLAT, 128), BF16),
            jax.ShapeDtypeStruct((FLAT, 128), F32),
        ),
        in_specs=[SMEM, SMEM, ANY, VMEM, VMEM, VMEM],
        out_specs=(VMEM, VMEM, VMEM, VMEM),
        input_output_aliases={3: 0, 4: 1},
        scratch_shapes=[pltpu.SemaphoreType.DMA],
        compiler_params=pltpu.CompilerParams(vmem_limit_bytes=4 << 20),
        cost_estimate=pl.CostEstimate(flops=20_000_000, bytes_accessed=9_000_000, transcendentals=0),
        name="polar",
    )(place, offsets, near, slots, turned, partial)


def tables_body(free, out):
    for k in range(4):
        fr = free[k, 0]
        fi = free[k, 1]
        out[k, :NB, :NB] = fr
        out[k, :NB, NB:] = fi
        out[k, NB:, :NB] = -fi
        out[k, NB:, NB:] = fr


def tables_call(free):
    return pl.pallas_call(
        tables_body,
        out_shape=jax.ShapeDtypeStruct((4, 2 * NB, 2 * NB), BF16),
        in_specs=[VMEM],
        out_specs=VMEM,
        compiler_params=pltpu.CompilerParams(vmem_limit_bytes=4 << 20),
        cost_estimate=pl.CostEstimate(flops=0, bytes_accessed=7_000_000, transcendentals=0),
        name="tables",
    )(free)


def window_copies(core, own, mate, near, far, slots, sems):
    copies = [
        pltpu.make_async_copy(own, slots.at[pl.ds(4, 4)], sems.at[0]),
        pltpu.make_async_copy(mate, slots.at[pl.ds(8 - 8 * core, 4)], sems.at[1]),
        pltpu.make_async_copy(near, slots.at[pl.ds(2 + 6 * core, 2)], sems.at[2]),
    ]
    if far is not None:
        copies.append(pltpu.make_async_copy(far, slots.at[pl.ds(10 * core, 2)], sems.at[3]))
    return copies


def born_body(early, *refs):
    if early:
        (place, offsets, occupation, coupling, own, mate, near, vertex, out, *rest) = refs
        far = None
    else:
        (place, offsets, occupation, coupling, own, mate, near, far, vertex, out, *rest) = refs
    slots, chosen, mixed, wide, stack, side, total, sems = rest
    core = place[0]
    loads = [
        pltpu.make_async_copy(vertex.at[coupling[0, k]], chosen.at[k], sems.at[4 + k])
        for k in range(4)
    ]
    loads += window_copies(core, own, mate, near, far, slots, sems)
    for load in loads:
        load.start()
    for load in loads:
        load.wait()
    energy = 2 * (1 - core) if early else 2 * core

    @pl.loop(0, 4)
    def _(k):
        vr = chosen[k, 0]
        vi = chosen[k, 1]
        wide[:NB, :NB] = vr
        wide[:NB, NB:] = -vi
        wide[NB:, :NB] = vi
        wide[NB:, NB:] = vr
        side[:NB, :NB] = vr
        side[:NB, NB:] = vi
        side[NB:, :NB] = -vi
        side[NB:, NB:] = vr
        span = offsets[k]
        weight = occupation[k]
        for item in range(2):
            at = energy + 4 + item
            for part in range(2):
                low = slots[at - span, part].astype(F32)
                high = slots[at + span, part].astype(F32)
                value = weight * low + (weight + 1.0) * high
                mixed[part * NB : (part + 1) * NB, item * NB : (item + 1) * NB] = value.astype(BF16)
        half = jnp.dot(wide[...], mixed[...], preferred_element_type=F32).astype(BF16)
        for item in range(2):
            for part in range(2):
                stack[item * NB : (item + 1) * NB, part * NB : (part + 1) * NB] = half[
                    part * NB : (part + 1) * NB, item * NB : (item + 1) * NB
                ]
        term = lax.dot_general(
            stack[...], side[...], (((1,), (1,)), ((), ())), preferred_element_type=F32
        )

        @pl.when(k == 0)
        def _():
            total[...] = term

        @pl.when(k > 0)
        def _():
            total[...] += term

    store = pltpu.make_async_copy(total, out, sems.at[0])
    store.start()
    store.wait()


def born_call(place, offsets, occupation, coupling, arrays, vertex):
    early = len(arrays) == 3
    size = 2 * NB
    return pl.pallas_call(
        lambda *refs: born_body(early, *refs),
        out_shape=jax.ShapeDtypeStruct((size, size), F32),
        in_specs=[SMEM] * 4 + [ANY] * (len(arrays) + 1),
        out_specs=ANY,
        scratch_shapes=[
            pltpu.VMEM((12, 2, NB, NB), BF16),
            pltpu.VMEM((4, 2, NB, NB), BF16),
            pltpu.VMEM((size, size), BF16),
            pltpu.VMEM((size, size), BF16),
            pltpu.VMEM((size, size), BF16),
            pltpu.VMEM((size, size), BF16),
            pltpu.VMEM((size, size), F32),
            pltpu.SemaphoreType.DMA((8,)),
        ],
        compiler_params=pltpu.CompilerParams(vmem_limit_bytes=FULL),
        cost_estimate=pl.CostEstimate(
            flops=16 * size**3, bytes_accessed=12_000_000, transcendentals=0
        ),
        name="born_early" if early else "born_late",
    )(place, offsets, occupation, coupling, *arrays, vertex)


def sum_body(bands, out, buffer, copies, sems):
    loads = [
        pltpu.make_async_copy(bands.at[pl.ds(16 * i, 16)], buffer.at[pl.ds(16 * i, 16)], sems.at[i])
        for i in range(4)
    ]
    for load in loads:
        load.start()
    total = jnp.zeros((ROWS, 128), F32)
    for i, load in enumerate(loads):
        load.wait()
        total = lax.fori_loop(
            16 * i, 16 * i + 16, lambda at, value: value + buffer[at].astype(F32), total
        )
    value = total.astype(BF16)
    for i in range(16):
        copies[i] = value
    stores = [
        pltpu.make_async_copy(copies, out.at[pl.ds(16 * i, 16)], sems.at[i]) for i in range(4)
    ]
    for store in stores:
        store.start()
    for store in stores:
        store.wait()


def sum_call(bands):
    return pl.pallas_call(
        sum_body,
        out_shape=jax.ShapeDtypeStruct(bands.shape, BF16),
        in_specs=[ANY],
        out_specs=ANY,
        scratch_shapes=[
            pltpu.VMEM(bands.shape, BF16),
            pltpu.VMEM((16, ROWS, 128), BF16),
            pltpu.SemaphoreType.DMA((4,)),
        ],
        compiler_params=pltpu.CompilerParams(vmem_limit_bytes=4 << 20),
        cost_estimate=pl.CostEstimate(flops=500_000, bytes_accessed=1_900_000, transcendentals=0),
        name="band_sum",
    )(bands)


def final_body(
    place, offsets, mine, other, tables, own, mate, near, far, early, late, out,
    slots, halves, joined, flipped, table, magnon, born, sems,
):
    core = place[0]
    polar = [
        pltpu.make_async_copy(mine, halves.at[0], sems.at[10]),
        pltpu.make_async_copy(other, halves.at[1], sems.at[11]),
    ]
    free = [pltpu.make_async_copy(tables.at[k], table.at[k], sems.at[k + 6]) for k in range(4)]
    loads = window_copies(core, own, mate, near, far, slots, sems) + [
        pltpu.make_async_copy(early, born.at[0], sems.at[4]),
        pltpu.make_async_copy(late, born.at[1], sems.at[5]),
    ]
    for load in polar + free + loads:
        load.start()
    for load in polar:
        load.wait()
    for item, half in ((0, core), (1, 1 - core)):
        rows = pl.ds(pl.multiple_of(half * HALF, HALF), HALF)
        for index in range(3):
            for part in range(2):
                for panel in range(3):
                    start = ((index * 2 + part) * 3 + panel) * HALF
                    joined[index, rows, part * NB + panel * 128 : part * NB + (panel + 1) * 128] = halves[
                        item, start : start + HALF, :
                    ]

    def product(left, k):
        value = jnp.dot(left[...], table[k], preferred_element_type=F32)
        return value.astype(BF16).astype(F32)

    top, bottom, first, last = offset_roles(offsets)
    for part in range(2):
        columns = slice(part * NB, (part + 1) * NB)
        flipped[:, columns] = joined[0, :, columns].astype(F32).T.astype(BF16)
    for load in free:
        load.wait()
    magnon[1] = product(joined.at[1], first)
    magnon[2] = product(joined.at[2], last)
    magnon[0] = product(joined.at[0], top)
    magnon[0] += product(flipped, bottom)
    for load in loads:
        load.wait()
    reach = spans(offsets, first, last)
    for source, energy in ((0, 2 * (1 - core)), (1, 2 * core)):
        for item in range(2):

            @pl.loop(0, NB // 16)
            def _(block):
                rows = pl.ds(pl.multiple_of(block * 16, 16), 16)
                begin = pl.ds(pl.multiple_of(item * NB + block * 16, 16), 16)
                real = born[source, begin, :NB]
                imag = born[source, begin, NB:]
                at = energy + 4 + item
                for index in range(3):
                    down = at - reach[index]
                    up = at + reach[index]
                    sr = slots[down, 0, rows, :].astype(F32) + slots[up, 0, rows, :].astype(F32)
                    si = slots[down, 1, rows, :].astype(F32) + slots[up, 1, rows, :].astype(F32)
                    mr = magnon[index, rows, :NB]
                    mi = magnon[index, rows, NB:]
                    real += mr * sr - mi * si
                    imag += mr * si + mi * sr
                out[energy + item, 0, 0, rows, :] = real.astype(BF16)
                out[energy + item, 0, 1, rows, :] = imag.astype(BF16)


def final_call(place, offsets, mine, other, tables, own, mate, near, far, early, late):
    return pl.pallas_call(
        final_body,
        out_shape=jax.ShapeDtypeStruct((4, 1, 2, NB, NB), BF16),
        in_specs=[SMEM, SMEM] + [ANY] * 9,
        out_specs=VMEM,
        scratch_shapes=[
            pltpu.VMEM((12, 2, NB, NB), BF16),
            pltpu.VMEM((2, FLAT, 128), BF16),
            pltpu.VMEM((3, NB, 2 * NB), BF16),
            pltpu.VMEM((NB, 2 * NB), BF16),
            pltpu.VMEM((4, 2 * NB, 2 * NB), BF16),
            pltpu.VMEM((3, NB, 2 * NB), F32),
            pltpu.VMEM((2, 2 * NB, 2 * NB), F32),
            pltpu.SemaphoreType.DMA((12,)),
        ],
        compiler_params=pltpu.CompilerParams(vmem_limit_bytes=FULL),
        cost_estimate=pl.CostEstimate(
            flops=2_000_000_000, bytes_accessed=18_000_000, transcendentals=0
        ),
        name="final",
    )(place, offsets, mine, other, tables, own, mate, near, far, early, late)


def per_device(green_blocks, offsets, occupation, coupling, vertex, magnon_free):
    count = lax.axis_size(ENERGY)
    core = lax.axis_index("core").astype(jnp.int32)
    place = core[None]
    own = green_blocks.reshape(4, 2, NB, NB)
    across = [(i, i + 1) for i in range(1, count - 1, 2)]
    across += [(target, source) for source, target in across]
    outer = cut_call(place, own, 0, 2)
    near = lax.ppermute(outer, ENERGY, across)
    mate = lax.ppermute(own, "core", SWAP)
    inner = cut_call(place, own, 2, -2)
    far = lax.ppermute(inner, ENERGY, across)
    slots, turned, partial = prepare_call(place, offsets, own, mate)
    tables = tables_call(magnon_free)
    _, _, send, keep = polar_call(place, offsets, near, slots, turned, partial)
    pair = keep + lax.ppermute(send, "core", SWAP).astype(F32)
    bands = lax.all_to_all(pair.astype(BF16).reshape(BANDS, ROWS, 128), OTHERS, 0, 0, tiled=True)
    early = born_call(place, offsets, occupation, coupling, (own, mate, near), vertex)
    copies = sum_call(bands)
    mine = lax.all_to_all(copies, OTHERS, 0, 0, tiled=True).reshape(FLAT, 128)
    late = born_call(
        place, offsets, occupation, coupling, (own, mate, near, far), vertex
    )
    other = lax.ppermute(mine, "core", SWAP)
    return final_call(place, offsets, mine, other, tables, own, mate, near, far, early, late)


def solution(mesh):
    fine = Mesh(mesh.devices.reshape(4, 2, 2, 2, 4), ("y", "xh", "core", "xl", "z"))
    blocks = P(ENERGY, LAYER, None, None, None)
    placed = (blocks, P(), P(), P(LAYER, None), P(), P())
    return jax.shard_map(
        per_device, mesh=fine, in_specs=placed, out_specs=blocks, check_vma=False
    )
```

time: 161 us -> 162 us (level)
  Pallas kernels: 46.7 us -> 60.4 us
  starting transfers between devices: 70.5 us -> 62.7 us
  other arithmetic: 2.21 us -> 0.24 us
  local copies, waits for them, and re-layouts: 7.89 us -> 6.26 us
    ppermute x1, starting transfers between devices: 29.4 us -> 22.4 us  [per_device(): pair = keep + lax.ppermute(send, 'core', SWAP).astype(F32)]
    pallas_call x1 -> x6, Pallas kernels: 6.86 us -> 13.4 us  [the longest x1 5.71 us: prepare_call(): pl.pallas_call(prepare_body, out_shape=(jax.ShapeDtypeStruct((12, 2, NB,...]
    pallas_call x2, Pallas kernels: 28.1 us -> 34 us  [born_call(): pl.pallas_call(lambda *refs: born_body(early, *refs), out_shape=jax.Shape...]
    unnamed x16 -> x18, local copies, waits for them, and re-layouts: 3.09 us -> 6.26 us
    dynamic_slice x1 -> x0, local copies, waits for them, and re-layouts: 3.03 us -> none  [per_device(): lax.dynamic_slice_in_dim(own, 2 - 2 * core, 2, 0)]
    all_to_all x1, waiting for transfers between devices: 8 us -> 5.51 us  [per_device(): mine = lax.all_to_all(copies, OTHERS, 0, 0, tiled=True).reshape(FLAT, 128)]
    reduce_sum x1 -> x0, other arithmetic: 1.97 us -> none  [per_device(): polar = jnp.sum(bands.astype(F32), axis=0).astype(BF16)]
    broadcast_in_dim x1 -> x0, local copies, waits for them, and re-layouts: 1.77 us -> none  [per_device(): jnp.broadcast_to(polar[None], (BANDS, ROWS, 128))]
  transfers between devices with their start and end apart: 6 -> 6, of which waited for: 3 -> 3; matrix products, arithmetic and copies ran while one was open for 2% -> 0% of each run, Pallas kernels for 17% -> 25%
where the time goes in v2:
time: 162 us; the launch traced here: 161 us
  starting transfers between devices  62.7 us (39%)
  Pallas kernels  60.4 us (37%)
  blocking collectives  22.3 us (14%)
  waiting for transfers between devices  9.32 us (6%)
  local copies, waits for them, and re-layouts  6.26 us (4%)
    pallas_call x2, Pallas kernels, born_call(): pl.pallas_call(lambda *refs: born_body(early, *refs), out_shape=jax.Shape...  34 us
    ppermute x1, starting transfers between devices, per_device(): other = lax.ppermute(mine, 'core', SWAP)  27 us
    ppermute x1, starting transfers between devices, per_device(): pair = keep + lax.ppermute(send, 'core', SWAP).astype(F32)  22.4 us
    all_to_all x1, blocking collectives, per_device(): lax.all_to_all(pair.astype(BF16).reshape(BANDS, ROWS, 128), OTHERS, 0, 0,...  22.3 us
    pallas_call x1, Pallas kernels, final_call(): pl.pallas_call(final_body, out_shape=jax.ShapeDtypeStruct((4, 1, 2, NB, N...  12.9 us
    all_to_all x1, starting transfers between devices, per_device(): mine = lax.all_to_all(copies, OTHERS, 0, 0, tiled=True).reshape(FLAT, 128)  11 us
    unnamed x18, local copies, waits for them, and re-layouts  6.26 us
    pallas_call x1, Pallas kernels, prepare_call(): pl.pallas_call(prepare_body, out_shape=(jax.ShapeDtypeStruct((12, 2, NB,...  5.71 us
  transfers between devices with their start and end apart: 6, of which 3 were waited for; matrix products, arithmetic and copies ran while one was open for 0% of the time, Pallas kernels for 25%

profile of v2, /device:TPU:93, one launch (start us, length us, event | category | flops | bytes accessed | tf_op | source)
XLA Modules:
  0.0 161.4 jit_solution(17145526116162854053)
XLA Ops:
  0.0 0.0 copy-start.6
  0.0 0.7 collective-permute-start.1
  0.7 0.0 copy-start
  0.7 1.7 %copy-done = bf16[4,1,2,384,384]{4,3,2,1,0:T(8,128)(2,1)S(1)} copy-done((bf16[4,1,2,384,384]{4,3,2,1,0:T(8,128)(2,1)S(1)}, bf16[4,1,2,384,384]{4,3,2,1,0:T(8,128)(2,1)}, u32[]{:S(2)}) %copy-start) | copy-done | bytes 2359320
  2.3 0.2 shard_map.64
  2.6 0.7 collective-permute-start
  3.3 1.7 %collective-permute-done.1.mate.refs_5_ = bf16[4,2,384,384]{3,2,1,0:T(8,128)(2,1)S(1)} collective-permute-done((bf16[4,2,384,384]{3,2,1,0:T(8,128)(2,1)}, bf16[4,2,384,384]{3,2,1,0:T(8,128)(2,1)S(1)}, u32[]{:S(2)}, u32[]{:S(2)}) %collective-permute-start.1) | collective-permute-done | bytes 2359328 | tf_op jit(solution)/shard_map/ppermute | solution.py:454
  5.1 0.0 copy-done.6
  5.1 0.0 copy-start.3
  5.1 5.7 %prepare.1 = (bf16[12,2,384,384]{3,2,1,0:T(8,128)(2,1)S(1)}, f32[8,2,384,384]{3,2,1,0:T(8,128)S(1)}, f32[3,2,384,384]{3,2,1,0:T(8,128)S(1)}) custom-call(s32[1]{0:T(128)} %bitcast.place.refs_0_, s32[4]{0:T(128)S(1)} %copy-done.6, bf16[4,2,384,384]{3,2,1,0:T(8,128)(2,1)S(1)} %bitcast.9, bf16[4,2,384,384]{3,2,1,0:T(8,128)(2,1)S(1)} %collective-permute-done.1.mate.refs_5_), custom_call_target="tpu_custom_call" | custom-call | flops 20000000 | bytes 9000000 | tf_op jit(solution)/shard_map/prepare/pallas_call | solution.py:124
  10.8 0.0 copy-done.3
  10.8 0.0 collective-permute-done.near.refs_6_
  10.8 0.0 copy-start.4
  10.8 4.3 %polar.1 = (bf16[12,2,384,384]{3,2,1,0:T(8,128)(2,1)S(1)}, f32[8,2,384,384]{3,2,1,0:T(8,128)S(1)}, bf16[3584,128]{1,0:T(8,128)(2,1)S(1)}, f32[3584,128]{1,0:T(8,128)S(1)}) custom-call(s32[1]{0:T(128)} %bitcast.place.refs_0_, s32[4]{0:T(128)S(1)} %copy-done.6, ...), custom_call_target="tpu_custom_call", output_to_operand_aliasing={{0}: (3, {}), {1}: (4, {})} | custom-call | flops 20000000 | bytes 9000000 | tf_op jit(solution)/shard_map/polar/pallas_call | solution.py:171
  15.2 0.0 copy-done.4
  15.2 22.4 %collective-permute-start.2 = (bf16[3584,128]{1,0:T(8,128)(2,1)S(1)}, bf16[3584,128]{1,0:T(8,128)(2,1)S(1)}, u32[]{:S(2)}, u32[]{:S(2)}) collective-permute-start(bf16[3584,128]{1,0:T(8,128)(2,1)S(1)} %get-tuple-element.14), channel_id=1, source_target_pairs={{0,8},{8,0},{1,9},{9,1},{2,10},{10,2},{3,11},{11,3},{4,12},{12,4},... | collective-permute-start | bytes 2752520 | tf_op jit(solution)/shard_map/ppermute | solution.py:460
  37.5 2.1 %collective-permute-done.2 = bf16[3584,128]{1,0:T(8,128)(2,1)S(1)} collective-permute-done((bf16[3584,128]{1,0:T(8,128)(2,1)S(1)}, bf16[3584,128]{1,0:T(8,128)(2,1)S(1)}, u32[]{:S(2)}, u32[]{:S(2)}) %collective-permute-start.2) | collective-permute-done | bytes 917536 | tf_op jit(solution)/shard_map/ppermute | solution.py:460
  39.6 0.2 add_convert_fusion
  39.9 0.0 copy-start.1
  39.9 22.3 %all_to_all.10.bands = bf16[64,56,128]{2,1,0:T(8,128)(2,1)S(1)} all-to-all(bf16[64,56,128]{2,1,0:T(8,128)(2,1)S(1)} %bitcast.11), channel_id=1, replica_groups=mesh['y'=4,'xh'=2,'core'=2,'xl'=2,'z'=4] {'y','xh','xl','z'}, dimensions={0} | all-to-all | bytes 1835008 | tf_op jit(solution)/shard_map/all_to_all | solution.py:461
  62.2 2.5 %band_sum.1 = bf16[64,56,128]{2,1,0:T(8,128)(2,1)} custom-call(bf16[64,56,128]{2,1,0:T(8,128)(2,1)S(1)} %all_to_all.10.bands), custom_call_target="tpu_custom_call" | custom-call | flops 500000 | bytes 1900000 | tf_op jit(solution)/shard_map/band_sum/pallas_call | solution.py:337
  64.7 11.0 %all-to-all-start.1 = ((bf16[64,56,128]{2,1,0:T(8,128)(2,1)}), bf16[64,56,128]{2,1,0:T(8,128)(2,1)}, u32[]{:S(2)}, u32[]{:S(2)}) async-start(bf16[64,56,128]{2,1,0:T(8,128)(2,1)} %band_sum.1), calls=%async_computation.1 | async-start | bytes 1835008 | tf_op jit(solution)/shard_map/all_to_all | solution.py:464
  75.7 0.0 copy-done.1
  75.7 0.0 copy-start.5
  75.7 0.3 shard_map.65
  76.0 0.9 collective-permute-start.4
  76.8 0.5 copy-done.5
  77.4 0.4 tables.1
  77.8 0.0 copy-start.2
  77.8 2.1 %copy-done.2 = bf16[4,768,768]{2,1,0:T(8,128)(2,1)} copy-done((bf16[4,768,768]{2,1,0:T(8,128)(2,1)}, bf16[4,768,768]{2,1,0:T(8,128)(2,1)S(1)}, u32[]{:S(2)}) %copy-start.2) | copy-done | bytes 4718616
  79.9 5.5 %all-to-all-done.1 = bf16[64,56,128]{2,1,0:T(8,128)(2,1)} async-done(((bf16[64,56,128]{2,1,0:T(8,128)(2,1)}), bf16[64,56,128]{2,1,0:T(8,128)(2,1)}, u32[]{:S(2)}, u32[]{:S(2)}) %all-to-all-start.1) | async-done | bytes 917536 | tf_op jit(solution)/shard_map/all_to_all | solution.py:464
  85.4 27.0 %collective-permute-start.3 = (bf16[3584,128]{1,0:T(8,128)(2,1)}, bf16[3584,128]{1,0:T(8,128)(2,1)S(1)}, u32[]{:S(2)}, u32[]{:S(2)}) collective-permute-start(bf16[3584,128]{1,0:T(8,128)(2,1)} %bitcast.3.mine), channel_id=1, source_target_pairs={{0,8},{8,0},{1,9},{9,1},{2,10},{10,2},{3,11},{11,3},{4,12},{12,4},... | collective-permute-start | bytes 2752520 | tf_op jit(solution)/shard_map/ppermute | solution.py:468
  112.5 16.9 %born_early.1.early = f32[768,768]{1,0:T(8,128)} custom-call(s32[1]{0:T(128)} %bitcast.place.refs_0_, s32[4]{0:T(128)} %offsets.5, f32[4]{0:T(128)} %refs_2_.3, s32[1,4]{1,0:T(1,128)} %refs_3_.3, bf16[4,2,384,384]{3,2,1,0:T(8,128)(2,1)} %bitcast.5, bf16[4,2,384,384]{3,2,1,0:T(8,128)(2,1)} %copy-done.3, bf16[2,2,384,384]{3,2,1,0:T(8,128)(2,1)} %copy-done.4, ...), custom_call_target="tpu_custom_call" | custom-call | flops 7247757312 | bytes 12000000 | tf_op jit(solution)/shard_map/born_early/pallas_call | solution.py:288
  129.3 0.0 collective-permute-done.4.refs_7_.far
  129.4 0.0 copy-start.7
  129.4 1.0 copy-done.7
  130.4 17.1 %born_late.1.late = f32[768,768]{1,0:T(8,128)} custom-call(s32[1]{0:T(128)} %bitcast.place.refs_0_, s32[4]{0:T(128)} %offsets.5, f32[4]{0:T(128)} %refs_2_.3, s32[1,4]{1,0:T(1,128)} %refs_3_.3, bf16[4,2,384,384]{3,2,1,0:T(8,128)(2,1)} %bitcast.6, bf16[4,2,384,384]{3,2,1,0:T(8,128)(2,1)} %copy-done.3, bf16[2,2,384,384]{3,2,1,0:T(8,128)(2,1)} %copy-done.4, ...), custom_call_target="tpu_custom_call" | custom-call | flops 7247757312 | bytes 12000000 | tf_op jit(solution)/shard_map/born_late/pallas_call | solution.py:288
  147.5 0.0 collective-permute-done.3.other
  147.5 0.0 copy-start.8
  147.6 0.9 copy-done.8
  148.5 12.9 %final.1 = bf16[4,1,2,384,384]{4,3,2,1,0:T(8,128)(2,1)} custom-call(s32[1]{0:T(128)} %bitcast.place.refs_0_, s32[4]{0:T(128)} %offsets.5, bf16[3584,128]{1,0:T(8,128)(2,1)} %bitcast.3.mine, bf16[3584,128]{1,0:T(8,128)(2,1)} %copy-done.8, bf16[4,768,768]{2,1,0:T(8,128)(2,1)} %copy-done.2, bf16[4,2,384,384]{3,2,1,0:T(8,128)(2,1)} %bitcast.7, ...), custom_call_target="tpu_custom_call" | custom-call | flops 2000000000 | bytes 18000000 | tf_op jit(solution)/shard_map/final/pallas_call | solution.py:422
Async XLA Ops:
  0.0 5.1 %copy-start.6 = (s32[4]{0:T(128)S(1)}, s32[4]{0:T(128)}, u32[]{:S(2)}) copy-start(s32[4]{0:T(128)} %offsets.5) | copy-start | bytes 52
  0.0 5.0 %collective-permute-start.1 = (bf16[4,2,384,384]{3,2,1,0:T(8,128)(2,1)}, bf16[4,2,384,384]{3,2,1,0:T(8,128)(2,1)S(1)}, u32[]{:S(2)}, u32[]{:S(2)}) collective-permute-start(bf16[4,2,384,384]{3,2,1,0:T(8,128)(2,1)} %bitcast.4), channel_id=1, source_target_pairs={{0,8},{8,0},{1,9},{9,1},{2,10},{10,2},{3,11},{11,3},{4,12},{12,4},... | collective-permute-start | bytes 7077896 | tf_op jit(solution)/shard_map/ppermute | solution.py:454
  0.7 1.7 %copy-start = (bf16[4,1,2,384,384]{4,3,2,1,0:T(8,128)(2,1)S(1)}, bf16[4,1,2,384,384]{4,3,2,1,0:T(8,128)(2,1)}, u32[]{:S(2)}) copy-start(bf16[4,1,2,384,384]{4,3,2,1,0:T(8,128)(2,1)} %param.6) | copy-start | bytes 7077892
  2.6 8.2 %collective-permute-start = (bf16[2,2,384,384]{3,2,1,0:T(8,128)(2,1)S(1)}, bf16[2,2,384,384]{3,2,1,0:T(8,128)(2,1)S(1)}, u32[]{:S(2)}, u32[]{:S(2)}) collective-permute-start(bf16[2,2,384,384]{3,2,1,0:T(8,128)(2,1)S(1)} %shard_map.64), channel_id=1, source_target_pairs={{8,16},{24,32},{40,48},{56,64},{72,80},{88,96},{104,112},{16,8},{3... | collective-permute-start | bytes 3538952 | tf_op jit(solution)/shard_map/ppermute | solution.py:453
  5.1 5.7 %copy-start.3 = (bf16[4,2,384,384]{3,2,1,0:T(8,128)(2,1)}, bf16[4,2,384,384]{3,2,1,0:T(8,128)(2,1)S(1)}, u32[]{:S(2)}) copy-start(bf16[4,2,384,384]{3,2,1,0:T(8,128)(2,1)S(1)} %collective-permute-done.1.mate.refs_5_) | copy-start | bytes 7077892
  10.8 4.4 %copy-start.4 = (bf16[2,2,384,384]{3,2,1,0:T(8,128)(2,1)}, bf16[2,2,384,384]{3,2,1,0:T(8,128)(2,1)S(1)}, u32[]{:S(2)}) copy-start(bf16[2,2,384,384]{3,2,1,0:T(8,128)(2,1)S(1)} %collective-permute-done.near.refs_6_) | copy-start | bytes 3538948
  15.2 24.5 %collective-permute-start.2 = (bf16[3584,128]{1,0:T(8,128)(2,1)S(1)}, bf16[3584,128]{1,0:T(8,128)(2,1)S(1)}, u32[]{:S(2)}, u32[]{:S(2)}) collective-permute-start(bf16[3584,128]{1,0:T(8,128)(2,1)S(1)} %get-tuple-element.14), channel_id=1, source_target_pairs={{0,8},{8,0},{1,9},{9,1},{2,10},{10,2},{3,11},{11,3},{4,12},{12,4},... | collective-permute-start | bytes 2752520 | tf_op jit(solution)/shard_map/ppermute | solution.py:460
  39.9 35.8 %copy-start.1 = (bf16[4,1,2,384,384]{4,3,2,1,0:T(8,128)(2,1)S(1)}, bf16[4,1,2,384,384]{4,3,2,1,0:T(8,128)(2,1)}, u32[]{:S(2)}) copy-start(bf16[4,1,2,384,384]{4,3,2,1,0:T(8,128)(2,1)} %param.6) | copy-start | bytes 7077892
  64.7 20.7 %all-to-all-start.1 = ((bf16[64,56,128]{2,1,0:T(8,128)(2,1)}), bf16[64,56,128]{2,1,0:T(8,128)(2,1)}, u32[]{:S(2)}, u32[]{:S(2)}) async-start(bf16[64,56,128]{2,1,0:T(8,128)(2,1)} %band_sum.1), calls=%async_computation.1 | async-start | bytes 1835008 | tf_op jit(solution)/shard_map/all_to_all | solution.py:464
  75.7 1.7 %copy-start.5 = (bf16[4,2,384,384]{3,2,1,0:T(8,128)(2,1)S(1)}, bf16[4,2,384,384]{3,2,1,0:T(8,128)(2,1)}, u32[]{:S(2)}) copy-start(bf16[4,2,384,384]{3,2,1,0:T(8,128)(2,1)} %free.1) | copy-start | bytes 7077892
  76.0 53.4 %collective-permute-start.4 = (bf16[2,2,384,384]{3,2,1,0:T(8,128)(2,1)S(1)}, bf16[2,2,384,384]{3,2,1,0:T(8,128)(2,1)S(1)}, u32[]{:S(2)}, u32[]{:S(2)}) collective-permute-start(bf16[2,2,384,384]{3,2,1,0:T(8,128)(2,1)S(1)} %shard_map.65), channel_id=1, source_target_pairs={{8,16},{24,32},{40,48},{56,64},{72,80},{88,96},{104,112},{16,8},{3... | collective-permute-start | bytes 3538952 | tf_op jit(solution)/shard_map/ppermute | solution.py:456
  77.8 2.1 %copy-start.2 = (bf16[4,768,768]{2,1,0:T(8,128)(2,1)}, bf16[4,768,768]{2,1,0:T(8,128)(2,1)S(1)}, u32[]{:S(2)}) copy-start(bf16[4,768,768]{2,1,0:T(8,128)(2,1)S(1)} %tables.1) | copy-start | bytes 14155780
  85.4 62.1 %collective-permute-start.3 = (bf16[3584,128]{1,0:T(8,128)(2,1)}, bf16[3584,128]{1,0:T(8,128)(2,1)S(1)}, u32[]{:S(2)}, u32[]{:S(2)}) collective-permute-start(bf16[3584,128]{1,0:T(8,128)(2,1)} %bitcast.3.mine), channel_id=1, source_target_pairs={{0,8},{8,0},{1,9},{9,1},{2,10},{10,2},{3,11},{11,3},{4,12},{12,4},... | collective-permute-start | bytes 2752520 | tf_op jit(solution)/shard_map/ppermute | solution.py:468
  129.4 1.0 copy-start.7
  147.5 0.9 copy-start.8

commit v3 on v2

--- a/solution.py
+++ b/solution.py
@@ -24,6 +24,10 @@
 VMEM = pl.BlockSpec(memory_space=pltpu.VMEM)
 
 
+def in_hbm(array):
+    return pltpu.with_memory_space_constraint(array, pltpu.HBM)
+
+
 def first_index(offsets, value):
     return jnp.where(
         offsets[0] == value, 0, jnp.where(offsets[1] == value, 1, jnp.where(offsets[2] == value, 2, 3))
@@ -137,7 +141,25 @@
     )(place, offsets, own, mate)
 
 
-def polar_body(place, offsets, near, slots_in, turned_in, partial, slots, turned, send, keep, sem):
+def polar_half(core, half, offsets, slots, turned, partial, target):
+    def each(index, block_sum):
+        @pl.loop(0, HALF // 16)
+        def _(block):
+            rows = pl.ds(pl.multiple_of(half * HALF + block * 16, 16), 16)
+            pair = block_sum(rows, partial[index, 0, rows, :], partial[index, 1, rows, :])
+            for part, value in enumerate(pair):
+                for panel in range(3):
+                    start = ((index * 2 + part) * 3 + panel) * HALF
+                    target[pl.ds(pl.multiple_of(start + block * 16, 16), 16), :] = value[
+                        :, panel * 128 : (panel + 1) * 128
+                    ].astype(target.dtype)
+
+    polar_pairs(core, True, slots, turned, offsets, each)
+    tail = pl.ds(18 * HALF, FLAT - 18 * HALF)
+    target[tail, :] = jnp.zeros((FLAT - 18 * HALF, 128), target.dtype)
+
+
+def polar_send_body(place, offsets, near, slots_in, turned_in, partial, slots, turned, send, sem):
     core = place[0]
     copy = pltpu.make_async_copy(near, slots.at[pl.ds(2 + 6 * core, 2)], sem)
     copy.start()
@@ -146,44 +168,42 @@
         slot = 6 * core + item
         for part in range(2):
             turned[slot, part] = slots[slot + 2, part].astype(F32).T
-
-    def each(index, block_sum):
-        for target, half in ((send, 1 - core), (keep, core)):
-
-            @pl.loop(0, HALF // 16)
-            def _(block):
-                rows = pl.ds(pl.multiple_of(half * HALF + block * 16, 16), 16)
-                pair = block_sum(rows, partial[index, 0, rows, :], partial[index, 1, rows, :])
-                for part, value in enumerate(pair):
-                    for panel in range(3):
-                        start = ((index * 2 + part) * 3 + panel) * HALF
-                        target[pl.ds(pl.multiple_of(start + block * 16, 16), 16), :] = value[
-                            :, panel * 128 : (panel + 1) * 128
-                        ].astype(target.dtype)
-
-    polar_pairs(core, True, slots, turned, offsets, each)
-    tail = pl.ds(18 * HALF, FLAT - 18 * HALF)
-    send[tail, :] = jnp.zeros((FLAT - 18 * HALF, 128), BF16)
-    keep[tail, :] = jnp.zeros((FLAT - 18 * HALF, 128), F32)
-
-
-def polar_call(place, offsets, near, slots, turned, partial):
-    return pl.pallas_call(
-        polar_body,
+    polar_half(core, 1 - core, offsets, slots, turned, partial, send)
+
+
+def polar_keep_body(place, offsets, slots, turned, partial, keep):
+    core = place[0]
+    polar_half(core, core, offsets, slots, turned, partial, keep)
+
+
+def polar_send_call(place, offsets, near, slots, turned, partial):
+    return pl.pallas_call(
+        polar_send_body,
         out_shape=(
             jax.ShapeDtypeStruct(slots.shape, BF16),
             jax.ShapeDtypeStruct(turned.shape, F32),
             jax.ShapeDtypeStruct((FLAT, 128), BF16),
-            jax.ShapeDtypeStruct((FLAT, 128), F32),
         ),
         in_specs=[SMEM, SMEM, ANY, VMEM, VMEM, VMEM],
-        out_specs=(VMEM, VMEM, VMEM, VMEM),
+        out_specs=(VMEM, VMEM, VMEM),
         input_output_aliases={3: 0, 4: 1},
         scratch_shapes=[pltpu.SemaphoreType.DMA],
         compiler_params=pltpu.CompilerParams(vmem_limit_bytes=4 << 20),
         cost_estimate=pl.CostEstimate(flops=20_000_000, bytes_accessed=9_000_000, transcendentals=0),
-        name="polar",
+        name="polar_send",
     )(place, offsets, near, slots, turned, partial)
+
+
+def polar_keep_call(place, offsets, slots, turned, partial):
+    return pl.pallas_call(
+        polar_keep_body,
+        out_shape=jax.ShapeDtypeStruct((FLAT, 128), F32),
+        in_specs=[SMEM, SMEM, VMEM, VMEM, VMEM],
+        out_specs=VMEM,
+        compiler_params=pltpu.CompilerParams(vmem_limit_bytes=4 << 20),
+        cost_estimate=pl.CostEstimate(flops=20_000_000, bytes_accessed=9_000_000, transcendentals=0),
+        name="polar_keep",
+    )(place, offsets, slots, turned, partial)
 
 
 def tables_body(free, out):
@@ -225,21 +245,30 @@
         far = None
     else:
         (place, offsets, occupation, coupling, own, mate, near, far, vertex, out, *rest) = refs
-    slots, chosen, mixed, wide, stack, side, total, sems = rest
+    chosen, lows, highs, mixed, wide, stack, side, total, sems = rest
     core = place[0]
-    loads = [
-        pltpu.make_async_copy(vertex.at[coupling[0, k]], chosen.at[k], sems.at[4 + k])
-        for k in range(4)
-    ]
-    loads += window_copies(core, own, mate, near, far, slots, sems)
-    for load in loads:
-        load.start()
-    for load in loads:
-        load.wait()
     energy = 2 * (1 - core) if early else 2 * core
+
+    def fetch(slot, target, sem):
+        sources = [(own, 4, 4), (mate, 8 - 8 * core, 4), (near, 2 + 6 * core, 2)]
+        if far is not None:
+            sources.append((far, 10 * core, 2))
+        for source, low, size in sources:
+
+            @pl.when((slot >= low) & (slot < low + size))
+            def _():
+                pltpu.make_async_copy(source.at[slot - low], target, sem).start()
+
+    for k in range(4):
+        pltpu.make_async_copy(vertex.at[coupling[0, k]], chosen.at[k], sems.at[k, 4]).start()
+        for item in range(2):
+            at = energy + 4 + item
+            fetch(at - offsets[k], lows.at[k, item], sems.at[k, 2 * item])
+            fetch(at + offsets[k], highs.at[k, item], sems.at[k, 2 * item + 1])
 
     @pl.loop(0, 4)
     def _(k):
+        pltpu.make_async_copy(vertex.at[0], chosen.at[k], sems.at[k, 4]).wait()
         vr = chosen[k, 0]
         vi = chosen[k, 1]
         wide[:NB, :NB] = vr
@@ -250,13 +279,14 @@
         side[:NB, NB:] = vi
         side[NB:, :NB] = -vi
         side[NB:, NB:] = vr
-        span = offsets[k]
         weight = occupation[k]
         for item in range(2):
-            at = energy + 4 + item
+            pltpu.make_async_copy(own.at[0], lows.at[k, item], sems.at[k, 2 * item]).wait()
+            pltpu.make_async_copy(own.at[0], highs.at[k, item], sems.at[k, 2 * item + 1]).wait()
+        for item in range(2):
             for part in range(2):
-                low = slots[at - span, part].astype(F32)
-                high = slots[at + span, part].astype(F32)
+                low = lows[k, item, part].astype(F32)
+                high = highs[k, item, part].astype(F32)
                 value = weight * low + (weight + 1.0) * high
                 mixed[part * NB : (part + 1) * NB, item * NB : (item + 1) * NB] = value.astype(BF16)
         half = jnp.dot(wide[...], mixed[...], preferred_element_type=F32).astype(BF16)
@@ -277,7 +307,7 @@
         def _():
             total[...] += term
 
-    store = pltpu.make_async_copy(total, out, sems.at[0])
+    store = pltpu.make_async_copy(total, out, sems.at[0, 0])
     store.start()
     store.wait()
 
@@ -291,14 +321,15 @@
         in_specs=[SMEM] * 4 + [ANY] * (len(arrays) + 1),
         out_specs=ANY,
         scratch_shapes=[
-            pltpu.VMEM((12, 2, NB, NB), BF16),
             pltpu.VMEM((4, 2, NB, NB), BF16),
+            pltpu.VMEM((4, 2, 2, NB, NB), BF16),
+            pltpu.VMEM((4, 2, 2, NB, NB), BF16),
             pltpu.VMEM((size, size), BF16),
             pltpu.VMEM((size, size), BF16),
             pltpu.VMEM((size, size), BF16),
             pltpu.VMEM((size, size), BF16),
             pltpu.VMEM((size, size), F32),
-            pltpu.SemaphoreType.DMA((8,)),
+            pltpu.SemaphoreType.DMA((4, 5)),
         ],
         compiler_params=pltpu.CompilerParams(vmem_limit_bytes=FULL),
         cost_estimate=pl.CostEstimate(
@@ -350,96 +381,136 @@
     )(bands)
 
 
-def final_body(
-    place, offsets, mine, other, tables, own, mate, near, far, early, late, out,
-    slots, halves, joined, flipped, table, magnon, born, sems,
+def half_products(offsets, half, source, joined, table, magnon, bottom_sum):
+    for index in range(3):
+        for part in range(2):
+            for panel in range(3):
+                start = ((index * 2 + part) * 3 + panel) * HALF
+                joined[index, :, part * NB + panel * 128 : part * NB + (panel + 1) * 128] = source[
+                    start : start + HALF, :
+                ]
+    top, bottom, first, last = offset_roles(offsets)
+    rows = pl.ds(pl.multiple_of(half * HALF, HALF), HALF)
+    for index, k in enumerate((top, first, last)):
+        value = jnp.dot(joined[index], table[k], preferred_element_type=F32)
+        magnon[index, rows, :] = value.astype(BF16).astype(F32)
+    for part in range(2):
+        turned = joined[0, :, part * NB : (part + 1) * NB].astype(F32).T.astype(BF16)
+        begin = pl.ds(pl.multiple_of(part * NB + half * HALF, HALF), HALF)
+        bottom_sum[...] += jnp.dot(turned, table[bottom, begin, :], preferred_element_type=F32)
+
+
+def start_body(
+    place, offsets, mine, tables, own, mate, near, far, early, late,
+    slots, table, born, magnon, bottom_sum, source, joined, sems,
 ):
     core = place[0]
-    polar = [
-        pltpu.make_async_copy(mine, halves.at[0], sems.at[10]),
-        pltpu.make_async_copy(other, halves.at[1], sems.at[11]),
-    ]
+    ready = pltpu.make_async_copy(mine, source, sems.at[10])
     free = [pltpu.make_async_copy(tables.at[k], table.at[k], sems.at[k + 6]) for k in range(4)]
     loads = window_copies(core, own, mate, near, far, slots, sems) + [
         pltpu.make_async_copy(early, born.at[0], sems.at[4]),
         pltpu.make_async_copy(late, born.at[1], sems.at[5]),
     ]
-    for load in polar + free + loads:
+    for load in [ready] + free + loads:
         load.start()
-    for load in polar:
+    bottom_sum[...] = jnp.zeros_like(bottom_sum)
+    for load in [ready] + free:
         load.wait()
-    for item, half in ((0, core), (1, 1 - core)):
-        rows = pl.ds(pl.multiple_of(half * HALF, HALF), HALF)
-        for index in range(3):
-            for part in range(2):
-                for panel in range(3):
-                    start = ((index * 2 + part) * 3 + panel) * HALF
-                    joined[index, rows, part * NB + panel * 128 : part * NB + (panel + 1) * 128] = halves[
-                        item, start : start + HALF, :
-                    ]
-
-    def product(left, k):
-        value = jnp.dot(left[...], table[k], preferred_element_type=F32)
-        return value.astype(BF16).astype(F32)
-
-    top, bottom, first, last = offset_roles(offsets)
-    for part in range(2):
-        columns = slice(part * NB, (part + 1) * NB)
-        flipped[:, columns] = joined[0, :, columns].astype(F32).T.astype(BF16)
-    for load in free:
-        load.wait()
-    magnon[1] = product(joined.at[1], first)
-    magnon[2] = product(joined.at[2], last)
-    magnon[0] = product(joined.at[0], top)
-    magnon[0] += product(flipped, bottom)
+    half_products(offsets, core, source, joined, table, magnon, bottom_sum)
     for load in loads:
         load.wait()
+
+
+def start_call(place, offsets, mine, tables, own, mate, near, far, early, late):
+    size = 2 * NB
+    return pl.pallas_call(
+        start_body,
+        out_shape=(
+            jax.ShapeDtypeStruct((12, 2, NB, NB), BF16),
+            jax.ShapeDtypeStruct((4, size, size), BF16),
+            jax.ShapeDtypeStruct((2, size, size), F32),
+            jax.ShapeDtypeStruct((3, NB, size), F32),
+            jax.ShapeDtypeStruct((NB, size), F32),
+        ),
+        in_specs=[SMEM, SMEM] + [ANY] * 8,
+        out_specs=(VMEM,) * 5,
+        scratch_shapes=[
+            pltpu.VMEM((FLAT, 128), BF16),
+            pltpu.VMEM((3, HALF, size), BF16),
+            pltpu.SemaphoreType.DMA((11,)),
+        ],
+        compiler_params=pltpu.CompilerParams(vmem_limit_bytes=8 << 20),
+        cost_estimate=pl.CostEstimate(
+            flops=1_000_000_000, bytes_accessed=18_000_000, transcendentals=0
+        ),
+        name="final_start",
+    )(place, offsets, mine, *(in_hbm(x) for x in (tables, own, mate, near, far, early, late)))
+
+
+def final_body(
+    place, offsets, other, slots, table, born, magnon_in, sum_in, out, magnon, bottom_sum,
+    source, joined, result, sems,
+):
+    core = place[0]
+    ready = pltpu.make_async_copy(other, source, sems.at[4])
+    ready.start()
+    ready.wait()
+    half_products(offsets, 1 - core, source, joined, table, magnon, bottom_sum)
+    magnon[0] += bottom_sum[...].astype(BF16).astype(F32)
+    _, _, first, last = offset_roles(offsets)
     reach = spans(offsets, first, last)
-    for source, energy in ((0, 2 * (1 - core)), (1, 2 * core)):
-        for item in range(2):
-
-            @pl.loop(0, NB // 16)
-            def _(block):
-                rows = pl.ds(pl.multiple_of(block * 16, 16), 16)
-                begin = pl.ds(pl.multiple_of(item * NB + block * 16, 16), 16)
-                real = born[source, begin, :NB]
-                imag = born[source, begin, NB:]
-                at = energy + 4 + item
-                for index in range(3):
-                    down = at - reach[index]
-                    up = at + reach[index]
-                    sr = slots[down, 0, rows, :].astype(F32) + slots[up, 0, rows, :].astype(F32)
-                    si = slots[down, 1, rows, :].astype(F32) + slots[up, 1, rows, :].astype(F32)
-                    mr = magnon[index, rows, :NB]
-                    mi = magnon[index, rows, NB:]
-                    real += mr * sr - mi * si
-                    imag += mr * si + mi * sr
-                out[energy + item, 0, 0, rows, :] = real.astype(BF16)
-                out[energy + item, 0, 1, rows, :] = imag.astype(BF16)
-
-
-def final_call(place, offsets, mine, other, tables, own, mate, near, far, early, late):
+    stores = []
+    for item, energy in enumerate((2 - 2 * core, 3 - 2 * core, 2 * core, 2 * core + 1)):
+
+        @pl.loop(0, NB // 16)
+        def _(block):
+            rows = pl.ds(pl.multiple_of(block * 16, 16), 16)
+            begin = pl.ds(pl.multiple_of((item % 2) * NB + block * 16, 16), 16)
+            real = born[item // 2, begin, :NB]
+            imag = born[item // 2, begin, NB:]
+            for index in range(3):
+                down = energy + 4 - reach[index]
+                up = energy + 4 + reach[index]
+                sr = slots[down, 0, rows, :].astype(F32) + slots[up, 0, rows, :].astype(F32)
+                si = slots[down, 1, rows, :].astype(F32) + slots[up, 1, rows, :].astype(F32)
+                mr = magnon[index, rows, :NB]
+                mi = magnon[index, rows, NB:]
+                real += mr * sr - mi * si
+                imag += mr * si + mi * sr
+            result[item, 0, rows, :] = real.astype(BF16)
+            result[item, 1, rows, :] = imag.astype(BF16)
+
+        store = pltpu.make_async_copy(result.at[item], out.at[energy, 0], sems.at[item])
+        store.start()
+        stores.append(store)
+    for store in stores:
+        store.wait()
+
+
+def final_call(place, offsets, other, slots, table, born, magnon, bottom_sum):
+    size = 2 * NB
     return pl.pallas_call(
         final_body,
-        out_shape=jax.ShapeDtypeStruct((4, 1, 2, NB, NB), BF16),
-        in_specs=[SMEM, SMEM] + [ANY] * 9,
-        out_specs=VMEM,
+        out_shape=(
+            jax.ShapeDtypeStruct((4, 1, 2, NB, NB), BF16),
+            jax.ShapeDtypeStruct(magnon.shape, F32),
+            jax.ShapeDtypeStruct(bottom_sum.shape, F32),
+        ),
+        in_specs=[SMEM, SMEM, ANY] + [VMEM] * 5,
+        out_specs=(ANY, VMEM, VMEM),
+        input_output_aliases={6: 1, 7: 2},
         scratch_shapes=[
-            pltpu.VMEM((12, 2, NB, NB), BF16),
-            pltpu.VMEM((2, FLAT, 128), BF16),
-            pltpu.VMEM((3, NB, 2 * NB), BF16),
-            pltpu.VMEM((NB, 2 * NB), BF16),
-            pltpu.VMEM((4, 2 * NB, 2 * NB), BF16),
-            pltpu.VMEM((3, NB, 2 * NB), F32),
-            pltpu.VMEM((2, 2 * NB, 2 * NB), F32),
-            pltpu.SemaphoreType.DMA((12,)),
+            pltpu.VMEM((FLAT, 128), BF16),
+            pltpu.VMEM((3, HALF, size), BF16),
+            pltpu.VMEM((4, 2, NB, NB), BF16),
+            pltpu.SemaphoreType.DMA((5,)),
         ],
-        compiler_params=pltpu.CompilerParams(vmem_limit_bytes=FULL),
+        compiler_params=pltpu.CompilerParams(vmem_limit_bytes=12 << 20),
         cost_estimate=pl.CostEstimate(
-            flops=2_000_000_000, bytes_accessed=18_000_000, transcendentals=0
+            flops=1_000_000_000, bytes_accessed=18_000_000, transcendentals=0
         ),
         name="final",
-    )(place, offsets, mine, other, tables, own, mate, near, far, early, late)
+    )(place, offsets, other, slots, table, born, magnon, bottom_sum)[0]
 
 
 def per_device(green_blocks, offsets, occupation, coupling, vertex, magnon_free):
@@ -456,8 +527,9 @@
     far = lax.ppermute(inner, ENERGY, across)
     slots, turned, partial = prepare_call(place, offsets, own, mate)
     tables = tables_call(magnon_free)
-    _, _, send, keep = polar_call(place, offsets, near, slots, turned, partial)
-    pair = keep + lax.ppermute(send, "core", SWAP).astype(F32)
+    slots, turned, send = polar_send_call(place, offsets, near, slots, turned, partial)
+    sent = lax.ppermute(send, "core", SWAP)
+    pair = polar_keep_call(place, offsets, slots, turned, partial) + sent.astype(F32)
     bands = lax.all_to_all(pair.astype(BF16).reshape(BANDS, ROWS, 128), OTHERS, 0, 0, tiled=True)
     early = born_call(place, offsets, occupation, coupling, (own, mate, near), vertex)
     copies = sum_call(bands)
@@ -466,7 +538,8 @@
         place, offsets, occupation, coupling, (own, mate, near, far), vertex
     )
     other = lax.ppermute(mine, "core", SWAP)
-    return final_call(place, offsets, mine, other, tables, own, mate, near, far, early, late)
+    held = start_call(place, offsets, mine, tables, own, mate, near, far, early, late)
+    return final_call(place, offsets, other, *held)
 
 
 def solution(mesh):

time: 162 us -> 159 us (0.981)
  the two profiles are of different devices: /device:TPU:93 before, /device:TPU:77 now
where the time goes in v3:
time: 159 us; the launch traced here: 158 us
  Pallas kernels  62 us (39%)
  starting transfers between devices  45 us (28%)
  waiting for transfers between devices  24.8 us (16%)
  blocking collectives  21.3 us (13%)
  local copies, waits for them, and re-layouts  4.82 us (3%)
    pallas_call x2, Pallas kernels, born_call(): pl.pallas_call(lambda *refs: born_body(early, *refs), out_shape=jax.Shape...  32.9 us
    ppermute x1, starting transfers between devices, per_device(): other = lax.ppermute(mine, 'core', SWAP)  26.6 us
    ppermute x1, waiting for transfers between devices, per_device(): near = lax.ppermute(outer, ENERGY, across)  23.2 us
    all_to_all x1, blocking collectives, per_device(): lax.all_to_all(pair.astype(BF16).reshape(BANDS, ROWS, 128), OTHERS, 0, 0,...  21.3 us
    all_to_all x1, starting transfers between devices, per_device(): mine = lax.all_to_all(copies, OTHERS, 0, 0, tiled=True).reshape(FLAT, 128)  9.44 us
    pallas_call x1, Pallas kernels, final_call(): pl.pallas_call(final_body, out_shape=(jax.ShapeDtypeStruct((4, 1, 2, NB,...  7.24 us
    pallas_call x1, Pallas kernels, start_call(): pl.pallas_call(start_body, out_shape=(jax.ShapeDtypeStruct((12, 2, NB, NB...  6.66 us
    pallas_call x1, Pallas kernels, prepare_call(): pl.pallas_call(prepare_body, out_shape=(jax.ShapeDtypeStruct((12, 2, NB,...  5.71 us
  transfers between devices with their start and end apart: 6, of which 3 were waited for; matrix products, arithmetic and copies ran while one was open for 0% of the time, Pallas kernels for 31%

profile of v3, /device:TPU:77, one launch (start us, length us, event | category | flops | bytes accessed | tf_op | source)
XLA Modules:
  0.0 158.4 jit_solution(2527778087173195267)
XLA Ops:
  0.0 0.0 copy-start.6
  0.0 0.7 collective-permute-start.1
  0.7 0.0 copy-start
  0.7 1.7 %copy-done = bf16[4,1,2,384,384]{4,3,2,1,0:T(8,128)(2,1)S(1)} copy-done((bf16[4,1,2,384,384]{4,3,2,1,0:T(8,128)(2,1)S(1)}, bf16[4,1,2,384,384]{4,3,2,1,0:T(8,128)(2,1)}, u32[]{:S(2)}) %copy-start) | copy-done | bytes 2359320
  2.3 0.2 shard_map.64
  2.6 3.0 %collective-permute-start = (bf16[2,2,384,384]{3,2,1,0:T(8,128)(2,1)S(1)}, bf16[2,2,384,384]{3,2,1,0:T(8,128)(2,1)S(1)}, u32[]{:S(2)}, u32[]{:S(2)}) collective-permute-start(bf16[2,2,384,384]{3,2,1,0:T(8,128)(2,1)S(1)} %shard_map.64), channel_id=1, source_target_pairs={{8,16},{24,32},{40,48},{56,64},{72,80},{88,96},{104,112},{16,8},{3... | collective-permute-start | bytes 3538952 | tf_op jit(solution)/shard_map/ppermute | solution.py:524
  5.7 0.0 collective-permute-done.1.mate.refs_5_
  5.7 0.0 copy-done.6
  5.7 0.0 copy-start.3
  5.7 5.7 %prepare.1 = (bf16[12,2,384,384]{3,2,1,0:T(8,128)(2,1)S(1)}, f32[8,2,384,384]{3,2,1,0:T(8,128)S(1)}, f32[3,2,384,384]{3,2,1,0:T(8,128)S(1)}) custom-call(s32[1]{0:T(128)} %bitcast.place.refs_0_, s32[4]{0:T(128)S(1)} %copy-done.6, bf16[4,2,384,384]{3,2,1,0:T(8,128)(2,1)S(1)} %bitcast.9, bf16[4,2,384,384]{3,2,1,0:T(8,128)(2,1)S(1)} %collective-permute-done.1.mate.refs_5_), custom_call_target="tpu_custom_call" | custom-call | flops 20000000 | bytes 9000000 | tf_op jit(solution)/shard_map/prepare/pallas_call | solution.py:128
  11.4 0.0 copy-done.3
  11.4 23.2 %collective-permute-done.near.refs_6_ = bf16[2,2,384,384]{3,2,1,0:T(8,128)(2,1)S(1)} collective-permute-done((bf16[2,2,384,384]{3,2,1,0:T(8,128)(2,1)S(1)}, bf16[2,2,384,384]{3,2,1,0:T(8,128)(2,1)S(1)}, u32[]{:S(2)}, u32[]{:S(2)}) %collective-permute-start) | collective-permute-done | bytes 1179680 | tf_op jit(solution)/shard_map/ppermute | solution.py:524
  34.6 0.0 copy-start.4
  34.6 2.9 %polar_send.1 = (bf16[12,2,384,384]{3,2,1,0:T(8,128)(2,1)S(1)}, f32[8,2,384,384]{3,2,1,0:T(8,128)S(1)}, bf16[3584,128]{1,0:T(8,128)(2,1)S(1)}) custom-call(s32[1]{0:T(128)} %bitcast.place.refs_0_, s32[4]{0:T(128)S(1)} %copy-done.6, bf16[2,2,384,384]{3,2,1,0:T(8,128)(2,1)S(1)} %collective-permute-done.near.refs_6_, ...), custom_call_target="tpu_custom_call", output_to_operand_aliasing={{0}: (3, {}), {1}: (4, {})} | custom-call | flops 20000000 | bytes 9000000 | tf_op jit(solution)/shard_map/polar_send/pallas_call | solution.py:180
  37.5 0.0 copy-done.4
  37.5 0.1 collective-permute-start.2
  37.6 2.0 %polar_keep.1 = f32[3584,128]{1,0:T(8,128)S(1)} custom-call(s32[1]{0:T(128)} %bitcast.place.refs_0_, s32[4]{0:T(128)S(1)} %copy-done.6, bf16[12,2,384,384]{3,2,1,0:T(8,128)(2,1)S(1)} %get-tuple-element.20.slots, f32[8,2,384,384]{3,2,1,0:T(8,128)S(1)} %get-tuple-element.21.turned, f32[3,2,384,384]{3,2,1,0:T(8,128)S(1)} %get-tuple-element.19.partial), custom_call_target="tpu_custom_call" | custom-call | flops 20000000 | bytes 9000000 | tf_op jit(solution)/shard_map/polar_keep/pallas_call | solution.py:198
  39.6 0.4 collective-permute-done.2
  40.0 0.2 add_convert_fusion
  40.2 0.0 copy-start.1
  40.2 21.3 %all_to_all.10.bands = bf16[64,56,128]{2,1,0:T(8,128)(2,1)S(1)} all-to-all(bf16[64,56,128]{2,1,0:T(8,128)(2,1)S(1)} %bitcast.13), channel_id=1, replica_groups=mesh['y'=4,'xh'=2,'core'=2,'xl'=2,'z'=4] {'y','xh','xl','z'}, dimensions={0} | all-to-all | bytes 1835008 | tf_op jit(solution)/shard_map/all_to_all | solution.py:533
  61.5 2.6 %band_sum.1 = bf16[64,56,128]{2,1,0:T(8,128)(2,1)} custom-call(bf16[64,56,128]{2,1,0:T(8,128)(2,1)S(1)} %all_to_all.10.bands), custom_call_target="tpu_custom_call" | custom-call | flops 500000 | bytes 1900000 | tf_op jit(solution)/shard_map/band_sum/pallas_call | solution.py:368
  64.1 9.4 %all-to-all-start.1 = ((bf16[64,56,128]{2,1,0:T(8,128)(2,1)}), bf16[64,56,128]{2,1,0:T(8,128)(2,1)S(1)}, u32[]{:S(2)}, u32[]{:S(2)}) async-start(bf16[64,56,128]{2,1,0:T(8,128)(2,1)} %band_sum.1), calls=%async_computation.1 | async-start | bytes 1835008 | tf_op jit(solution)/shard_map/all_to_all | solution.py:536
  73.5 0.0 copy-done.1
  73.5 0.0 copy-start.5
  73.5 1.3 shard_map.65
  74.9 5.2 %collective-permute-start.4 = (bf16[2,2,384,384]{3,2,1,0:T(8,128)(2,1)}, bf16[2,2,384,384]{3,2,1,0:T(8,128)(2,1)S(1)}, u32[]{:S(2)}, u32[]{:S(2)}) collective-permute-start(bf16[2,2,384,384]{3,2,1,0:T(8,128)(2,1)} %shard_map.65), channel_id=1, source_target_pairs={{8,16},{24,32},{40,48},{56,64},{72,80},{88,96},{104,112},{16,8},{3... | collective-permute-start | bytes 3538952 | tf_op jit(solution)/shard_map/ppermute | solution.py:527
  80.0 0.0 copy-done.5
  80.1 0.4 tables.1
  80.5 0.0 copy-start.2
  80.5 2.1 %copy-done.2 = bf16[4,768,768]{2,1,0:T(8,128)(2,1)} copy-done((bf16[4,768,768]{2,1,0:T(8,128)(2,1)}, bf16[4,768,768]{2,1,0:T(8,128)(2,1)S(1)}, u32[]{:S(2)}) %copy-start.2) | copy-done | bytes 4718616
  82.6 1.1 all-to-all-done.1
  83.7 26.6 %collective-permute-start.3 = (bf16[3584,128]{1,0:T(8,128)(2,1)S(1)}, bf16[3584,128]{1,0:T(8,128)(2,1)S(1)}, u32[]{:S(2)}, u32[]{:S(2)}) collective-permute-start(bf16[3584,128]{1,0:T(8,128)(2,1)S(1)} %bitcast.11), channel_id=1, source_target_pairs={{0,8},{8,0},{1,9},{9,1},{2,10},{10,2},{3,11},{11,3},{4,12},{12,4},... | collective-permute-start | bytes 2752520 | tf_op jit(solution)/shard_map/ppermute | solution.py:540
  110.4 16.4 %born_early.1.early = f32[768,768]{1,0:T(8,128)} custom-call(s32[1]{0:T(128)} %bitcast.place.refs_0_, s32[4]{0:T(128)} %offsets.9, f32[4]{0:T(128)} %refs_2_.3, s32[1,4]{1,0:T(1,128)} %refs_3_.3, bf16[4,2,384,384]{3,2,1,0:T(8,128)(2,1)} %bitcast.5, bf16[4,2,384,384]{3,2,1,0:T(8,128)(2,1)} %copy-done.3, bf16[2,2,384,384]{3,2,1,0:T(8,128)(2,1)} %copy-done.4, ...), custom_call_target="tpu_custom_call" | custom-call | flops 7247757312 | bytes 12000000 | tf_op jit(solution)/shard_map/born_early/pallas_call | solution.py:318
  126.8 0.0 copy-start.7
  126.8 0.0 collective-permute-done.4.refs_7_.far
  126.8 0.0 copy-start.8
  126.8 1.0 copy-done.8
  127.8 16.5 %born_late.1.late = f32[768,768]{1,0:T(8,128)} custom-call(s32[1]{0:T(128)} %bitcast.place.refs_0_, s32[4]{0:T(128)} %offsets.9, f32[4]{0:T(128)} %refs_2_.3, s32[1,4]{1,0:T(1,128)} %refs_3_.3, bf16[4,2,384,384]{3,2,1,0:T(8,128)(2,1)} %bitcast.6, bf16[4,2,384,384]{3,2,1,0:T(8,128)(2,1)} %copy-done.3, bf16[2,2,384,384]{3,2,1,0:T(8,128)(2,1)} %copy-done.4, ...), custom_call_target="tpu_custom_call" | custom-call | flops 7247757312 | bytes 12000000 | tf_op jit(solution)/shard_map/born_late/pallas_call | solution.py:318
  144.4 0.0 copy-done.7
  144.4 6.7 %final_start.1 = (bf16[12,2,384,384]{3,2,1,0:T(8,128)(2,1)S(1)}, bf16[4,768,768]{2,1,0:T(8,128)(2,1)S(1)}, f32[2,768,768]{2,1,0:T(8,128)S(1)}, f32[3,384,768]{2,1,0:T(8,128)S(1)}, f32[384,768]{1,0:T(8,128)S(1)}) custom-call(s32[1]{0:T(128)} %bitcast.place.refs_0_, s32[4]{0:T(128)S(1)} %copy-done.7, bf16[3584,128]{1,0:T(8,128)(2,1)S(1)} %bitcast.12, ...), custom_call_target="tpu_custom_call" | custom-call | flops 1000000000 | bytes 18000000 | tf_op jit(solution)/shard_map/final_start/pallas_call | solution.py:426
  151.0 0.0 collective-permute-done.3.other
  151.0 7.2 %final.1 = (bf16[4,1,2,384,384]{4,3,2,1,0:T(8,128)(2,1)}, f32[3,384,768]{2,1,0:T(8,128)S(1)}, f32[384,768]{1,0:T(8,128)S(1)}) custom-call(s32[1]{0:T(128)} %bitcast.place.refs_0_, s32[4]{0:T(128)S(1)} %copy-done.7, bf16[3584,128]{1,0:T(8,128)(2,1)S(1)} %collective-permute-done.3.other, ...), custom_call_target="tpu_custom_call", output_to_operand_aliasing={{1}: (6, {}), {2}: (7, {})} | custom-call | flops 1000000000 | bytes 18000000 | tf_op jit(solution)/shard_map/final/pallas_call | solution.py:492
Async XLA Ops:
  0.0 5.7 %copy-start.6 = (s32[4]{0:T(128)S(1)}, s32[4]{0:T(128)}, u32[]{:S(2)}) copy-start(s32[4]{0:T(128)} %offsets.9) | copy-start | bytes 52
  0.0 5.7 %collective-permute-start.1 = (bf16[4,2,384,384]{3,2,1,0:T(8,128)(2,1)}, bf16[4,2,384,384]{3,2,1,0:T(8,128)(2,1)S(1)}, u32[]{:S(2)}, u32[]{:S(2)}) collective-permute-start(bf16[4,2,384,384]{3,2,1,0:T(8,128)(2,1)} %bitcast.4), channel_id=1, source_target_pairs={{0,8},{8,0},{1,9},{9,1},{2,10},{10,2},{3,11},{11,3},{4,12},{12,4},... | collective-permute-start | bytes 7077896 | tf_op jit(solution)/shard_map/ppermute | solution.py:525
  0.7 1.7 %copy-start = (bf16[4,1,2,384,384]{4,3,2,1,0:T(8,128)(2,1)S(1)}, bf16[4,1,2,384,384]{4,3,2,1,0:T(8,128)(2,1)}, u32[]{:S(2)}) copy-start(bf16[4,1,2,384,384]{4,3,2,1,0:T(8,128)(2,1)} %param.6) | copy-start | bytes 7077892
  2.6 32.0 %collective-permute-start = (bf16[2,2,384,384]{3,2,1,0:T(8,128)(2,1)S(1)}, bf16[2,2,384,384]{3,2,1,0:T(8,128)(2,1)S(1)}, u32[]{:S(2)}, u32[]{:S(2)}) collective-permute-start(bf16[2,2,384,384]{3,2,1,0:T(8,128)(2,1)S(1)} %shard_map.64), channel_id=1, source_target_pairs={{8,16},{24,32},{40,48},{56,64},{72,80},{88,96},{104,112},{16,8},{3... | collective-permute-start | bytes 3538952 | tf_op jit(solution)/shard_map/ppermute | solution.py:524
  5.7 5.7 %copy-start.3 = (bf16[4,2,384,384]{3,2,1,0:T(8,128)(2,1)}, bf16[4,2,384,384]{3,2,1,0:T(8,128)(2,1)S(1)}, u32[]{:S(2)}) copy-start(bf16[4,2,384,384]{3,2,1,0:T(8,128)(2,1)S(1)} %collective-permute-done.1.mate.refs_5_) | copy-start | bytes 7077892
  34.6 2.9 %copy-start.4 = (bf16[2,2,384,384]{3,2,1,0:T(8,128)(2,1)}, bf16[2,2,384,384]{3,2,1,0:T(8,128)(2,1)S(1)}, u32[]{:S(2)}) copy-start(bf16[2,2,384,384]{3,2,1,0:T(8,128)(2,1)S(1)} %collective-permute-done.near.refs_6_) | copy-start | bytes 3538948
  37.5 2.6 %collective-permute-start.2 = (bf16[3584,128]{1,0:T(8,128)(2,1)S(1)}, bf16[3584,128]{1,0:T(8,128)(2,1)S(1)}, u32[]{:S(2)}, u32[]{:S(2)}) collective-permute-start(bf16[3584,128]{1,0:T(8,128)(2,1)S(1)} %get-tuple-element.22), channel_id=1, source_target_pairs={{0,8},{8,0},{1,9},{9,1},{2,10},{10,2},{3,11},{11,3},{4,12},{12,4},... | collective-permute-start | bytes 2752520 | tf_op jit(solution)/shard_map/ppermute | solution.py:531
  40.2 33.3 %copy-start.1 = (bf16[4,1,2,384,384]{4,3,2,1,0:T(8,128)(2,1)S(1)}, bf16[4,1,2,384,384]{4,3,2,1,0:T(8,128)(2,1)}, u32[]{:S(2)}) copy-start(bf16[4,1,2,384,384]{4,3,2,1,0:T(8,128)(2,1)} %param.6) | copy-start | bytes 7077892
  64.1 19.7 %all-to-all-start.1 = ((bf16[64,56,128]{2,1,0:T(8,128)(2,1)}), bf16[64,56,128]{2,1,0:T(8,128)(2,1)S(1)}, u32[]{:S(2)}, u32[]{:S(2)}) async-start(bf16[64,56,128]{2,1,0:T(8,128)(2,1)} %band_sum.1), calls=%async_computation.1 | async-start | bytes 1835008 | tf_op jit(solution)/shard_map/all_to_all | solution.py:536
  73.5 6.5 %copy-start.5 = (bf16[4,2,384,384]{3,2,1,0:T(8,128)(2,1)S(1)}, bf16[4,2,384,384]{3,2,1,0:T(8,128)(2,1)}, u32[]{:S(2)}) copy-start(bf16[4,2,384,384]{3,2,1,0:T(8,128)(2,1)} %free.1) | copy-start | bytes 7077892
  74.9 51.9 %collective-permute-start.4 = (bf16[2,2,384,384]{3,2,1,0:T(8,128)(2,1)}, bf16[2,2,384,384]{3,2,1,0:T(8,128)(2,1)S(1)}, u32[]{:S(2)}, u32[]{:S(2)}) collective-permute-start(bf16[2,2,384,384]{3,2,1,0:T(8,128)(2,1)} %shard_map.65), channel_id=1, source_target_pairs={{8,16},{24,32},{40,48},{56,64},{72,80},{88,96},{104,112},{16,8},{3... | collective-permute-start | bytes 3538952 | tf_op jit(solution)/shard_map/ppermute | solution.py:527
  80.5 2.1 %copy-start.2 = (bf16[4,768,768]{2,1,0:T(8,128)(2,1)}, bf16[4,768,768]{2,1,0:T(8,128)(2,1)S(1)}, u32[]{:S(2)}) copy-start(bf16[4,768,768]{2,1,0:T(8,128)(2,1)S(1)} %tables.1) | copy-start | bytes 14155780
  83.7 67.3 %collective-permute-start.3 = (bf16[3584,128]{1,0:T(8,128)(2,1)S(1)}, bf16[3584,128]{1,0:T(8,128)(2,1)S(1)}, u32[]{:S(2)}, u32[]{:S(2)}) collective-permute-start(bf16[3584,128]{1,0:T(8,128)(2,1)S(1)} %bitcast.11), channel_id=1, source_target_pairs={{0,8},{8,0},{1,9},{9,1},{2,10},{10,2},{3,11},{11,3},{4,12},{12,4},... | collective-permute-start | bytes 2752520 | tf_op jit(solution)/shard_map/ppermute | solution.py:540
  126.8 17.6 %copy-start.7 = (s32[4]{0:T(128)S(1)}, s32[4]{0:T(128)}, u32[]{:S(2)}) copy-start(s32[4]{0:T(128)} %offsets.9) | copy-start | bytes 52
  126.8 1.0 copy-start.8

commit v4 on v3

--- a/solution.py
+++ b/solution.py
@@ -143,14 +143,14 @@
 
 def polar_half(core, half, offsets, slots, turned, partial, target):
     def each(index, block_sum):
-        @pl.loop(0, HALF // 16)
+        @pl.loop(0, HALF // 32)
         def _(block):
-            rows = pl.ds(pl.multiple_of(half * HALF + block * 16, 16), 16)
+            rows = pl.ds(pl.multiple_of(half * HALF + block * 32, 32), 32)
             pair = block_sum(rows, partial[index, 0, rows, :], partial[index, 1, rows, :])
             for part, value in enumerate(pair):
                 for panel in range(3):
                     start = ((index * 2 + part) * 3 + panel) * HALF
-                    target[pl.ds(pl.multiple_of(start + block * 16, 16), 16), :] = value[
+                    target[pl.ds(pl.multiple_of(start + block * 32, 32), 32), :] = value[
                         :, panel * 128 : (panel + 1) * 128
                     ].astype(target.dtype)
 
@@ -206,26 +206,30 @@
     )(place, offsets, slots, turned, partial)
 
 
-def tables_body(free, out):
-    for k in range(4):
-        fr = free[k, 0]
-        fi = free[k, 1]
-        out[k, :NB, :NB] = fr
-        out[k, :NB, NB:] = fi
-        out[k, NB:, :NB] = -fi
-        out[k, NB:, NB:] = fr
-
-
-def tables_call(free):
-    return pl.pallas_call(
-        tables_body,
-        out_shape=jax.ShapeDtypeStruct((4, 2 * NB, 2 * NB), BF16),
-        in_specs=[VMEM],
-        out_specs=VMEM,
-        compiler_params=pltpu.CompilerParams(vmem_limit_bytes=4 << 20),
-        cost_estimate=pl.CostEstimate(flops=0, bytes_accessed=7_000_000, transcendentals=0),
-        name="tables",
-    )(free)
+def add_body(kept, sent, out, total, sems):
+    third = FLAT // 4
+    stores = []
+    for i in range(4):
+        rows = pl.ds(i * third, third)
+        total[rows, :] = (kept[rows, :] + sent[rows, :].astype(F32)).astype(BF16)
+        store = pltpu.make_async_copy(total.at[rows], out.at[rows], sems.at[i])
+        store.start()
+        stores.append(store)
+    for store in stores:
+        store.wait()
+
+
+def add_call(kept, sent):
+    return pl.pallas_call(
+        add_body,
+        out_shape=jax.ShapeDtypeStruct((FLAT, 128), BF16),
+        in_specs=[VMEM, VMEM],
+        out_specs=ANY,
+        scratch_shapes=[pltpu.VMEM((FLAT, 128), BF16), pltpu.SemaphoreType.DMA((4,))],
+        compiler_params=pltpu.CompilerParams(vmem_limit_bytes=3 << 20),
+        cost_estimate=pl.CostEstimate(flops=500_000, bytes_accessed=3_000_000, transcendentals=0),
+        name="pair_add",
+    )(kept, sent)
 
 
 def window_copies(core, own, mate, near, far, slots, sems):
@@ -307,9 +311,7 @@
         def _():
             total[...] += term
 
-    store = pltpu.make_async_copy(total, out, sems.at[0, 0])
-    store.start()
-    store.wait()
+    out[...] = total[...].astype(BF16)
 
 
 def born_call(place, offsets, occupation, coupling, arrays, vertex):
@@ -317,9 +319,9 @@
     size = 2 * NB
     return pl.pallas_call(
         lambda *refs: born_body(early, *refs),
-        out_shape=jax.ShapeDtypeStruct((size, size), F32),
+        out_shape=jax.ShapeDtypeStruct((size, size), BF16),
         in_specs=[SMEM] * 4 + [ANY] * (len(arrays) + 1),
-        out_specs=ANY,
+        out_specs=VMEM,
         scratch_shapes=[
             pltpu.VMEM((4, 2, NB, NB), BF16),
             pltpu.VMEM((4, 2, 2, NB, NB), BF16),
@@ -349,9 +351,8 @@
     total = jnp.zeros((ROWS, 128), F32)
     for i, load in enumerate(loads):
         load.wait()
-        total = lax.fori_loop(
-            16 * i, 16 * i + 16, lambda at, value: value + buffer[at].astype(F32), total
-        )
+        for at in range(16 * i, 16 * i + 16):
+            total += buffer[at].astype(F32)
     value = total.astype(BF16)
     for i in range(16):
         copies[i] = value
@@ -401,54 +402,60 @@
 
 
 def start_body(
-    place, offsets, mine, tables, own, mate, near, far, early, late,
-    slots, table, born, magnon, bottom_sum, source, joined, sems,
+    place, offsets, mine, free, own, mate, near, far,
+    slots, magnon, bottom_sum, table, source, plain, joined, sems,
 ):
     core = place[0]
-    ready = pltpu.make_async_copy(mine, source, sems.at[10])
-    free = [pltpu.make_async_copy(tables.at[k], table.at[k], sems.at[k + 6]) for k in range(4)]
-    loads = window_copies(core, own, mate, near, far, slots, sems) + [
-        pltpu.make_async_copy(early, born.at[0], sems.at[4]),
-        pltpu.make_async_copy(late, born.at[1], sems.at[5]),
+    ready = [
+        pltpu.make_async_copy(mine, source, sems.at[4]),
+        pltpu.make_async_copy(free, plain, sems.at[5]),
     ]
-    for load in [ready] + free + loads:
+    loads = window_copies(core, own, mate, near, far, slots, sems)
+    for load in ready + loads:
         load.start()
     bottom_sum[...] = jnp.zeros_like(bottom_sum)
-    for load in [ready] + free:
+    for load in ready:
         load.wait()
+    for k in range(4):
+        fr = plain[k, 0]
+        fi = plain[k, 1]
+        table[k, :NB, :NB] = fr
+        table[k, :NB, NB:] = fi
+        table[k, NB:, :NB] = -fi
+        table[k, NB:, NB:] = fr
     half_products(offsets, core, source, joined, table, magnon, bottom_sum)
     for load in loads:
         load.wait()
 
 
-def start_call(place, offsets, mine, tables, own, mate, near, far, early, late):
+def start_call(place, offsets, mine, free, own, mate, near, far):
     size = 2 * NB
     return pl.pallas_call(
         start_body,
         out_shape=(
             jax.ShapeDtypeStruct((12, 2, NB, NB), BF16),
-            jax.ShapeDtypeStruct((4, size, size), BF16),
-            jax.ShapeDtypeStruct((2, size, size), F32),
             jax.ShapeDtypeStruct((3, NB, size), F32),
             jax.ShapeDtypeStruct((NB, size), F32),
-        ),
-        in_specs=[SMEM, SMEM] + [ANY] * 8,
-        out_specs=(VMEM,) * 5,
+            jax.ShapeDtypeStruct((4, size, size), BF16),
+        ),
+        in_specs=[SMEM, SMEM] + [ANY] * 6,
+        out_specs=(VMEM,) * 4,
         scratch_shapes=[
             pltpu.VMEM((FLAT, 128), BF16),
+            pltpu.VMEM((4, 2, NB, NB), BF16),
             pltpu.VMEM((3, HALF, size), BF16),
-            pltpu.SemaphoreType.DMA((11,)),
+            pltpu.SemaphoreType.DMA((6,)),
         ],
-        compiler_params=pltpu.CompilerParams(vmem_limit_bytes=8 << 20),
+        compiler_params=pltpu.CompilerParams(vmem_limit_bytes=10 << 20),
         cost_estimate=pl.CostEstimate(
-            flops=1_000_000_000, bytes_accessed=18_000_000, transcendentals=0
+            flops=1_000_000_000, bytes_accessed=10_000_000, transcendentals=0
         ),
         name="final_start",
-    )(place, offsets, mine, *(in_hbm(x) for x in (tables, own, mate, near, far, early, late)))
+    )(place, offsets, mine, *(in_hbm(x) for x in (free, own, mate, near, far)))
 
 
 def final_body(
-    place, offsets, other, slots, table, born, magnon_in, sum_in, out, magnon, bottom_sum,
+    place, offsets, other, early, late, slots, magnon_in, sum_in, table, out, magnon, bottom_sum,
     source, joined, result, sems,
 ):
     core = place[0]
@@ -461,13 +468,14 @@
     reach = spans(offsets, first, last)
     stores = []
     for item, energy in enumerate((2 - 2 * core, 3 - 2 * core, 2 * core, 2 * core + 1)):
+        born = early if item < 2 else late
 
         @pl.loop(0, NB // 16)
         def _(block):
             rows = pl.ds(pl.multiple_of(block * 16, 16), 16)
             begin = pl.ds(pl.multiple_of((item % 2) * NB + block * 16, 16), 16)
-            real = born[item // 2, begin, :NB]
-            imag = born[item // 2, begin, NB:]
+            real = born[begin, :NB].astype(F32)
+            imag = born[begin, NB:].astype(F32)
             for index in range(3):
                 down = energy + 4 - reach[index]
                 up = energy + 4 + reach[index]
@@ -487,7 +495,7 @@
         store.wait()
 
 
-def final_call(place, offsets, other, slots, table, born, magnon, bottom_sum):
+def final_call(place, offsets, other, early, late, slots, magnon, bottom_sum, table):
     size = 2 * NB
     return pl.pallas_call(
         final_body,
@@ -496,7 +504,7 @@
             jax.ShapeDtypeStruct(magnon.shape, F32),
             jax.ShapeDtypeStruct(bottom_sum.shape, F32),
         ),
-        in_specs=[SMEM, SMEM, ANY] + [VMEM] * 5,
+        in_specs=[SMEM, SMEM, ANY] + [VMEM] * 6,
         out_specs=(ANY, VMEM, VMEM),
         input_output_aliases={6: 1, 7: 2},
         scratch_shapes=[
@@ -510,7 +518,7 @@
             flops=1_000_000_000, bytes_accessed=18_000_000, transcendentals=0
         ),
         name="final",
-    )(place, offsets, other, slots, table, born, magnon, bottom_sum)[0]
+    )(place, offsets, other, early, late, slots, magnon, bottom_sum, table)[0]
 
 
 def per_device(green_blocks, offsets, occupation, coupling, vertex, magnon_free):
@@ -526,11 +534,13 @@
     inner = cut_call(place, own, 2, -2)
     far = lax.ppermute(inner, ENERGY, across)
     slots, turned, partial = prepare_call(place, offsets, own, mate)
-    tables = tables_call(magnon_free)
     slots, turned, send = polar_send_call(place, offsets, near, slots, turned, partial)
     sent = lax.ppermute(send, "core", SWAP)
-    pair = polar_keep_call(place, offsets, slots, turned, partial) + sent.astype(F32)
-    bands = lax.all_to_all(pair.astype(BF16).reshape(BANDS, ROWS, 128), OTHERS, 0, 0, tiled=True)
+    kept = polar_keep_call(place, offsets, slots, turned, partial)
+    pair = add_call(kept, sent)
+    bands = lax.all_to_all(
+        pair.reshape(BANDS, ROWS, 128), OTHERS, 0, 0, tiled=True
+    )
     early = born_call(place, offsets, occupation, coupling, (own, mate, near), vertex)
     copies = sum_call(bands)
     mine = lax.all_to_all(copies, OTHERS, 0, 0, tiled=True).reshape(FLAT, 128)
@@ -538,8 +548,8 @@
         place, offsets, occupation, coupling, (own, mate, near, far), vertex
     )
     other = lax.ppermute(mine, "core", SWAP)
-    held = start_call(place, offsets, mine, tables, own, mate, near, far, early, late)
-    return final_call(place, offsets, other, *held)
+    held = start_call(place, offsets, mine, magnon_free, own, mate, near, far)
+    return final_call(place, offsets, other, early, late, *held)
 
 
 def solution(mesh):

time: 159 us -> 157 us (0.987)
  waiting for transfers between devices: 24.8 us -> 27.4 us
  Pallas kernels: 62 us -> 59.7 us
  local copies, waits for them, and re-layouts: 4.82 us -> 2.72 us
    all_to_all x1, waiting for transfers between devices: 1.15 us -> 3.72 us  [per_device(): mine = lax.all_to_all(copies, OTHERS, 0, 0, tiled=True).reshape(FLAT, 128)]
    pallas_call x1, Pallas kernels: 6.66 us -> 4.52 us  [start_call(): pl.pallas_call(start_body, out_shape=(jax.ShapeDtypeStruct((12, 2, NB, NB...]
    unnamed x18, local copies, waits for them, and re-layouts: 4.82 us -> 2.72 us
  transfers between devices with their start and end apart: 6 -> 6, of which waited for: 3 -> 3; matrix products, arithmetic and copies ran while one was open for 0% -> 0% of each run, Pallas kernels for 31% -> 29%
where the time goes in v4:
time: 157 us
  Pallas kernels  59.7 us (38%)
  starting transfers between devices  45 us (29%)
  waiting for transfers between devices  27.4 us (17%)
  blocking collectives  21.3 us (14%)
  local copies, waits for them, and re-layouts  2.72 us (2%)
    pallas_call x2, Pallas kernels, born_call(): pl.pallas_call(lambda *refs: born_body(early, *refs), out_shape=jax.Shape...  32.3 us
    ppermute x1, starting transfers between devices, per_device(): other = lax.ppermute(mine, 'core', SWAP)  26.6 us
    ppermute x1, waiting for transfers between devices, per_device(): near = lax.ppermute(outer, ENERGY, across)  23.2 us
    all_to_all x1, blocking collectives, per_device(): lax.all_to_all(pair.reshape(BANDS, ROWS, 128), OTHERS, 0, 0, tiled=True)  21.3 us
    all_to_all x1, starting transfers between devices, per_device(): mine = lax.all_to_all(copies, OTHERS, 0, 0, tiled=True).reshape(FLAT, 128)  9.44 us
    pallas_call x1, Pallas kernels, final_call(): pl.pallas_call(final_body, out_shape=(jax.ShapeDtypeStruct((4, 1, 2, NB,...  7.4 us
    pallas_call x1, Pallas kernels, prepare_call(): pl.pallas_call(prepare_body, out_shape=(jax.ShapeDtypeStruct((12, 2, NB,...  5.71 us
    ppermute x1, starting transfers between devices, per_device(): far = lax.ppermute(inner, ENERGY, across)  5.17 us
  transfers between devices with their start and end apart: 6, of which 3 were waited for; matrix products, arithmetic and copies ran while one was open for 0% of the time, Pallas kernels for 29%

profile of v4, /device:TPU:77, one launch (start us, length us, event | category | flops | bytes accessed | tf_op | source)
XLA Modules:
  0.0 156.6 jit_solution(6529757659404208595)
XLA Ops:
  0.0 0.0 copy-start.6
  0.0 0.7 collective-permute-start.1
  0.7 0.0 copy-start
  0.7 1.7 %copy-done = bf16[4,1,2,384,384]{4,3,2,1,0:T(8,128)(2,1)S(1)} copy-done((bf16[4,1,2,384,384]{4,3,2,1,0:T(8,128)(2,1)S(1)}, bf16[4,1,2,384,384]{4,3,2,1,0:T(8,128)(2,1)}, u32[]{:S(2)}) %copy-start) | copy-done | bytes 2359320
  2.3 0.2 shard_map.64
  2.6 3.0 %collective-permute-start = (bf16[2,2,384,384]{3,2,1,0:T(8,128)(2,1)S(1)}, bf16[2,2,384,384]{3,2,1,0:T(8,128)(2,1)S(1)}, u32[]{:S(2)}, u32[]{:S(2)}) collective-permute-start(bf16[2,2,384,384]{3,2,1,0:T(8,128)(2,1)S(1)} %shard_map.64), channel_id=1, source_target_pairs={{8,16},{24,32},{40,48},{56,64},{72,80},{88,96},{104,112},{16,8},{3... | collective-permute-start | bytes 3538952 | tf_op jit(solution)/shard_map/ppermute | solution.py:532
  5.7 0.0 collective-permute-done.1.mate.refs_5_
  5.7 0.0 copy-done.6
  5.7 0.0 copy-start.2
  5.7 5.7 %prepare.1 = (bf16[12,2,384,384]{3,2,1,0:T(8,128)(2,1)S(1)}, f32[8,2,384,384]{3,2,1,0:T(8,128)S(1)}, f32[3,2,384,384]{3,2,1,0:T(8,128)S(1)}) custom-call(s32[1]{0:T(128)} %bitcast.place.refs_0_, s32[4]{0:T(128)S(1)} %copy-done.6, bf16[4,2,384,384]{3,2,1,0:T(8,128)(2,1)S(1)} %bitcast.9, bf16[4,2,384,384]{3,2,1,0:T(8,128)(2,1)S(1)} %collective-permute-done.1.mate.refs_5_), custom_call_target="tpu_custom_call" | custom-call | flops 20000000 | bytes 9000000 | tf_op jit(solution)/shard_map/prepare/pallas_call | solution.py:128
  11.4 0.0 copy-done.2
  11.4 23.2 %collective-permute-done.near.refs_6_ = bf16[2,2,384,384]{3,2,1,0:T(8,128)(2,1)S(1)} collective-permute-done((bf16[2,2,384,384]{3,2,1,0:T(8,128)(2,1)S(1)}, bf16[2,2,384,384]{3,2,1,0:T(8,128)(2,1)S(1)}, u32[]{:S(2)}, u32[]{:S(2)}) %collective-permute-start) | collective-permute-done | bytes 1179680 | tf_op jit(solution)/shard_map/ppermute | solution.py:532
  34.6 0.0 copy-start.3
  34.6 2.7 %polar_send.1 = (bf16[12,2,384,384]{3,2,1,0:T(8,128)(2,1)S(1)}, f32[8,2,384,384]{3,2,1,0:T(8,128)S(1)}, bf16[3584,128]{1,0:T(8,128)(2,1)S(1)}) custom-call(s32[1]{0:T(128)} %bitcast.place.refs_0_, s32[4]{0:T(128)S(1)} %copy-done.6, bf16[2,2,384,384]{3,2,1,0:T(8,128)(2,1)S(1)} %collective-permute-done.near.refs_6_, ...), custom_call_target="tpu_custom_call", output_to_operand_aliasing={{0}: (3, {}), {1}: (4, {})} | custom-call | flops 20000000 | bytes 9000000 | tf_op jit(solution)/shard_map/polar_send/pallas_call | solution.py:180
  37.3 0.0 copy-done.3
  37.3 0.1 collective-permute-start.2
  37.4 2.0 %polar_keep.1.kept = f32[3584,128]{1,0:T(8,128)S(1)} custom-call(s32[1]{0:T(128)} %bitcast.place.refs_0_, s32[4]{0:T(128)S(1)} %copy-done.6, bf16[12,2,384,384]{3,2,1,0:T(8,128)(2,1)S(1)} %get-tuple-element.19.slots, f32[8,2,384,384]{3,2,1,0:T(8,128)S(1)} %get-tuple-element.20.turned, f32[3,2,384,384]{3,2,1,0:T(8,128)S(1)} %get-tuple-element.18.partial), custom_call_target="tpu_custom_call" | custom-call | flops 20000000 | bytes 9000000 | tf_op jit(solution)/shard_map/polar_keep/pallas_call | solution.py:198
  39.3 0.5 collective-permute-done.2.sent
  39.8 1.4 pair_add.1
  41.2 0.0 copy-start.1
  41.2 21.3 %all_to_all.10.bands = bf16[64,56,128]{2,1,0:T(8,128)(2,1)S(1)} all-to-all(bf16[64,56,128]{2,1,0:T(8,128)(2,1)S(1)} %bitcast.11), channel_id=1, replica_groups=mesh['y'=4,'xh'=2,'core'=2,'xl'=2,'z'=4] {'y','xh','xl','z'}, dimensions={0} | all-to-all | bytes 1835008 | tf_op jit(solution)/shard_map/all_to_all | solution.py:541
  62.5 2.3 %band_sum.1 = bf16[64,56,128]{2,1,0:T(8,128)(2,1)} custom-call(bf16[64,56,128]{2,1,0:T(8,128)(2,1)S(1)} %all_to_all.10.bands), custom_call_target="tpu_custom_call" | custom-call | flops 500000 | bytes 1900000 | tf_op jit(solution)/shard_map/band_sum/pallas_call | solution.py:369
  64.8 9.4 %all-to-all-start.1 = ((bf16[64,56,128]{2,1,0:T(8,128)(2,1)}), bf16[64,56,128]{2,1,0:T(8,128)(2,1)S(1)}, u32[]{:S(2)}, u32[]{:S(2)}) async-start(bf16[64,56,128]{2,1,0:T(8,128)(2,1)} %band_sum.1), calls=%async_computation.1 | async-start | bytes 1835008 | tf_op jit(solution)/shard_map/all_to_all | solution.py:546
  74.2 0.0 copy-done.1
  74.3 1.3 shard_map.65
  75.6 5.2 %collective-permute-start.4 = (bf16[2,2,384,384]{3,2,1,0:T(8,128)(2,1)}, bf16[2,2,384,384]{3,2,1,0:T(8,128)(2,1)S(1)}, u32[]{:S(2)}, u32[]{:S(2)}) collective-permute-start(bf16[2,2,384,384]{3,2,1,0:T(8,128)(2,1)} %shard_map.65), channel_id=1, source_target_pairs={{8,16},{24,32},{40,48},{56,64},{72,80},{88,96},{104,112},{16,8},{3... | collective-permute-start | bytes 3538952 | tf_op jit(solution)/shard_map/ppermute | solution.py:535
  80.7 3.7 %all-to-all-done.1 = bf16[64,56,128]{2,1,0:T(8,128)(2,1)S(1)} async-done(((bf16[64,56,128]{2,1,0:T(8,128)(2,1)}), bf16[64,56,128]{2,1,0:T(8,128)(2,1)S(1)}, u32[]{:S(2)}, u32[]{:S(2)}) %all-to-all-start.1) | async-done | bytes 917536 | tf_op jit(solution)/shard_map/all_to_all | solution.py:546
  84.5 26.6 %collective-permute-start.3 = (bf16[3584,128]{1,0:T(8,128)(2,1)S(1)}, bf16[3584,128]{1,0:T(8,128)(2,1)S(1)}, u32[]{:S(2)}, u32[]{:S(2)}) collective-permute-start(bf16[3584,128]{1,0:T(8,128)(2,1)S(1)} %bitcast.12), channel_id=1, source_target_pairs={{0,8},{8,0},{1,9},{9,1},{2,10},{10,2},{3,11},{11,3},{4,12},{12,4},... | collective-permute-start | bytes 2752520 | tf_op jit(solution)/shard_map/ppermute | solution.py:550
  111.1 16.2 %born_early.1.early = bf16[768,768]{1,0:T(8,128)(2,1)} custom-call(s32[1]{0:T(128)} %bitcast.place.refs_0_, s32[4]{0:T(128)} %offsets.9, f32[4]{0:T(128)} %refs_2_.3, s32[1,4]{1,0:T(1,128)} %refs_3_.3, bf16[4,2,384,384]{3,2,1,0:T(8,128)(2,1)} %bitcast.5, bf16[4,2,384,384]{3,2,1,0:T(8,128)(2,1)} %copy-done.2, bf16[2,2,384,384]{3,2,1,0:T(8,128)(2,1)} %copy-done.3, ...), custom_call_target="tpu_custom_call" | custom-call | flops 7247757312 | bytes 12000000 | tf_op jit(solution)/shard_map/born_early/pallas_call | solution.py:320
  127.3 0.0 copy-start.7
  127.3 0.0 collective-permute-done.4.refs_7_.far
  127.3 0.0 copy-start.8
  127.3 1.0 copy-done.8
  128.3 16.1 %born_late.1.late = bf16[768,768]{1,0:T(8,128)(2,1)} custom-call(s32[1]{0:T(128)} %bitcast.place.refs_0_, s32[4]{0:T(128)} %offsets.9, f32[4]{0:T(128)} %refs_2_.3, s32[1,4]{1,0:T(1,128)} %refs_3_.3, bf16[4,2,384,384]{3,2,1,0:T(8,128)(2,1)} %bitcast.6, bf16[4,2,384,384]{3,2,1,0:T(8,128)(2,1)} %copy-done.2, bf16[2,2,384,384]{3,2,1,0:T(8,128)(2,1)} %copy-done.3, ...), custom_call_target="tpu_custom_call" | custom-call | flops 7247757312 | bytes 12000000 | tf_op jit(solution)/shard_map/born_late/pallas_call | solution.py:320
  144.4 0.0 copy-done.7
  144.4 0.0 copy-start.4
  144.4 0.0 copy-start.5
  144.5 4.5 %final_start.1 = (bf16[12,2,384,384]{3,2,1,0:T(8,128)(2,1)S(1)}, f32[3,384,768]{2,1,0:T(8,128)S(1)}, f32[384,768]{1,0:T(8,128)S(1)}, bf16[4,768,768]{2,1,0:T(8,128)(2,1)S(1)}) custom-call(s32[1]{0:T(128)} %bitcast.place.refs_0_, s32[4]{0:T(128)S(1)} %copy-done.7, bf16[3584,128]{1,0:T(8,128)(2,1)S(1)} %bitcast.13, bf16[4,2,384,384]{3,2,1,0:T(8,128)(2,1)} %free.1, ...), custom_call_target="tpu_custom_call" | custom-call | flops 1000000000 | bytes 10000000 | tf_op jit(solution)/shard_map/final_start/pallas_call | solution.py:433
  149.0 0.0 collective-permute-done.3.other
  149.0 0.0 copy-done.4
  149.0 0.0 copy-done.5
  149.0 7.4 %final.1 = (bf16[4,1,2,384,384]{4,3,2,1,0:T(8,128)(2,1)}, f32[3,384,768]{2,1,0:T(8,128)S(1)}, f32[384,768]{1,0:T(8,128)S(1)}) custom-call(s32[1]{0:T(128)} %bitcast.place.refs_0_, s32[4]{0:T(128)S(1)} %copy-done.7, bf16[3584,128]{1,0:T(8,128)(2,1)S(1)} %collective-permute-done.3.other, ...), custom_call_target="tpu_custom_call", output_to_operand_aliasing={{1}: (6, {}), {2}: (7, {})} | custom-call | flops 1000000000 | bytes 18000000 | tf_op jit(solution)/shard_map/final/pallas_call | solution.py:500
Async XLA Ops:
  0.0 5.7 %copy-start.6 = (s32[4]{0:T(128)S(1)}, s32[4]{0:T(128)}, u32[]{:S(2)}) copy-start(s32[4]{0:T(128)} %offsets.9) | copy-start | bytes 52
  0.0 5.7 %collective-permute-start.1 = (bf16[4,2,384,384]{3,2,1,0:T(8,128)(2,1)}, bf16[4,2,384,384]{3,2,1,0:T(8,128)(2,1)S(1)}, u32[]{:S(2)}, u32[]{:S(2)}) collective-permute-start(bf16[4,2,384,384]{3,2,1,0:T(8,128)(2,1)} %bitcast.4), channel_id=1, source_target_pairs={{0,8},{8,0},{1,9},{9,1},{2,10},{10,2},{3,11},{11,3},{4,12},{12,4},... | collective-permute-start | bytes 7077896 | tf_op jit(solution)/shard_map/ppermute | solution.py:533
  0.7 1.7 %copy-start = (bf16[4,1,2,384,384]{4,3,2,1,0:T(8,128)(2,1)S(1)}, bf16[4,1,2,384,384]{4,3,2,1,0:T(8,128)(2,1)}, u32[]{:S(2)}) copy-start(bf16[4,1,2,384,384]{4,3,2,1,0:T(8,128)(2,1)} %param.6) | copy-start | bytes 7077892
  2.6 32.0 %collective-permute-start = (bf16[2,2,384,384]{3,2,1,0:T(8,128)(2,1)S(1)}, bf16[2,2,384,384]{3,2,1,0:T(8,128)(2,1)S(1)}, u32[]{:S(2)}, u32[]{:S(2)}) collective-permute-start(bf16[2,2,384,384]{3,2,1,0:T(8,128)(2,1)S(1)} %shard_map.64), channel_id=1, source_target_pairs={{8,16},{24,32},{40,48},{56,64},{72,80},{88,96},{104,112},{16,8},{3... | collective-permute-start | bytes 3538952 | tf_op jit(solution)/shard_map/ppermute | solution.py:532
  5.7 5.7 %copy-start.2 = (bf16[4,2,384,384]{3,2,1,0:T(8,128)(2,1)}, bf16[4,2,384,384]{3,2,1,0:T(8,128)(2,1)S(1)}, u32[]{:S(2)}) copy-start(bf16[4,2,384,384]{3,2,1,0:T(8,128)(2,1)S(1)} %collective-permute-done.1.mate.refs_5_) | copy-start | bytes 7077892
  34.6 2.7 %copy-start.3 = (bf16[2,2,384,384]{3,2,1,0:T(8,128)(2,1)}, bf16[2,2,384,384]{3,2,1,0:T(8,128)(2,1)S(1)}, u32[]{:S(2)}) copy-start(bf16[2,2,384,384]{3,2,1,0:T(8,128)(2,1)S(1)} %collective-permute-done.near.refs_6_) | copy-start | bytes 3538948
  37.3 2.6 %collective-permute-start.2 = (bf16[3584,128]{1,0:T(8,128)(2,1)S(1)}, bf16[3584,128]{1,0:T(8,128)(2,1)S(1)}, u32[]{:S(2)}, u32[]{:S(2)}) collective-permute-start(bf16[3584,128]{1,0:T(8,128)(2,1)S(1)} %get-tuple-element.21), channel_id=1, source_target_pairs={{0,8},{8,0},{1,9},{9,1},{2,10},{10,2},{3,11},{11,3},{4,12},{12,4},... | collective-permute-start | bytes 2752520 | tf_op jit(solution)/shard_map/ppermute | solution.py:538
  41.2 33.0 %copy-start.1 = (bf16[4,1,2,384,384]{4,3,2,1,0:T(8,128)(2,1)S(1)}, bf16[4,1,2,384,384]{4,3,2,1,0:T(8,128)(2,1)}, u32[]{:S(2)}) copy-start(bf16[4,1,2,384,384]{4,3,2,1,0:T(8,128)(2,1)} %param.6) | copy-start | bytes 7077892
  64.8 19.7 %all-to-all-start.1 = ((bf16[64,56,128]{2,1,0:T(8,128)(2,1)}), bf16[64,56,128]{2,1,0:T(8,128)(2,1)S(1)}, u32[]{:S(2)}, u32[]{:S(2)}) async-start(bf16[64,56,128]{2,1,0:T(8,128)(2,1)} %band_sum.1), calls=%async_computation.1 | async-start | bytes 1835008 | tf_op jit(solution)/shard_map/all_to_all | solution.py:546
  75.6 51.7 %collective-permute-start.4 = (bf16[2,2,384,384]{3,2,1,0:T(8,128)(2,1)}, bf16[2,2,384,384]{3,2,1,0:T(8,128)(2,1)S(1)}, u32[]{:S(2)}, u32[]{:S(2)}) collective-permute-start(bf16[2,2,384,384]{3,2,1,0:T(8,128)(2,1)} %shard_map.65), channel_id=1, source_target_pairs={{8,16},{24,32},{40,48},{56,64},{72,80},{88,96},{104,112},{16,8},{3... | collective-permute-start | bytes 3538952 | tf_op jit(solution)/shard_map/ppermute | solution.py:535
  84.5 64.5 %collective-permute-start.3 = (bf16[3584,128]{1,0:T(8,128)(2,1)S(1)}, bf16[3584,128]{1,0:T(8,128)(2,1)S(1)}, u32[]{:S(2)}, u32[]{:S(2)}) collective-permute-start(bf16[3584,128]{1,0:T(8,128)(2,1)S(1)} %bitcast.12), channel_id=1, source_target_pairs={{0,8},{8,0},{1,9},{9,1},{2,10},{10,2},{3,11},{11,3},{4,12},{12,4},... | collective-permute-start | bytes 2752520 | tf_op jit(solution)/shard_map/ppermute | solution.py:550
  127.3 17.2 %copy-start.7 = (s32[4]{0:T(128)S(1)}, s32[4]{0:T(128)}, u32[]{:S(2)}) copy-start(s32[4]{0:T(128)} %offsets.9) | copy-start | bytes 52
  127.3 1.0 copy-start.8
  144.4 4.6 %copy-start.4 = (bf16[768,768]{1,0:T(8,128)(2,1)S(1)}, bf16[768,768]{1,0:T(8,128)(2,1)}, u32[]{:S(2)}) copy-start(bf16[768,768]{1,0:T(8,128)(2,1)} %born_early.1.early) | copy-start | bytes 3538948
  144.4 4.6 %copy-start.5 = (bf16[768,768]{1,0:T(8,128)(2,1)S(1)}, bf16[768,768]{1,0:T(8,128)(2,1)}, u32[]{:S(2)}) copy-start(bf16[768,768]{1,0:T(8,128)(2,1)} %born_late.1.late) | copy-start | bytes 3538948

commit v5 on v4

--- a/solution.py
+++ b/solution.py
@@ -9,14 +9,15 @@
 
 NB = 384
 HALF = NB // 2
-BANDS = 64
-ROWS = 56
+BANDS = 16
+ROWS = 18 * HALF // BANDS
 FLAT = BANDS * ROWS
 FULL = 60 << 20
 F32 = jnp.float32
 BF16 = jnp.bfloat16
 SWAP = [(0, 1), (1, 0)]
-OTHERS = ("y", "xh", "xl", "z")
+PLANE = ("y", "z")
+ROW = ("xh", "xl")
 ENERGY = ("y", "xh", "core")
 LAYER = ("xl", "z")
 ANY = pl.BlockSpec(memory_space=pl.ANY)
@@ -63,7 +64,7 @@
         scratch_shapes=[pltpu.SemaphoreType.DMA],
         compiler_params=pltpu.CompilerParams(vmem_limit_bytes=4 << 20),
         cost_estimate=pl.CostEstimate(flops=0, bytes_accessed=2_400_000, transcendentals=0),
-    )(place, own)
+    )(place, in_hbm(own))
 
 
 def polar_pairs(core, near, slots, turned, offsets, each):
@@ -155,8 +156,6 @@
                     ].astype(target.dtype)
 
     polar_pairs(core, True, slots, turned, offsets, each)
-    tail = pl.ds(18 * HALF, FLAT - 18 * HALF)
-    target[tail, :] = jnp.zeros((FLAT - 18 * HALF, 128), target.dtype)
 
 
 def polar_send_body(place, offsets, near, slots_in, turned_in, partial, slots, turned, send, sem):
@@ -269,6 +268,8 @@
             at = energy + 4 + item
             fetch(at - offsets[k], lows.at[k, item], sems.at[k, 2 * item])
             fetch(at + offsets[k], highs.at[k, item], sems.at[k, 2 * item + 1])
+
+    total[...] = jnp.zeros_like(total)
 
     @pl.loop(0, 4)
     def _(k):
@@ -293,23 +294,22 @@
                 high = highs[k, item, part].astype(F32)
                 value = weight * low + (weight + 1.0) * high
                 mixed[part * NB : (part + 1) * NB, item * NB : (item + 1) * NB] = value.astype(BF16)
-        half = jnp.dot(wide[...], mixed[...], preferred_element_type=F32).astype(BF16)
-        for item in range(2):
-            for part in range(2):
-                stack[item * NB : (item + 1) * NB, part * NB : (part + 1) * NB] = half[
-                    part * NB : (part + 1) * NB, item * NB : (item + 1) * NB
+        for piece in range(2):
+            begin = piece * 384
+            part, row = begin // NB, begin % NB
+            half = jnp.dot(
+                wide[begin : begin + 384, :], mixed[...], preferred_element_type=F32
+            ).astype(BF16)
+            for item in range(2):
+                stack[item * NB + row : item * NB + row + 384, part * NB : (part + 1) * NB] = half[
+                    :, item * NB : (item + 1) * NB
                 ]
-        term = lax.dot_general(
-            stack[...], side[...], (((1,), (1,)), ((), ())), preferred_element_type=F32
-        )
-
-        @pl.when(k == 0)
-        def _():
-            total[...] = term
-
-        @pl.when(k > 0)
-        def _():
-            total[...] += term
+        for piece in range(2):
+            rows = slice(piece * 384, (piece + 1) * 384)
+            term = lax.dot_general(
+                stack[rows, :], side[...], (((1,), (1,)), ((), ())), preferred_element_type=F32
+            )
+            total[rows, :] += term
 
     out[...] = total[...].astype(BF16)
 
@@ -341,44 +341,44 @@
     )(place, offsets, occupation, coupling, *arrays, vertex)
 
 
-def sum_body(bands, out, buffer, copies, sems):
+def sum_body(count, copies, bands, out, buffer, value, *sems):
     loads = [
-        pltpu.make_async_copy(bands.at[pl.ds(16 * i, 16)], buffer.at[pl.ds(16 * i, 16)], sems.at[i])
-        for i in range(4)
+        pltpu.make_async_copy(bands.at[i], buffer.at[i], sems[0].at[i]) for i in range(count)
     ]
     for load in loads:
         load.start()
-    total = jnp.zeros((ROWS, 128), F32)
-    for i, load in enumerate(loads):
+    for load in loads:
         load.wait()
-        for at in range(16 * i, 16 * i + 16):
-            total += buffer[at].astype(F32)
-    value = total.astype(BF16)
-    for i in range(16):
-        copies[i] = value
-    stores = [
-        pltpu.make_async_copy(copies, out.at[pl.ds(16 * i, 16)], sems.at[i]) for i in range(4)
-    ]
+
+    for begin in range(0, ROWS, 64):
+        rows = slice(begin, min(begin + 64, ROWS))
+        total = buffer[0, rows, :].astype(F32)
+        for i in range(1, count):
+            total += buffer[i, rows, :].astype(F32)
+        value[rows, :] = total.astype(BF16)
+
+    stores = [pltpu.make_async_copy(value, out.at[i], sems[1].at[i]) for i in range(copies)]
     for store in stores:
         store.start()
     for store in stores:
         store.wait()
 
 
-def sum_call(bands):
-    return pl.pallas_call(
-        sum_body,
-        out_shape=jax.ShapeDtypeStruct(bands.shape, BF16),
+def sum_call(bands, copies):
+    count = bands.shape[0]
+    return pl.pallas_call(
+        lambda *refs: sum_body(count, copies, *refs),
+        out_shape=jax.ShapeDtypeStruct((copies, ROWS, 128), BF16),
         in_specs=[ANY],
         out_specs=ANY,
         scratch_shapes=[
             pltpu.VMEM(bands.shape, BF16),
-            pltpu.VMEM((16, ROWS, 128), BF16),
-            pltpu.SemaphoreType.DMA((4,)),
+            pltpu.VMEM((ROWS, 128), BF16),
+            pltpu.SemaphoreType.DMA((count,)),
+            pltpu.SemaphoreType.DMA((copies,)),
         ],
         compiler_params=pltpu.CompilerParams(vmem_limit_bytes=4 << 20),
         cost_estimate=pl.CostEstimate(flops=500_000, bytes_accessed=1_900_000, transcendentals=0),
-        name="band_sum",
     )(bands)
 
 
@@ -538,12 +538,12 @@
     sent = lax.ppermute(send, "core", SWAP)
     kept = polar_keep_call(place, offsets, slots, turned, partial)
     pair = add_call(kept, sent)
-    bands = lax.all_to_all(
-        pair.reshape(BANDS, ROWS, 128), OTHERS, 0, 0, tiled=True
-    )
+    bands = lax.all_to_all(pair.reshape(BANDS, ROWS, 128), PLANE, 0, 0, tiled=True)
     early = born_call(place, offsets, occupation, coupling, (own, mate, near), vertex)
-    copies = sum_call(bands)
-    mine = lax.all_to_all(copies, OTHERS, 0, 0, tiled=True).reshape(FLAT, 128)
+    copies = sum_call(bands, 4)
+    bands = lax.all_to_all(copies, ROW, 0, 0, tiled=True)
+    copies = sum_call(bands, BANDS)
+    mine = lax.all_to_all(copies, PLANE, 0, 0, tiled=True).reshape(FLAT, 128)
     late = born_call(
         place, offsets, occupation, coupling, (own, mate, near, far), vertex
     )

time: 157 us -> 139 us (0.89)
  the two profiles are of different devices: /device:TPU:77 before, /device:TPU:5 now
where the time goes in v5:
time: 139 us; the launch traced here: 138 us
  Pallas kernels  58.6 us (42%)
  waiting for transfers between devices  28.5 us (21%)
  blocking collectives  28.4 us (20%)
  starting transfers between devices  22.4 us (16%)
    pallas_call x2, Pallas kernels, born_call(): pl.pallas_call(lambda *refs: born_body(early, *refs), out_shape=jax.Shape...  27.9 us
    ppermute x1, waiting for transfers between devices, per_device(): near = lax.ppermute(outer, ENERGY, across)  21.7 us
    all_to_all x1, blocking collectives, per_device(): lax.all_to_all(pair.reshape(BANDS, ROWS, 128), PLANE, 0, 0, tiled=True)  21.3 us
    ppermute x1, starting transfers between devices, per_device(): far = lax.ppermute(inner, ENERGY, across)  8.46 us
    pallas_call x1, Pallas kernels, final_call(): pl.pallas_call(final_body, out_shape=(jax.ShapeDtypeStruct((4, 1, 2, NB,...  7.36 us
    pallas_call x1, Pallas kernels, prepare_call(): pl.pallas_call(prepare_body, out_shape=(jax.ShapeDtypeStruct((12, 2, NB,...  7.2 us
    all_to_all x1, blocking collectives, per_device(): bands = lax.all_to_all(copies, ROW, 0, 0, tiled=True)  7.03 us
    ppermute x1, starting transfers between devices, per_device(): other = lax.ppermute(mine, 'core', SWAP)  5.88 us
  transfers between devices with their start and end apart: 6, of which 4 were waited for; matrix products, arithmetic and copies ran while one was open for 0% of the time, Pallas kernels for 32%

profile of v5, /device:TPU:5, one launch (start us, length us, event | category | flops | bytes accessed | tf_op | source)
XLA Modules:
  0.0 138.1 jit_solution(6889386892955683218)
XLA Ops:
  0.0 0.0 copy-start
  0.0 0.0 copy-start.4
  0.0 0.7 collective-permute-start.1
  0.7 1.3 shard_map.64
  2.0 3.2 %collective-permute-start = (bf16[2,2,384,384]{3,2,1,0:T(8,128)(2,1)S(1)}, bf16[2,2,384,384]{3,2,1,0:T(8,128)(2,1)S(1)}, u32[]{:S(2)}, u32[]{:S(2)}) collective-permute-start(bf16[2,2,384,384]{3,2,1,0:T(8,128)(2,1)S(1)} %shard_map.64), channel_id=1, source_target_pairs={{8,16},{24,32},{40,48},{56,64},{72,80},{88,96},{104,112},{16,8},{3... | collective-permute-start | bytes 3538952 | tf_op jit(solution)/shard_map/ppermute | solution.py:532
  5.2 0.0 collective-permute-done.1.mate.refs_5_
  5.2 0.0 copy-done
  5.2 0.0 copy-done.4
  5.2 7.2 %prepare.1 = (bf16[12,2,384,384]{3,2,1,0:T(8,128)(2,1)S(1)}, f32[8,2,384,384]{3,2,1,0:T(8,128)S(1)}, f32[3,2,384,384]{3,2,1,0:T(8,128)S(1)}) custom-call(s32[1]{0:T(128)} %bitcast.place.refs_0_, s32[4]{0:T(128)S(1)} %copy-done.4, bf16[4,2,384,384]{3,2,1,0:T(8,128)(2,1)S(1)} %bitcast.10, bf16[4,2,384,384]{3,2,1,0:T(8,128)(2,1)} %collective-permute-done.1.mate.refs_5_), custom_call_target="tpu_custom_call" | custom-call | flops 20000000 | bytes 9000000 | tf_op jit(solution)/shard_map/prepare/pallas_call | solution.py:129
  12.4 21.7 %collective-permute-done.near.refs_6_ = bf16[2,2,384,384]{3,2,1,0:T(8,128)(2,1)S(1)} collective-permute-done((bf16[2,2,384,384]{3,2,1,0:T(8,128)(2,1)S(1)}, bf16[2,2,384,384]{3,2,1,0:T(8,128)(2,1)S(1)}, u32[]{:S(2)}, u32[]{:S(2)}) %collective-permute-start) | collective-permute-done | bytes 1179680 | tf_op jit(solution)/shard_map/ppermute | solution.py:532
  34.1 0.0 copy-start.1
  34.1 2.7 %polar_send.1 = (bf16[12,2,384,384]{3,2,1,0:T(8,128)(2,1)S(1)}, f32[8,2,384,384]{3,2,1,0:T(8,128)S(1)}, bf16[3456,128]{1,0:T(8,128)(2,1)S(1)}) custom-call(s32[1]{0:T(128)} %bitcast.place.refs_0_, s32[4]{0:T(128)S(1)} %copy-done.4, bf16[2,2,384,384]{3,2,1,0:T(8,128)(2,1)S(1)} %collective-permute-done.near.refs_6_, ...), custom_call_target="tpu_custom_call", output_to_operand_aliasing={{0}: (3, {}), {1}: (4, {})} | custom-call | flops 20000000 | bytes 9000000 | tf_op jit(solution)/shard_map/polar_send/pallas_call | solution.py:179
  36.8 0.0 copy-done.1
  36.8 0.1 collective-permute-start.2
  36.9 2.0 %polar_keep.1.kept = f32[3456,128]{1,0:T(8,128)S(1)} custom-call(s32[1]{0:T(128)} %bitcast.place.refs_0_, s32[4]{0:T(128)S(1)} %copy-done.4, bf16[12,2,384,384]{3,2,1,0:T(8,128)(2,1)S(1)} %get-tuple-element.19.slots, f32[8,2,384,384]{3,2,1,0:T(8,128)S(1)} %get-tuple-element.20.turned, f32[3,2,384,384]{3,2,1,0:T(8,128)S(1)} %get-tuple-element.18.partial), custom_call_target="tpu_custom_call" | custom-call | flops 20000000 | bytes 9000000 | tf_op jit(solution)/shard_map/polar_keep/pallas_call | solution.py:197
  38.9 0.4 collective-permute-done.2.sent
  39.3 1.3 pair_add.1
  40.6 21.3 %all_to_all.15.refs_0_ = bf16[16,216,128]{2,1,0:T(8,128)(2,1)S(1)} all-to-all(bf16[16,216,128]{2,1,0:T(8,128)(2,1)S(1)} %bitcast.11), channel_id=1, replica_groups=mesh['y'=4,'xh'=2,'core'=2,'xl'=2,'z'=4] {'y','z'}, dimensions={0} | all-to-all | bytes 1769472 | tf_op jit(solution)/shard_map/all_to_all | solution.py:541
  62.0 1.7 %shard_map.65 = bf16[4,216,128]{2,1,0:T(8,128)(2,1)S(1)} custom-call(bf16[16,216,128]{2,1,0:T(8,128)(2,1)S(1)} %all_to_all.15.refs_0_), custom_call_target="tpu_custom_call" | custom-call | flops 500000 | bytes 1900000 | tf_op jit(solution)/shard_map/pallas_call | solution.py:369
  63.7 7.0 %all_to_all.16.refs_0_ = bf16[4,216,128]{2,1,0:T(8,128)(2,1)S(1)} all-to-all(bf16[4,216,128]{2,1,0:T(8,128)(2,1)S(1)} %shard_map.65), channel_id=1, replica_groups=mesh['y'=4,'xh'=2,'core'=2,'xl'=2,'z'=4] {'xh','xl'}, dimensions={0} | all-to-all | bytes 442368 | tf_op jit(solution)/shard_map/all_to_all | solution.py:544
  70.7 1.4 shard_map.66
  72.1 4.1 %all-to-all-start.2 = ((bf16[16,216,128]{2,1,0:T(8,128)(2,1)}), bf16[16,216,128]{2,1,0:T(8,128)(2,1)S(1)}, u32[]{:S(2)}, u32[]{:S(2)}) async-start(bf16[16,216,128]{2,1,0:T(8,128)(2,1)} %shard_map.66), calls=%async_computation.2 | async-start | bytes 1769472 | tf_op jit(solution)/shard_map/all_to_all | solution.py:546
  76.2 1.3 shard_map.67
  77.5 8.5 %collective-permute-start.4 = (bf16[2,2,384,384]{3,2,1,0:T(8,128)(2,1)S(1)}, bf16[2,2,384,384]{3,2,1,0:T(8,128)(2,1)}, u32[]{:S(2)}, u32[]{:S(2)}) collective-permute-start(bf16[2,2,384,384]{3,2,1,0:T(8,128)(2,1)S(1)} %shard_map.67), channel_id=1, source_target_pairs={{8,16},{24,32},{40,48},{56,64},{72,80},{88,96},{104,112},{16,8},{3... | collective-permute-start | bytes 3538952 | tf_op jit(solution)/shard_map/ppermute | solution.py:535
  86.0 1.0 all-to-all-done.2
  87.0 5.9 %collective-permute-start.3 = (bf16[3456,128]{1,0:T(8,128)(2,1)S(1)}, bf16[3456,128]{1,0:T(8,128)(2,1)S(1)}, u32[]{:S(2)}, u32[]{:S(2)}) collective-permute-start(bf16[3456,128]{1,0:T(8,128)(2,1)S(1)} %bitcast.12), channel_id=1, source_target_pairs={{0,8},{8,0},{1,9},{9,1},{2,10},{10,2},{3,11},{11,3},{4,12},{12,4},... | collective-permute-start | bytes 2654216 | tf_op jit(solution)/shard_map/ppermute | solution.py:550
  92.9 14.0 %born_early.1.early = bf16[768,768]{1,0:T(8,128)(2,1)} custom-call(s32[1]{0:T(128)} %bitcast.place.refs_0_, s32[4]{0:T(128)} %offsets.9, f32[4]{0:T(128)} %refs_2_.3, s32[1,4]{1,0:T(1,128)} %refs_3_.3, bf16[4,2,384,384]{3,2,1,0:T(8,128)(2,1)} %bitcast.7, bf16[4,2,384,384]{3,2,1,0:T(8,128)(2,1)} %collective-permute-done.1.mate.refs_5_, ...), custom_call_target="tpu_custom_call" | custom-call | flops 7247757312 | bytes 12000000 | tf_op jit(solution)/shard_map/born_early/pallas_call | solution.py:320
  106.9 0.0 copy-start.5
  106.9 5.3 %collective-permute-done.4.refs_7_.far = bf16[2,2,384,384]{3,2,1,0:T(8,128)(2,1)} collective-permute-done((bf16[2,2,384,384]{3,2,1,0:T(8,128)(2,1)S(1)}, bf16[2,2,384,384]{3,2,1,0:T(8,128)(2,1)}, u32[]{:S(2)}, u32[]{:S(2)}) %collective-permute-start.4) | collective-permute-done | bytes 1179680 | tf_op jit(solution)/shard_map/ppermute | solution.py:535
  112.3 13.9 %born_late.1.late = bf16[768,768]{1,0:T(8,128)(2,1)} custom-call(s32[1]{0:T(128)} %bitcast.place.refs_0_, s32[4]{0:T(128)} %offsets.9, f32[4]{0:T(128)} %refs_2_.3, s32[1,4]{1,0:T(1,128)} %refs_3_.3, bf16[4,2,384,384]{3,2,1,0:T(8,128)(2,1)} %bitcast.8, bf16[4,2,384,384]{3,2,1,0:T(8,128)(2,1)} %collective-permute-done.1.mate.refs_5_, ...), custom_call_target="tpu_custom_call" | custom-call | flops 7247757312 | bytes 12000000 | tf_op jit(solution)/shard_map/born_late/pallas_call | solution.py:320
  126.2 0.0 copy-done.5
  126.2 0.0 copy-start.2
  126.2 0.0 copy-start.3
  126.2 4.5 %final_start.1 = (bf16[12,2,384,384]{3,2,1,0:T(8,128)(2,1)S(1)}, f32[3,384,768]{2,1,0:T(8,128)S(1)}, f32[384,768]{1,0:T(8,128)S(1)}, bf16[4,768,768]{2,1,0:T(8,128)(2,1)S(1)}) custom-call(s32[1]{0:T(128)} %bitcast.place.refs_0_, s32[4]{0:T(128)S(1)} %copy-done.5, bf16[3456,128]{1,0:T(8,128)(2,1)S(1)} %bitcast.13, bf16[4,2,384,384]{3,2,1,0:T(8,128)(2,1)} %free.1, ...), custom_call_target="tpu_custom_call" | custom-call | flops 1000000000 | bytes 10000000 | tf_op jit(solution)/shard_map/final_start/pallas_call | solution.py:433
  130.7 0.0 collective-permute-done.3.other
  130.7 0.0 copy-done.2
  130.7 0.0 copy-done.3
  130.8 7.4 %final.1 = (bf16[4,1,2,384,384]{4,3,2,1,0:T(8,128)(2,1)}, f32[3,384,768]{2,1,0:T(8,128)S(1)}, f32[384,768]{1,0:T(8,128)S(1)}) custom-call(s32[1]{0:T(128)} %bitcast.place.refs_0_, s32[4]{0:T(128)S(1)} %copy-done.5, bf16[3456,128]{1,0:T(8,128)(2,1)S(1)} %collective-permute-done.3.other, ...), custom_call_target="tpu_custom_call", output_to_operand_aliasing={{1}: (6, {}), {2}: (7, {})} | custom-call | flops 1000000000 | bytes 18000000 | tf_op jit(solution)/shard_map/final/pallas_call | solution.py:500
Async XLA Ops:
  0.0 5.2 %copy-start = (bf16[4,1,2,384,384]{4,3,2,1,0:T(8,128)(2,1)S(1)}, bf16[4,1,2,384,384]{4,3,2,1,0:T(8,128)(2,1)}, u32[]{:S(2)}) copy-start(bf16[4,1,2,384,384]{4,3,2,1,0:T(8,128)(2,1)} %param.6) | copy-start | bytes 7077892
  0.0 5.2 %copy-start.4 = (s32[4]{0:T(128)S(1)}, s32[4]{0:T(128)}, u32[]{:S(2)}) copy-start(s32[4]{0:T(128)} %offsets.9) | copy-start | bytes 52
  0.0 5.2 %collective-permute-start.1 = (bf16[4,2,384,384]{3,2,1,0:T(8,128)(2,1)}, bf16[4,2,384,384]{3,2,1,0:T(8,128)(2,1)}, u32[]{:S(2)}, u32[]{:S(2)}) collective-permute-start(bf16[4,2,384,384]{3,2,1,0:T(8,128)(2,1)} %bitcast.4), channel_id=1, source_target_pairs={{0,8},{8,0},{1,9},{9,1},{2,10},{10,2},{3,11},{11,3},{4,12},{12,4},... | collective-permute-start | bytes 7077896 | tf_op jit(solution)/shard_map/ppermute | solution.py:533
  2.0 32.1 %collective-permute-start = (bf16[2,2,384,384]{3,2,1,0:T(8,128)(2,1)S(1)}, bf16[2,2,384,384]{3,2,1,0:T(8,128)(2,1)S(1)}, u32[]{:S(2)}, u32[]{:S(2)}) collective-permute-start(bf16[2,2,384,384]{3,2,1,0:T(8,128)(2,1)S(1)} %shard_map.64), channel_id=1, source_target_pairs={{8,16},{24,32},{40,48},{56,64},{72,80},{88,96},{104,112},{16,8},{3... | collective-permute-start | bytes 3538952 | tf_op jit(solution)/shard_map/ppermute | solution.py:532
  34.1 2.7 %copy-start.1 = (bf16[2,2,384,384]{3,2,1,0:T(8,128)(2,1)}, bf16[2,2,384,384]{3,2,1,0:T(8,128)(2,1)S(1)}, u32[]{:S(2)}) copy-start(bf16[2,2,384,384]{3,2,1,0:T(8,128)(2,1)S(1)} %collective-permute-done.near.refs_6_) | copy-start | bytes 3538948
  36.8 2.5 %collective-permute-start.2 = (bf16[3456,128]{1,0:T(8,128)(2,1)S(1)}, bf16[3456,128]{1,0:T(8,128)(2,1)S(1)}, u32[]{:S(2)}, u32[]{:S(2)}) collective-permute-start(bf16[3456,128]{1,0:T(8,128)(2,1)S(1)} %get-tuple-element.21), channel_id=1, source_target_pairs={{0,8},{8,0},{1,9},{9,1},{2,10},{10,2},{3,11},{11,3},{4,12},{12,4},... | collective-permute-start | bytes 2654216 | tf_op jit(solution)/shard_map/ppermute | solution.py:538
  72.1 15.0 %all-to-all-start.2 = ((bf16[16,216,128]{2,1,0:T(8,128)(2,1)}), bf16[16,216,128]{2,1,0:T(8,128)(2,1)S(1)}, u32[]{:S(2)}, u32[]{:S(2)}) async-start(bf16[16,216,128]{2,1,0:T(8,128)(2,1)} %shard_map.66), calls=%async_computation.2 | async-start | bytes 1769472 | tf_op jit(solution)/shard_map/all_to_all | solution.py:546
  77.5 34.7 %collective-permute-start.4 = (bf16[2,2,384,384]{3,2,1,0:T(8,128)(2,1)S(1)}, bf16[2,2,384,384]{3,2,1,0:T(8,128)(2,1)}, u32[]{:S(2)}, u32[]{:S(2)}) collective-permute-start(bf16[2,2,384,384]{3,2,1,0:T(8,128)(2,1)S(1)} %shard_map.67), channel_id=1, source_target_pairs={{8,16},{24,32},{40,48},{56,64},{72,80},{88,96},{104,112},{16,8},{3... | collective-permute-start | bytes 3538952 | tf_op jit(solution)/shard_map/ppermute | solution.py:535
  87.0 43.7 %collective-permute-start.3 = (bf16[3456,128]{1,0:T(8,128)(2,1)S(1)}, bf16[3456,128]{1,0:T(8,128)(2,1)S(1)}, u32[]{:S(2)}, u32[]{:S(2)}) collective-permute-start(bf16[3456,128]{1,0:T(8,128)(2,1)S(1)} %bitcast.12), channel_id=1, source_target_pairs={{0,8},{8,0},{1,9},{9,1},{2,10},{10,2},{3,11},{11,3},{4,12},{12,4},... | collective-permute-start | bytes 2654216 | tf_op jit(solution)/shard_map/ppermute | solution.py:550
  106.9 19.3 %copy-start.5 = (s32[4]{0:T(128)S(1)}, s32[4]{0:T(128)}, u32[]{:S(2)}) copy-start(s32[4]{0:T(128)} %offsets.9) | copy-start | bytes 52
  126.2 4.5 %copy-start.2 = (bf16[768,768]{1,0:T(8,128)(2,1)S(1)}, bf16[768,768]{1,0:T(8,128)(2,1)}, u32[]{:S(2)}) copy-start(bf16[768,768]{1,0:T(8,128)(2,1)} %born_early.1.early) | copy-start | bytes 3538948
  126.2 4.5 %copy-start.3 = (bf16[768,768]{1,0:T(8,128)(2,1)S(1)}, bf16[768,768]{1,0:T(8,128)(2,1)}, u32[]{:S(2)}) copy-start(bf16[768,768]{1,0:T(8,128)(2,1)} %born_late.1.late) | copy-start | bytes 3538948

commit v6 on v5

--- a/solution.py
+++ b/solution.py
@@ -12,7 +12,6 @@
 BANDS = 16
 ROWS = 18 * HALF // BANDS
 FLAT = BANDS * ROWS
-FULL = 60 << 20
 F32 = jnp.float32
 BF16 = jnp.bfloat16
 SWAP = [(0, 1), (1, 0)]
@@ -67,71 +66,90 @@
     )(place, in_hbm(own))
 
 
-def polar_pairs(core, near, slots, turned, offsets, each):
-    _, _, first, last = offset_roles(offsets)
-    for index, span in enumerate(spans(offsets, first, last)):
-        base = jnp.clip(4 - span, 0, 2)
-        split = jnp.where(core == 0, jnp.maximum(base, 2), jnp.maximum(base, 6 - span))
-        outer = (core == 0) == near
-        begin = jnp.where(outer, base, split)
-        end = jnp.where(outer, split, base + 4)
-        if index == 0:
-            back = jnp.bool_(False)
-        else:
-            back = offsets[first if index == 1 else last] < 0
-        plain = jnp.where(back, span, 0)
-        cross = jnp.where(back, 0, span)
-
-        def block_sum(rows, real, imag):
-            def step(s, carry):
-                real, imag = carry
-                ar = slots[s + plain + 2, 0, rows, :].astype(F32)
-                ai = slots[s + plain + 2, 1, rows, :].astype(F32)
-                br = turned[s + cross, 0, rows, :]
-                bi = turned[s + cross, 1, rows, :]
-                return real + (ar * br - ai * bi), imag + (ar * bi + ai * br)
-
-            return lax.fori_loop(begin, end, step, (real, imag))
-
-        each(index, block_sum)
-
-
-def prepare_body(place, offsets, own, mate, slots, turned, partial, sems):
+def edge_body(place, own, same, cross, whole, sems):
+    core = place[0]
+
+    @pl.when(core == 1)
+    def _():
+        copies = [
+            pltpu.make_async_copy(own.at[pl.ds(2, 2), :, pl.ds(HALF, HALF), :], same, sems.at[0]),
+            pltpu.make_async_copy(own.at[pl.ds(2, 2), :, pl.ds(0, HALF), :], cross, sems.at[1]),
+        ]
+        for copy in copies:
+            copy.start()
+        for copy in copies:
+            copy.wait()
+
+    @pl.when(core == 0)
+    def _():
+        copy = pltpu.make_async_copy(own.at[pl.ds(0, 2)], whole, sems.at[0])
+        copy.start()
+        copy.wait()
+        for item in range(2):
+            for part in range(2):
+                value = whole[item, part].astype(F32).T.astype(BF16)
+                same[item, part] = value[:HALF]
+                cross[item, part] = value[HALF:]
+
+
+def edge_call(place, own):
+    half = jax.ShapeDtypeStruct((2, 2, HALF, NB), BF16)
+    return pl.pallas_call(
+        edge_body,
+        out_shape=(half, half),
+        in_specs=[SMEM, ANY],
+        out_specs=(VMEM, VMEM),
+        scratch_shapes=[pltpu.VMEM((2, 2, NB, NB), BF16), pltpu.SemaphoreType.DMA((2,))],
+        compiler_params=pltpu.CompilerParams(vmem_limit_bytes=6 << 20),
+        cost_estimate=pl.CostEstimate(flops=0, bytes_accessed=2_400_000, transcendentals=0),
+        name="edge",
+    )(place, in_hbm(own))
+
+
+def prepare_body(place, offsets, own, mate, chip, turned, partial, sems):
     core = place[0]
     copies = [
-        pltpu.make_async_copy(own, slots.at[pl.ds(4, 4)], sems.at[0]),
-        pltpu.make_async_copy(mate, slots.at[pl.ds(8 - 8 * core, 4)], sems.at[1]),
+        pltpu.make_async_copy(own, chip.at[pl.ds(4 * core, 4)], sems.at[0]),
+        pltpu.make_async_copy(mate, chip.at[pl.ds(4 - 4 * core, 4)], sems.at[1]),
     ]
     for copy in copies:
         copy.start()
     for copy in copies:
         copy.wait()
 
-    @pl.loop(0, 12)
+    @pl.loop(2, 16)
     def _(step):
-        slot = step // 2 + 2 - 2 * core
-        part = step % 2
-        turned[slot, part] = slots[slot + 2, part].astype(F32).T
-
-    def each(index, block_sum):
-        @pl.loop(0, NB // 16)
+        turned[step // 2, step % 2] = chip[step // 2, step % 2].astype(F32).T
+
+    _, _, first, last = offset_roles(offsets)
+    for index, span in enumerate(spans(offsets, first, last)):
+
+        @pl.loop(0, HALF // 32)
         def _(block):
-            rows = pl.ds(pl.multiple_of(block * 16, 16), 16)
-            zero = jnp.zeros((16, NB), F32)
-            real, imag = block_sum(rows, zero, zero)
+            rows = pl.ds(pl.multiple_of(block * 32, 32), 32)
+            there = pl.ds(pl.multiple_of(core * HALF + block * 32, 32), 32)
+
+            def step(s, carry):
+                real, imag = carry
+                ar = chip[s, 0, there, :].astype(F32)
+                ai = chip[s, 1, there, :].astype(F32)
+                br = turned[s + span, 0, there, :]
+                bi = turned[s + span, 1, there, :]
+                return real + (ar * br - ai * bi), imag + (ar * bi + ai * br)
+
+            zero = jnp.zeros((32, NB), F32)
+            real, imag = lax.fori_loop(0, 8 - span, step, (zero, zero))
             partial[index, 0, rows, :] = real
             partial[index, 1, rows, :] = imag
 
-    polar_pairs(core, False, slots, turned, offsets, each)
-
 
 def prepare_call(place, offsets, own, mate):
     return pl.pallas_call(
         prepare_body,
         out_shape=(
-            jax.ShapeDtypeStruct((12, 2, NB, NB), BF16),
+            jax.ShapeDtypeStruct((8, 2, NB, NB), BF16),
             jax.ShapeDtypeStruct((8, 2, NB, NB), F32),
-            jax.ShapeDtypeStruct((3, 2, NB, NB), F32),
+            jax.ShapeDtypeStruct((3, 2, HALF, NB), F32),
         ),
         in_specs=[SMEM, SMEM, ANY, ANY],
         out_specs=(VMEM, VMEM, VMEM),
@@ -142,104 +160,113 @@
     )(place, offsets, own, mate)
 
 
-def polar_half(core, half, offsets, slots, turned, partial, target):
-    def each(index, block_sum):
+def polar_body(place, offsets, same, cross, chip, turned, partial, out, edges, flat, sems):
+    core = place[0]
+    copies = [
+        pltpu.make_async_copy(same, edges.at[1 - core], sems.at[0]),
+        pltpu.make_async_copy(cross, edges.at[core], sems.at[1]),
+    ]
+    for copy in copies:
+        copy.start()
+    for copy in copies:
+        copy.wait()
+    _, _, first, last = offset_roles(offsets)
+    stores = []
+    for index, span in enumerate(spans(offsets, first, last)):
+
         @pl.loop(0, HALF // 32)
         def _(block):
-            rows = pl.ds(pl.multiple_of(half * HALF + block * 32, 32), 32)
-            pair = block_sum(rows, partial[index, 0, rows, :], partial[index, 1, rows, :])
+            rows = pl.ds(pl.multiple_of(block * 32, 32), 32)
+            there = pl.ds(pl.multiple_of(core * HALF + block * 32, 32), 32)
+
+            def multiply(carry, ar, ai, br, bi):
+                real, imag = carry
+                return real + (ar * br - ai * bi), imag + (ar * bi + ai * br)
+
+            def before(j, carry):
+                return multiply(
+                    carry,
+                    edges[0, 1 - j, 0, rows, :].astype(F32),
+                    edges[0, 1 - j, 1, rows, :].astype(F32),
+                    turned[span - 1 - j, 0, there, :],
+                    turned[span - 1 - j, 1, there, :],
+                )
+
+            def after(j, carry):
+                return multiply(
+                    carry,
+                    chip[8 - span + j, 0, there, :].astype(F32),
+                    chip[8 - span + j, 1, there, :].astype(F32),
+                    edges[1, j, 0, rows, :].astype(F32),
+                    edges[1, j, 1, rows, :].astype(F32),
+                )
+
+            pair = (partial[index, 0, rows, :], partial[index, 1, rows, :])
+            pair = lax.fori_loop(0, jnp.maximum(span - 2, 0), before, pair)
+            pair = lax.fori_loop(0, jnp.minimum(span, 2), after, pair)
             for part, value in enumerate(pair):
                 for panel in range(3):
                     start = ((index * 2 + part) * 3 + panel) * HALF
-                    target[pl.ds(pl.multiple_of(start + block * 32, 32), 32), :] = value[
+                    flat[pl.ds(pl.multiple_of(start + block * 32, 32), 32), :] = value[
                         :, panel * 128 : (panel + 1) * 128
-                    ].astype(target.dtype)
-
-    polar_pairs(core, True, slots, turned, offsets, each)
-
-
-def polar_send_body(place, offsets, near, slots_in, turned_in, partial, slots, turned, send, sem):
-    core = place[0]
-    copy = pltpu.make_async_copy(near, slots.at[pl.ds(2 + 6 * core, 2)], sem)
-    copy.start()
-    copy.wait()
-    for item in range(2):
-        slot = 6 * core + item
-        for part in range(2):
-            turned[slot, part] = slots[slot + 2, part].astype(F32).T
-    polar_half(core, 1 - core, offsets, slots, turned, partial, send)
-
-
-def polar_keep_body(place, offsets, slots, turned, partial, keep):
-    core = place[0]
-    polar_half(core, core, offsets, slots, turned, partial, keep)
-
-
-def polar_send_call(place, offsets, near, slots, turned, partial):
-    return pl.pallas_call(
-        polar_send_body,
-        out_shape=(
-            jax.ShapeDtypeStruct(slots.shape, BF16),
-            jax.ShapeDtypeStruct(turned.shape, F32),
-            jax.ShapeDtypeStruct((FLAT, 128), BF16),
-        ),
-        in_specs=[SMEM, SMEM, ANY, VMEM, VMEM, VMEM],
-        out_specs=(VMEM, VMEM, VMEM),
-        input_output_aliases={3: 0, 4: 1},
-        scratch_shapes=[pltpu.SemaphoreType.DMA],
-        compiler_params=pltpu.CompilerParams(vmem_limit_bytes=4 << 20),
-        cost_estimate=pl.CostEstimate(flops=20_000_000, bytes_accessed=9_000_000, transcendentals=0),
-        name="polar_send",
-    )(place, offsets, near, slots, turned, partial)
-
-
-def polar_keep_call(place, offsets, slots, turned, partial):
-    return pl.pallas_call(
-        polar_keep_body,
-        out_shape=jax.ShapeDtypeStruct((FLAT, 128), F32),
-        in_specs=[SMEM, SMEM, VMEM, VMEM, VMEM],
-        out_specs=VMEM,
-        compiler_params=pltpu.CompilerParams(vmem_limit_bytes=4 << 20),
-        cost_estimate=pl.CostEstimate(flops=20_000_000, bytes_accessed=9_000_000, transcendentals=0),
-        name="polar_keep",
-    )(place, offsets, slots, turned, partial)
-
-
-def add_body(kept, sent, out, total, sems):
-    third = FLAT // 4
-    stores = []
-    for i in range(4):
-        rows = pl.ds(i * third, third)
-        total[rows, :] = (kept[rows, :] + sent[rows, :].astype(F32)).astype(BF16)
-        store = pltpu.make_async_copy(total.at[rows], out.at[rows], sems.at[i])
+                    ].astype(BF16)
+
+        done = pl.ds(index * 6 * HALF, 6 * HALF)
+        store = pltpu.make_async_copy(flat.at[done], out.at[done], sems.at[2 + index])
         store.start()
         stores.append(store)
     for store in stores:
         store.wait()
 
 
-def add_call(kept, sent):
-    return pl.pallas_call(
-        add_body,
+def polar_call(place, offsets, same, cross, chip, turned, partial):
+    return pl.pallas_call(
+        polar_body,
         out_shape=jax.ShapeDtypeStruct((FLAT, 128), BF16),
-        in_specs=[VMEM, VMEM],
+        in_specs=[SMEM, SMEM, ANY, ANY, VMEM, VMEM, VMEM],
         out_specs=ANY,
-        scratch_shapes=[pltpu.VMEM((FLAT, 128), BF16), pltpu.SemaphoreType.DMA((4,))],
-        compiler_params=pltpu.CompilerParams(vmem_limit_bytes=3 << 20),
-        cost_estimate=pl.CostEstimate(flops=500_000, bytes_accessed=3_000_000, transcendentals=0),
-        name="pair_add",
-    )(kept, sent)
-
-
-def window_copies(core, own, mate, near, far, slots, sems):
+        scratch_shapes=[
+            pltpu.VMEM((2, 2, 2, HALF, NB), BF16),
+            pltpu.VMEM((FLAT, 128), BF16),
+            pltpu.SemaphoreType.DMA((5,)),
+        ],
+        compiler_params=pltpu.CompilerParams(vmem_limit_bytes=6 << 20),
+        cost_estimate=pl.CostEstimate(flops=20_000_000, bytes_accessed=9_000_000, transcendentals=0),
+        name="polar",
+    )(place, offsets, same, cross, chip, turned, partial)
+
+
+def near_body(place, swapped, cross, out, sems):
+    core = place[0]
     copies = [
-        pltpu.make_async_copy(own, slots.at[pl.ds(4, 4)], sems.at[0]),
-        pltpu.make_async_copy(mate, slots.at[pl.ds(8 - 8 * core, 4)], sems.at[1]),
-        pltpu.make_async_copy(near, slots.at[pl.ds(2 + 6 * core, 2)], sems.at[2]),
+        pltpu.make_async_copy(cross, out.at[:, :, pl.ds(core * HALF, HALF), :], sems.at[0]),
+        pltpu.make_async_copy(
+            swapped, out.at[:, :, pl.ds(HALF - core * HALF, HALF), :], sems.at[1]
+        ),
     ]
-    if far is not None:
-        copies.append(pltpu.make_async_copy(far, slots.at[pl.ds(10 * core, 2)], sems.at[3]))
-    return copies
+    for copy in copies:
+        copy.start()
+    for copy in copies:
+        copy.wait()
+
+    @pl.when(core == 1)
+    def _():
+        for item in range(2):
+            for part in range(2):
+                out[item, part] = out[item, part].astype(F32).T.astype(BF16)
+
+
+def near_call(place, swapped, cross):
+    return pl.pallas_call(
+        near_body,
+        out_shape=jax.ShapeDtypeStruct((2, 2, NB, NB), BF16),
+        in_specs=[SMEM, ANY, ANY],
+        out_specs=VMEM,
+        scratch_shapes=[pltpu.SemaphoreType.DMA((2,))],
+        compiler_params=pltpu.CompilerParams(vmem_limit_bytes=4 << 20),
+        cost_estimate=pl.CostEstimate(flops=0, bytes_accessed=2_400_000, transcendentals=0),
+        name="near_join",
+    )(place, swapped, cross)
 
 
 def born_body(early, *refs):
@@ -333,12 +360,12 @@
             pltpu.VMEM((size, size), F32),
             pltpu.SemaphoreType.DMA((4, 5)),
         ],
-        compiler_params=pltpu.CompilerParams(vmem_limit_bytes=FULL),
+        compiler_params=pltpu.CompilerParams(vmem_limit_bytes=22 << 20),
         cost_estimate=pl.CostEstimate(
             flops=16 * size**3, bytes_accessed=12_000_000, transcendentals=0
         ),
         name="born_early" if early else "born_late",
-    )(place, offsets, occupation, coupling, *arrays, vertex)
+    )(place, offsets, occupation, coupling, *map(in_hbm, arrays[:3]), *arrays[3:], in_hbm(vertex))
 
 
 def sum_body(count, copies, bands, out, buffer, value, *sems):
@@ -382,7 +409,7 @@
     )(bands)
 
 
-def half_products(offsets, half, source, joined, table, magnon, bottom_sum):
+def half_products(begin, offsets, half, source, joined, table, magnon, sums):
     for index in range(3):
         for part in range(2):
             for panel in range(3):
@@ -392,17 +419,29 @@
                 ]
     top, bottom, first, last = offset_roles(offsets)
     rows = pl.ds(pl.multiple_of(half * HALF, HALF), HALF)
-    for index, k in enumerate((top, first, last)):
+
+    def direct(index, k):
         value = jnp.dot(joined[index], table[k], preferred_element_type=F32)
         magnon[index, rows, :] = value.astype(BF16).astype(F32)
-    for part in range(2):
-        turned = joined[0, :, part * NB : (part + 1) * NB].astype(F32).T.astype(BF16)
-        begin = pl.ds(pl.multiple_of(part * NB + half * HALF, HALF), HALF)
-        bottom_sum[...] += jnp.dot(turned, table[bottom, begin, :], preferred_element_type=F32)
+
+    def transposed(index, k):
+        value = None
+        for part in range(2):
+            turned = joined[index, :, part * NB : (part + 1) * NB].astype(F32).T.astype(BF16)
+            these = pl.ds(pl.multiple_of(part * NB + half * HALF, HALF), HALF)
+            term = jnp.dot(turned, table[k, these, :], preferred_element_type=F32)
+            value = term if value is None else value + term
+        sums[index] = value if begin else sums[index] + value
+
+    direct(0, top)
+    transposed(0, bottom)
+    for index, k in ((1, first), (2, last)):
+        pl.when(offsets[k] > 0)(lambda: direct(index, k))
+        pl.when(offsets[k] < 0)(lambda: transposed(index, k))
 
 
 def start_body(
-    place, offsets, mine, free, own, mate, near, far,
+    place, offsets, mine, free, own, mate,
     slots, magnon, bottom_sum, table, source, plain, joined, sems,
 ):
     core = place[0]
@@ -410,10 +449,12 @@
         pltpu.make_async_copy(mine, source, sems.at[4]),
         pltpu.make_async_copy(free, plain, sems.at[5]),
     ]
-    loads = window_copies(core, own, mate, near, far, slots, sems)
+    loads = [
+        pltpu.make_async_copy(own, slots.at[pl.ds(4, 4)], sems.at[0]),
+        pltpu.make_async_copy(mate, slots.at[pl.ds(8 - 8 * core, 4)], sems.at[1]),
+    ]
     for load in ready + loads:
         load.start()
-    bottom_sum[...] = jnp.zeros_like(bottom_sum)
     for load in ready:
         load.wait()
     for k in range(4):
@@ -423,22 +464,22 @@
         table[k, :NB, NB:] = fi
         table[k, NB:, :NB] = -fi
         table[k, NB:, NB:] = fr
-    half_products(offsets, core, source, joined, table, magnon, bottom_sum)
+    half_products(True, offsets, core, source, joined, table, magnon, bottom_sum)
     for load in loads:
         load.wait()
 
 
-def start_call(place, offsets, mine, free, own, mate, near, far):
+def start_call(place, offsets, mine, free, own, mate):
     size = 2 * NB
     return pl.pallas_call(
         start_body,
         out_shape=(
             jax.ShapeDtypeStruct((12, 2, NB, NB), BF16),
             jax.ShapeDtypeStruct((3, NB, size), F32),
-            jax.ShapeDtypeStruct((NB, size), F32),
+            jax.ShapeDtypeStruct((3, NB, size), F32),
             jax.ShapeDtypeStruct((4, size, size), BF16),
         ),
-        in_specs=[SMEM, SMEM] + [ANY] * 6,
+        in_specs=[SMEM, SMEM] + [ANY] * 4,
         out_specs=(VMEM,) * 4,
         scratch_shapes=[
             pltpu.VMEM((FLAT, 128), BF16),
@@ -451,20 +492,34 @@
             flops=1_000_000_000, bytes_accessed=10_000_000, transcendentals=0
         ),
         name="final_start",
-    )(place, offsets, mine, *(in_hbm(x) for x in (free, own, mate, near, far)))
+    )(place, offsets, mine, *(in_hbm(x) for x in (free, own, mate)))
 
 
 def final_body(
-    place, offsets, other, early, late, slots, magnon_in, sum_in, table, out, magnon, bottom_sum,
-    source, joined, result, sems,
+    place, offsets, other, near, far, early, late, slots_in, magnon_in, sum_in, table,
+    out, slots, magnon, bottom_sum, source, joined, result, sems,
 ):
     core = place[0]
+    loads = [
+        pltpu.make_async_copy(near, slots.at[pl.ds(2 + 6 * core, 2)], sems.at[5]),
+        pltpu.make_async_copy(far, slots.at[pl.ds(10 * core, 2)], sems.at[6]),
+    ]
     ready = pltpu.make_async_copy(other, source, sems.at[4])
     ready.start()
+    for load in loads:
+        load.start()
     ready.wait()
-    half_products(offsets, 1 - core, source, joined, table, magnon, bottom_sum)
-    magnon[0] += bottom_sum[...].astype(BF16).astype(F32)
+    half_products(False, offsets, 1 - core, source, joined, table, magnon, bottom_sum)
     _, _, first, last = offset_roles(offsets)
+    magnon[0] += bottom_sum[0].astype(BF16).astype(F32)
+    for index, k in ((1, first), (2, last)):
+
+        @pl.when(offsets[k] < 0)
+        def _():
+            magnon[index] = bottom_sum[index].astype(BF16).astype(F32)
+
+    for load in loads:
+        load.wait()
     reach = spans(offsets, first, last)
     stores = []
     for item, energy in enumerate((2 - 2 * core, 3 - 2 * core, 2 * core, 2 * core + 1)):
@@ -495,30 +550,31 @@
         store.wait()
 
 
-def final_call(place, offsets, other, early, late, slots, magnon, bottom_sum, table):
+def final_call(place, offsets, other, near, far, early, late, slots, magnon, bottom_sum, table):
     size = 2 * NB
     return pl.pallas_call(
         final_body,
         out_shape=(
             jax.ShapeDtypeStruct((4, 1, 2, NB, NB), BF16),
+            jax.ShapeDtypeStruct(slots.shape, BF16),
             jax.ShapeDtypeStruct(magnon.shape, F32),
             jax.ShapeDtypeStruct(bottom_sum.shape, F32),
         ),
-        in_specs=[SMEM, SMEM, ANY] + [VMEM] * 6,
-        out_specs=(ANY, VMEM, VMEM),
-        input_output_aliases={6: 1, 7: 2},
+        in_specs=[SMEM, SMEM, ANY, ANY, ANY] + [VMEM] * 6,
+        out_specs=(ANY, VMEM, VMEM, VMEM),
+        input_output_aliases={7: 1, 8: 2, 9: 3},
         scratch_shapes=[
             pltpu.VMEM((FLAT, 128), BF16),
             pltpu.VMEM((3, HALF, size), BF16),
             pltpu.VMEM((4, 2, NB, NB), BF16),
-            pltpu.SemaphoreType.DMA((5,)),
+            pltpu.SemaphoreType.DMA((7,)),
         ],
         compiler_params=pltpu.CompilerParams(vmem_limit_bytes=12 << 20),
         cost_estimate=pl.CostEstimate(
             flops=1_000_000_000, bytes_accessed=18_000_000, transcendentals=0
         ),
         name="final",
-    )(place, offsets, other, early, late, slots, magnon, bottom_sum, table)[0]
+    )(place, offsets, other, in_hbm(near), in_hbm(far), early, late, slots, magnon, bottom_sum, table)[0]
 
 
 def per_device(green_blocks, offsets, occupation, coupling, vertex, magnon_free):
@@ -528,16 +584,18 @@
     own = green_blocks.reshape(4, 2, NB, NB)
     across = [(i, i + 1) for i in range(1, count - 1, 2)]
     across += [(target, source) for source, target in across]
-    outer = cut_call(place, own, 0, 2)
-    near = lax.ppermute(outer, ENERGY, across)
+    along = [(i, i + 2) for i in range(1, count - 2, 2)]
+    along += [(i + 1, i - 1) for i in range(1, count - 2, 2)]
+    to_same, to_cross = edge_call(place, own)
+    cross = lax.ppermute(to_cross, ENERGY, across)
+    same = lax.ppermute(to_same, ENERGY, along)
     mate = lax.ppermute(own, "core", SWAP)
     inner = cut_call(place, own, 2, -2)
     far = lax.ppermute(inner, ENERGY, across)
-    slots, turned, partial = prepare_call(place, offsets, own, mate)
-    slots, turned, send = polar_send_call(place, offsets, near, slots, turned, partial)
-    sent = lax.ppermute(send, "core", SWAP)
-    kept = polar_keep_call(place, offsets, slots, turned, partial)
-    pair = add_call(kept, sent)
+    chip, turned, partial = prepare_call(place, offsets, own, mate)
+    pair = polar_call(place, offsets, same, cross, chip, turned, partial)
+    swapped = lax.ppermute(same, "core", SWAP)
+    near = near_call(place, swapped, cross)
     bands = lax.all_to_all(pair.reshape(BANDS, ROWS, 128), PLANE, 0, 0, tiled=True)
     early = born_call(place, offsets, occupation, coupling, (own, mate, near), vertex)
     copies = sum_call(bands, 4)
@@ -548,8 +606,8 @@
         place, offsets, occupation, coupling, (own, mate, near, far), vertex
     )
     other = lax.ppermute(mine, "core", SWAP)
-    held = start_call(place, offsets, mine, magnon_free, own, mate, near, far)
-    return final_call(place, offsets, other, early, late, *held)
+    held = start_call(place, offsets, mine, magnon_free, own, mate)
+    return final_call(place, offsets, other, near, far, early, late, *held)
 
 
 def solution(mesh):

time: 139 us -> 139 us (level)
  the two profiles are of different devices: /device:TPU:5 before, /device:TPU:17 now
where the time goes in v6:
time: 139 us; the launch traced here: 138 us
  Pallas kernels  56.3 us (41%)
  blocking collectives  29.8 us (21%)
  waiting for transfers between devices  29.5 us (21%)
  starting transfers between devices  21.4 us (15%)
    pallas_call x2, Pallas kernels, born_call(): pl.pallas_call(lambda *refs: born_body(early, *refs), out_shape=jax.Shape...  24.9 us
    all_to_all x1, blocking collectives, per_device(): lax.all_to_all(pair.reshape(BANDS, ROWS, 128), PLANE, 0, 0, tiled=True)  19.8 us
    ppermute x1, waiting for transfers between devices, per_device(): cross = lax.ppermute(to_cross, ENERGY, across)  12.8 us
    all_to_all x1, blocking collectives, per_device(): bands = lax.all_to_all(copies, ROW, 0, 0, tiled=True)  10 us
    ppermute x1, waiting for transfers between devices, per_device(): far = lax.ppermute(inner, ENERGY, across)  9.33 us
    pallas_call x1, Pallas kernels, final_call(): pl.pallas_call(final_body, out_shape=(jax.ShapeDtypeStruct((4, 1, 2, NB,...  8.32 us
    pallas_call x1, Pallas kernels, prepare_call(): pl.pallas_call(prepare_body, out_shape=(jax.ShapeDtypeStruct((8, 2, NB, N...  7.34 us
    all_to_all x1, starting transfers between devices, per_device(): mine = lax.all_to_all(copies, PLANE, 0, 0, tiled=True).reshape(FLAT, 128)  5.82 us
  transfers between devices with their start and end apart: 7, of which 4 were waited for; matrix products, arithmetic and copies ran while one was open for 0% of the time, Pallas kernels for 30%

profile of v6, /device:TPU:17, one launch (start us, length us, event | category | flops | bytes accessed | tf_op | source)
XLA Modules:
  0.0 138.4 jit_solution(813864610274302876)
XLA Ops:
  0.0 0.0 copy-start
  0.0 0.0 copy-start.3
  0.0 0.7 collective-permute-start.2
  0.7 1.3 edge.1
  2.0 4.7 %collective-permute-start = (bf16[2,2,192,384]{3,2,1,0:T(8,128)(2,1)S(1)}, bf16[2,2,192,384]{3,2,1,0:T(8,128)(2,1)S(1)}, u32[]{:S(2)}, u32[]{:S(2)}) collective-permute-start(bf16[2,2,192,384]{3,2,1,0:T(8,128)(2,1)S(1)} %get-tuple-element.15), channel_id=1, source_target_pairs={{8,24},{24,40},{40,56},{56,72},{72,88},{88,104},{104,120},{16,0},{... | collective-permute-start | bytes 1769480 | tf_op jit(solution)/shard_map/ppermute | solution.py:591
  6.7 2.8 %collective-permute-start.1 = (bf16[2,2,192,384]{3,2,1,0:T(8,128)(2,1)S(1)}, bf16[2,2,192,384]{3,2,1,0:T(8,128)(2,1)S(1)}, u32[]{:S(2)}, u32[]{:S(2)}) collective-permute-start(bf16[2,2,192,384]{3,2,1,0:T(8,128)(2,1)S(1)} %get-tuple-element.16), channel_id=1, source_target_pairs={{8,16},{24,32},{40,48},{56,64},{72,80},{88,96},{104,112},{16,8},{3... | collective-permute-start | bytes 1769480 | tf_op jit(solution)/shard_map/ppermute | solution.py:590
  9.5 0.0 collective-permute-done.2.mate.refs_5_
  9.5 0.0 copy-done
  9.5 0.0 copy-done.3
  9.5 7.3 %prepare.1 = (bf16[8,2,384,384]{3,2,1,0:T(8,128)(2,1)S(1)}, f32[8,2,384,384]{3,2,1,0:T(8,128)S(1)}, f32[3,2,192,384]{3,2,1,0:T(8,128)S(1)}) custom-call(s32[1]{0:T(128)} %bitcast.place.refs_0_, s32[4]{0:T(128)S(1)} %copy-done.3, bf16[4,2,384,384]{3,2,1,0:T(8,128)(2,1)S(1)} %bitcast.10, bf16[4,2,384,384]{3,2,1,0:T(8,128)(2,1)} %collective-permute-done.2.mate.refs_5_), custom_call_target="tpu_custom_call" | custom-call | flops 20000000 | bytes 9000000 | tf_op jit(solution)/shard_map/prepare/pallas_call | solution.py:147
  16.9 4.5 %collective-permute-done.same = bf16[2,2,192,384]{3,2,1,0:T(8,128)(2,1)S(1)} collective-permute-done((bf16[2,2,192,384]{3,2,1,0:T(8,128)(2,1)S(1)}, bf16[2,2,192,384]{3,2,1,0:T(8,128)(2,1)S(1)}, u32[]{:S(2)}, u32[]{:S(2)}) %collective-permute-start) | collective-permute-done | bytes 589856 | tf_op jit(solution)/shard_map/ppermute | solution.py:591
  21.3 12.8 %collective-permute-done.1.cross = bf16[2,2,192,384]{3,2,1,0:T(8,128)(2,1)S(1)} collective-permute-done((bf16[2,2,192,384]{3,2,1,0:T(8,128)(2,1)S(1)}, bf16[2,2,192,384]{3,2,1,0:T(8,128)(2,1)S(1)}, u32[]{:S(2)}, u32[]{:S(2)}) %collective-permute-start.1) | collective-permute-done | bytes 589856 | tf_op jit(solution)/shard_map/ppermute | solution.py:590
  34.1 3.5 %polar.1 = bf16[3456,128]{1,0:T(8,128)(2,1)S(1)} custom-call(s32[1]{0:T(128)} %bitcast.place.refs_0_, s32[4]{0:T(128)S(1)} %copy-done.3, bf16[2,2,192,384]{3,2,1,0:T(8,128)(2,1)S(1)} %collective-permute-done.same, bf16[2,2,192,384]{3,2,1,0:T(8,128)(2,1)S(1)} %collective-permute-done.1.cross, bf16[8,2,384,384]{3,2,1,0:T(8,128)(2,1)S(1)} %get-tuple-element.17.chip, ...), custom_call_target="tpu_custom_call" | custom-call | flops 20000000 | bytes 9000000 | tf_op jit(solution)/shard_map/polar/pallas_call | solution.py:223
  37.6 19.8 %all_to_all.15.refs_0_ = bf16[16,216,128]{2,1,0:T(8,128)(2,1)S(1)} all-to-all(bf16[16,216,128]{2,1,0:T(8,128)(2,1)S(1)} %bitcast.13), channel_id=1, replica_groups=mesh['y'=4,'xh'=2,'core'=2,'xl'=2,'z'=4] {'y','z'}, dimensions={0} | all-to-all | bytes 1769472 | tf_op jit(solution)/shard_map/all_to_all | solution.py:599
  57.4 1.7 %shard_map.64 = bf16[4,216,128]{2,1,0:T(8,128)(2,1)S(1)} custom-call(bf16[16,216,128]{2,1,0:T(8,128)(2,1)S(1)} %all_to_all.15.refs_0_), custom_call_target="tpu_custom_call" | custom-call | flops 500000 | bytes 1900000 | tf_op jit(solution)/shard_map/pallas_call | solution.py:396
  59.1 10.0 %all_to_all.16.refs_0_ = bf16[4,216,128]{2,1,0:T(8,128)(2,1)S(1)} all-to-all(bf16[4,216,128]{2,1,0:T(8,128)(2,1)S(1)} %shard_map.64), channel_id=1, replica_groups=mesh['y'=4,'xh'=2,'core'=2,'xl'=2,'z'=4] {'xh','xl'}, dimensions={0} | all-to-all | bytes 442368 | tf_op jit(solution)/shard_map/all_to_all | solution.py:602
  69.1 1.4 shard_map.65
  70.5 5.8 %all-to-all-start.2 = ((bf16[16,216,128]{2,1,0:T(8,128)(2,1)}), bf16[16,216,128]{2,1,0:T(8,128)(2,1)S(1)}, u32[]{:S(2)}, u32[]{:S(2)}) async-start(bf16[16,216,128]{2,1,0:T(8,128)(2,1)} %shard_map.65), calls=%async_computation.2 | async-start | bytes 1769472 | tf_op jit(solution)/shard_map/all_to_all | solution.py:604
  76.3 0.0 copy-start.4
  76.3 0.0 copy-start.5
  76.3 2.1 %collective-permute-start.4 = (bf16[2,2,192,384]{3,2,1,0:T(8,128)(2,1)S(1)}, bf16[2,2,192,384]{3,2,1,0:T(8,128)(2,1)S(1)}, u32[]{:S(2)}, u32[]{:S(2)}) collective-permute-start(bf16[2,2,192,384]{3,2,1,0:T(8,128)(2,1)S(1)} %collective-permute-done.same), channel_id=1, source_target_pairs={{0,8},{8,0},{1,9},{9,1},{2,10},{10,2},{3,11},{11,3},{4,12},{12,4},... | collective-permute-start | bytes 1769480 | tf_op jit(solution)/shard_map/ppermute | solution.py:597
  78.4 2.3 %shard_map.66 = bf16[2,2,384,384]{3,2,1,0:T(8,128)(2,1)} custom-call(s32[1]{0:T(128)} %bitcast.place.refs_0_, bf16[4,2,384,384]{3,2,1,0:T(8,128)(2,1)} %bitcast.6), custom_call_target="tpu_custom_call" | custom-call | bytes 2400000 | tf_op jit(solution)/shard_map/pallas_call | solution.py:58
  80.7 2.5 %collective-permute-start.5 = (bf16[2,2,384,384]{3,2,1,0:T(8,128)(2,1)}, bf16[2,2,384,384]{3,2,1,0:T(8,128)(2,1)S(1)}, u32[]{:S(2)}, u32[]{:S(2)}) collective-permute-start(bf16[2,2,384,384]{3,2,1,0:T(8,128)(2,1)} %shard_map.66), channel_id=1, source_target_pairs={{8,16},{24,32},{40,48},{56,64},{72,80},{88,96},{104,112},{16,8},{3... | collective-permute-start | bytes 3538952 | tf_op jit(solution)/shard_map/ppermute | solution.py:594
  83.2 0.0 collective-permute-done.4.swapped
  83.2 0.5 near_join.1.refs_6_.near
  83.7 0.0 copy-start.1
  83.7 1.0 copy-done.1
  84.8 3.0 %all-to-all-done.2 = bf16[16,216,128]{2,1,0:T(8,128)(2,1)S(1)} async-done(((bf16[16,216,128]{2,1,0:T(8,128)(2,1)}), bf16[16,216,128]{2,1,0:T(8,128)(2,1)S(1)}, u32[]{:S(2)}, u32[]{:S(2)}) %all-to-all-start.2) | async-done | bytes 884768 | tf_op jit(solution)/shard_map/all_to_all | solution.py:604
  87.7 2.9 %collective-permute-start.3 = (bf16[3456,128]{1,0:T(8,128)(2,1)S(1)}, bf16[3456,128]{1,0:T(8,128)(2,1)S(1)}, u32[]{:S(2)}, u32[]{:S(2)}) collective-permute-start(bf16[3456,128]{1,0:T(8,128)(2,1)S(1)} %bitcast.11), channel_id=1, source_target_pairs={{0,8},{8,0},{1,9},{9,1},{2,10},{10,2},{3,11},{11,3},{4,12},{12,4},... | collective-permute-start | bytes 2654216 | tf_op jit(solution)/shard_map/ppermute | solution.py:608
  90.6 0.0 copy-done.4
  90.6 0.0 copy-done.5
  90.6 12.9 %born_early.1.early = bf16[768,768]{1,0:T(8,128)(2,1)S(1)} custom-call(s32[1]{0:T(128)} %bitcast.place.refs_0_, s32[4]{0:T(128)S(1)} %copy-done.3, f32[4]{0:T(128)S(1)} %copy-done.4, s32[1,4]{1,0:T(1,128)S(1)} %copy-done.5, bf16[4,2,384,384]{3,2,1,0:T(8,128)(2,1)} %bitcast.7, bf16[4,2,384,384]{3,2,1,0:T(8,128)(2,1)} %collective-permute-done.2.mate.refs_5_, ...), custom_call_target="tpu_custom_call" | custom-call | flops 7247757312 | bytes 12000000 | tf_op jit(solution)/shard_map/born_early/pallas_call | solution.py:347
  103.5 9.3 %collective-permute-done.5.refs_7_.far = bf16[2,2,384,384]{3,2,1,0:T(8,128)(2,1)S(1)} collective-permute-done((bf16[2,2,384,384]{3,2,1,0:T(8,128)(2,1)}, bf16[2,2,384,384]{3,2,1,0:T(8,128)(2,1)S(1)}, u32[]{:S(2)}, u32[]{:S(2)}) %collective-permute-start.5) | collective-permute-done | bytes 1179680 | tf_op jit(solution)/shard_map/ppermute | solution.py:594
  112.8 0.0 copy-start.2
  112.8 12.0 %born_late.1.late = bf16[768,768]{1,0:T(8,128)(2,1)S(1)} custom-call(s32[1]{0:T(128)} %bitcast.place.refs_0_, s32[4]{0:T(128)S(1)} %copy-done.3, f32[4]{0:T(128)S(1)} %copy-done.4, s32[1,4]{1,0:T(1,128)S(1)} %copy-done.5, bf16[4,2,384,384]{3,2,1,0:T(8,128)(2,1)} %bitcast.8, bf16[4,2,384,384]{3,2,1,0:T(8,128)(2,1)} %collective-permute-done.2.mate.refs_5_, ...), custom_call_target="tpu_custom_call" | custom-call | flops 7247757312 | bytes 12000000 | tf_op jit(solution)/shard_map/born_late/pallas_call | solution.py:347
  124.8 0.0 copy-done.2
  124.9 5.1 %final_start.1 = (bf16[12,2,384,384]{3,2,1,0:T(8,128)(2,1)S(1)}, f32[3,384,768]{2,1,0:T(8,128)S(1)}, f32[3,384,768]{2,1,0:T(8,128)S(1)}, bf16[4,768,768]{2,1,0:T(8,128)(2,1)S(1)}) custom-call(s32[1]{0:T(128)} %bitcast.place.refs_0_, s32[4]{0:T(128)S(1)} %copy-done.3, bf16[3456,128]{1,0:T(8,128)(2,1)S(1)} %bitcast.12, bf16[4,2,384,384]{3,2,1,0:T(8,128)(2,1)} %free.1, ...), custom_call_target="tpu_custom_call" | custom-call | flops 1000000000 | bytes 10000000 | tf_op jit(solution)/shard_map/final_start/pallas_call | solution.py:474
  130.0 0.0 collective-permute-done.3.other
  130.0 8.3 %final.1 = (bf16[4,1,2,384,384]{4,3,2,1,0:T(8,128)(2,1)}, bf16[12,2,384,384]{3,2,1,0:T(8,128)(2,1)S(1)}, f32[3,384,768]{2,1,0:T(8,128)S(1)}, f32[3,384,768]{2,1,0:T(8,128)S(1)}) custom-call(s32[1]{0:T(128)} %bitcast.place.refs_0_, s32[4]{0:T(128)S(1)} %copy-done.3, ...), custom_call_target="tpu_custom_call", output_to_operand_aliasing={{1}: (7, {}), {2}: (8, {}), {3}: (9, {})} | custom-call | flops 1000000000 | bytes 18000000 | tf_op jit(solution)/shard_map/final/pallas_call | solution.py:555
Async XLA Ops:
  0.0 9.5 %copy-start = (bf16[4,1,2,384,384]{4,3,2,1,0:T(8,128)(2,1)S(1)}, bf16[4,1,2,384,384]{4,3,2,1,0:T(8,128)(2,1)}, u32[]{:S(2)}) copy-start(bf16[4,1,2,384,384]{4,3,2,1,0:T(8,128)(2,1)} %param.6) | copy-start | bytes 7077892
  0.0 9.5 %copy-start.3 = (s32[4]{0:T(128)S(1)}, s32[4]{0:T(128)}, u32[]{:S(2)}) copy-start(s32[4]{0:T(128)} %offsets.7) | copy-start | bytes 52
  0.0 9.5 %collective-permute-start.2 = (bf16[4,2,384,384]{3,2,1,0:T(8,128)(2,1)}, bf16[4,2,384,384]{3,2,1,0:T(8,128)(2,1)}, u32[]{:S(2)}, u32[]{:S(2)}) collective-permute-start(bf16[4,2,384,384]{3,2,1,0:T(8,128)(2,1)} %bitcast.4), channel_id=1, source_target_pairs={{0,8},{8,0},{1,9},{9,1},{2,10},{10,2},{3,11},{11,3},{4,12},{12,4},... | collective-permute-start | bytes 7077896 | tf_op jit(solution)/shard_map/ppermute | solution.py:592
  2.0 19.3 %collective-permute-start = (bf16[2,2,192,384]{3,2,1,0:T(8,128)(2,1)S(1)}, bf16[2,2,192,384]{3,2,1,0:T(8,128)(2,1)S(1)}, u32[]{:S(2)}, u32[]{:S(2)}) collective-permute-start(bf16[2,2,192,384]{3,2,1,0:T(8,128)(2,1)S(1)} %get-tuple-element.15), channel_id=1, source_target_pairs={{8,24},{24,40},{40,56},{56,72},{72,88},{88,104},{104,120},{16,0},{... | collective-permute-start | bytes 1769480 | tf_op jit(solution)/shard_map/ppermute | solution.py:591
  6.7 27.4 %collective-permute-start.1 = (bf16[2,2,192,384]{3,2,1,0:T(8,128)(2,1)S(1)}, bf16[2,2,192,384]{3,2,1,0:T(8,128)(2,1)S(1)}, u32[]{:S(2)}, u32[]{:S(2)}) collective-permute-start(bf16[2,2,192,384]{3,2,1,0:T(8,128)(2,1)S(1)} %get-tuple-element.16), channel_id=1, source_target_pairs={{8,16},{24,32},{40,48},{56,64},{72,80},{88,96},{104,112},{16,8},{3... | collective-permute-start | bytes 1769480 | tf_op jit(solution)/shard_map/ppermute | solution.py:590
  70.5 17.2 %all-to-all-start.2 = ((bf16[16,216,128]{2,1,0:T(8,128)(2,1)}), bf16[16,216,128]{2,1,0:T(8,128)(2,1)S(1)}, u32[]{:S(2)}, u32[]{:S(2)}) async-start(bf16[16,216,128]{2,1,0:T(8,128)(2,1)} %shard_map.65), calls=%async_computation.2 | async-start | bytes 1769472 | tf_op jit(solution)/shard_map/all_to_all | solution.py:604
  76.3 14.3 %copy-start.4 = (f32[4]{0:T(128)S(1)}, f32[4]{0:T(128)}, u32[]{:S(2)}) copy-start(f32[4]{0:T(128)} %refs_2_.3) | copy-start | bytes 52
  76.3 14.3 %copy-start.5 = (s32[1,4]{1,0:T(1,128)S(1)}, s32[1,4]{1,0:T(1,128)}, u32[]{:S(2)}) copy-start(s32[1,4]{1,0:T(1,128)} %refs_3_.3) | copy-start | bytes 52
  76.3 6.8 %collective-permute-start.4 = (bf16[2,2,192,384]{3,2,1,0:T(8,128)(2,1)S(1)}, bf16[2,2,192,384]{3,2,1,0:T(8,128)(2,1)S(1)}, u32[]{:S(2)}, u32[]{:S(2)}) collective-permute-start(bf16[2,2,192,384]{3,2,1,0:T(8,128)(2,1)S(1)} %collective-permute-done.same), channel_id=1, source_target_pairs={{0,8},{8,0},{1,9},{9,1},{2,10},{10,2},{3,11},{11,3},{4,12},{12,4},... | collective-permute-start | bytes 1769480 | tf_op jit(solution)/shard_map/ppermute | solution.py:597
  80.7 32.1 %collective-permute-start.5 = (bf16[2,2,384,384]{3,2,1,0:T(8,128)(2,1)}, bf16[2,2,384,384]{3,2,1,0:T(8,128)(2,1)S(1)}, u32[]{:S(2)}, u32[]{:S(2)}) collective-permute-start(bf16[2,2,384,384]{3,2,1,0:T(8,128)(2,1)} %shard_map.66), channel_id=1, source_target_pairs={{8,16},{24,32},{40,48},{56,64},{72,80},{88,96},{104,112},{16,8},{3... | collective-permute-start | bytes 3538952 | tf_op jit(solution)/shard_map/ppermute | solution.py:594
  83.7 1.0 copy-start.1
  87.7 42.2 %collective-permute-start.3 = (bf16[3456,128]{1,0:T(8,128)(2,1)S(1)}, bf16[3456,128]{1,0:T(8,128)(2,1)S(1)}, u32[]{:S(2)}, u32[]{:S(2)}) collective-permute-start(bf16[3456,128]{1,0:T(8,128)(2,1)S(1)} %bitcast.11), channel_id=1, source_target_pairs={{0,8},{8,0},{1,9},{9,1},{2,10},{10,2},{3,11},{11,3},{4,12},{12,4},... | collective-permute-start | bytes 2654216 | tf_op jit(solution)/shard_map/ppermute | solution.py:608
  112.8 12.0 %copy-start.2 = (bf16[2,2,384,384]{3,2,1,0:T(8,128)(2,1)}, bf16[2,2,384,384]{3,2,1,0:T(8,128)(2,1)S(1)}, u32[]{:S(2)}) copy-start(bf16[2,2,384,384]{3,2,1,0:T(8,128)(2,1)S(1)} %collective-permute-done.5.refs_7_.far) | copy-start | bytes 3538948

commit v7 on v6

--- a/solution.py
+++ b/solution.py
@@ -160,75 +160,84 @@
     )(place, offsets, own, mate)
 
 
-def polar_body(place, offsets, same, cross, chip, turned, partial, out, edges, flat, sems):
+def polar_body(place, offsets, same, cross, chip, turned, partial, out, flat, sems):
     core = place[0]
-    copies = [
-        pltpu.make_async_copy(same, edges.at[1 - core], sems.at[0]),
-        pltpu.make_async_copy(cross, edges.at[core], sems.at[1]),
-    ]
-    for copy in copies:
-        copy.start()
-    for copy in copies:
-        copy.wait()
-    _, _, first, last = offset_roles(offsets)
-    stores = []
-    for index, span in enumerate(spans(offsets, first, last)):
-
-        @pl.loop(0, HALF // 32)
-        def _(block):
-            rows = pl.ds(pl.multiple_of(block * 32, 32), 32)
-            there = pl.ds(pl.multiple_of(core * HALF + block * 32, 32), 32)
-
-            def multiply(carry, ar, ai, br, bi):
-                real, imag = carry
-                return real + (ar * br - ai * bi), imag + (ar * bi + ai * br)
-
-            def before(j, carry):
-                return multiply(
-                    carry,
-                    edges[0, 1 - j, 0, rows, :].astype(F32),
-                    edges[0, 1 - j, 1, rows, :].astype(F32),
-                    turned[span - 1 - j, 0, there, :],
-                    turned[span - 1 - j, 1, there, :],
-                )
-
-            def after(j, carry):
-                return multiply(
-                    carry,
-                    chip[8 - span + j, 0, there, :].astype(F32),
-                    chip[8 - span + j, 1, there, :].astype(F32),
-                    edges[1, j, 0, rows, :].astype(F32),
-                    edges[1, j, 1, rows, :].astype(F32),
-                )
-
-            pair = (partial[index, 0, rows, :], partial[index, 1, rows, :])
-            pair = lax.fori_loop(0, jnp.maximum(span - 2, 0), before, pair)
-            pair = lax.fori_loop(0, jnp.minimum(span, 2), after, pair)
-            for part, value in enumerate(pair):
-                for panel in range(3):
-                    start = ((index * 2 + part) * 3 + panel) * HALF
-                    flat[pl.ds(pl.multiple_of(start + block * 32, 32), 32), :] = value[
-                        :, panel * 128 : (panel + 1) * 128
-                    ].astype(BF16)
-
+
+    def run(edges):
+        _, _, first, last = offset_roles(offsets)
+        for index, span in enumerate(spans(offsets, first, last)):
+
+            @pl.loop(0, HALF // 32)
+            def _(block):
+                rows = pl.ds(pl.multiple_of(block * 32, 32), 32)
+                there = pl.ds(pl.multiple_of(core * HALF + block * 32, 32), 32)
+
+                def multiply(carry, ar, ai, br, bi):
+                    real, imag = carry
+                    return real + (ar * br - ai * bi), imag + (ar * bi + ai * br)
+
+                def before(j, carry):
+                    ar = edges[0][1 - j, 0, rows, :].astype(F32)
+                    ai = edges[0][1 - j, 1, rows, :].astype(F32)
+                    if index > 0:
+                        keep = jnp.where(span > 2 + j, 1.0, 0.0)
+                        ar, ai = ar * keep, ai * keep
+                    at = jnp.maximum(span - 1 - j, 1)
+                    return multiply(carry, ar, ai, turned[at, 0, there, :], turned[at, 1, there, :])
+
+                def after(j, carry):
+                    at = jnp.minimum(8 - span + j, 7)
+                    ar = chip[at, 0, there, :].astype(F32)
+                    ai = chip[at, 1, there, :].astype(F32)
+                    if index > 0 and j > 0:
+                        keep = jnp.where(span > j, 1.0, 0.0)
+                        ar, ai = ar * keep, ai * keep
+                    return multiply(
+                        carry,
+                        ar,
+                        ai,
+                        edges[1][j, 0, rows, :].astype(F32),
+                        edges[1][j, 1, rows, :].astype(F32),
+                    )
+
+                pair = (partial[index, 0, rows, :], partial[index, 1, rows, :])
+                for j in range(2):
+                    pair = before(j, pair)
+                for j in range(2):
+                    pair = after(j, pair)
+                for part, value in enumerate(pair):
+                    for panel in range(3):
+                        start = ((index * 2 + part) * 3 + panel) * HALF
+                        flat[pl.ds(pl.multiple_of(start + block * 32, 32), 32), :] = value[
+                            :, panel * 128 : (panel + 1) * 128
+                        ].astype(BF16)
+
+            done = pl.ds(index * 6 * HALF, 6 * HALF)
+            store = pltpu.make_async_copy(flat.at[done], out.at[done], sems.at[index])
+            store.start()
+
+    @pl.when(core == 0)
+    def _():
+        run((cross, same))
+
+    @pl.when(core == 1)
+    def _():
+        run((same, cross))
+
+    for index in range(3):
         done = pl.ds(index * 6 * HALF, 6 * HALF)
-        store = pltpu.make_async_copy(flat.at[done], out.at[done], sems.at[2 + index])
-        store.start()
-        stores.append(store)
-    for store in stores:
-        store.wait()
+        pltpu.make_async_copy(flat.at[done], out.at[done], sems.at[index]).wait()
 
 
 def polar_call(place, offsets, same, cross, chip, turned, partial):
     return pl.pallas_call(
         polar_body,
-        out_shape=jax.ShapeDtypeStruct((FLAT, 128), BF16),
-        in_specs=[SMEM, SMEM, ANY, ANY, VMEM, VMEM, VMEM],
+        out_shape=pltpu.HBM((FLAT, 128), BF16),
+        in_specs=[SMEM, SMEM, VMEM, VMEM, VMEM, VMEM, VMEM],
         out_specs=ANY,
         scratch_shapes=[
-            pltpu.VMEM((2, 2, 2, HALF, NB), BF16),
             pltpu.VMEM((FLAT, 128), BF16),
-            pltpu.SemaphoreType.DMA((5,)),
+            pltpu.SemaphoreType.DMA((3,)),
         ],
         compiler_params=pltpu.CompilerParams(vmem_limit_bytes=6 << 20),
         cost_estimate=pl.CostEstimate(flops=20_000_000, bytes_accessed=9_000_000, transcendentals=0),
@@ -236,7 +245,7 @@
     )(place, offsets, same, cross, chip, turned, partial)
 
 
-def near_body(place, swapped, cross, out, sems):
+def near_body(place, swapped, cross, target, out, sems):
     core = place[0]
     copies = [
         pltpu.make_async_copy(cross, out.at[:, :, pl.ds(core * HALF, HALF), :], sems.at[0]),
@@ -255,27 +264,31 @@
             for part in range(2):
                 out[item, part] = out[item, part].astype(F32).T.astype(BF16)
 
+    store = pltpu.make_async_copy(out, target, sems.at[0])
+    store.start()
+    store.wait()
+
 
 def near_call(place, swapped, cross):
     return pl.pallas_call(
         near_body,
-        out_shape=jax.ShapeDtypeStruct((2, 2, NB, NB), BF16),
+        out_shape=pltpu.HBM((2, 2, NB, NB), BF16),
         in_specs=[SMEM, ANY, ANY],
-        out_specs=VMEM,
-        scratch_shapes=[pltpu.SemaphoreType.DMA((2,))],
+        out_specs=ANY,
+        scratch_shapes=[pltpu.VMEM((2, 2, NB, NB), BF16), pltpu.SemaphoreType.DMA((2,))],
         compiler_params=pltpu.CompilerParams(vmem_limit_bytes=4 << 20),
         cost_estimate=pl.CostEstimate(flops=0, bytes_accessed=2_400_000, transcendentals=0),
         name="near_join",
-    )(place, swapped, cross)
-
-
-def born_body(early, *refs):
-    if early:
-        (place, offsets, occupation, coupling, own, mate, near, vertex, out, *rest) = refs
-        far = None
-    else:
-        (place, offsets, occupation, coupling, own, mate, near, far, vertex, out, *rest) = refs
-    chosen, lows, highs, mixed, wide, stack, side, total, sems = rest
+    )(place, swapped, in_hbm(cross))
+
+
+def born_body(early, window, resumed, *refs):
+    refs = list(refs)
+    place, offsets, occupation, coupling, own, mate, near = refs[:7]
+    refs = refs[7:]
+    far = None if early else refs.pop(0)
+    base = refs.pop(0) if resumed else None
+    vertex, out, chosen, lows, highs, mixed, wide, stack, side, total, rounded, sems = refs
     core = place[0]
     energy = 2 * (1 - core) if early else 2 * core
 
@@ -289,16 +302,21 @@
             def _():
                 pltpu.make_async_copy(source.at[slot - low], target, sem).start()
 
-    for k in range(4):
+    for k in range(*window):
         pltpu.make_async_copy(vertex.at[coupling[0, k]], chosen.at[k], sems.at[k, 4]).start()
         for item in range(2):
             at = energy + 4 + item
             fetch(at - offsets[k], lows.at[k, item], sems.at[k, 2 * item])
             fetch(at + offsets[k], highs.at[k, item], sems.at[k, 2 * item + 1])
 
-    total[...] = jnp.zeros_like(total)
-
-    @pl.loop(0, 4)
+    if resumed:
+        resume = pltpu.make_async_copy(base, total, sems.at[0, 0])
+        resume.start()
+        resume.wait()
+    else:
+        total[...] = jnp.zeros_like(total)
+
+    @pl.loop(*window)
     def _(k):
         pltpu.make_async_copy(vertex.at[0], chosen.at[k], sems.at[k, 4]).wait()
         vr = chosen[k, 0]
@@ -338,17 +356,24 @@
             )
             total[rows, :] += term
 
-    out[...] = total[...].astype(BF16)
-
-
-def born_call(place, offsets, occupation, coupling, arrays, vertex):
+    if out.dtype == BF16:
+        rounded[...] = total[...].astype(BF16)
+    store = pltpu.make_async_copy(rounded if out.dtype == BF16 else total, out, sems.at[0, 0])
+    store.start()
+    store.wait()
+
+
+def born_call(place, offsets, occupation, coupling, arrays, vertex, window, base=None, kind=BF16):
     early = len(arrays) == 3
+    resumed = base is not None
     size = 2 * NB
-    return pl.pallas_call(
-        lambda *refs: born_body(early, *refs),
-        out_shape=jax.ShapeDtypeStruct((size, size), BF16),
-        in_specs=[SMEM] * 4 + [ANY] * (len(arrays) + 1),
-        out_specs=VMEM,
+    held = (*map(in_hbm, arrays[:3]), *arrays[3:]) + ((in_hbm(base),) if resumed else ())
+    part = window[1] - window[0]
+    return pl.pallas_call(
+        lambda *refs: born_body(early, window, resumed, *refs),
+        out_shape=pltpu.HBM((size, size), kind),
+        in_specs=[SMEM] * 4 + [ANY] * (len(held) + 1),
+        out_specs=ANY,
         scratch_shapes=[
             pltpu.VMEM((4, 2, NB, NB), BF16),
             pltpu.VMEM((4, 2, 2, NB, NB), BF16),
@@ -358,14 +383,15 @@
             pltpu.VMEM((size, size), BF16),
             pltpu.VMEM((size, size), BF16),
             pltpu.VMEM((size, size), F32),
+            pltpu.VMEM((size, size), BF16),
             pltpu.SemaphoreType.DMA((4, 5)),
         ],
         compiler_params=pltpu.CompilerParams(vmem_limit_bytes=22 << 20),
         cost_estimate=pl.CostEstimate(
-            flops=16 * size**3, bytes_accessed=12_000_000, transcendentals=0
+            flops=4 * part * size**3, bytes_accessed=3_000_000 * part, transcendentals=0
         ),
-        name="born_early" if early else "born_late",
-    )(place, offsets, occupation, coupling, *map(in_hbm, arrays[:3]), *arrays[3:], in_hbm(vertex))
+        name="born_early" if early else "born_resumed" if resumed else "born_late",
+    )(place, offsets, occupation, coupling, *held, in_hbm(vertex))
 
 
 def sum_body(count, copies, bands, out, buffer, value, *sems):
@@ -395,7 +421,7 @@
     count = bands.shape[0]
     return pl.pallas_call(
         lambda *refs: sum_body(count, copies, *refs),
-        out_shape=jax.ShapeDtypeStruct((copies, ROWS, 128), BF16),
+        out_shape=pltpu.HBM((copies, ROWS, 128), BF16),
         in_specs=[ANY],
         out_specs=ANY,
         scratch_shapes=[
@@ -409,7 +435,7 @@
     )(bands)
 
 
-def half_products(begin, offsets, half, source, joined, table, magnon, sums):
+def unpack_half(source, joined):
     for index in range(3):
         for part in range(2):
             for panel in range(3):
@@ -417,54 +443,65 @@
                 joined[index, :, part * NB + panel * 128 : part * NB + (panel + 1) * 128] = source[
                     start : start + HALF, :
                 ]
-    top, bottom, first, last = offset_roles(offsets)
+
+
+def direct(index, role, half, joined, table, magnon):
     rows = pl.ds(pl.multiple_of(half * HALF, HALF), HALF)
-
-    def direct(index, k):
-        value = jnp.dot(joined[index], table[k], preferred_element_type=F32)
-        magnon[index, rows, :] = value.astype(BF16).astype(F32)
-
-    def transposed(index, k):
-        value = None
-        for part in range(2):
-            turned = joined[index, :, part * NB : (part + 1) * NB].astype(F32).T.astype(BF16)
-            these = pl.ds(pl.multiple_of(part * NB + half * HALF, HALF), HALF)
-            term = jnp.dot(turned, table[k, these, :], preferred_element_type=F32)
-            value = term if value is None else value + term
-        sums[index] = value if begin else sums[index] + value
-
-    direct(0, top)
-    transposed(0, bottom)
-    for index, k in ((1, first), (2, last)):
-        pl.when(offsets[k] > 0)(lambda: direct(index, k))
-        pl.when(offsets[k] < 0)(lambda: transposed(index, k))
+    value = jnp.dot(joined[index], table[role], preferred_element_type=F32)
+    magnon[index, rows, :] = value.astype(BF16).astype(F32)
+
+
+def transposed(index, role, half, joined, table):
+    value = None
+    for part in range(2):
+        turned = joined[index, :, part * NB : (part + 1) * NB].astype(F32).T.astype(BF16)
+        these = pl.ds(pl.multiple_of(part * NB + half * HALF, HALF), HALF)
+        term = jnp.dot(turned, table[role, these, :], preferred_element_type=F32)
+        value = term if value is None else value + term
+    return value
 
 
 def start_body(
     place, offsets, mine, free, own, mate,
-    slots, magnon, bottom_sum, table, source, plain, joined, sems,
+    slots, magnon, sums, table, source, plain, joined, sems,
 ):
     core = place[0]
-    ready = [
-        pltpu.make_async_copy(mine, source, sems.at[4]),
-        pltpu.make_async_copy(free, plain, sems.at[5]),
+    roles = offset_roles(offsets)
+    ready = pltpu.make_async_copy(mine, source, sems.at[6])
+    tables = [
+        pltpu.make_async_copy(free.at[k], plain.at[role], sems.at[role])
+        for role, k in enumerate(roles)
     ]
     loads = [
-        pltpu.make_async_copy(own, slots.at[pl.ds(4, 4)], sems.at[0]),
-        pltpu.make_async_copy(mate, slots.at[pl.ds(8 - 8 * core, 4)], sems.at[1]),
+        pltpu.make_async_copy(own, slots.at[pl.ds(4, 4)], sems.at[4]),
+        pltpu.make_async_copy(mate, slots.at[pl.ds(8 - 8 * core, 4)], sems.at[5]),
     ]
-    for load in ready + loads:
+    for load in [ready] + tables + loads:
         load.start()
-    for load in ready:
-        load.wait()
-    for k in range(4):
-        fr = plain[k, 0]
-        fi = plain[k, 1]
-        table[k, :NB, :NB] = fr
-        table[k, :NB, NB:] = fi
-        table[k, NB:, :NB] = -fi
-        table[k, NB:, NB:] = fr
-    half_products(True, offsets, core, source, joined, table, magnon, bottom_sum)
+    ready.wait()
+    unpack_half(source, joined)
+    for role in range(4):
+        tables[role].wait()
+        fr = plain[role, 0]
+        fi = plain[role, 1]
+        table[role, :NB, :NB] = fr
+        table[role, :NB, NB:] = fi
+        table[role, NB:, :NB] = -fi
+        table[role, NB:, NB:] = fr
+        if role == 0:
+            direct(0, 0, core, joined, table, magnon)
+        elif role == 1:
+            sums[0] = transposed(0, 1, core, joined, table)
+        else:
+
+            @pl.when(offsets[roles[role]] > 0)
+            def _():
+                direct(role - 1, role, core, joined, table, magnon)
+
+            @pl.when(offsets[roles[role]] < 0)
+            def _():
+                sums[role - 1] = transposed(role - 1, role, core, joined, table)
+
     for load in loads:
         load.wait()
 
@@ -485,7 +522,7 @@
             pltpu.VMEM((FLAT, 128), BF16),
             pltpu.VMEM((4, 2, NB, NB), BF16),
             pltpu.VMEM((3, HALF, size), BF16),
-            pltpu.SemaphoreType.DMA((6,)),
+            pltpu.SemaphoreType.DMA((7,)),
         ],
         compiler_params=pltpu.CompilerParams(vmem_limit_bytes=10 << 20),
         cost_estimate=pl.CostEstimate(
@@ -496,8 +533,8 @@
 
 
 def final_body(
-    place, offsets, other, near, far, early, late, slots_in, magnon_in, sum_in, table,
-    out, slots, magnon, bottom_sum, source, joined, result, sems,
+    place, offsets, other, near, far, early, late, slots_in, magnon_in, sums, table,
+    out, slots, magnon, source, joined, result, sems,
 ):
     core = place[0]
     loads = [
@@ -509,14 +546,23 @@
     for load in loads:
         load.start()
     ready.wait()
-    half_products(False, offsets, 1 - core, source, joined, table, magnon, bottom_sum)
-    _, _, first, last = offset_roles(offsets)
-    magnon[0] += bottom_sum[0].astype(BF16).astype(F32)
-    for index, k in ((1, first), (2, last)):
-
-        @pl.when(offsets[k] < 0)
+    unpack_half(source, joined)
+    roles = offset_roles(offsets)
+    _, _, first, last = roles
+    half = 1 - core
+    direct(0, 0, half, joined, table, magnon)
+    total = sums[0] + transposed(0, 1, half, joined, table)
+    magnon[0] += total.astype(BF16).astype(F32)
+    for role in (2, 3):
+
+        @pl.when(offsets[roles[role]] > 0)
         def _():
-            magnon[index] = bottom_sum[index].astype(BF16).astype(F32)
+            direct(role - 1, role, half, joined, table, magnon)
+
+        @pl.when(offsets[roles[role]] < 0)
+        def _():
+            total = sums[role - 1] + transposed(role - 1, role, half, joined, table)
+            magnon[role - 1] = total.astype(BF16).astype(F32)
 
     for load in loads:
         load.wait()
@@ -525,10 +571,10 @@
     for item, energy in enumerate((2 - 2 * core, 3 - 2 * core, 2 * core, 2 * core + 1)):
         born = early if item < 2 else late
 
-        @pl.loop(0, NB // 16)
+        @pl.loop(0, NB // 32)
         def _(block):
-            rows = pl.ds(pl.multiple_of(block * 16, 16), 16)
-            begin = pl.ds(pl.multiple_of((item % 2) * NB + block * 16, 16), 16)
+            rows = pl.ds(pl.multiple_of(block * 32, 32), 32)
+            begin = pl.ds(pl.multiple_of((item % 2) * NB + block * 32, 32), 32)
             real = born[begin, :NB].astype(F32)
             imag = born[begin, NB:].astype(F32)
             for index in range(3):
@@ -550,7 +596,7 @@
         store.wait()
 
 
-def final_call(place, offsets, other, near, far, early, late, slots, magnon, bottom_sum, table):
+def final_call(place, offsets, other, near, far, early, late, slots, magnon, sums, table):
     size = 2 * NB
     return pl.pallas_call(
         final_body,
@@ -558,11 +604,10 @@
             jax.ShapeDtypeStruct((4, 1, 2, NB, NB), BF16),
             jax.ShapeDtypeStruct(slots.shape, BF16),
             jax.ShapeDtypeStruct(magnon.shape, F32),
-            jax.ShapeDtypeStruct(bottom_sum.shape, F32),
         ),
         in_specs=[SMEM, SMEM, ANY, ANY, ANY] + [VMEM] * 6,
-        out_specs=(ANY, VMEM, VMEM, VMEM),
-        input_output_aliases={7: 1, 8: 2, 9: 3},
+        out_specs=(ANY, VMEM, VMEM),
+        input_output_aliases={7: 1, 8: 2},
         scratch_shapes=[
             pltpu.VMEM((FLAT, 128), BF16),
             pltpu.VMEM((3, HALF, size), BF16),
@@ -574,7 +619,7 @@
             flops=1_000_000_000, bytes_accessed=18_000_000, transcendentals=0
         ),
         name="final",
-    )(place, offsets, other, in_hbm(near), in_hbm(far), early, late, slots, magnon, bottom_sum, table)[0]
+    )(place, offsets, other, in_hbm(near), in_hbm(far), early, late, slots, magnon, sums, table)[0]
 
 
 def per_device(green_blocks, offsets, occupation, coupling, vertex, magnon_free):
@@ -597,13 +642,16 @@
     swapped = lax.ppermute(same, "core", SWAP)
     near = near_call(place, swapped, cross)
     bands = lax.all_to_all(pair.reshape(BANDS, ROWS, 128), PLANE, 0, 0, tiled=True)
-    early = born_call(place, offsets, occupation, coupling, (own, mate, near), vertex)
+    early = born_call(place, offsets, occupation, coupling, (own, mate, near), vertex, (0, 4))
     copies = sum_call(bands, 4)
     bands = lax.all_to_all(copies, ROW, 0, 0, tiled=True)
+    base = born_call(
+        place, offsets, occupation, coupling, (own, mate, near, far), vertex, (0, 1), None, F32
+    )
     copies = sum_call(bands, BANDS)
     mine = lax.all_to_all(copies, PLANE, 0, 0, tiled=True).reshape(FLAT, 128)
     late = born_call(
-        place, offsets, occupation, coupling, (own, mate, near, far), vertex
+        place, offsets, occupation, coupling, (own, mate, near, far), vertex, (1, 4), base
     )
     other = lax.ppermute(mine, "core", SWAP)
     held = start_call(place, offsets, mine, magnon_free, own, mate)

time: 139 us -> 146 us (1.050)
  the two profiles are of different devices: /device:TPU:17 before, /device:TPU:0 now
where the time goes in v7:
time: 146 us; the launch traced here: 144 us
  Pallas kernels  63.6 us (44%)
  waiting for transfers between devices  31.4 us (22%)
  starting transfers between devices  30.6 us (21%)
  blocking collectives  17.5 us (12%)
    pallas_call x3, Pallas kernels, born_call(): pl.pallas_call(lambda *refs: born_body(early, window, resumed, *refs), ou...  32.6 us
    all_to_all x1, starting transfers between devices, per_device(): lax.all_to_all(pair.reshape(BANDS, ROWS, 128), PLANE, 0, 0, tiled=True)  20.9 us
    all_to_all x1, blocking collectives, per_device(): bands = lax.all_to_all(copies, ROW, 0, 0, tiled=True)  17.5 us
    all_to_all x1, waiting for transfers between devices, per_device(): lax.all_to_all(pair.reshape(BANDS, ROWS, 128), PLANE, 0, 0, tiled=True)  13.3 us
    ppermute x1, waiting for transfers between devices, per_device(): same = lax.ppermute(to_same, ENERGY, along)  9.02 us
    pallas_call x1, Pallas kernels, final_call(): pl.pallas_call(final_body, out_shape=(jax.ShapeDtypeStruct((4, 1, 2, NB,...  7.75 us
    pallas_call x1, Pallas kernels, prepare_call(): pl.pallas_call(prepare_body, out_shape=(jax.ShapeDtypeStruct((8, 2, NB, N...  7.35 us
    all_to_all x1, starting transfers between devices, per_device(): mine = lax.all_to_all(copies, PLANE, 0, 0, tiled=True).reshape(FLAT, 128)  6.94 us
  transfers between devices with their start and end apart: 8, of which 5 were waited for; matrix products, arithmetic and copies ran while one was open for 0% of the time, Pallas kernels for 37%

profile of v7, /device:TPU:0, one launch (start us, length us, event | category | flops | bytes accessed | tf_op | source)
XLA Modules:
  0.0 143.6 jit_solution(17550636615727529274)
XLA Ops:
  0.0 0.0 copy-start
  0.0 0.0 copy-start.6
  0.0 0.0 collective-permute-start.2
  0.0 1.8 %edge.1 = (bf16[2,2,192,384]{3,2,1,0:T(8,128)(2,1)S(1)}, bf16[2,2,192,384]{3,2,1,0:T(8,128)(2,1)S(1)}) custom-call(s32[1]{0:T(128)} %bitcast.place.refs_0_, bf16[4,2,384,384]{3,2,1,0:T(8,128)(2,1)} %bitcast.5), custom_call_target="tpu_custom_call" | custom-call | bytes 2400000 | tf_op jit(solution)/shard_map/edge/pallas_call | solution.py:97
  1.8 1.3 collective-permute-start
  3.1 0.7 collective-permute-start.1
  3.8 1.0 collective-permute-done.2.mate.refs_5_
  4.9 0.0 copy-done
  4.9 0.0 copy-done.6
  4.9 7.4 %prepare.1 = (bf16[8,2,384,384]{3,2,1,0:T(8,128)(2,1)S(1)}, f32[8,2,384,384]{3,2,1,0:T(8,128)S(1)}, f32[3,2,192,384]{3,2,1,0:T(8,128)S(1)}) custom-call(s32[1]{0:T(128)} %bitcast.place.refs_0_, s32[4]{0:T(128)S(1)} %copy-done.6, bf16[4,2,384,384]{3,2,1,0:T(8,128)(2,1)S(1)} %bitcast.11, bf16[4,2,384,384]{3,2,1,0:T(8,128)(2,1)} %collective-permute-done.2.mate.refs_5_), custom_call_target="tpu_custom_call" | custom-call | flops 20000000 | bytes 9000000 | tf_op jit(solution)/shard_map/prepare/pallas_call | solution.py:147
  12.2 9.0 %collective-permute-done.same = bf16[2,2,192,384]{3,2,1,0:T(8,128)(2,1)S(1)} collective-permute-done((bf16[2,2,192,384]{3,2,1,0:T(8,128)(2,1)S(1)}, bf16[2,2,192,384]{3,2,1,0:T(8,128)(2,1)S(1)}, u32[]{:S(2)}, u32[]{:S(2)}) %collective-permute-start) | collective-permute-done | bytes 589856 | tf_op jit(solution)/shard_map/ppermute | solution.py:636
  21.3 0.0 copy-start.5
  21.3 0.0 collective-permute-done.1.cross
  21.3 0.0 copy-start.2
  21.3 2.9 %polar.1 = bf16[3456,128]{1,0:T(8,128)(2,1)} custom-call(s32[1]{0:T(128)} %bitcast.place.refs_0_, s32[4]{0:T(128)S(1)} %copy-done.6, bf16[2,2,192,384]{3,2,1,0:T(8,128)(2,1)S(1)} %collective-permute-done.same, bf16[2,2,192,384]{3,2,1,0:T(8,128)(2,1)S(1)} %collective-permute-done.1.cross, bf16[8,2,384,384]{3,2,1,0:T(8,128)(2,1)S(1)} %get-tuple-element.17.chip, ...), custom_call_target="tpu_custom_call" | custom-call | flops 20000000 | bytes 9000000 | tf_op jit(solution)/shard_map/polar/pallas_call | solution.py:233
  24.2 0.0 copy-done.5
  24.2 0.0 copy-done.2
  24.2 20.9 %all-to-all-start = ((bf16[16,216,128]{2,1,0:T(8,128)(2,1)}), bf16[16,216,128]{2,1,0:T(8,128)(2,1)S(1)}, u32[]{:S(2)}, u32[]{:S(2)}) async-start(bf16[16,216,128]{2,1,0:T(8,128)(2,1)} %bitcast.14), calls=%async_computation | async-start | bytes 1769472 | tf_op jit(solution)/shard_map/all_to_all | solution.py:644
  45.1 1.3 shard_map.66
  46.4 0.7 collective-permute-start.5
  47.2 13.3 %all-to-all-done.refs_0_ = bf16[16,216,128]{2,1,0:T(8,128)(2,1)S(1)} async-done(((bf16[16,216,128]{2,1,0:T(8,128)(2,1)}), bf16[16,216,128]{2,1,0:T(8,128)(2,1)S(1)}, u32[]{:S(2)}, u32[]{:S(2)}) %all-to-all-start) | async-done | bytes 884768 | tf_op jit(solution)/shard_map/all_to_all | solution.py:644
  60.5 2.1 %shard_map.64 = bf16[4,216,128]{2,1,0:T(8,128)(2,1)} custom-call(bf16[16,216,128]{2,1,0:T(8,128)(2,1)S(1)} %all-to-all-done.refs_0_), custom_call_target="tpu_custom_call" | custom-call | flops 500000 | bytes 1900000 | tf_op jit(solution)/shard_map/pallas_call | solution.py:422
  62.6 17.5 %all_to_all.15.refs_0_ = bf16[4,216,128]{2,1,0:T(8,128)(2,1)S(1)} all-to-all(bf16[4,216,128]{2,1,0:T(8,128)(2,1)} %shard_map.64), channel_id=1, replica_groups=mesh['y'=4,'xh'=2,'core'=2,'xl'=2,'z'=4] {'xh','xl'}, dimensions={0} | all-to-all | bytes 442368 | tf_op jit(solution)/shard_map/all_to_all | solution.py:647
  80.1 0.0 copy-start.7
  80.1 0.0 copy-start.8
  80.1 1.4 shard_map.65
  81.5 6.9 %all-to-all-start.2 = ((bf16[16,216,128]{2,1,0:T(8,128)(2,1)}), bf16[16,216,128]{2,1,0:T(8,128)(2,1)S(1)}, u32[]{:S(2)}, u32[]{:S(2)}) async-start(bf16[16,216,128]{2,1,0:T(8,128)(2,1)} %shard_map.65), calls=%async_computation.2 | async-start | bytes 1769472 | tf_op jit(solution)/shard_map/all_to_all | solution.py:652
  88.5 0.1 collective-permute-start.4
  88.6 2.2 %collective-permute-done.4.swapped = bf16[2,2,192,384]{3,2,1,0:T(8,128)(2,1)S(1)} collective-permute-done((bf16[2,2,192,384]{3,2,1,0:T(8,128)(2,1)}, bf16[2,2,192,384]{3,2,1,0:T(8,128)(2,1)S(1)}, u32[]{:S(2)}, u32[]{:S(2)}) %collective-permute-start.4) | collective-permute-done | bytes 589856 | tf_op jit(solution)/shard_map/ppermute | solution.py:642
  90.8 2.1 %near_join.1.refs_6_.near = bf16[2,2,384,384]{3,2,1,0:T(8,128)(2,1)} custom-call(s32[1]{0:T(128)} %bitcast.place.refs_0_, bf16[2,2,192,384]{3,2,1,0:T(8,128)(2,1)S(1)} %collective-permute-done.4.swapped, bf16[2,2,192,384]{3,2,1,0:T(8,128)(2,1)} %copy-done.2), custom_call_target="tpu_custom_call" | custom-call | bytes 2400000 | tf_op jit(solution)/shard_map/near_join/pallas_call | solution.py:273
  92.9 0.0 collective-permute-done.5.refs_7_.far
  92.9 0.0 copy-done.7
  92.9 0.0 copy-done.8
  92.9 0.0 copy-start.1
  92.9 5.9 %born_late.1.refs_8_ = f32[768,768]{1,0:T(8,128)} custom-call(s32[1]{0:T(128)} %bitcast.place.refs_0_, s32[4]{0:T(128)S(1)} %copy-done.6, f32[4]{0:T(128)S(1)} %copy-done.7, s32[1,4]{1,0:T(1,128)S(1)} %copy-done.8, bf16[4,2,384,384]{3,2,1,0:T(8,128)(2,1)} %bitcast.7, bf16[4,2,384,384]{3,2,1,0:T(8,128)(2,1)} %collective-permute-done.2.mate.refs_5_, ...), custom_call_target="tpu_custom_call" | custom-call | flops 1811939328 | bytes 3000000 | tf_op jit(solution)/shard_map/born_late/pallas_call | solution.py:372
  98.8 5.7 %all-to-all-done.2 = bf16[16,216,128]{2,1,0:T(8,128)(2,1)S(1)} async-done(((bf16[16,216,128]{2,1,0:T(8,128)(2,1)}), bf16[16,216,128]{2,1,0:T(8,128)(2,1)S(1)}, u32[]{:S(2)}, u32[]{:S(2)}) %all-to-all-start.2) | async-done | bytes 884768 | tf_op jit(solution)/shard_map/all_to_all | solution.py:652
  104.5 0.0 collective-permute-start.3
  104.5 0.0 copy-done.1
  104.5 12.9 %born_resumed.1.late = bf16[768,768]{1,0:T(8,128)(2,1)} custom-call(s32[1]{0:T(128)} %bitcast.place.refs_0_, s32[4]{0:T(128)S(1)} %copy-done.6, f32[4]{0:T(128)S(1)} %copy-done.7, s32[1,4]{1,0:T(1,128)S(1)} %copy-done.8, bf16[4,2,384,384]{3,2,1,0:T(8,128)(2,1)} %bitcast.8, bf16[4,2,384,384]{3,2,1,0:T(8,128)(2,1)} %collective-permute-done.2.mate.refs_5_, ...), custom_call_target="tpu_custom_call" | custom-call | flops 5435817984 | bytes 9000000 | tf_op jit(solution)/shard_map/born_resumed/pallas_call | solution.py:372
  117.5 13.8 %born_early.1.early = bf16[768,768]{1,0:T(8,128)(2,1)} custom-call(s32[1]{0:T(128)} %bitcast.place.refs_0_, s32[4]{0:T(128)S(1)} %copy-done.6, f32[4]{0:T(128)S(1)} %copy-done.7, s32[1,4]{1,0:T(1,128)S(1)} %copy-done.8, bf16[4,2,384,384]{3,2,1,0:T(8,128)(2,1)} %bitcast.9, bf16[4,2,384,384]{3,2,1,0:T(8,128)(2,1)} %collective-permute-done.2.mate.refs_5_, ...), custom_call_target="tpu_custom_call" | custom-call | flops 7247757312 | bytes 12000000 | tf_op jit(solution)/shard_map/born_early/pallas_call | solution.py:372
  131.3 0.0 copy-start.3
  131.3 0.0 copy-start.4
  131.3 4.3 %final_start.1 = (bf16[12,2,384,384]{3,2,1,0:T(8,128)(2,1)S(1)}, f32[3,384,768]{2,1,0:T(8,128)S(1)}, f32[3,384,768]{2,1,0:T(8,128)S(1)}, bf16[4,768,768]{2,1,0:T(8,128)(2,1)S(1)}) custom-call(s32[1]{0:T(128)} %bitcast.place.refs_0_, s32[4]{0:T(128)S(1)} %copy-done.6, bf16[3456,128]{1,0:T(8,128)(2,1)S(1)} %bitcast.13, bf16[4,2,384,384]{3,2,1,0:T(8,128)(2,1)} %free.1, ...), custom_call_target="tpu_custom_call" | custom-call | flops 1000000000 | bytes 10000000 | tf_op jit(solution)/shard_map/final_start/pallas_call | solution.py:511
  135.6 0.0 collective-permute-done.3.other
  135.6 0.0 copy-done.3
  135.6 0.0 copy-done.4
  135.6 7.7 %final.1 = (bf16[4,1,2,384,384]{4,3,2,1,0:T(8,128)(2,1)}, bf16[12,2,384,384]{3,2,1,0:T(8,128)(2,1)S(1)}, f32[3,384,768]{2,1,0:T(8,128)S(1)}) custom-call(s32[1]{0:T(128)} %bitcast.place.refs_0_, s32[4]{0:T(128)S(1)} %copy-done.6, bf16[3456,128]{1,0:T(8,128)(2,1)S(1)} %collective-permute-done.3.other, ...), custom_call_target="tpu_custom_call", output_to_operand_aliasing={{1}: (7, {}), {2}: (8, {})} | custom-call | flops 1000000000 | bytes 18000000 | tf_op jit(solution)/shard_map/final/pallas_call | solution.py:601
Async XLA Ops:
  0.0 4.9 %copy-start = (bf16[4,1,2,384,384]{4,3,2,1,0:T(8,128)(2,1)S(1)}, bf16[4,1,2,384,384]{4,3,2,1,0:T(8,128)(2,1)}, u32[]{:S(2)}) copy-start(bf16[4,1,2,384,384]{4,3,2,1,0:T(8,128)(2,1)} %param.6) | copy-start | bytes 7077892
  0.0 4.9 %copy-start.6 = (s32[4]{0:T(128)S(1)}, s32[4]{0:T(128)}, u32[]{:S(2)}) copy-start(s32[4]{0:T(128)} %offsets.7) | copy-start | bytes 52
  0.0 4.9 %collective-permute-start.2 = (bf16[4,2,384,384]{3,2,1,0:T(8,128)(2,1)}, bf16[4,2,384,384]{3,2,1,0:T(8,128)(2,1)}, u32[]{:S(2)}, u32[]{:S(2)}) collective-permute-start(bf16[4,2,384,384]{3,2,1,0:T(8,128)(2,1)} %bitcast.4), channel_id=1, source_target_pairs={{0,8},{8,0},{1,9},{9,1},{2,10},{10,2},{3,11},{11,3},{4,12},{12,4},... | collective-permute-start | bytes 7077896 | tf_op jit(solution)/shard_map/ppermute | solution.py:637
  1.8 19.4 %collective-permute-start = (bf16[2,2,192,384]{3,2,1,0:T(8,128)(2,1)S(1)}, bf16[2,2,192,384]{3,2,1,0:T(8,128)(2,1)S(1)}, u32[]{:S(2)}, u32[]{:S(2)}) collective-permute-start(bf16[2,2,192,384]{3,2,1,0:T(8,128)(2,1)S(1)} %get-tuple-element.15), channel_id=1, source_target_pairs={{8,24},{24,40},{40,56},{56,72},{72,88},{88,104},{104,120},{16,0},{... | collective-permute-start | bytes 1769480 | tf_op jit(solution)/shard_map/ppermute | solution.py:636
  3.1 18.1 %collective-permute-start.1 = (bf16[2,2,192,384]{3,2,1,0:T(8,128)(2,1)S(1)}, bf16[2,2,192,384]{3,2,1,0:T(8,128)(2,1)S(1)}, u32[]{:S(2)}, u32[]{:S(2)}) collective-permute-start(bf16[2,2,192,384]{3,2,1,0:T(8,128)(2,1)S(1)} %get-tuple-element.16), channel_id=1, source_target_pairs={{8,16},{24,32},{40,48},{56,64},{72,80},{88,96},{104,112},{16,8},{3... | collective-permute-start | bytes 1769480 | tf_op jit(solution)/shard_map/ppermute | solution.py:635
  21.3 2.9 %copy-start.5 = (bf16[2,2,192,384]{3,2,1,0:T(8,128)(2,1)}, bf16[2,2,192,384]{3,2,1,0:T(8,128)(2,1)S(1)}, u32[]{:S(2)}) copy-start(bf16[2,2,192,384]{3,2,1,0:T(8,128)(2,1)S(1)} %collective-permute-done.same) | copy-start | bytes 1769476
  21.3 3.0 %copy-start.2 = (bf16[2,2,192,384]{3,2,1,0:T(8,128)(2,1)}, bf16[2,2,192,384]{3,2,1,0:T(8,128)(2,1)S(1)}, u32[]{:S(2)}) copy-start(bf16[2,2,192,384]{3,2,1,0:T(8,128)(2,1)S(1)} %collective-permute-done.1.cross) | copy-start | bytes 1769476
  24.2 36.3 %all-to-all-start = ((bf16[16,216,128]{2,1,0:T(8,128)(2,1)}), bf16[16,216,128]{2,1,0:T(8,128)(2,1)S(1)}, u32[]{:S(2)}, u32[]{:S(2)}) async-start(bf16[16,216,128]{2,1,0:T(8,128)(2,1)} %bitcast.14), calls=%async_computation | async-start | bytes 1769472 | tf_op jit(solution)/shard_map/all_to_all | solution.py:644
  46.4 46.5 %collective-permute-start.5 = (bf16[2,2,384,384]{3,2,1,0:T(8,128)(2,1)S(1)}, bf16[2,2,384,384]{3,2,1,0:T(8,128)(2,1)S(1)}, u32[]{:S(2)}, u32[]{:S(2)}) collective-permute-start(bf16[2,2,384,384]{3,2,1,0:T(8,128)(2,1)S(1)} %shard_map.66), channel_id=1, source_target_pairs={{8,16},{24,32},{40,48},{56,64},{72,80},{88,96},{104,112},{16,8},{3... | collective-permute-start | bytes 3538952 | tf_op jit(solution)/shard_map/ppermute | solution.py:639
  80.1 12.8 %copy-start.7 = (f32[4]{0:T(128)S(1)}, f32[4]{0:T(128)}, u32[]{:S(2)}) copy-start(f32[4]{0:T(128)} %refs_2_.5) | copy-start | bytes 52
  80.1 12.8 %copy-start.8 = (s32[1,4]{1,0:T(1,128)S(1)}, s32[1,4]{1,0:T(1,128)}, u32[]{:S(2)}) copy-start(s32[1,4]{1,0:T(1,128)} %refs_3_.5) | copy-start | bytes 52
  81.5 23.0 %all-to-all-start.2 = ((bf16[16,216,128]{2,1,0:T(8,128)(2,1)}), bf16[16,216,128]{2,1,0:T(8,128)(2,1)S(1)}, u32[]{:S(2)}, u32[]{:S(2)}) async-start(bf16[16,216,128]{2,1,0:T(8,128)(2,1)} %shard_map.65), calls=%async_computation.2 | async-start | bytes 1769472 | tf_op jit(solution)/shard_map/all_to_all | solution.py:652
  88.5 2.3 %collective-permute-start.4 = (bf16[2,2,192,384]{3,2,1,0:T(8,128)(2,1)}, bf16[2,2,192,384]{3,2,1,0:T(8,128)(2,1)S(1)}, u32[]{:S(2)}, u32[]{:S(2)}) collective-permute-start(bf16[2,2,192,384]{3,2,1,0:T(8,128)(2,1)} %copy-done.5), channel_id=1, source_target_pairs={{0,8},{8,0},{1,9},{9,1},{2,10},{10,2},{3,11},{11,3},{4,12},{12,4},... | collective-permute-start | bytes 1769480 | tf_op jit(solution)/shard_map/ppermute | solution.py:642
  92.9 11.6 %copy-start.1 = (bf16[2,2,384,384]{3,2,1,0:T(8,128)(2,1)}, bf16[2,2,384,384]{3,2,1,0:T(8,128)(2,1)S(1)}, u32[]{:S(2)}) copy-start(bf16[2,2,384,384]{3,2,1,0:T(8,128)(2,1)S(1)} %collective-permute-done.5.refs_7_.far) | copy-start | bytes 3538948
  104.5 31.1 %collective-permute-start.3 = (bf16[3456,128]{1,0:T(8,128)(2,1)S(1)}, bf16[3456,128]{1,0:T(8,128)(2,1)S(1)}, u32[]{:S(2)}, u32[]{:S(2)}) collective-permute-start(bf16[3456,128]{1,0:T(8,128)(2,1)S(1)} %bitcast.12), channel_id=1, source_target_pairs={{0,8},{8,0},{1,9},{9,1},{2,10},{10,2},{3,11},{11,3},{4,12},{12,4},... | collective-permute-start | bytes 2654216 | tf_op jit(solution)/shard_map/ppermute | solution.py:656
  131.3 4.3 %copy-start.3 = (bf16[768,768]{1,0:T(8,128)(2,1)S(1)}, bf16[768,768]{1,0:T(8,128)(2,1)}, u32[]{:S(2)}) copy-start(bf16[768,768]{1,0:T(8,128)(2,1)} %born_resumed.1.late) | copy-start | bytes 3538948
  131.3 4.3 %copy-start.4 = (bf16[768,768]{1,0:T(8,128)(2,1)S(1)}, bf16[768,768]{1,0:T(8,128)(2,1)}, u32[]{:S(2)}) copy-start(bf16[768,768]{1,0:T(8,128)(2,1)} %born_early.1.early) | copy-start | bytes 3538948

commit v8 on v7

--- a/solution.py
+++ b/solution.py
@@ -245,7 +245,7 @@
     )(place, offsets, same, cross, chip, turned, partial)
 
 
-def near_body(place, swapped, cross, target, out, sems):
+def near_body(place, swapped, cross, out, sems):
     core = place[0]
     copies = [
         pltpu.make_async_copy(cross, out.at[:, :, pl.ds(core * HALF, HALF), :], sems.at[0]),
@@ -264,30 +264,25 @@
             for part in range(2):
                 out[item, part] = out[item, part].astype(F32).T.astype(BF16)
 
-    store = pltpu.make_async_copy(out, target, sems.at[0])
-    store.start()
-    store.wait()
-
 
 def near_call(place, swapped, cross):
     return pl.pallas_call(
         near_body,
-        out_shape=pltpu.HBM((2, 2, NB, NB), BF16),
+        out_shape=jax.ShapeDtypeStruct((2, 2, NB, NB), BF16),
         in_specs=[SMEM, ANY, ANY],
-        out_specs=ANY,
-        scratch_shapes=[pltpu.VMEM((2, 2, NB, NB), BF16), pltpu.SemaphoreType.DMA((2,))],
+        out_specs=VMEM,
+        scratch_shapes=[pltpu.SemaphoreType.DMA((2,))],
         compiler_params=pltpu.CompilerParams(vmem_limit_bytes=4 << 20),
         cost_estimate=pl.CostEstimate(flops=0, bytes_accessed=2_400_000, transcendentals=0),
         name="near_join",
     )(place, swapped, in_hbm(cross))
 
 
-def born_body(early, window, resumed, *refs):
+def born_body(early, *refs):
     refs = list(refs)
     place, offsets, occupation, coupling, own, mate, near = refs[:7]
     refs = refs[7:]
     far = None if early else refs.pop(0)
-    base = refs.pop(0) if resumed else None
     vertex, out, chosen, lows, highs, mixed, wide, stack, side, total, rounded, sems = refs
     core = place[0]
     energy = 2 * (1 - core) if early else 2 * core
@@ -302,21 +297,16 @@
             def _():
                 pltpu.make_async_copy(source.at[slot - low], target, sem).start()
 
-    for k in range(*window):
+    for k in range(4):
         pltpu.make_async_copy(vertex.at[coupling[0, k]], chosen.at[k], sems.at[k, 4]).start()
         for item in range(2):
             at = energy + 4 + item
             fetch(at - offsets[k], lows.at[k, item], sems.at[k, 2 * item])
             fetch(at + offsets[k], highs.at[k, item], sems.at[k, 2 * item + 1])
 
-    if resumed:
-        resume = pltpu.make_async_copy(base, total, sems.at[0, 0])
-        resume.start()
-        resume.wait()
-    else:
-        total[...] = jnp.zeros_like(total)
-
-    @pl.loop(*window)
+    total[...] = jnp.zeros_like(total)
+
+    @pl.loop(0, 4)
     def _(k):
         pltpu.make_async_copy(vertex.at[0], chosen.at[k], sems.at[k, 4]).wait()
         vr = chosen[k, 0]
@@ -356,24 +346,25 @@
             )
             total[rows, :] += term
 
-    if out.dtype == BF16:
+    if early:
         rounded[...] = total[...].astype(BF16)
-    store = pltpu.make_async_copy(rounded if out.dtype == BF16 else total, out, sems.at[0, 0])
-    store.start()
-    store.wait()
-
-
-def born_call(place, offsets, occupation, coupling, arrays, vertex, window, base=None, kind=BF16):
+        store = pltpu.make_async_copy(rounded, out, sems.at[0, 0])
+        store.start()
+        store.wait()
+    else:
+        out[...] = total[...].astype(BF16)
+
+
+def born_call(place, offsets, occupation, coupling, arrays, vertex):
     early = len(arrays) == 3
-    resumed = base is not None
     size = 2 * NB
-    held = (*map(in_hbm, arrays[:3]), *arrays[3:]) + ((in_hbm(base),) if resumed else ())
-    part = window[1] - window[0]
-    return pl.pallas_call(
-        lambda *refs: born_body(early, window, resumed, *refs),
-        out_shape=pltpu.HBM((size, size), kind),
+    held = (*map(in_hbm, arrays[:2]), *arrays[2:])
+    shape = (size, size)
+    return pl.pallas_call(
+        lambda *refs: born_body(early, *refs),
+        out_shape=pltpu.HBM(shape, BF16) if early else jax.ShapeDtypeStruct(shape, BF16),
         in_specs=[SMEM] * 4 + [ANY] * (len(held) + 1),
-        out_specs=ANY,
+        out_specs=ANY if early else VMEM,
         scratch_shapes=[
             pltpu.VMEM((4, 2, NB, NB), BF16),
             pltpu.VMEM((4, 2, 2, NB, NB), BF16),
@@ -388,9 +379,9 @@
         ],
         compiler_params=pltpu.CompilerParams(vmem_limit_bytes=22 << 20),
         cost_estimate=pl.CostEstimate(
-            flops=4 * part * size**3, bytes_accessed=3_000_000 * part, transcendentals=0
+            flops=16 * size**3, bytes_accessed=12_000_000, transcendentals=0
         ),
-        name="born_early" if early else "born_resumed" if resumed else "born_late",
+        name="born_early" if early else "born_late",
     )(place, offsets, occupation, coupling, *held, in_hbm(vertex))
 
 
@@ -642,16 +633,13 @@
     swapped = lax.ppermute(same, "core", SWAP)
     near = near_call(place, swapped, cross)
     bands = lax.all_to_all(pair.reshape(BANDS, ROWS, 128), PLANE, 0, 0, tiled=True)
-    early = born_call(place, offsets, occupation, coupling, (own, mate, near), vertex, (0, 4))
+    early = born_call(place, offsets, occupation, coupling, (own, mate, near), vertex)
     copies = sum_call(bands, 4)
     bands = lax.all_to_all(copies, ROW, 0, 0, tiled=True)
-    base = born_call(
-        place, offsets, occupation, coupling, (own, mate, near, far), vertex, (0, 1), None, F32
-    )
     copies = sum_call(bands, BANDS)
     mine = lax.all_to_all(copies, PLANE, 0, 0, tiled=True).reshape(FLAT, 128)
     late = born_call(
-        place, offsets, occupation, coupling, (own, mate, near, far), vertex, (1, 4), base
+        place, offsets, occupation, coupling, (own, mate, near, far), vertex
     )
     other = lax.ppermute(mine, "core", SWAP)
     held = start_call(place, offsets, mine, magnon_free, own, mate)

time: 146 us -> 139 us (0.952)
  the two profiles are of different devices: /device:TPU:0 before, /device:TPU:17 now
where the time goes in v8:
time: 139 us; the launch traced here: 138 us
  Pallas kernels  57 us (41%)
  blocking collectives  30.2 us (22%)
  waiting for transfers between devices  29.8 us (21%)
  starting transfers between devices  21 us (15%)
    pallas_call x2, Pallas kernels, born_call(): pl.pallas_call(lambda *refs: born_body(early, *refs), out_shape=pltpu.HBM...  25.3 us
    all_to_all x1, blocking collectives, per_device(): lax.all_to_all(pair.reshape(BANDS, ROWS, 128), PLANE, 0, 0, tiled=True)  20 us
    ppermute x1, waiting for transfers between devices, per_device(): cross = lax.ppermute(to_cross, ENERGY, across)  12.7 us
    all_to_all x1, blocking collectives, per_device(): bands = lax.all_to_all(copies, ROW, 0, 0, tiled=True)  10.2 us
    ppermute x1, waiting for transfers between devices, per_device(): far = lax.ppermute(inner, ENERGY, across)  8.78 us
    pallas_call x1, Pallas kernels, final_call(): pl.pallas_call(final_body, out_shape=(jax.ShapeDtypeStruct((4, 1, 2, NB,...  7.74 us
    pallas_call x1, Pallas kernels, prepare_call(): pl.pallas_call(prepare_body, out_shape=(jax.ShapeDtypeStruct((8, 2, NB, N...  7.36 us
    all_to_all x1, starting transfers between devices, per_device(): mine = lax.all_to_all(copies, PLANE, 0, 0, tiled=True).reshape(FLAT, 128)  6.22 us
  transfers between devices with their start and end apart: 7, of which 4 were waited for; matrix products, arithmetic and copies ran while one was open for 0% of the time, Pallas kernels for 30%

profile of v8, /device:TPU:17, one launch (start us, length us, event | category | flops | bytes accessed | tf_op | source)
XLA Modules:
  0.0 138.4 jit_solution(18292016280989548894)
XLA Ops:
  0.0 0.0 copy-start
  0.0 0.0 copy-start.5
  0.0 0.7 collective-permute-start.2
  0.7 1.3 edge.1
  2.0 4.7 %collective-permute-start = (bf16[2,2,192,384]{3,2,1,0:T(8,128)(2,1)S(1)}, bf16[2,2,192,384]{3,2,1,0:T(8,128)(2,1)}, u32[]{:S(2)}, u32[]{:S(2)}) collective-permute-start(bf16[2,2,192,384]{3,2,1,0:T(8,128)(2,1)S(1)} %get-tuple-element.15), channel_id=1, source_target_pairs={{8,24},{24,40},{40,56},{56,72},{72,88},{88,104},{104,120},{16,0},{... | collective-permute-start | bytes 1769480 | tf_op jit(solution)/shard_map/ppermute | solution.py:627
  6.7 2.8 %collective-permute-start.1 = (bf16[2,2,192,384]{3,2,1,0:T(8,128)(2,1)S(1)}, bf16[2,2,192,384]{3,2,1,0:T(8,128)(2,1)S(1)}, u32[]{:S(2)}, u32[]{:S(2)}) collective-permute-start(bf16[2,2,192,384]{3,2,1,0:T(8,128)(2,1)S(1)} %get-tuple-element.16), channel_id=1, source_target_pairs={{8,16},{24,32},{40,48},{56,64},{72,80},{88,96},{104,112},{16,8},{3... | collective-permute-start | bytes 1769480 | tf_op jit(solution)/shard_map/ppermute | solution.py:626
  9.5 0.0 collective-permute-done.2.mate.refs_5_
  9.5 0.0 copy-done
  9.5 0.0 copy-done.5
  9.5 7.4 %prepare.1 = (bf16[8,2,384,384]{3,2,1,0:T(8,128)(2,1)S(1)}, f32[8,2,384,384]{3,2,1,0:T(8,128)S(1)}, f32[3,2,192,384]{3,2,1,0:T(8,128)S(1)}) custom-call(s32[1]{0:T(128)} %bitcast.place.refs_0_, s32[4]{0:T(128)S(1)} %copy-done.5, bf16[4,2,384,384]{3,2,1,0:T(8,128)(2,1)S(1)} %bitcast.10, bf16[4,2,384,384]{3,2,1,0:T(8,128)(2,1)} %collective-permute-done.2.mate.refs_5_), custom_call_target="tpu_custom_call" | custom-call | flops 20000000 | bytes 9000000 | tf_op jit(solution)/shard_map/prepare/pallas_call | solution.py:147
  16.9 4.6 %collective-permute-done.same = bf16[2,2,192,384]{3,2,1,0:T(8,128)(2,1)} collective-permute-done((bf16[2,2,192,384]{3,2,1,0:T(8,128)(2,1)S(1)}, bf16[2,2,192,384]{3,2,1,0:T(8,128)(2,1)}, u32[]{:S(2)}, u32[]{:S(2)}) %collective-permute-start) | collective-permute-done | bytes 589856 | tf_op jit(solution)/shard_map/ppermute | solution.py:627
  21.4 12.7 %collective-permute-done.1.cross = bf16[2,2,192,384]{3,2,1,0:T(8,128)(2,1)S(1)} collective-permute-done((bf16[2,2,192,384]{3,2,1,0:T(8,128)(2,1)S(1)}, bf16[2,2,192,384]{3,2,1,0:T(8,128)(2,1)S(1)}, u32[]{:S(2)}, u32[]{:S(2)}) %collective-permute-start.1) | collective-permute-done | bytes 589856 | tf_op jit(solution)/shard_map/ppermute | solution.py:626
  34.1 0.0 copy-start.2
  34.1 3.7 %polar.1 = bf16[3456,128]{1,0:T(8,128)(2,1)} custom-call(s32[1]{0:T(128)} %bitcast.place.refs_0_, s32[4]{0:T(128)S(1)} %copy-done.5, bf16[2,2,192,384]{3,2,1,0:T(8,128)(2,1)} %collective-permute-done.same, bf16[2,2,192,384]{3,2,1,0:T(8,128)(2,1)S(1)} %collective-permute-done.1.cross, bf16[8,2,384,384]{3,2,1,0:T(8,128)(2,1)S(1)} %get-tuple-element.17.chip, ...), custom_call_target="tpu_custom_call" | custom-call | flops 20000000 | bytes 9000000 | tf_op jit(solution)/shard_map/polar/pallas_call | solution.py:233
  37.8 0.0 copy-done.2
  37.8 20.0 %all_to_all.15.refs_0_ = bf16[16,216,128]{2,1,0:T(8,128)(2,1)S(1)} all-to-all(bf16[16,216,128]{2,1,0:T(8,128)(2,1)} %bitcast.13), channel_id=1, replica_groups=mesh['y'=4,'xh'=2,'core'=2,'xl'=2,'z'=4] {'y','z'}, dimensions={0} | all-to-all | bytes 1769472 | tf_op jit(solution)/shard_map/all_to_all | solution.py:635
  57.8 2.1 %shard_map.64 = bf16[4,216,128]{2,1,0:T(8,128)(2,1)} custom-call(bf16[16,216,128]{2,1,0:T(8,128)(2,1)S(1)} %all_to_all.15.refs_0_), custom_call_target="tpu_custom_call" | custom-call | flops 500000 | bytes 1900000 | tf_op jit(solution)/shard_map/pallas_call | solution.py:413
  59.9 10.2 %all_to_all.16.refs_0_ = bf16[4,216,128]{2,1,0:T(8,128)(2,1)S(1)} all-to-all(bf16[4,216,128]{2,1,0:T(8,128)(2,1)} %shard_map.64), channel_id=1, replica_groups=mesh['y'=4,'xh'=2,'core'=2,'xl'=2,'z'=4] {'xh','xl'}, dimensions={0} | all-to-all | bytes 442368 | tf_op jit(solution)/shard_map/all_to_all | solution.py:638
  70.1 1.4 shard_map.65
  71.5 6.2 %all-to-all-start.2 = ((bf16[16,216,128]{2,1,0:T(8,128)(2,1)}), bf16[16,216,128]{2,1,0:T(8,128)(2,1)S(1)}, u32[]{:S(2)}, u32[]{:S(2)}) async-start(bf16[16,216,128]{2,1,0:T(8,128)(2,1)} %shard_map.65), calls=%async_computation.2 | async-start | bytes 1769472 | tf_op jit(solution)/shard_map/all_to_all | solution.py:640
  77.7 0.0 copy-start.6
  77.7 0.0 copy-start.7
  77.7 1.7 %collective-permute-start.4 = (bf16[2,2,192,384]{3,2,1,0:T(8,128)(2,1)}, bf16[2,2,192,384]{3,2,1,0:T(8,128)(2,1)S(1)}, u32[]{:S(2)}, u32[]{:S(2)}) collective-permute-start(bf16[2,2,192,384]{3,2,1,0:T(8,128)(2,1)} %collective-permute-done.same), channel_id=1, source_target_pairs={{0,8},{8,0},{1,9},{9,1},{2,10},{10,2},{3,11},{11,3},{4,12},{12,4},... | collective-permute-start | bytes 1769480 | tf_op jit(solution)/shard_map/ppermute | solution.py:633
  79.4 2.3 %shard_map.66 = bf16[2,2,384,384]{3,2,1,0:T(8,128)(2,1)} custom-call(s32[1]{0:T(128)} %bitcast.place.refs_0_, bf16[4,2,384,384]{3,2,1,0:T(8,128)(2,1)} %bitcast.6), custom_call_target="tpu_custom_call" | custom-call | bytes 2400000 | tf_op jit(solution)/shard_map/pallas_call | solution.py:58
  81.7 2.5 %collective-permute-start.5 = (bf16[2,2,384,384]{3,2,1,0:T(8,128)(2,1)}, bf16[2,2,384,384]{3,2,1,0:T(8,128)(2,1)S(1)}, u32[]{:S(2)}, u32[]{:S(2)}) collective-permute-start(bf16[2,2,384,384]{3,2,1,0:T(8,128)(2,1)} %shard_map.66), channel_id=1, source_target_pairs={{8,16},{24,32},{40,48},{56,64},{72,80},{88,96},{104,112},{16,8},{3... | collective-permute-start | bytes 3538952 | tf_op jit(solution)/shard_map/ppermute | solution.py:630
  84.2 0.0 collective-permute-done.4.swapped
  84.2 1.5 %near_join.1.refs_6_.near = bf16[2,2,384,384]{3,2,1,0:T(8,128)(2,1)S(1)} custom-call(s32[1]{0:T(128)} %bitcast.place.refs_0_, bf16[2,2,192,384]{3,2,1,0:T(8,128)(2,1)S(1)} %collective-permute-done.4.swapped, bf16[2,2,192,384]{3,2,1,0:T(8,128)(2,1)} %copy-done.2), custom_call_target="tpu_custom_call" | custom-call | bytes 2400000 | tf_op jit(solution)/shard_map/near_join/pallas_call | solution.py:269
  85.7 0.0 copy-start.1
  85.7 3.8 %all-to-all-done.2 = bf16[16,216,128]{2,1,0:T(8,128)(2,1)S(1)} async-done(((bf16[16,216,128]{2,1,0:T(8,128)(2,1)}), bf16[16,216,128]{2,1,0:T(8,128)(2,1)S(1)}, u32[]{:S(2)}, u32[]{:S(2)}) %all-to-all-start.2) | async-done | bytes 884768 | tf_op jit(solution)/shard_map/all_to_all | solution.py:640
  89.5 2.5 %collective-permute-start.3 = (bf16[3456,128]{1,0:T(8,128)(2,1)S(1)}, bf16[3456,128]{1,0:T(8,128)(2,1)S(1)}, u32[]{:S(2)}, u32[]{:S(2)}) collective-permute-start(bf16[3456,128]{1,0:T(8,128)(2,1)S(1)} %bitcast.11), channel_id=1, source_target_pairs={{0,8},{8,0},{1,9},{9,1},{2,10},{10,2},{3,11},{11,3},{4,12},{12,4},... | collective-permute-start | bytes 2654216 | tf_op jit(solution)/shard_map/ppermute | solution.py:644
  91.9 0.0 copy-done.6
  91.9 0.0 copy-done.7
  91.9 13.1 %born_early.1.early = bf16[768,768]{1,0:T(8,128)(2,1)} custom-call(s32[1]{0:T(128)} %bitcast.place.refs_0_, s32[4]{0:T(128)S(1)} %copy-done.5, f32[4]{0:T(128)S(1)} %copy-done.6, s32[1,4]{1,0:T(1,128)S(1)} %copy-done.7, bf16[4,2,384,384]{3,2,1,0:T(8,128)(2,1)} %bitcast.7, bf16[4,2,384,384]{3,2,1,0:T(8,128)(2,1)} %collective-permute-done.2.mate.refs_5_, ...), custom_call_target="tpu_custom_call" | custom-call | flops 7247757312 | bytes 12000000 | tf_op jit(solution)/shard_map/born_early/pallas_call | solution.py:363
  105.0 8.8 %collective-permute-done.5.refs_7_.far = bf16[2,2,384,384]{3,2,1,0:T(8,128)(2,1)S(1)} collective-permute-done((bf16[2,2,384,384]{3,2,1,0:T(8,128)(2,1)}, bf16[2,2,384,384]{3,2,1,0:T(8,128)(2,1)S(1)}, u32[]{:S(2)}, u32[]{:S(2)}) %collective-permute-start.5) | collective-permute-done | bytes 1179680 | tf_op jit(solution)/shard_map/ppermute | solution.py:630
  113.8 0.0 copy-done.1
  113.8 0.0 copy-start.3
  113.8 12.2 %born_late.1.late = bf16[768,768]{1,0:T(8,128)(2,1)S(1)} custom-call(s32[1]{0:T(128)} %bitcast.place.refs_0_, s32[4]{0:T(128)S(1)} %copy-done.5, f32[4]{0:T(128)S(1)} %copy-done.6, s32[1,4]{1,0:T(1,128)S(1)} %copy-done.7, bf16[4,2,384,384]{3,2,1,0:T(8,128)(2,1)} %bitcast.8, bf16[4,2,384,384]{3,2,1,0:T(8,128)(2,1)} %collective-permute-done.2.mate.refs_5_, ...), custom_call_target="tpu_custom_call" | custom-call | flops 7247757312 | bytes 12000000 | tf_op jit(solution)/shard_map/born_late/pallas_call | solution.py:363
  126.0 0.0 copy-done.3
  126.0 0.0 copy-start.4
  126.0 4.5 %final_start.1 = (bf16[12,2,384,384]{3,2,1,0:T(8,128)(2,1)S(1)}, f32[3,384,768]{2,1,0:T(8,128)S(1)}, f32[3,384,768]{2,1,0:T(8,128)S(1)}, bf16[4,768,768]{2,1,0:T(8,128)(2,1)S(1)}) custom-call(s32[1]{0:T(128)} %bitcast.place.refs_0_, s32[4]{0:T(128)S(1)} %copy-done.5, bf16[3456,128]{1,0:T(8,128)(2,1)S(1)} %bitcast.12, bf16[4,2,384,384]{3,2,1,0:T(8,128)(2,1)} %free.1, ...), custom_call_target="tpu_custom_call" | custom-call | flops 1000000000 | bytes 10000000 | tf_op jit(solution)/shard_map/final_start/pallas_call | solution.py:502
  130.5 0.0 collective-permute-done.3.other
  130.5 0.0 copy-done.4
  130.5 7.7 %final.1 = (bf16[4,1,2,384,384]{4,3,2,1,0:T(8,128)(2,1)}, bf16[12,2,384,384]{3,2,1,0:T(8,128)(2,1)S(1)}, f32[3,384,768]{2,1,0:T(8,128)S(1)}) custom-call(s32[1]{0:T(128)} %bitcast.place.refs_0_, s32[4]{0:T(128)S(1)} %copy-done.5, bf16[3456,128]{1,0:T(8,128)(2,1)S(1)} %collective-permute-done.3.other, ...), custom_call_target="tpu_custom_call", output_to_operand_aliasing={{1}: (7, {}), {2}: (8, {})} | custom-call | flops 1000000000 | bytes 18000000 | tf_op jit(solution)/shard_map/final/pallas_call | solution.py:592
Async XLA Ops:
  0.0 9.5 %copy-start = (bf16[4,1,2,384,384]{4,3,2,1,0:T(8,128)(2,1)S(1)}, bf16[4,1,2,384,384]{4,3,2,1,0:T(8,128)(2,1)}, u32[]{:S(2)}) copy-start(bf16[4,1,2,384,384]{4,3,2,1,0:T(8,128)(2,1)} %param.6) | copy-start | bytes 7077892
  0.0 9.5 %copy-start.5 = (s32[4]{0:T(128)S(1)}, s32[4]{0:T(128)}, u32[]{:S(2)}) copy-start(s32[4]{0:T(128)} %offsets.7) | copy-start | bytes 52
  0.0 9.5 %collective-permute-start.2 = (bf16[4,2,384,384]{3,2,1,0:T(8,128)(2,1)}, bf16[4,2,384,384]{3,2,1,0:T(8,128)(2,1)}, u32[]{:S(2)}, u32[]{:S(2)}) collective-permute-start(bf16[4,2,384,384]{3,2,1,0:T(8,128)(2,1)} %bitcast.4), channel_id=1, source_target_pairs={{0,8},{8,0},{1,9},{9,1},{2,10},{10,2},{3,11},{11,3},{4,12},{12,4},... | collective-permute-start | bytes 7077896 | tf_op jit(solution)/shard_map/ppermute | solution.py:628
  2.0 19.5 %collective-permute-start = (bf16[2,2,192,384]{3,2,1,0:T(8,128)(2,1)S(1)}, bf16[2,2,192,384]{3,2,1,0:T(8,128)(2,1)}, u32[]{:S(2)}, u32[]{:S(2)}) collective-permute-start(bf16[2,2,192,384]{3,2,1,0:T(8,128)(2,1)S(1)} %get-tuple-element.15), channel_id=1, source_target_pairs={{8,24},{24,40},{40,56},{56,72},{72,88},{88,104},{104,120},{16,0},{... | collective-permute-start | bytes 1769480 | tf_op jit(solution)/shard_map/ppermute | solution.py:627
  6.7 27.4 %collective-permute-start.1 = (bf16[2,2,192,384]{3,2,1,0:T(8,128)(2,1)S(1)}, bf16[2,2,192,384]{3,2,1,0:T(8,128)(2,1)S(1)}, u32[]{:S(2)}, u32[]{:S(2)}) collective-permute-start(bf16[2,2,192,384]{3,2,1,0:T(8,128)(2,1)S(1)} %get-tuple-element.16), channel_id=1, source_target_pairs={{8,16},{24,32},{40,48},{56,64},{72,80},{88,96},{104,112},{16,8},{3... | collective-permute-start | bytes 1769480 | tf_op jit(solution)/shard_map/ppermute | solution.py:626
  34.1 3.7 %copy-start.2 = (bf16[2,2,192,384]{3,2,1,0:T(8,128)(2,1)}, bf16[2,2,192,384]{3,2,1,0:T(8,128)(2,1)S(1)}, u32[]{:S(2)}) copy-start(bf16[2,2,192,384]{3,2,1,0:T(8,128)(2,1)S(1)} %collective-permute-done.1.cross) | copy-start | bytes 1769476
  71.5 18.0 %all-to-all-start.2 = ((bf16[16,216,128]{2,1,0:T(8,128)(2,1)}), bf16[16,216,128]{2,1,0:T(8,128)(2,1)S(1)}, u32[]{:S(2)}, u32[]{:S(2)}) async-start(bf16[16,216,128]{2,1,0:T(8,128)(2,1)} %shard_map.65), calls=%async_computation.2 | async-start | bytes 1769472 | tf_op jit(solution)/shard_map/all_to_all | solution.py:640
  77.7 14.2 %copy-start.6 = (f32[4]{0:T(128)S(1)}, f32[4]{0:T(128)}, u32[]{:S(2)}) copy-start(f32[4]{0:T(128)} %refs_2_.3) | copy-start | bytes 52
  77.7 14.2 %copy-start.7 = (s32[1,4]{1,0:T(1,128)S(1)}, s32[1,4]{1,0:T(1,128)}, u32[]{:S(2)}) copy-start(s32[1,4]{1,0:T(1,128)} %refs_3_.3) | copy-start | bytes 52
  77.7 6.4 %collective-permute-start.4 = (bf16[2,2,192,384]{3,2,1,0:T(8,128)(2,1)}, bf16[2,2,192,384]{3,2,1,0:T(8,128)(2,1)S(1)}, u32[]{:S(2)}, u32[]{:S(2)}) collective-permute-start(bf16[2,2,192,384]{3,2,1,0:T(8,128)(2,1)} %collective-permute-done.same), channel_id=1, source_target_pairs={{0,8},{8,0},{1,9},{9,1},{2,10},{10,2},{3,11},{11,3},{4,12},{12,4},... | collective-permute-start | bytes 1769480 | tf_op jit(solution)/shard_map/ppermute | solution.py:633
  81.7 32.1 %collective-permute-start.5 = (bf16[2,2,384,384]{3,2,1,0:T(8,128)(2,1)}, bf16[2,2,384,384]{3,2,1,0:T(8,128)(2,1)S(1)}, u32[]{:S(2)}, u32[]{:S(2)}) collective-permute-start(bf16[2,2,384,384]{3,2,1,0:T(8,128)(2,1)} %shard_map.66), channel_id=1, source_target_pairs={{8,16},{24,32},{40,48},{56,64},{72,80},{88,96},{104,112},{16,8},{3... | collective-permute-start | bytes 3538952 | tf_op jit(solution)/shard_map/ppermute | solution.py:630
  85.7 28.2 %copy-start.1 = (bf16[2,2,384,384]{3,2,1,0:T(8,128)(2,1)}, bf16[2,2,384,384]{3,2,1,0:T(8,128)(2,1)S(1)}, u32[]{:S(2)}) copy-start(bf16[2,2,384,384]{3,2,1,0:T(8,128)(2,1)S(1)} %near_join.1.refs_6_.near) | copy-start | bytes 3538948
  89.5 41.0 %collective-permute-start.3 = (bf16[3456,128]{1,0:T(8,128)(2,1)S(1)}, bf16[3456,128]{1,0:T(8,128)(2,1)S(1)}, u32[]{:S(2)}, u32[]{:S(2)}) collective-permute-start(bf16[3456,128]{1,0:T(8,128)(2,1)S(1)} %bitcast.11), channel_id=1, source_target_pairs={{0,8},{8,0},{1,9},{9,1},{2,10},{10,2},{3,11},{11,3},{4,12},{12,4},... | collective-permute-start | bytes 2654216 | tf_op jit(solution)/shard_map/ppermute | solution.py:644
  113.8 12.2 %copy-start.3 = (bf16[2,2,384,384]{3,2,1,0:T(8,128)(2,1)}, bf16[2,2,384,384]{3,2,1,0:T(8,128)(2,1)S(1)}, u32[]{:S(2)}) copy-start(bf16[2,2,384,384]{3,2,1,0:T(8,128)(2,1)S(1)} %collective-permute-done.5.refs_7_.far) | copy-start | bytes 3538948
  126.0 4.5 %copy-start.4 = (bf16[768,768]{1,0:T(8,128)(2,1)S(1)}, bf16[768,768]{1,0:T(8,128)(2,1)}, u32[]{:S(2)}) copy-start(bf16[768,768]{1,0:T(8,128)(2,1)} %born_early.1.early) | copy-start | bytes 3538948

commit v9 on v8

--- a/solution.py
+++ b/solution.py
@@ -385,44 +385,54 @@
     )(place, offsets, occupation, coupling, *held, in_hbm(vertex))
 
 
-def sum_body(count, copies, bands, out, buffer, value, *sems):
-    loads = [
-        pltpu.make_async_copy(bands.at[i], buffer.at[i], sems[0].at[i]) for i in range(count)
-    ]
-    for load in loads:
-        load.start()
-    for load in loads:
-        load.wait()
-
+def band_total(bands, rows):
+    total = bands[0, rows, :].astype(F32)
+    for i in range(1, bands.shape[0]):
+        total += bands[i, rows, :].astype(F32)
+    return total.astype(BF16)
+
+
+def plane_body(bands, out):
     for begin in range(0, ROWS, 64):
         rows = slice(begin, min(begin + 64, ROWS))
-        total = buffer[0, rows, :].astype(F32)
-        for i in range(1, count):
-            total += buffer[i, rows, :].astype(F32)
-        value[rows, :] = total.astype(BF16)
-
-    stores = [pltpu.make_async_copy(value, out.at[i], sems[1].at[i]) for i in range(copies)]
+        value = band_total(bands, rows)
+        for i in range(out.shape[0]):
+            out[i, rows, :] = value
+
+
+def plane_call(bands):
+    return pl.pallas_call(
+        plane_body,
+        out_shape=jax.ShapeDtypeStruct((4, ROWS, 128), BF16),
+        in_specs=[VMEM],
+        out_specs=VMEM,
+        compiler_params=pltpu.CompilerParams(vmem_limit_bytes=4 << 20),
+        cost_estimate=pl.CostEstimate(flops=500_000, bytes_accessed=1_200_000, transcendentals=0),
+        name="plane_sum",
+    )(bands)
+
+
+def row_body(bands, out, value, sems):
+    for begin in range(0, ROWS, 64):
+        rows = slice(begin, min(begin + 64, ROWS))
+        value[rows, :] = band_total(bands, rows)
+    stores = [pltpu.make_async_copy(value, out.at[i], sems.at[i]) for i in range(BANDS)]
     for store in stores:
         store.start()
     for store in stores:
         store.wait()
 
 
-def sum_call(bands, copies):
-    count = bands.shape[0]
-    return pl.pallas_call(
-        lambda *refs: sum_body(count, copies, *refs),
-        out_shape=pltpu.HBM((copies, ROWS, 128), BF16),
-        in_specs=[ANY],
+def row_call(bands):
+    return pl.pallas_call(
+        row_body,
+        out_shape=pltpu.HBM((BANDS, ROWS, 128), BF16),
+        in_specs=[VMEM],
         out_specs=ANY,
-        scratch_shapes=[
-            pltpu.VMEM(bands.shape, BF16),
-            pltpu.VMEM((ROWS, 128), BF16),
-            pltpu.SemaphoreType.DMA((count,)),
-            pltpu.SemaphoreType.DMA((copies,)),
-        ],
+        scratch_shapes=[pltpu.VMEM((ROWS, 128), BF16), pltpu.SemaphoreType.DMA((BANDS,))],
         compiler_params=pltpu.CompilerParams(vmem_limit_bytes=4 << 20),
-        cost_estimate=pl.CostEstimate(flops=500_000, bytes_accessed=1_900_000, transcendentals=0),
+        cost_estimate=pl.CostEstimate(flops=500_000, bytes_accessed=1_200_000, transcendentals=0),
+        name="row_sum",
     )(bands)
 
 
@@ -454,11 +464,10 @@
 
 def start_body(
     place, offsets, mine, free, own, mate,
-    slots, magnon, sums, table, source, plain, joined, sems,
+    slots, magnon, sums, table, plain, joined, sems,
 ):
     core = place[0]
     roles = offset_roles(offsets)
-    ready = pltpu.make_async_copy(mine, source, sems.at[6])
     tables = [
         pltpu.make_async_copy(free.at[k], plain.at[role], sems.at[role])
         for role, k in enumerate(roles)
@@ -467,10 +476,9 @@
         pltpu.make_async_copy(own, slots.at[pl.ds(4, 4)], sems.at[4]),
         pltpu.make_async_copy(mate, slots.at[pl.ds(8 - 8 * core, 4)], sems.at[5]),
     ]
-    for load in [ready] + tables + loads:
+    for load in tables + loads:
         load.start()
-    ready.wait()
-    unpack_half(source, joined)
+    unpack_half(mine, joined)
     for role in range(4):
         tables[role].wait()
         fr = plain[role, 0]
@@ -507,13 +515,12 @@
             jax.ShapeDtypeStruct((3, NB, size), F32),
             jax.ShapeDtypeStruct((4, size, size), BF16),
         ),
-        in_specs=[SMEM, SMEM] + [ANY] * 4,
+        in_specs=[SMEM, SMEM, VMEM] + [ANY] * 3,
         out_specs=(VMEM,) * 4,
         scratch_shapes=[
-            pltpu.VMEM((FLAT, 128), BF16),
             pltpu.VMEM((4, 2, NB, NB), BF16),
             pltpu.VMEM((3, HALF, size), BF16),
-            pltpu.SemaphoreType.DMA((7,)),
+            pltpu.SemaphoreType.DMA((6,)),
         ],
         compiler_params=pltpu.CompilerParams(vmem_limit_bytes=10 << 20),
         cost_estimate=pl.CostEstimate(
@@ -525,19 +532,16 @@
 
 def final_body(
     place, offsets, other, near, far, early, late, slots_in, magnon_in, sums, table,
-    out, slots, magnon, source, joined, result, sems,
+    out, slots, magnon, joined, result, sems,
 ):
     core = place[0]
     loads = [
         pltpu.make_async_copy(near, slots.at[pl.ds(2 + 6 * core, 2)], sems.at[5]),
         pltpu.make_async_copy(far, slots.at[pl.ds(10 * core, 2)], sems.at[6]),
     ]
-    ready = pltpu.make_async_copy(other, source, sems.at[4])
-    ready.start()
     for load in loads:
         load.start()
-    ready.wait()
-    unpack_half(source, joined)
+    unpack_half(other, joined)
     roles = offset_roles(offsets)
     _, _, first, last = roles
     half = 1 - core
@@ -596,11 +600,10 @@
             jax.ShapeDtypeStruct(slots.shape, BF16),
             jax.ShapeDtypeStruct(magnon.shape, F32),
         ),
-        in_specs=[SMEM, SMEM, ANY, ANY, ANY] + [VMEM] * 6,
+        in_specs=[SMEM, SMEM, VMEM, ANY, ANY] + [VMEM] * 6,
         out_specs=(ANY, VMEM, VMEM),
         input_output_aliases={7: 1, 8: 2},
         scratch_shapes=[
-            pltpu.VMEM((FLAT, 128), BF16),
             pltpu.VMEM((3, HALF, size), BF16),
             pltpu.VMEM((4, 2, NB, NB), BF16),
             pltpu.SemaphoreType.DMA((7,)),
@@ -634,9 +637,9 @@
     near = near_call(place, swapped, cross)
     bands = lax.all_to_all(pair.reshape(BANDS, ROWS, 128), PLANE, 0, 0, tiled=True)
     early = born_call(place, offsets, occupation, coupling, (own, mate, near), vertex)
-    copies = sum_call(bands, 4)
+    copies = plane_call(bands)
     bands = lax.all_to_all(copies, ROW, 0, 0, tiled=True)
-    copies = sum_call(bands, BANDS)
+    copies = row_call(bands)
     mine = lax.all_to_all(copies, PLANE, 0, 0, tiled=True).reshape(FLAT, 128)
     late = born_call(
         place, offsets, occupation, coupling, (own, mate, near, far), vertex

time: 139 us -> 136 us (0.978)
  Pallas kernels: 57 us -> 54.4 us
    pallas_call x2, Pallas kernels: 3.45 us -> 1.22 us  [the longest x1 1.09 us: row_call(): pl.pallas_call(row_body, out_shape=pltpu.HBM((BANDS, ROWS, 128), BF16), i...]
  transfers between devices with their start and end apart: 7 -> 7, of which waited for: 4 -> 4; matrix products, arithmetic and copies ran while one was open for 0% -> 0% of each run, Pallas kernels for 30% -> 31%
where the time goes in v9:
time: 136 us
  Pallas kernels  54.4 us (40%)
  blocking collectives  30 us (22%)
  waiting for transfers between devices  29.8 us (22%)
  starting transfers between devices  21 us (15%)
    pallas_call x2, Pallas kernels, born_call(): pl.pallas_call(lambda *refs: born_body(early, *refs), out_shape=pltpu.HBM...  25.3 us
    all_to_all x1, blocking collectives, per_device(): lax.all_to_all(pair.reshape(BANDS, ROWS, 128), PLANE, 0, 0, tiled=True)  20 us
    ppermute x1, waiting for transfers between devices, per_device(): cross = lax.ppermute(to_cross, ENERGY, across)  12.7 us
    all_to_all x1, blocking collectives, per_device(): bands = lax.all_to_all(copies, ROW, 0, 0, tiled=True)  10 us
    ppermute x1, waiting for transfers between devices, per_device(): far = lax.ppermute(inner, ENERGY, across)  8.77 us
    pallas_call x1, Pallas kernels, final_call(): pl.pallas_call(final_body, out_shape=(jax.ShapeDtypeStruct((4, 1, 2, NB,...  7.56 us
    pallas_call x1, Pallas kernels, prepare_call(): pl.pallas_call(prepare_body, out_shape=(jax.ShapeDtypeStruct((8, 2, NB, N...  7.36 us
    all_to_all x1, starting transfers between devices, per_device(): mine = lax.all_to_all(copies, PLANE, 0, 0, tiled=True).reshape(FLAT, 128)  6.22 us
  transfers between devices with their start and end apart: 7, of which 4 were waited for; matrix products, arithmetic and copies ran while one was open for 0% of the time, Pallas kernels for 31%

profile of v9, /device:TPU:17, one launch (start us, length us, event | category | flops | bytes accessed | tf_op | source)
XLA Modules:
  0.0 135.6 jit_solution(801033019341389076)
XLA Ops:
  0.0 0.0 copy-start
  0.0 0.0 copy-start.5
  0.0 0.7 collective-permute-start.2
  0.7 1.3 edge.1
  2.0 4.7 %collective-permute-start = (bf16[2,2,192,384]{3,2,1,0:T(8,128)(2,1)S(1)}, bf16[2,2,192,384]{3,2,1,0:T(8,128)(2,1)}, u32[]{:S(2)}, u32[]{:S(2)}) collective-permute-start(bf16[2,2,192,384]{3,2,1,0:T(8,128)(2,1)S(1)} %get-tuple-element.15), channel_id=1, source_target_pairs={{8,24},{24,40},{40,56},{56,72},{72,88},{88,104},{104,120},{16,0},{... | collective-permute-start | bytes 1769480 | tf_op jit(solution)/shard_map/ppermute | solution.py:630
  6.7 2.8 %collective-permute-start.1 = (bf16[2,2,192,384]{3,2,1,0:T(8,128)(2,1)S(1)}, bf16[2,2,192,384]{3,2,1,0:T(8,128)(2,1)S(1)}, u32[]{:S(2)}, u32[]{:S(2)}) collective-permute-start(bf16[2,2,192,384]{3,2,1,0:T(8,128)(2,1)S(1)} %get-tuple-element.16), channel_id=1, source_target_pairs={{8,16},{24,32},{40,48},{56,64},{72,80},{88,96},{104,112},{16,8},{3... | collective-permute-start | bytes 1769480 | tf_op jit(solution)/shard_map/ppermute | solution.py:629
  9.5 0.0 collective-permute-done.2.mate.refs_5_
  9.5 0.0 copy-done
  9.5 0.0 copy-done.5
  9.5 7.4 %prepare.1 = (bf16[8,2,384,384]{3,2,1,0:T(8,128)(2,1)S(1)}, f32[8,2,384,384]{3,2,1,0:T(8,128)S(1)}, f32[3,2,192,384]{3,2,1,0:T(8,128)S(1)}) custom-call(s32[1]{0:T(128)} %bitcast.place.refs_0_, s32[4]{0:T(128)S(1)} %copy-done.5, bf16[4,2,384,384]{3,2,1,0:T(8,128)(2,1)S(1)} %bitcast.10, bf16[4,2,384,384]{3,2,1,0:T(8,128)(2,1)} %collective-permute-done.2.mate.refs_5_), custom_call_target="tpu_custom_call" | custom-call | flops 20000000 | bytes 9000000 | tf_op jit(solution)/shard_map/prepare/pallas_call | solution.py:147
  16.9 4.6 %collective-permute-done.same = bf16[2,2,192,384]{3,2,1,0:T(8,128)(2,1)} collective-permute-done((bf16[2,2,192,384]{3,2,1,0:T(8,128)(2,1)S(1)}, bf16[2,2,192,384]{3,2,1,0:T(8,128)(2,1)}, u32[]{:S(2)}, u32[]{:S(2)}) %collective-permute-start) | collective-permute-done | bytes 589856 | tf_op jit(solution)/shard_map/ppermute | solution.py:630
  21.4 12.7 %collective-permute-done.1.cross = bf16[2,2,192,384]{3,2,1,0:T(8,128)(2,1)S(1)} collective-permute-done((bf16[2,2,192,384]{3,2,1,0:T(8,128)(2,1)S(1)}, bf16[2,2,192,384]{3,2,1,0:T(8,128)(2,1)S(1)}, u32[]{:S(2)}, u32[]{:S(2)}) %collective-permute-start.1) | collective-permute-done | bytes 589856 | tf_op jit(solution)/shard_map/ppermute | solution.py:629
  34.1 0.0 copy-start.2
  34.1 3.7 %polar.1 = bf16[3456,128]{1,0:T(8,128)(2,1)} custom-call(s32[1]{0:T(128)} %bitcast.place.refs_0_, s32[4]{0:T(128)S(1)} %copy-done.5, bf16[2,2,192,384]{3,2,1,0:T(8,128)(2,1)} %collective-permute-done.same, bf16[2,2,192,384]{3,2,1,0:T(8,128)(2,1)S(1)} %collective-permute-done.1.cross, bf16[8,2,384,384]{3,2,1,0:T(8,128)(2,1)S(1)} %get-tuple-element.17.chip, ...), custom_call_target="tpu_custom_call" | custom-call | flops 20000000 | bytes 9000000 | tf_op jit(solution)/shard_map/polar/pallas_call | solution.py:233
  37.8 0.0 copy-done.2
  37.8 20.0 %all_to_all.15.bands = bf16[16,216,128]{2,1,0:T(8,128)(2,1)S(1)} all-to-all(bf16[16,216,128]{2,1,0:T(8,128)(2,1)} %bitcast.13), channel_id=1, replica_groups=mesh['y'=4,'xh'=2,'core'=2,'xl'=2,'z'=4] {'y','z'}, dimensions={0} | all-to-all | bytes 1769472 | tf_op jit(solution)/shard_map/all_to_all | solution.py:638
  57.8 0.1 plane_sum.1
  57.9 10.0 %all_to_all.16.bands = bf16[4,216,128]{2,1,0:T(8,128)(2,1)S(1)} all-to-all(bf16[4,216,128]{2,1,0:T(8,128)(2,1)S(1)} %plane_sum.1), channel_id=1, replica_groups=mesh['y'=4,'xh'=2,'core'=2,'xl'=2,'z'=4] {'xh','xl'}, dimensions={0} | all-to-all | bytes 442368 | tf_op jit(solution)/shard_map/all_to_all | solution.py:641
  68.0 1.1 row_sum.1
  69.1 6.2 %all-to-all-start.2 = ((bf16[16,216,128]{2,1,0:T(8,128)(2,1)}), bf16[16,216,128]{2,1,0:T(8,128)(2,1)S(1)}, u32[]{:S(2)}, u32[]{:S(2)}) async-start(bf16[16,216,128]{2,1,0:T(8,128)(2,1)} %row_sum.1), calls=%async_computation.2 | async-start | bytes 1769472 | tf_op jit(solution)/shard_map/all_to_all | solution.py:643
  75.3 0.0 copy-start.6
  75.3 0.0 copy-start.7
  75.3 1.7 %collective-permute-start.4 = (bf16[2,2,192,384]{3,2,1,0:T(8,128)(2,1)}, bf16[2,2,192,384]{3,2,1,0:T(8,128)(2,1)S(1)}, u32[]{:S(2)}, u32[]{:S(2)}) collective-permute-start(bf16[2,2,192,384]{3,2,1,0:T(8,128)(2,1)} %collective-permute-done.same), channel_id=1, source_target_pairs={{0,8},{8,0},{1,9},{9,1},{2,10},{10,2},{3,11},{11,3},{4,12},{12,4},... | collective-permute-start | bytes 1769480 | tf_op jit(solution)/shard_map/ppermute | solution.py:636
  77.0 2.3 %shard_map.64 = bf16[2,2,384,384]{3,2,1,0:T(8,128)(2,1)} custom-call(s32[1]{0:T(128)} %bitcast.place.refs_0_, bf16[4,2,384,384]{3,2,1,0:T(8,128)(2,1)} %bitcast.6), custom_call_target="tpu_custom_call" | custom-call | bytes 2400000 | tf_op jit(solution)/shard_map/pallas_call | solution.py:58
  79.3 2.5 %collective-permute-start.5 = (bf16[2,2,384,384]{3,2,1,0:T(8,128)(2,1)}, bf16[2,2,384,384]{3,2,1,0:T(8,128)(2,1)S(1)}, u32[]{:S(2)}, u32[]{:S(2)}) collective-permute-start(bf16[2,2,384,384]{3,2,1,0:T(8,128)(2,1)} %shard_map.64), channel_id=1, source_target_pairs={{8,16},{24,32},{40,48},{56,64},{72,80},{88,96},{104,112},{16,8},{3... | collective-permute-start | bytes 3538952 | tf_op jit(solution)/shard_map/ppermute | solution.py:633
  81.7 0.0 collective-permute-done.4.swapped
  81.7 1.5 %near_join.1.refs_6_.near = bf16[2,2,384,384]{3,2,1,0:T(8,128)(2,1)S(1)} custom-call(s32[1]{0:T(128)} %bitcast.place.refs_0_, bf16[2,2,192,384]{3,2,1,0:T(8,128)(2,1)S(1)} %collective-permute-done.4.swapped, bf16[2,2,192,384]{3,2,1,0:T(8,128)(2,1)} %copy-done.2), custom_call_target="tpu_custom_call" | custom-call | bytes 2400000 | tf_op jit(solution)/shard_map/near_join/pallas_call | solution.py:269
  83.2 0.0 copy-start.1
  83.2 3.8 %all-to-all-done.2 = bf16[16,216,128]{2,1,0:T(8,128)(2,1)S(1)} async-done(((bf16[16,216,128]{2,1,0:T(8,128)(2,1)}), bf16[16,216,128]{2,1,0:T(8,128)(2,1)S(1)}, u32[]{:S(2)}, u32[]{:S(2)}) %all-to-all-start.2) | async-done | bytes 884768 | tf_op jit(solution)/shard_map/all_to_all | solution.py:643
  87.0 2.5 %collective-permute-start.3 = (bf16[3456,128]{1,0:T(8,128)(2,1)S(1)}, bf16[3456,128]{1,0:T(8,128)(2,1)S(1)}, u32[]{:S(2)}, u32[]{:S(2)}) collective-permute-start(bf16[3456,128]{1,0:T(8,128)(2,1)S(1)} %bitcast.11), channel_id=1, source_target_pairs={{0,8},{8,0},{1,9},{9,1},{2,10},{10,2},{3,11},{11,3},{4,12},{12,4},... | collective-permute-start | bytes 2654216 | tf_op jit(solution)/shard_map/ppermute | solution.py:647
  89.5 0.0 copy-done.6
  89.5 0.0 copy-done.7
  89.5 13.1 %born_early.1.early = bf16[768,768]{1,0:T(8,128)(2,1)} custom-call(s32[1]{0:T(128)} %bitcast.place.refs_0_, s32[4]{0:T(128)S(1)} %copy-done.5, f32[4]{0:T(128)S(1)} %copy-done.6, s32[1,4]{1,0:T(1,128)S(1)} %copy-done.7, bf16[4,2,384,384]{3,2,1,0:T(8,128)(2,1)} %bitcast.7, bf16[4,2,384,384]{3,2,1,0:T(8,128)(2,1)} %collective-permute-done.2.mate.refs_5_, ...), custom_call_target="tpu_custom_call" | custom-call | flops 7247757312 | bytes 12000000 | tf_op jit(solution)/shard_map/born_early/pallas_call | solution.py:363
  102.6 8.8 %collective-permute-done.5.refs_7_.far = bf16[2,2,384,384]{3,2,1,0:T(8,128)(2,1)S(1)} collective-permute-done((bf16[2,2,384,384]{3,2,1,0:T(8,128)(2,1)}, bf16[2,2,384,384]{3,2,1,0:T(8,128)(2,1)S(1)}, u32[]{:S(2)}, u32[]{:S(2)}) %collective-permute-start.5) | collective-permute-done | bytes 1179680 | tf_op jit(solution)/shard_map/ppermute | solution.py:633
  111.4 0.0 copy-done.1
  111.4 0.0 copy-start.3
  111.4 12.2 %born_late.1.late = bf16[768,768]{1,0:T(8,128)(2,1)S(1)} custom-call(s32[1]{0:T(128)} %bitcast.place.refs_0_, s32[4]{0:T(128)S(1)} %copy-done.5, f32[4]{0:T(128)S(1)} %copy-done.6, s32[1,4]{1,0:T(1,128)S(1)} %copy-done.7, bf16[4,2,384,384]{3,2,1,0:T(8,128)(2,1)} %bitcast.8, bf16[4,2,384,384]{3,2,1,0:T(8,128)(2,1)} %collective-permute-done.2.mate.refs_5_, ...), custom_call_target="tpu_custom_call" | custom-call | flops 7247757312 | bytes 12000000 | tf_op jit(solution)/shard_map/born_late/pallas_call | solution.py:363
  123.6 0.0 copy-done.3
  123.6 0.0 copy-start.4
  123.6 4.3 %final_start.1 = (bf16[12,2,384,384]{3,2,1,0:T(8,128)(2,1)S(1)}, f32[3,384,768]{2,1,0:T(8,128)S(1)}, f32[3,384,768]{2,1,0:T(8,128)S(1)}, bf16[4,768,768]{2,1,0:T(8,128)(2,1)S(1)}) custom-call(s32[1]{0:T(128)} %bitcast.place.refs_0_, s32[4]{0:T(128)S(1)} %copy-done.5, bf16[3456,128]{1,0:T(8,128)(2,1)S(1)} %bitcast.12, bf16[4,2,384,384]{3,2,1,0:T(8,128)(2,1)} %free.1, ...), custom_call_target="tpu_custom_call" | custom-call | flops 1000000000 | bytes 10000000 | tf_op jit(solution)/shard_map/final_start/pallas_call | solution.py:510
  127.9 0.0 collective-permute-done.3.other
  127.9 0.0 copy-done.4
  127.9 7.6 %final.1 = (bf16[4,1,2,384,384]{4,3,2,1,0:T(8,128)(2,1)}, bf16[12,2,384,384]{3,2,1,0:T(8,128)(2,1)S(1)}, f32[3,384,768]{2,1,0:T(8,128)S(1)}) custom-call(s32[1]{0:T(128)} %bitcast.place.refs_0_, s32[4]{0:T(128)S(1)} %copy-done.5, bf16[3456,128]{1,0:T(8,128)(2,1)S(1)} %collective-permute-done.3.other, ...), custom_call_target="tpu_custom_call", output_to_operand_aliasing={{1}: (7, {}), {2}: (8, {})} | custom-call | flops 1000000000 | bytes 18000000 | tf_op jit(solution)/shard_map/final/pallas_call | solution.py:596
Async XLA Ops:
  0.0 9.5 %copy-start = (bf16[4,1,2,384,384]{4,3,2,1,0:T(8,128)(2,1)S(1)}, bf16[4,1,2,384,384]{4,3,2,1,0:T(8,128)(2,1)}, u32[]{:S(2)}) copy-start(bf16[4,1,2,384,384]{4,3,2,1,0:T(8,128)(2,1)} %param.6) | copy-start | bytes 7077892
  0.0 9.5 %copy-start.5 = (s32[4]{0:T(128)S(1)}, s32[4]{0:T(128)}, u32[]{:S(2)}) copy-start(s32[4]{0:T(128)} %offsets.7) | copy-start | bytes 52
  0.0 9.5 %collective-permute-start.2 = (bf16[4,2,384,384]{3,2,1,0:T(8,128)(2,1)}, bf16[4,2,384,384]{3,2,1,0:T(8,128)(2,1)}, u32[]{:S(2)}, u32[]{:S(2)}) collective-permute-start(bf16[4,2,384,384]{3,2,1,0:T(8,128)(2,1)} %bitcast.4), channel_id=1, source_target_pairs={{0,8},{8,0},{1,9},{9,1},{2,10},{10,2},{3,11},{11,3},{4,12},{12,4},... | collective-permute-start | bytes 7077896 | tf_op jit(solution)/shard_map/ppermute | solution.py:631
  2.0 19.5 %collective-permute-start = (bf16[2,2,192,384]{3,2,1,0:T(8,128)(2,1)S(1)}, bf16[2,2,192,384]{3,2,1,0:T(8,128)(2,1)}, u32[]{:S(2)}, u32[]{:S(2)}) collective-permute-start(bf16[2,2,192,384]{3,2,1,0:T(8,128)(2,1)S(1)} %get-tuple-element.15), channel_id=1, source_target_pairs={{8,24},{24,40},{40,56},{56,72},{72,88},{88,104},{104,120},{16,0},{... | collective-permute-start | bytes 1769480 | tf_op jit(solution)/shard_map/ppermute | solution.py:630
  6.7 27.4 %collective-permute-start.1 = (bf16[2,2,192,384]{3,2,1,0:T(8,128)(2,1)S(1)}, bf16[2,2,192,384]{3,2,1,0:T(8,128)(2,1)S(1)}, u32[]{:S(2)}, u32[]{:S(2)}) collective-permute-start(bf16[2,2,192,384]{3,2,1,0:T(8,128)(2,1)S(1)} %get-tuple-element.16), channel_id=1, source_target_pairs={{8,16},{24,32},{40,48},{56,64},{72,80},{88,96},{104,112},{16,8},{3... | collective-permute-start | bytes 1769480 | tf_op jit(solution)/shard_map/ppermute | solution.py:629
  34.1 3.7 %copy-start.2 = (bf16[2,2,192,384]{3,2,1,0:T(8,128)(2,1)}, bf16[2,2,192,384]{3,2,1,0:T(8,128)(2,1)S(1)}, u32[]{:S(2)}) copy-start(bf16[2,2,192,384]{3,2,1,0:T(8,128)(2,1)S(1)} %collective-permute-done.1.cross) | copy-start | bytes 1769476
  69.1 18.0 %all-to-all-start.2 = ((bf16[16,216,128]{2,1,0:T(8,128)(2,1)}), bf16[16,216,128]{2,1,0:T(8,128)(2,1)S(1)}, u32[]{:S(2)}, u32[]{:S(2)}) async-start(bf16[16,216,128]{2,1,0:T(8,128)(2,1)} %row_sum.1), calls=%async_computation.2 | async-start | bytes 1769472 | tf_op jit(solution)/shard_map/all_to_all | solution.py:643
  75.3 14.2 %copy-start.6 = (f32[4]{0:T(128)S(1)}, f32[4]{0:T(128)}, u32[]{:S(2)}) copy-start(f32[4]{0:T(128)} %refs_2_.3) | copy-start | bytes 52
  75.3 14.2 %copy-start.7 = (s32[1,4]{1,0:T(1,128)S(1)}, s32[1,4]{1,0:T(1,128)}, u32[]{:S(2)}) copy-start(s32[1,4]{1,0:T(1,128)} %refs_3_.3) | copy-start | bytes 52
  75.3 6.4 %collective-permute-start.4 = (bf16[2,2,192,384]{3,2,1,0:T(8,128)(2,1)}, bf16[2,2,192,384]{3,2,1,0:T(8,128)(2,1)S(1)}, u32[]{:S(2)}, u32[]{:S(2)}) collective-permute-start(bf16[2,2,192,384]{3,2,1,0:T(8,128)(2,1)} %collective-permute-done.same), channel_id=1, source_target_pairs={{0,8},{8,0},{1,9},{9,1},{2,10},{10,2},{3,11},{11,3},{4,12},{12,4},... | collective-permute-start | bytes 1769480 | tf_op jit(solution)/shard_map/ppermute | solution.py:636
  79.3 32.1 %collective-permute-start.5 = (bf16[2,2,384,384]{3,2,1,0:T(8,128)(2,1)}, bf16[2,2,384,384]{3,2,1,0:T(8,128)(2,1)S(1)}, u32[]{:S(2)}, u32[]{:S(2)}) collective-permute-start(bf16[2,2,384,384]{3,2,1,0:T(8,128)(2,1)} %shard_map.64), channel_id=1, source_target_pairs={{8,16},{24,32},{40,48},{56,64},{72,80},{88,96},{104,112},{16,8},{3... | collective-permute-start | bytes 3538952 | tf_op jit(solution)/shard_map/ppermute | solution.py:633
  83.2 28.2 %copy-start.1 = (bf16[2,2,384,384]{3,2,1,0:T(8,128)(2,1)}, bf16[2,2,384,384]{3,2,1,0:T(8,128)(2,1)S(1)}, u32[]{:S(2)}) copy-start(bf16[2,2,384,384]{3,2,1,0:T(8,128)(2,1)S(1)} %near_join.1.refs_6_.near) | copy-start | bytes 3538948
  87.0 40.9 %collective-permute-start.3 = (bf16[3456,128]{1,0:T(8,128)(2,1)S(1)}, bf16[3456,128]{1,0:T(8,128)(2,1)S(1)}, u32[]{:S(2)}, u32[]{:S(2)}) collective-permute-start(bf16[3456,128]{1,0:T(8,128)(2,1)S(1)} %bitcast.11), channel_id=1, source_target_pairs={{0,8},{8,0},{1,9},{9,1},{2,10},{10,2},{3,11},{11,3},{4,12},{12,4},... | collective-permute-start | bytes 2654216 | tf_op jit(solution)/shard_map/ppermute | solution.py:647
  111.4 12.2 %copy-start.3 = (bf16[2,2,384,384]{3,2,1,0:T(8,128)(2,1)}, bf16[2,2,384,384]{3,2,1,0:T(8,128)(2,1)S(1)}, u32[]{:S(2)}) copy-start(bf16[2,2,384,384]{3,2,1,0:T(8,128)(2,1)S(1)} %collective-permute-done.5.refs_7_.far) | copy-start | bytes 3538948
  123.6 4.3 %copy-start.4 = (bf16[768,768]{1,0:T(8,128)(2,1)S(1)}, bf16[768,768]{1,0:T(8,128)(2,1)}, u32[]{:S(2)}) copy-start(bf16[768,768]{1,0:T(8,128)(2,1)} %born_early.1.early) | copy-start | bytes 3538948

commit v10 on v9

--- a/solution.py
+++ b/solution.py
@@ -28,6 +28,10 @@
     return pltpu.with_memory_space_constraint(array, pltpu.HBM)
 
 
+def in_vmem(array):
+    return pltpu.with_memory_space_constraint(array, pltpu.VMEM)
+
+
 def first_index(offsets, value):
     return jnp.where(
         offsets[0] == value, 0, jnp.where(offsets[1] == value, 1, jnp.where(offsets[2] == value, 2, 3))
@@ -242,7 +246,7 @@
         compiler_params=pltpu.CompilerParams(vmem_limit_bytes=6 << 20),
         cost_estimate=pl.CostEstimate(flops=20_000_000, bytes_accessed=9_000_000, transcendentals=0),
         name="polar",
-    )(place, offsets, same, cross, chip, turned, partial)
+    )(place, offsets, in_vmem(same), in_vmem(cross), chip, turned, partial)
 
 
 def near_body(place, swapped, cross, out, sems):
@@ -282,15 +286,18 @@
     refs = list(refs)
     place, offsets, occupation, coupling, own, mate, near = refs[:7]
     refs = refs[7:]
-    far = None if early else refs.pop(0)
+    fars = () if early else (refs.pop(0), refs.pop(0))
+    side_of = None if early else refs.pop(0)
     vertex, out, chosen, lows, highs, mixed, wide, stack, side, total, rounded, sems = refs
     core = place[0]
     energy = 2 * (1 - core) if early else 2 * core
 
     def fetch(slot, target, sem):
         sources = [(own, 4, 4), (mate, 8 - 8 * core, 4), (near, 2 + 6 * core, 2)]
-        if far is not None:
-            sources.append((far, 10 * core, 2))
+        if fars:
+            crossing = side_of[0] == core
+            sources.append((fars[0], jnp.where(crossing, 10 * core, 16), 2))
+            sources.append((fars[1], jnp.where(crossing, 16, 10 * core), 2))
         for source, low, size in sources:
 
             @pl.when((slot >= low) & (slot < low + size))
@@ -346,25 +353,27 @@
             )
             total[rows, :] += term
 
-    if early:
-        rounded[...] = total[...].astype(BF16)
-        store = pltpu.make_async_copy(rounded, out, sems.at[0, 0])
+    stores = []
+    for piece in range(2):
+        rows = slice(piece * NB, (piece + 1) * NB)
+        rounded[rows, :] = total[rows, :].astype(BF16)
+        store = pltpu.make_async_copy(rounded.at[rows], out.at[rows], sems.at[piece, 0])
         store.start()
+        stores.append(store)
+    for store in stores:
         store.wait()
-    else:
-        out[...] = total[...].astype(BF16)
-
-
-def born_call(place, offsets, occupation, coupling, arrays, vertex):
+
+
+def born_call(place, offsets, occupation, coupling, arrays, vertex, *extra):
     early = len(arrays) == 3
     size = 2 * NB
     held = (*map(in_hbm, arrays[:2]), *arrays[2:])
     shape = (size, size)
     return pl.pallas_call(
         lambda *refs: born_body(early, *refs),
-        out_shape=pltpu.HBM(shape, BF16) if early else jax.ShapeDtypeStruct(shape, BF16),
-        in_specs=[SMEM] * 4 + [ANY] * (len(held) + 1),
-        out_specs=ANY if early else VMEM,
+        out_shape=pltpu.HBM(shape, BF16),
+        in_specs=[SMEM] * 4 + [ANY] * len(arrays) + [SMEM] * len(extra) + [ANY],
+        out_specs=ANY,
         scratch_shapes=[
             pltpu.VMEM((4, 2, NB, NB), BF16),
             pltpu.VMEM((4, 2, 2, NB, NB), BF16),
@@ -382,7 +391,7 @@
             flops=16 * size**3, bytes_accessed=12_000_000, transcendentals=0
         ),
         name="born_early" if early else "born_late",
-    )(place, offsets, occupation, coupling, *held, in_hbm(vertex))
+    )(place, offsets, occupation, coupling, *held, *extra, in_hbm(vertex))
 
 
 def band_total(bands, rows):
@@ -531,16 +540,19 @@
 
 
 def final_body(
-    place, offsets, other, near, far, early, late, slots_in, magnon_in, sums, table,
+    place, side_of, offsets, other, near, far_cross, far_row, early, late, slots_in, magnon_in, sums, table,
     out, slots, magnon, joined, result, sems,
 ):
     core = place[0]
     loads = [
         pltpu.make_async_copy(near, slots.at[pl.ds(2 + 6 * core, 2)], sems.at[5]),
-        pltpu.make_async_copy(far, slots.at[pl.ds(10 * core, 2)], sems.at[6]),
+        pltpu.make_async_copy(far_cross, slots.at[pl.ds(10 * core, 2)], sems.at[6]),
+        pltpu.make_async_copy(far_row, slots.at[pl.ds(10 * core, 2)], sems.at[6]),
     ]
-    for load in loads:
-        load.start()
+    crossing = side_of[0] == core
+    loads[0].start()
+    pl.when(crossing)(loads[1].start)
+    pl.when(jnp.logical_not(crossing))(loads[2].start)
     unpack_half(other, joined)
     roles = offset_roles(offsets)
     _, _, first, last = roles
@@ -559,7 +571,7 @@
             total = sums[role - 1] + transposed(role - 1, role, half, joined, table)
             magnon[role - 1] = total.astype(BF16).astype(F32)
 
-    for load in loads:
+    for load in loads[:2]:
         load.wait()
     reach = spans(offsets, first, last)
     stores = []
@@ -591,7 +603,7 @@
         store.wait()
 
 
-def final_call(place, offsets, other, near, far, early, late, slots, magnon, sums, table):
+def final_call(place, side_of, offsets, other, near, far_cross, far_row, early, late, slots, magnon, sums, table):
     size = 2 * NB
     return pl.pallas_call(
         final_body,
@@ -600,9 +612,9 @@
             jax.ShapeDtypeStruct(slots.shape, BF16),
             jax.ShapeDtypeStruct(magnon.shape, F32),
         ),
-        in_specs=[SMEM, SMEM, VMEM, ANY, ANY] + [VMEM] * 6,
+        in_specs=[SMEM, SMEM, SMEM, VMEM, ANY, ANY, ANY] + [VMEM] * 6,
         out_specs=(ANY, VMEM, VMEM),
-        input_output_aliases={7: 1, 8: 2},
+        input_output_aliases={9: 1, 10: 2},
         scratch_shapes=[
             pltpu.VMEM((3, HALF, size), BF16),
             pltpu.VMEM((4, 2, NB, NB), BF16),
@@ -613,16 +625,19 @@
             flops=1_000_000_000, bytes_accessed=18_000_000, transcendentals=0
         ),
         name="final",
-    )(place, offsets, other, in_hbm(near), in_hbm(far), early, late, slots, magnon, sums, table)[0]
+    )(place, side_of, offsets, other, in_hbm(near), in_hbm(far_cross), in_hbm(far_row), early, late, slots, magnon, sums, table)[0]
 
 
 def per_device(green_blocks, offsets, occupation, coupling, vertex, magnon_free):
     count = lax.axis_size(ENERGY)
     core = lax.axis_index("core").astype(jnp.int32)
     place = core[None]
+    side_of = lax.axis_index("xh").astype(jnp.int32)[None]
     own = green_blocks.reshape(4, 2, NB, NB)
     across = [(i, i + 1) for i in range(1, count - 1, 2)]
     across += [(target, source) for source, target in across]
+    rowwise = [(i, j) for i, j in across if min(i, j) % 4 == 1]
+    crosswise = [(i, j) for i, j in across if min(i, j) % 4 == 3]
     along = [(i, i + 2) for i in range(1, count - 2, 2)]
     along += [(i + 1, i - 1) for i in range(1, count - 2, 2)]
     to_same, to_cross = edge_call(place, own)
@@ -630,7 +645,8 @@
     same = lax.ppermute(to_same, ENERGY, along)
     mate = lax.ppermute(own, "core", SWAP)
     inner = cut_call(place, own, 2, -2)
-    far = lax.ppermute(inner, ENERGY, across)
+    far_cross = lax.ppermute(inner, ENERGY, crosswise)
+    far_row = lax.ppermute(inner, ENERGY, rowwise)
     chip, turned, partial = prepare_call(place, offsets, own, mate)
     pair = polar_call(place, offsets, same, cross, chip, turned, partial)
     swapped = lax.ppermute(same, "core", SWAP)
@@ -642,11 +658,11 @@
     copies = row_call(bands)
     mine = lax.all_to_all(copies, PLANE, 0, 0, tiled=True).reshape(FLAT, 128)
     late = born_call(
-        place, offsets, occupation, coupling, (own, mate, near, far), vertex
+        place, offsets, occupation, coupling, (own, mate, near, far_cross, far_row), vertex, side_of
     )
     other = lax.ppermute(mine, "core", SWAP)
     held = start_call(place, offsets, mine, magnon_free, own, mate)
-    return final_call(place, offsets, other, near, far, early, late, *held)
+    return final_call(place, side_of, offsets, other, near, far_cross, far_row, early, late, *held)
 
 
 def solution(mesh):

time: 136 us -> 138 us (1.015)
  the two profiles are of different devices: /device:TPU:17 before, /device:TPU:24 now
where the time goes in v10:
time: 138 us; the launch traced here: 137 us
  Pallas kernels  56.2 us (41%)
  blocking collectives  31.7 us (23%)
  waiting for transfers between devices  29.8 us (22%)
  starting transfers between devices  17.3 us (13%)
  local copies, waits for them, and re-layouts  1.92 us (1%)
    pallas_call x2, Pallas kernels, born_call(): pl.pallas_call(lambda *refs: born_body(early, *refs), out_shape=pltpu.HBM...  26.8 us
    all_to_all x1, blocking collectives, per_device(): lax.all_to_all(pair.reshape(BANDS, ROWS, 128), PLANE, 0, 0, tiled=True)  21.8 us
    ppermute x1, waiting for transfers between devices, per_device(): cross = lax.ppermute(to_cross, ENERGY, across)  13.1 us
    all_to_all x1, blocking collectives, per_device(): bands = lax.all_to_all(copies, ROW, 0, 0, tiled=True)  9.9 us
    ppermute x1, waiting for transfers between devices, per_device(): far_cross = lax.ppermute(inner, ENERGY, crosswise)  9.34 us
    pallas_call x1, Pallas kernels, final_call(): pl.pallas_call(final_body, out_shape=(jax.ShapeDtypeStruct((4, 1, 2, NB,...  7.57 us
    pallas_call x1, Pallas kernels, prepare_call(): pl.pallas_call(prepare_body, out_shape=(jax.ShapeDtypeStruct((8, 2, NB, N...  7.36 us
    all_to_all x1, starting transfers between devices, per_device(): mine = lax.all_to_all(copies, PLANE, 0, 0, tiled=True).reshape(FLAT, 128)  5.72 us
  transfers between devices with their start and end apart: 8, of which 4 were waited for; matrix products, arithmetic and copies ran while one was open for 0% of the time, Pallas kernels for 32%

profile of v10, /device:TPU:24, one launch (start us, length us, event | category | flops | bytes accessed | tf_op | source)
XLA Modules:
  0.0 137.4 jit_solution(8447944428485051486)
XLA Ops:
  0.0 0.0 copy-start
  0.0 0.0 copy-start.8
  0.0 0.0 collective-permute-start.2
  0.0 1.8 %edge.1 = (bf16[2,2,192,384]{3,2,1,0:T(8,128)(2,1)S(1)}, bf16[2,2,192,384]{3,2,1,0:T(8,128)(2,1)S(1)}) custom-call(s32[1]{0:T(128)} %bitcast.place.refs_0_, bf16[4,2,384,384]{3,2,1,0:T(8,128)(2,1)} %bitcast.6), custom_call_target="tpu_custom_call" | custom-call | bytes 2400000 | tf_op jit(solution)/shard_map/edge/pallas_call | solution.py:101
  1.9 5.1 %collective-permute-start = (bf16[2,2,192,384]{3,2,1,0:T(8,128)(2,1)S(1)}, bf16[2,2,192,384]{3,2,1,0:T(8,128)(2,1)}, u32[]{:S(2)}, u32[]{:S(2)}) collective-permute-start(bf16[2,2,192,384]{3,2,1,0:T(8,128)(2,1)S(1)} %get-tuple-element.15), channel_id=1, source_target_pairs={{8,24},{24,40},{40,56},{56,72},{72,88},{88,104},{104,120},{16,0},{... | collective-permute-start | bytes 1769480 | tf_op jit(solution)/shard_map/ppermute | solution.py:645
  7.0 2.4 %collective-permute-start.1 = (bf16[2,2,192,384]{3,2,1,0:T(8,128)(2,1)S(1)}, bf16[2,2,192,384]{3,2,1,0:T(8,128)(2,1)S(1)}, u32[]{:S(2)}, u32[]{:S(2)}) collective-permute-start(bf16[2,2,192,384]{3,2,1,0:T(8,128)(2,1)S(1)} %get-tuple-element.16), channel_id=1, source_target_pairs={{8,16},{24,32},{40,48},{56,64},{72,80},{88,96},{104,112},{16,8},{3... | collective-permute-start | bytes 1769480 | tf_op jit(solution)/shard_map/ppermute | solution.py:644
  9.4 0.0 collective-permute-done.2.mate.refs_5_
  9.4 0.0 copy-done
  9.4 0.0 copy-done.8
  9.4 7.4 %prepare.1 = (bf16[8,2,384,384]{3,2,1,0:T(8,128)(2,1)S(1)}, f32[8,2,384,384]{3,2,1,0:T(8,128)S(1)}, f32[3,2,192,384]{3,2,1,0:T(8,128)S(1)}) custom-call(s32[1]{0:T(128)} %bitcast.place.refs_0_, s32[4]{0:T(128)S(1)} %copy-done.8, bf16[4,2,384,384]{3,2,1,0:T(8,128)(2,1)S(1)} %bitcast.11, bf16[4,2,384,384]{3,2,1,0:T(8,128)(2,1)} %collective-permute-done.2.mate.refs_5_), custom_call_target="tpu_custom_call" | custom-call | flops 20000000 | bytes 9000000 | tf_op jit(solution)/shard_map/prepare/pallas_call | solution.py:151
  16.8 3.9 %collective-permute-done.same = bf16[2,2,192,384]{3,2,1,0:T(8,128)(2,1)} collective-permute-done((bf16[2,2,192,384]{3,2,1,0:T(8,128)(2,1)S(1)}, bf16[2,2,192,384]{3,2,1,0:T(8,128)(2,1)}, u32[]{:S(2)}, u32[]{:S(2)}) %collective-permute-start) | collective-permute-done | bytes 589856 | tf_op jit(solution)/shard_map/ppermute | solution.py:645
  20.7 13.1 %collective-permute-done.1.cross = bf16[2,2,192,384]{3,2,1,0:T(8,128)(2,1)S(1)} collective-permute-done((bf16[2,2,192,384]{3,2,1,0:T(8,128)(2,1)S(1)}, bf16[2,2,192,384]{3,2,1,0:T(8,128)(2,1)S(1)}, u32[]{:S(2)}, u32[]{:S(2)}) %collective-permute-start.1) | collective-permute-done | bytes 589856 | tf_op jit(solution)/shard_map/ppermute | solution.py:644
  33.7 3.7 %polar.1 = bf16[3456,128]{1,0:T(8,128)(2,1)} custom-call(s32[1]{0:T(128)} %bitcast.place.refs_0_, s32[4]{0:T(128)S(1)} %copy-done.8, bf16[2,2,192,384]{3,2,1,0:T(8,128)(2,1)} %collective-permute-done.same, bf16[2,2,192,384]{3,2,1,0:T(8,128)(2,1)S(1)} %collective-permute-done.1.cross, bf16[8,2,384,384]{3,2,1,0:T(8,128)(2,1)S(1)} %get-tuple-element.17.chip, ...), custom_call_target="tpu_custom_call" | custom-call | flops 20000000 | bytes 9000000 | tf_op jit(solution)/shard_map/polar/pallas_call | solution.py:237
  37.4 0.0 copy-done.2
  37.4 21.8 %all_to_all.15.bands = bf16[16,216,128]{2,1,0:T(8,128)(2,1)S(1)} all-to-all(bf16[16,216,128]{2,1,0:T(8,128)(2,1)} %bitcast.14), channel_id=1, replica_groups=mesh['y'=4,'xh'=2,'core'=2,'xl'=2,'z'=4] {'y','z'}, dimensions={0} | all-to-all | bytes 1769472 | tf_op jit(solution)/shard_map/all_to_all | solution.py:654
  59.2 0.1 plane_sum.1
  59.3 9.9 %all_to_all.16.bands = bf16[4,216,128]{2,1,0:T(8,128)(2,1)S(1)} all-to-all(bf16[4,216,128]{2,1,0:T(8,128)(2,1)S(1)} %plane_sum.1), channel_id=1, replica_groups=mesh['y'=4,'xh'=2,'core'=2,'xl'=2,'z'=4] {'xh','xl'}, dimensions={0} | all-to-all | bytes 442368 | tf_op jit(solution)/shard_map/all_to_all | solution.py:657
  69.3 1.1 row_sum.1
  70.4 5.7 %all-to-all-start.2 = ((bf16[16,216,128]{2,1,0:T(8,128)(2,1)}), bf16[16,216,128]{2,1,0:T(8,128)(2,1)S(1)}, u32[]{:S(2)}, u32[]{:S(2)}) async-start(bf16[16,216,128]{2,1,0:T(8,128)(2,1)} %row_sum.1), calls=%async_computation.2 | async-start | bytes 1769472 | tf_op jit(solution)/shard_map/all_to_all | solution.py:659
  76.1 0.0 copy-start.10
  76.1 0.1 collective-permute-start.4
  76.2 2.3 %shard_map.64 = bf16[2,2,384,384]{3,2,1,0:T(8,128)(2,1)} custom-call(s32[1]{0:T(128)} %bitcast.place.refs_0_, bf16[4,2,384,384]{3,2,1,0:T(8,128)(2,1)} %bitcast.7), custom_call_target="tpu_custom_call" | custom-call | bytes 2400000 | tf_op jit(solution)/shard_map/pallas_call | solution.py:62
  78.5 0.7 collective-permute-start.6
  79.3 3.2 %collective-permute-start.5 = (bf16[2,2,384,384]{3,2,1,0:T(8,128)(2,1)}, bf16[2,2,384,384]{3,2,1,0:T(8,128)(2,1)}, u32[]{:S(2)}, u32[]{:S(2)}) collective-permute-start(bf16[2,2,384,384]{3,2,1,0:T(8,128)(2,1)} %shard_map.64), channel_id=1, source_target_pairs={{24,32},{56,64},{88,96},{32,24},{64,56},{96,88},{25,33},{57,65},{8... | collective-permute-start | bytes 3538952 | tf_op jit(solution)/shard_map/ppermute | solution.py:648
  82.5 0.0 collective-permute-done.4.swapped
  82.5 0.0 copy-start.6
  82.5 0.8 copy-done.6
  83.3 1.1 copy-done.7
  84.4 1.1 near_join.1.refs_6_.near
  85.5 0.0 copy-start.1
  85.5 3.6 %all-to-all-done.2 = bf16[16,216,128]{2,1,0:T(8,128)(2,1)S(1)} async-done(((bf16[16,216,128]{2,1,0:T(8,128)(2,1)}), bf16[16,216,128]{2,1,0:T(8,128)(2,1)S(1)}, u32[]{:S(2)}, u32[]{:S(2)}) %all-to-all-start.2) | async-done | bytes 884768 | tf_op jit(solution)/shard_map/all_to_all | solution.py:659
  89.1 0.0 collective-permute-start.3
  89.1 0.0 copy-done.9
  89.1 0.0 copy-done.10
  89.1 13.0 %born_early.1.early = bf16[768,768]{1,0:T(8,128)(2,1)} custom-call(s32[1]{0:T(128)} %bitcast.place.refs_0_, s32[4]{0:T(128)S(1)} %copy-done.8, f32[4]{0:T(128)S(1)} %copy-done.9, s32[1,4]{1,0:T(1,128)S(1)} %copy-done.10, bf16[4,2,384,384]{3,2,1,0:T(8,128)(2,1)} %bitcast.8, bf16[4,2,384,384]{3,2,1,0:T(8,128)(2,1)} %collective-permute-done.2.mate.refs_5_, ...), custom_call_target="tpu_custom_call" | custom-call | flops 7247757312 | bytes 12000000 | tf_op jit(solution)/shard_map/born_early/pallas_call | solution.py:372
  102.1 0.0 collective-permute-done.6.refs_8_.far_row
  102.1 0.0 copy-start.3
  102.1 9.3 %collective-permute-done.5.refs_7_.far_cross = bf16[2,2,384,384]{3,2,1,0:T(8,128)(2,1)} collective-permute-done((bf16[2,2,384,384]{3,2,1,0:T(8,128)(2,1)}, bf16[2,2,384,384]{3,2,1,0:T(8,128)(2,1)}, u32[]{:S(2)}, u32[]{:S(2)}) %collective-permute-start.5) | collective-permute-done | bytes 1179680 | tf_op jit(solution)/shard_map/ppermute | solution.py:648
  111.5 0.0 copy-done.1
  111.5 13.8 %born_late.1.late = bf16[768,768]{1,0:T(8,128)(2,1)} custom-call(s32[1]{0:T(128)} %bitcast.place.refs_0_, s32[4]{0:T(128)S(1)} %copy-done.8, f32[4]{0:T(128)S(1)} %copy-done.9, s32[1,4]{1,0:T(1,128)S(1)} %copy-done.10, bf16[4,2,384,384]{3,2,1,0:T(8,128)(2,1)} %bitcast.9, bf16[4,2,384,384]{3,2,1,0:T(8,128)(2,1)} %collective-permute-done.2.mate.refs_5_, ...), custom_call_target="tpu_custom_call" | custom-call | flops 7247757312 | bytes 12000000 | tf_op jit(solution)/shard_map/born_late/pallas_call | solution.py:372
  125.2 0.0 copy-done.3
  125.2 0.0 copy-start.4
  125.2 0.0 copy-start.5
  125.3 4.4 %final_start.1 = (bf16[12,2,384,384]{3,2,1,0:T(8,128)(2,1)S(1)}, f32[3,384,768]{2,1,0:T(8,128)S(1)}, f32[3,384,768]{2,1,0:T(8,128)S(1)}, bf16[4,768,768]{2,1,0:T(8,128)(2,1)S(1)}) custom-call(s32[1]{0:T(128)} %bitcast.place.refs_0_, s32[4]{0:T(128)S(1)} %copy-done.8, bf16[3456,128]{1,0:T(8,128)(2,1)S(1)} %bitcast.13, bf16[4,2,384,384]{3,2,1,0:T(8,128)(2,1)} %free.1, ...), custom_call_target="tpu_custom_call" | custom-call | flops 1000000000 | bytes 10000000 | tf_op jit(solution)/shard_map/final_start/pallas_call | solution.py:519
  129.7 0.0 collective-permute-done.3.other
  129.7 0.0 copy-done.4
  129.7 0.0 copy-done.5
  129.7 7.6 %final.1 = (bf16[4,1,2,384,384]{4,3,2,1,0:T(8,128)(2,1)}, bf16[12,2,384,384]{3,2,1,0:T(8,128)(2,1)S(1)}, f32[3,384,768]{2,1,0:T(8,128)S(1)}) custom-call(s32[1]{0:T(128)} %bitcast.place.refs_0_, s32[1]{0:T(128)} %bitcast.1.refs_9_.side_of, s32[4]{0:T(128)S(1)} %copy-done.8, ...), custom_call_target="tpu_custom_call", output_to_operand_aliasing={{1}: (9, {}), {2}: (10, {})} | custom-call | flops 1000000000 | bytes 18000000 | tf_op jit(solution)/shard_map/final/pallas_call | solution.py:608
  (3 shorter events, 0.0 us)
Async XLA Ops:
  0.0 9.4 %copy-start = (bf16[4,1,2,384,384]{4,3,2,1,0:T(8,128)(2,1)S(1)}, bf16[4,1,2,384,384]{4,3,2,1,0:T(8,128)(2,1)}, u32[]{:S(2)}) copy-start(bf16[4,1,2,384,384]{4,3,2,1,0:T(8,128)(2,1)} %param.6) | copy-start | bytes 7077892
  0.0 9.4 %copy-start.8 = (s32[4]{0:T(128)S(1)}, s32[4]{0:T(128)}, u32[]{:S(2)}) copy-start(s32[4]{0:T(128)} %offsets.7) | copy-start | bytes 52
  0.0 9.4 %collective-permute-start.2 = (bf16[4,2,384,384]{3,2,1,0:T(8,128)(2,1)}, bf16[4,2,384,384]{3,2,1,0:T(8,128)(2,1)}, u32[]{:S(2)}, u32[]{:S(2)}) collective-permute-start(bf16[4,2,384,384]{3,2,1,0:T(8,128)(2,1)} %bitcast.5), channel_id=1, source_target_pairs={{0,8},{8,0},{1,9},{9,1},{2,10},{10,2},{3,11},{11,3},{4,12},{12,4},... | collective-permute-start | bytes 7077896 | tf_op jit(solution)/shard_map/ppermute | solution.py:646
  1.9 18.8 %collective-permute-start = (bf16[2,2,192,384]{3,2,1,0:T(8,128)(2,1)S(1)}, bf16[2,2,192,384]{3,2,1,0:T(8,128)(2,1)}, u32[]{:S(2)}, u32[]{:S(2)}) collective-permute-start(bf16[2,2,192,384]{3,2,1,0:T(8,128)(2,1)S(1)} %get-tuple-element.15), channel_id=1, source_target_pairs={{8,24},{24,40},{40,56},{56,72},{72,88},{88,104},{104,120},{16,0},{... | collective-permute-start | bytes 1769480 | tf_op jit(solution)/shard_map/ppermute | solution.py:645
  7.0 26.8 %collective-permute-start.1 = (bf16[2,2,192,384]{3,2,1,0:T(8,128)(2,1)S(1)}, bf16[2,2,192,384]{3,2,1,0:T(8,128)(2,1)S(1)}, u32[]{:S(2)}, u32[]{:S(2)}) collective-permute-start(bf16[2,2,192,384]{3,2,1,0:T(8,128)(2,1)S(1)} %get-tuple-element.16), channel_id=1, source_target_pairs={{8,16},{24,32},{40,48},{56,64},{72,80},{88,96},{104,112},{16,8},{3... | collective-permute-start | bytes 1769480 | tf_op jit(solution)/shard_map/ppermute | solution.py:644
  33.7 3.7 %copy-start.2 = (bf16[2,2,192,384]{3,2,1,0:T(8,128)(2,1)}, bf16[2,2,192,384]{3,2,1,0:T(8,128)(2,1)S(1)}, u32[]{:S(2)}) copy-start(bf16[2,2,192,384]{3,2,1,0:T(8,128)(2,1)S(1)} %collective-permute-done.1.cross) | copy-start | bytes 1769476
  70.4 18.7 %all-to-all-start.2 = ((bf16[16,216,128]{2,1,0:T(8,128)(2,1)}), bf16[16,216,128]{2,1,0:T(8,128)(2,1)S(1)}, u32[]{:S(2)}, u32[]{:S(2)}) async-start(bf16[16,216,128]{2,1,0:T(8,128)(2,1)} %row_sum.1), calls=%async_computation.2 | async-start | bytes 1769472 | tf_op jit(solution)/shard_map/all_to_all | solution.py:659
  76.1 13.0 %copy-start.9 = (f32[4]{0:T(128)S(1)}, f32[4]{0:T(128)}, u32[]{:S(2)}) copy-start(f32[4]{0:T(128)} %refs_2_.3) | copy-start | bytes 52
  76.1 13.0 %copy-start.10 = (s32[1,4]{1,0:T(1,128)S(1)}, s32[1,4]{1,0:T(1,128)}, u32[]{:S(2)}) copy-start(s32[1,4]{1,0:T(1,128)} %refs_3_.3) | copy-start | bytes 52
  76.1 6.4 %collective-permute-start.4 = (bf16[2,2,192,384]{3,2,1,0:T(8,128)(2,1)}, bf16[2,2,192,384]{3,2,1,0:T(8,128)(2,1)S(1)}, u32[]{:S(2)}, u32[]{:S(2)}) collective-permute-start(bf16[2,2,192,384]{3,2,1,0:T(8,128)(2,1)} %collective-permute-done.same), channel_id=1, source_target_pairs={{0,8},{8,0},{1,9},{9,1},{2,10},{10,2},{3,11},{11,3},{4,12},{12,4},... | collective-permute-start | bytes 1769480 | tf_op jit(solution)/shard_map/ppermute | solution.py:652
  78.5 23.6 %collective-permute-start.6 = (bf16[2,2,384,384]{3,2,1,0:T(8,128)(2,1)}, bf16[2,2,384,384]{3,2,1,0:T(8,128)(2,1)S(1)}, u32[]{:S(2)}, u32[]{:S(2)}) collective-permute-start(bf16[2,2,384,384]{3,2,1,0:T(8,128)(2,1)} %shard_map.64), channel_id=1, source_target_pairs={{8,16},{40,48},{72,80},{104,112},{16,8},{48,40},{80,72},{112,104},... | collective-permute-start | bytes 3538952 | tf_op jit(solution)/shard_map/ppermute | solution.py:649
  79.3 32.2 %collective-permute-start.5 = (bf16[2,2,384,384]{3,2,1,0:T(8,128)(2,1)}, bf16[2,2,384,384]{3,2,1,0:T(8,128)(2,1)}, u32[]{:S(2)}, u32[]{:S(2)}) collective-permute-start(bf16[2,2,384,384]{3,2,1,0:T(8,128)(2,1)} %shard_map.64), channel_id=1, source_target_pairs={{24,32},{56,64},{88,96},{32,24},{64,56},{96,88},{25,33},{57,65},{8... | collective-permute-start | bytes 3538952 | tf_op jit(solution)/shard_map/ppermute | solution.py:648
  82.5 0.8 copy-start.6
  83.3 1.1 copy-start.7
  85.5 26.0 %copy-start.1 = (bf16[2,2,384,384]{3,2,1,0:T(8,128)(2,1)}, bf16[2,2,384,384]{3,2,1,0:T(8,128)(2,1)S(1)}, u32[]{:S(2)}) copy-start(bf16[2,2,384,384]{3,2,1,0:T(8,128)(2,1)S(1)} %near_join.1.refs_6_.near) | copy-start | bytes 3538948
  89.1 40.6 %collective-permute-start.3 = (bf16[3456,128]{1,0:T(8,128)(2,1)S(1)}, bf16[3456,128]{1,0:T(8,128)(2,1)S(1)}, u32[]{:S(2)}, u32[]{:S(2)}) collective-permute-start(bf16[3456,128]{1,0:T(8,128)(2,1)S(1)} %bitcast.12), channel_id=1, source_target_pairs={{0,8},{8,0},{1,9},{9,1},{2,10},{10,2},{3,11},{11,3},{4,12},{12,4},... | collective-permute-start | bytes 2654216 | tf_op jit(solution)/shard_map/ppermute | solution.py:663
  102.1 23.1 %copy-start.3 = (bf16[2,2,384,384]{3,2,1,0:T(8,128)(2,1)}, bf16[2,2,384,384]{3,2,1,0:T(8,128)(2,1)S(1)}, u32[]{:S(2)}) copy-start(bf16[2,2,384,384]{3,2,1,0:T(8,128)(2,1)S(1)} %collective-permute-done.6.refs_8_.far_row) | copy-start | bytes 3538948
  125.2 4.5 %copy-start.4 = (bf16[768,768]{1,0:T(8,128)(2,1)S(1)}, bf16[768,768]{1,0:T(8,128)(2,1)}, u32[]{:S(2)}) copy-start(bf16[768,768]{1,0:T(8,128)(2,1)} %born_early.1.early) | copy-start | bytes 3538948
  125.2 4.5 %copy-start.5 = (bf16[768,768]{1,0:T(8,128)(2,1)S(1)}, bf16[768,768]{1,0:T(8,128)(2,1)}, u32[]{:S(2)}) copy-start(bf16[768,768]{1,0:T(8,128)(2,1)} %born_late.1.late) | copy-start | bytes 3538948

commit v11 on v10

--- a/solution.py
+++ b/solution.py
@@ -53,15 +53,15 @@
 
 
 def cut_body(place, base, sign, own, out, sem):
-    copy = pltpu.make_async_copy(own.at[pl.ds(base + sign * place[0], 2)], out, sem)
+    copy = pltpu.make_async_copy(own.at[pl.ds(base + sign * place[0], out.shape[0])], out, sem)
     copy.start()
     copy.wait()
 
 
-def cut_call(place, own, base, sign):
+def cut_call(place, own, base, sign, size):
     return pl.pallas_call(
         lambda place, own, out, sem: cut_body(place, base, sign, own, out, sem),
-        out_shape=jax.ShapeDtypeStruct((2, 2, NB, NB), BF16),
+        out_shape=jax.ShapeDtypeStruct((size, 2, NB, NB), BF16),
         in_specs=[SMEM, ANY],
         out_specs=VMEM,
         scratch_shapes=[pltpu.SemaphoreType.DMA],
@@ -286,7 +286,7 @@
     refs = list(refs)
     place, offsets, occupation, coupling, own, mate, near = refs[:7]
     refs = refs[7:]
-    fars = () if early else (refs.pop(0), refs.pop(0))
+    fars = () if early else (refs.pop(0), refs.pop(0), refs.pop(0))
     side_of = None if early else refs.pop(0)
     vertex, out, chosen, lows, highs, mixed, wide, stack, side, total, rounded, sems = refs
     core = place[0]
@@ -297,7 +297,8 @@
         if fars:
             crossing = side_of[0] == core
             sources.append((fars[0], jnp.where(crossing, 10 * core, 16), 2))
-            sources.append((fars[1], jnp.where(crossing, 16, 10 * core), 2))
+            sources.append((fars[1], jnp.where(crossing, 16, 10 * core), 1))
+            sources.append((fars[2], jnp.where(crossing, 16, 10 * core + 1), 1))
         for source, low, size in sources:
 
             @pl.when((slot >= low) & (slot < low + size))
@@ -540,19 +541,21 @@
 
 
 def final_body(
-    place, side_of, offsets, other, near, far_cross, far_row, early, late, slots_in, magnon_in, sums, table,
+    place, side_of, offsets, other, near, far_cross, far_soon, far_late, early, late, slots_in, magnon_in, sums, table,
     out, slots, magnon, joined, result, sems,
 ):
     core = place[0]
     loads = [
         pltpu.make_async_copy(near, slots.at[pl.ds(2 + 6 * core, 2)], sems.at[5]),
         pltpu.make_async_copy(far_cross, slots.at[pl.ds(10 * core, 2)], sems.at[6]),
-        pltpu.make_async_copy(far_row, slots.at[pl.ds(10 * core, 2)], sems.at[6]),
+        pltpu.make_async_copy(far_soon, slots.at[pl.ds(10 * core, 1)], sems.at[6]),
+        pltpu.make_async_copy(far_late, slots.at[pl.ds(10 * core + 1, 1)], sems.at[6]),
     ]
     crossing = side_of[0] == core
     loads[0].start()
     pl.when(crossing)(loads[1].start)
     pl.when(jnp.logical_not(crossing))(loads[2].start)
+    pl.when(jnp.logical_not(crossing))(loads[3].start)
     unpack_half(other, joined)
     roles = offset_roles(offsets)
     _, _, first, last = roles
@@ -603,7 +606,7 @@
         store.wait()
 
 
-def final_call(place, side_of, offsets, other, near, far_cross, far_row, early, late, slots, magnon, sums, table):
+def final_call(place, side_of, offsets, other, near, far_cross, far_soon, far_late, early, late, slots, magnon, sums, table):
     size = 2 * NB
     return pl.pallas_call(
         final_body,
@@ -612,9 +615,9 @@
             jax.ShapeDtypeStruct(slots.shape, BF16),
             jax.ShapeDtypeStruct(magnon.shape, F32),
         ),
-        in_specs=[SMEM, SMEM, SMEM, VMEM, ANY, ANY, ANY] + [VMEM] * 6,
+        in_specs=[SMEM, SMEM, SMEM, VMEM, ANY, ANY, ANY, ANY] + [VMEM] * 6,
         out_specs=(ANY, VMEM, VMEM),
-        input_output_aliases={9: 1, 10: 2},
+        input_output_aliases={10: 1, 11: 2},
         scratch_shapes=[
             pltpu.VMEM((3, HALF, size), BF16),
             pltpu.VMEM((4, 2, NB, NB), BF16),
@@ -625,7 +628,7 @@
             flops=1_000_000_000, bytes_accessed=18_000_000, transcendentals=0
         ),
         name="final",
-    )(place, side_of, offsets, other, in_hbm(near), in_hbm(far_cross), in_hbm(far_row), early, late, slots, magnon, sums, table)[0]
+    )(place, side_of, offsets, other, in_hbm(near), in_hbm(far_cross), in_hbm(far_soon), in_hbm(far_late), early, late, slots, magnon, sums, table)[0]
 
 
 def per_device(green_blocks, offsets, occupation, coupling, vertex, magnon_free):
@@ -644,9 +647,12 @@
     cross = lax.ppermute(to_cross, ENERGY, across)
     same = lax.ppermute(to_same, ENERGY, along)
     mate = lax.ppermute(own, "core", SWAP)
-    inner = cut_call(place, own, 2, -2)
+    inner = cut_call(place, own, 2, -2, 2)
+    inner_soon = cut_call(place, own, 2, -2, 1)
+    inner_late = cut_call(place, own, 3, -2, 1)
     far_cross = lax.ppermute(inner, ENERGY, crosswise)
-    far_row = lax.ppermute(inner, ENERGY, rowwise)
+    far_soon = lax.ppermute(inner_soon, ENERGY, rowwise)
+    far_late = lax.ppermute(inner_late, ENERGY, rowwise)
     chip, turned, partial = prepare_call(place, offsets, own, mate)
     pair = polar_call(place, offsets, same, cross, chip, turned, partial)
     swapped = lax.ppermute(same, "core", SWAP)
@@ -658,11 +664,13 @@
     copies = row_call(bands)
     mine = lax.all_to_all(copies, PLANE, 0, 0, tiled=True).reshape(FLAT, 128)
     late = born_call(
-        place, offsets, occupation, coupling, (own, mate, near, far_cross, far_row), vertex, side_of
+        place, offsets, occupation, coupling, (own, mate, near, far_cross, far_soon, far_late), vertex, side_of
     )
     other = lax.ppermute(mine, "core", SWAP)
     held = start_call(place, offsets, mine, magnon_free, own, mate)
-    return final_call(place, side_of, offsets, other, near, far_cross, far_row, early, late, *held)
+    return final_call(
+        place, side_of, offsets, other, near, far_cross, far_soon, far_late, early, late, *held
+    )
 
 
 def solution(mesh):

time: 138 us -> 139 us (level)
  the two profiles are of different devices: /device:TPU:24 before, /device:TPU:1 now
where the time goes in v11:
time: 139 us; the launch traced here: 138 us
  Pallas kernels  59.9 us (43%)
  blocking collectives  33 us (24%)
  starting transfers between devices  21.8 us (16%)
  waiting for transfers between devices  21.4 us (15%)
  local copies, waits for them, and re-layouts  1.92 us (1%)
    pallas_call x2, Pallas kernels, born_call(): pl.pallas_call(lambda *refs: born_body(early, *refs), out_shape=pltpu.HBM...  26.8 us
    all_to_all x1, blocking collectives, per_device(): lax.all_to_all(pair.reshape(BANDS, ROWS, 128), PLANE, 0, 0, tiled=True)  21.9 us
    ppermute x1, waiting for transfers between devices, per_device(): cross = lax.ppermute(to_cross, ENERGY, across)  17 us
    all_to_all x1, blocking collectives, per_device(): bands = lax.all_to_all(copies, ROW, 0, 0, tiled=True)  11.1 us
    pallas_call x1, Pallas kernels, final_call(): pl.pallas_call(final_body, out_shape=(jax.ShapeDtypeStruct((4, 1, 2, NB,...  7.59 us
    pallas_call x1, Pallas kernels, prepare_call(): pl.pallas_call(prepare_body, out_shape=(jax.ShapeDtypeStruct((8, 2, NB, N...  7.36 us
    pallas_call x3, Pallas kernels, cut_call(): pl.pallas_call(lambda place, own, out, sem: cut_body(place, base, sign, o...  6.11 us
    ppermute x1, starting transfers between devices, per_device(): same = lax.ppermute(to_same, ENERGY, along)  5.64 us
  transfers between devices with their start and end apart: 9, of which 2 were waited for; matrix products, arithmetic and copies ran while one was open for 0% of the time, Pallas kernels for 34%

profile of v11, /device:TPU:1, one launch (start us, length us, event | category | flops | bytes accessed | tf_op | source)
XLA Modules:
  0.0 138.4 jit_solution(8299285992700678695)
XLA Ops:
  0.0 1.4 collective-permute-start.2
  1.4 1.3 edge.1
  2.7 5.6 %collective-permute-start = (bf16[2,2,192,384]{3,2,1,0:T(8,128)(2,1)S(1)}, bf16[2,2,192,384]{3,2,1,0:T(8,128)(2,1)}, u32[]{:S(2)}, u32[]{:S(2)}) collective-permute-start(bf16[2,2,192,384]{3,2,1,0:T(8,128)(2,1)S(1)} %get-tuple-element.15), channel_id=1, source_target_pairs={{8,24},{24,40},{40,56},{56,72},{72,88},{88,104},{104,120},{16,0},{... | collective-permute-start | bytes 1769480 | tf_op jit(solution)/shard_map/ppermute | solution.py:648
  8.3 1.9 %collective-permute-start.1 = (bf16[2,2,192,384]{3,2,1,0:T(8,128)(2,1)S(1)}, bf16[2,2,192,384]{3,2,1,0:T(8,128)(2,1)S(1)}, u32[]{:S(2)}, u32[]{:S(2)}) collective-permute-start(bf16[2,2,192,384]{3,2,1,0:T(8,128)(2,1)S(1)} %get-tuple-element.16), channel_id=1, source_target_pairs={{8,16},{24,32},{40,48},{56,64},{72,80},{88,96},{104,112},{16,8},{3... | collective-permute-start | bytes 1769480 | tf_op jit(solution)/shard_map/ppermute | solution.py:647
  10.2 0.0 collective-permute-done.2.mate.refs_5_
  10.2 0.0 copy-done
  10.2 0.0 copy-done.8
  10.2 7.4 %prepare.1 = (bf16[8,2,384,384]{3,2,1,0:T(8,128)(2,1)S(1)}, f32[8,2,384,384]{3,2,1,0:T(8,128)S(1)}, f32[3,2,192,384]{3,2,1,0:T(8,128)S(1)}) custom-call(s32[1]{0:T(128)} %bitcast.place.refs_0_, s32[4]{0:T(128)S(1)} %copy-done.8, bf16[4,2,384,384]{3,2,1,0:T(8,128)(2,1)S(1)} %bitcast.13, bf16[4,2,384,384]{3,2,1,0:T(8,128)(2,1)} %collective-permute-done.2.mate.refs_5_), custom_call_target="tpu_custom_call" | custom-call | flops 20000000 | bytes 9000000 | tf_op jit(solution)/shard_map/prepare/pallas_call | solution.py:151
  17.6 0.0 collective-permute-done.same
  17.6 17.0 %collective-permute-done.1.cross = bf16[2,2,192,384]{3,2,1,0:T(8,128)(2,1)S(1)} collective-permute-done((bf16[2,2,192,384]{3,2,1,0:T(8,128)(2,1)S(1)}, bf16[2,2,192,384]{3,2,1,0:T(8,128)(2,1)S(1)}, u32[]{:S(2)}, u32[]{:S(2)}) %collective-permute-start.1) | collective-permute-done | bytes 589856 | tf_op jit(solution)/shard_map/ppermute | solution.py:647
  34.6 3.7 %polar.1 = bf16[3456,128]{1,0:T(8,128)(2,1)} custom-call(s32[1]{0:T(128)} %bitcast.place.refs_0_, s32[4]{0:T(128)S(1)} %copy-done.8, bf16[2,2,192,384]{3,2,1,0:T(8,128)(2,1)} %collective-permute-done.same, bf16[2,2,192,384]{3,2,1,0:T(8,128)(2,1)S(1)} %collective-permute-done.1.cross, bf16[8,2,384,384]{3,2,1,0:T(8,128)(2,1)S(1)} %get-tuple-element.17.chip, ...), custom_call_target="tpu_custom_call" | custom-call | flops 20000000 | bytes 9000000 | tf_op jit(solution)/shard_map/polar/pallas_call | solution.py:237
  38.3 0.0 copy-done.2
  38.3 21.9 %all_to_all.15.bands = bf16[16,216,128]{2,1,0:T(8,128)(2,1)S(1)} all-to-all(bf16[16,216,128]{2,1,0:T(8,128)(2,1)} %bitcast.16), channel_id=1, replica_groups=mesh['y'=4,'xh'=2,'core'=2,'xl'=2,'z'=4] {'y','z'}, dimensions={0} | all-to-all | bytes 1769472 | tf_op jit(solution)/shard_map/all_to_all | solution.py:660
  60.2 0.1 plane_sum.1
  60.4 11.1 %all_to_all.16.bands = bf16[4,216,128]{2,1,0:T(8,128)(2,1)S(1)} all-to-all(bf16[4,216,128]{2,1,0:T(8,128)(2,1)S(1)} %plane_sum.1), channel_id=1, replica_groups=mesh['y'=4,'xh'=2,'core'=2,'xl'=2,'z'=4] {'xh','xl'}, dimensions={0} | all-to-all | bytes 442368 | tf_op jit(solution)/shard_map/all_to_all | solution.py:663
  71.5 1.1 row_sum.1
  72.6 3.6 %all-to-all-start.2 = ((bf16[16,216,128]{2,1,0:T(8,128)(2,1)}), bf16[16,216,128]{2,1,0:T(8,128)(2,1)S(1)}, u32[]{:S(2)}, u32[]{:S(2)}) async-start(bf16[16,216,128]{2,1,0:T(8,128)(2,1)} %row_sum.1), calls=%async_computation.2 | async-start | bytes 1769472 | tf_op jit(solution)/shard_map/all_to_all | solution.py:665
  76.2 1.3 collective-permute-start.4
  77.5 2.3 %shard_map.64 = bf16[2,2,384,384]{3,2,1,0:T(8,128)(2,1)} custom-call(s32[1]{0:T(128)} %bitcast.place.refs_0_, bf16[4,2,384,384]{3,2,1,0:T(8,128)(2,1)} %bitcast.7), custom_call_target="tpu_custom_call" | custom-call | bytes 2400000 | tf_op jit(solution)/shard_map/pallas_call | solution.py:62
  79.8 0.7 collective-permute-start.5
  80.6 1.9 %shard_map.65 = bf16[1,2,384,384]{3,2,1,0:T(8,128)(2,1)} custom-call(s32[1]{0:T(128)} %bitcast.place.refs_0_, bf16[4,2,384,384]{3,2,1,0:T(8,128)(2,1)} %bitcast.8), custom_call_target="tpu_custom_call" | custom-call | bytes 2400000 | tf_op jit(solution)/shard_map/pallas_call | solution.py:62
  82.5 0.0 copy-start.9
  82.5 0.0 copy-start.10
  82.5 2.5 %collective-permute-start.6 = (bf16[1,2,384,384]{3,2,1,0:T(8,128)(2,1)}, bf16[1,2,384,384]{3,2,1,0:T(8,128)(2,1)}, u32[]{:S(2)}, u32[]{:S(2)}) collective-permute-start(bf16[1,2,384,384]{3,2,1,0:T(8,128)(2,1)} %shard_map.65), channel_id=1, source_target_pairs={{8,16},{40,48},{72,80},{104,112},{16,8},{48,40},{80,72},{112,104},... | collective-permute-start | bytes 1769480 | tf_op jit(solution)/shard_map/ppermute | solution.py:654
  85.0 1.9 %shard_map.66 = bf16[1,2,384,384]{3,2,1,0:T(8,128)(2,1)} custom-call(s32[1]{0:T(128)} %bitcast.place.refs_0_, bf16[4,2,384,384]{3,2,1,0:T(8,128)(2,1)} %bitcast.9), custom_call_target="tpu_custom_call" | custom-call | bytes 2400000 | tf_op jit(solution)/shard_map/pallas_call | solution.py:62
  86.9 4.6 %collective-permute-start.7 = (bf16[1,2,384,384]{3,2,1,0:T(8,128)(2,1)}, bf16[1,2,384,384]{3,2,1,0:T(8,128)(2,1)}, u32[]{:S(2)}, u32[]{:S(2)}) collective-permute-start(bf16[1,2,384,384]{3,2,1,0:T(8,128)(2,1)} %shard_map.66), channel_id=1, source_target_pairs={{8,16},{40,48},{72,80},{104,112},{16,8},{48,40},{80,72},{112,104},... | collective-permute-start | bytes 1769480 | tf_op jit(solution)/shard_map/ppermute | solution.py:655
  91.5 0.0 collective-permute-done.4.swapped
  91.5 0.0 copy-start.6
  91.5 0.8 copy-done.6
  92.3 1.1 copy-done.7
  93.4 1.5 %near_join.1.refs_6_.near = bf16[2,2,384,384]{3,2,1,0:T(8,128)(2,1)S(1)} custom-call(s32[1]{0:T(128)} %bitcast.place.refs_0_, bf16[2,2,192,384]{3,2,1,0:T(8,128)(2,1)S(1)} %copy-done.7, bf16[2,2,192,384]{3,2,1,0:T(8,128)(2,1)} %copy-done.2), custom_call_target="tpu_custom_call" | custom-call | bytes 2400000 | tf_op jit(solution)/shard_map/near_join/pallas_call | solution.py:273
  94.9 0.0 copy-start.1
  94.9 0.0 all-to-all-done.2
  94.9 0.1 collective-permute-start.3
  95.0 0.0 copy-done.9
  95.0 0.0 copy-done.10
  95.0 13.0 %born_early.1.early = bf16[768,768]{1,0:T(8,128)(2,1)} custom-call(s32[1]{0:T(128)} %bitcast.place.refs_0_, s32[4]{0:T(128)S(1)} %copy-done.8, f32[4]{0:T(128)S(1)} %copy-done.9, s32[1,4]{1,0:T(1,128)S(1)} %copy-done.10, bf16[4,2,384,384]{3,2,1,0:T(8,128)(2,1)} %bitcast.10, bf16[4,2,384,384]{3,2,1,0:T(8,128)(2,1)} %collective-permute-done.2.mate.refs_5_, ...), custom_call_target="tpu_custom_call" | custom-call | flops 7247757312 | bytes 12000000 | tf_op jit(solution)/shard_map/born_early/pallas_call | solution.py:373
  108.0 0.0 collective-permute-done.6.refs_8_.far_soon
  108.0 4.4 %collective-permute-done.7.refs_9_.far_late = bf16[1,2,384,384]{3,2,1,0:T(8,128)(2,1)} collective-permute-done((bf16[1,2,384,384]{3,2,1,0:T(8,128)(2,1)}, bf16[1,2,384,384]{3,2,1,0:T(8,128)(2,1)}, u32[]{:S(2)}, u32[]{:S(2)}) %collective-permute-start.7) | collective-permute-done | bytes 589856 | tf_op jit(solution)/shard_map/ppermute | solution.py:655
  112.4 0.0 collective-permute-done.5.refs_7_.far_cross
  112.4 0.0 copy-done.1
  112.4 13.7 %born_late.1.late = bf16[768,768]{1,0:T(8,128)(2,1)} custom-call(s32[1]{0:T(128)} %bitcast.place.refs_0_, s32[4]{0:T(128)S(1)} %copy-done.8, f32[4]{0:T(128)S(1)} %copy-done.9, s32[1,4]{1,0:T(1,128)S(1)} %copy-done.10, bf16[4,2,384,384]{3,2,1,0:T(8,128)(2,1)} %bitcast.11, bf16[4,2,384,384]{3,2,1,0:T(8,128)(2,1)} %collective-permute-done.2.mate.refs_5_, ...), custom_call_target="tpu_custom_call" | custom-call | flops 7247757312 | bytes 12000000 | tf_op jit(solution)/shard_map/born_late/pallas_call | solution.py:373
  126.2 0.0 copy-done.3
  126.2 0.0 copy-start.4
  126.2 0.0 copy-start.5
  126.2 4.4 %final_start.1 = (bf16[12,2,384,384]{3,2,1,0:T(8,128)(2,1)S(1)}, f32[3,384,768]{2,1,0:T(8,128)S(1)}, f32[3,384,768]{2,1,0:T(8,128)S(1)}, bf16[4,768,768]{2,1,0:T(8,128)(2,1)S(1)}) custom-call(s32[1]{0:T(128)} %bitcast.place.refs_0_, s32[4]{0:T(128)S(1)} %copy-done.8, bf16[3456,128]{1,0:T(8,128)(2,1)S(1)} %bitcast.15, bf16[4,2,384,384]{3,2,1,0:T(8,128)(2,1)} %free.1, ...), custom_call_target="tpu_custom_call" | custom-call | flops 1000000000 | bytes 10000000 | tf_op jit(solution)/shard_map/final_start/pallas_call | solution.py:520
  130.6 0.0 collective-permute-done.3.other
  130.7 7.6 %final.1 = (bf16[4,1,2,384,384]{4,3,2,1,0:T(8,128)(2,1)}, bf16[12,2,384,384]{3,2,1,0:T(8,128)(2,1)S(1)}, f32[3,384,768]{2,1,0:T(8,128)S(1)}) custom-call(s32[1]{0:T(128)} %bitcast.place.refs_0_, s32[1]{0:T(128)} %bitcast.1.refs_10_.side_of, s32[4]{0:T(128)S(1)} %copy-done.8, ...), custom_call_target="tpu_custom_call", output_to_operand_aliasing={{1}: (10, {}), {2}: (11, {})} | custom-call | flops 1000000000 | bytes 18000000 | tf_op jit(solution)/shard_map/final/pallas_call | solution.py:611
  (7 shorter events, 0.0 us)
Async XLA Ops:
  0.0 10.2 %copy-start = (bf16[4,1,2,384,384]{4,3,2,1,0:T(8,128)(2,1)S(1)}, bf16[4,1,2,384,384]{4,3,2,1,0:T(8,128)(2,1)}, u32[]{:S(2)}) copy-start(bf16[4,1,2,384,384]{4,3,2,1,0:T(8,128)(2,1)} %param.6) | copy-start | bytes 7077892
  0.0 10.2 %copy-start.8 = (s32[4]{0:T(128)S(1)}, s32[4]{0:T(128)}, u32[]{:S(2)}) copy-start(s32[4]{0:T(128)} %offsets.7) | copy-start | bytes 52
  0.0 10.2 %collective-permute-start.2 = (bf16[4,2,384,384]{3,2,1,0:T(8,128)(2,1)}, bf16[4,2,384,384]{3,2,1,0:T(8,128)(2,1)}, u32[]{:S(2)}, u32[]{:S(2)}) collective-permute-start(bf16[4,2,384,384]{3,2,1,0:T(8,128)(2,1)} %bitcast.5), channel_id=1, source_target_pairs={{0,8},{8,0},{1,9},{9,1},{2,10},{10,2},{3,11},{11,3},{4,12},{12,4},... | collective-permute-start | bytes 7077896 | tf_op jit(solution)/shard_map/ppermute | solution.py:649
  2.7 14.9 %collective-permute-start = (bf16[2,2,192,384]{3,2,1,0:T(8,128)(2,1)S(1)}, bf16[2,2,192,384]{3,2,1,0:T(8,128)(2,1)}, u32[]{:S(2)}, u32[]{:S(2)}) collective-permute-start(bf16[2,2,192,384]{3,2,1,0:T(8,128)(2,1)S(1)} %get-tuple-element.15), channel_id=1, source_target_pairs={{8,24},{24,40},{40,56},{56,72},{72,88},{88,104},{104,120},{16,0},{... | collective-permute-start | bytes 1769480 | tf_op jit(solution)/shard_map/ppermute | solution.py:648
  8.3 26.3 %collective-permute-start.1 = (bf16[2,2,192,384]{3,2,1,0:T(8,128)(2,1)S(1)}, bf16[2,2,192,384]{3,2,1,0:T(8,128)(2,1)S(1)}, u32[]{:S(2)}, u32[]{:S(2)}) collective-permute-start(bf16[2,2,192,384]{3,2,1,0:T(8,128)(2,1)S(1)} %get-tuple-element.16), channel_id=1, source_target_pairs={{8,16},{24,32},{40,48},{56,64},{72,80},{88,96},{104,112},{16,8},{3... | collective-permute-start | bytes 1769480 | tf_op jit(solution)/shard_map/ppermute | solution.py:647
  34.6 3.7 %copy-start.2 = (bf16[2,2,192,384]{3,2,1,0:T(8,128)(2,1)}, bf16[2,2,192,384]{3,2,1,0:T(8,128)(2,1)S(1)}, u32[]{:S(2)}) copy-start(bf16[2,2,192,384]{3,2,1,0:T(8,128)(2,1)S(1)} %collective-permute-done.1.cross) | copy-start | bytes 1769476
  72.6 22.3 %all-to-all-start.2 = ((bf16[16,216,128]{2,1,0:T(8,128)(2,1)}), bf16[16,216,128]{2,1,0:T(8,128)(2,1)S(1)}, u32[]{:S(2)}, u32[]{:S(2)}) async-start(bf16[16,216,128]{2,1,0:T(8,128)(2,1)} %row_sum.1), calls=%async_computation.2 | async-start | bytes 1769472 | tf_op jit(solution)/shard_map/all_to_all | solution.py:665
  76.2 15.3 %collective-permute-start.4 = (bf16[2,2,192,384]{3,2,1,0:T(8,128)(2,1)}, bf16[2,2,192,384]{3,2,1,0:T(8,128)(2,1)S(1)}, u32[]{:S(2)}, u32[]{:S(2)}) collective-permute-start(bf16[2,2,192,384]{3,2,1,0:T(8,128)(2,1)} %collective-permute-done.same), channel_id=1, source_target_pairs={{0,8},{8,0},{1,9},{9,1},{2,10},{10,2},{3,11},{11,3},{4,12},{12,4},... | collective-permute-start | bytes 1769480 | tf_op jit(solution)/shard_map/ppermute | solution.py:658
  79.8 32.6 %collective-permute-start.5 = (bf16[2,2,384,384]{3,2,1,0:T(8,128)(2,1)}, bf16[2,2,384,384]{3,2,1,0:T(8,128)(2,1)S(1)}, u32[]{:S(2)}, u32[]{:S(2)}) collective-permute-start(bf16[2,2,384,384]{3,2,1,0:T(8,128)(2,1)} %shard_map.64), channel_id=1, source_target_pairs={{24,32},{56,64},{88,96},{32,24},{64,56},{96,88},{25,33},{57,65},{8... | collective-permute-start | bytes 3538952 | tf_op jit(solution)/shard_map/ppermute | solution.py:653
  82.5 12.5 %copy-start.9 = (f32[4]{0:T(128)S(1)}, f32[4]{0:T(128)}, u32[]{:S(2)}) copy-start(f32[4]{0:T(128)} %refs_2_.3) | copy-start | bytes 52
  82.5 12.5 %copy-start.10 = (s32[1,4]{1,0:T(1,128)S(1)}, s32[1,4]{1,0:T(1,128)}, u32[]{:S(2)}) copy-start(s32[1,4]{1,0:T(1,128)} %refs_3_.3) | copy-start | bytes 52
  82.5 25.5 %collective-permute-start.6 = (bf16[1,2,384,384]{3,2,1,0:T(8,128)(2,1)}, bf16[1,2,384,384]{3,2,1,0:T(8,128)(2,1)}, u32[]{:S(2)}, u32[]{:S(2)}) collective-permute-start(bf16[1,2,384,384]{3,2,1,0:T(8,128)(2,1)} %shard_map.65), channel_id=1, source_target_pairs={{8,16},{40,48},{72,80},{104,112},{16,8},{48,40},{80,72},{112,104},... | collective-permute-start | bytes 1769480 | tf_op jit(solution)/shard_map/ppermute | solution.py:654
  86.9 25.5 %collective-permute-start.7 = (bf16[1,2,384,384]{3,2,1,0:T(8,128)(2,1)}, bf16[1,2,384,384]{3,2,1,0:T(8,128)(2,1)}, u32[]{:S(2)}, u32[]{:S(2)}) collective-permute-start(bf16[1,2,384,384]{3,2,1,0:T(8,128)(2,1)} %shard_map.66), channel_id=1, source_target_pairs={{8,16},{40,48},{72,80},{104,112},{16,8},{48,40},{80,72},{112,104},... | collective-permute-start | bytes 1769480 | tf_op jit(solution)/shard_map/ppermute | solution.py:655
  91.5 0.8 copy-start.6
  92.3 1.1 copy-start.7
  94.9 17.5 %copy-start.1 = (bf16[2,2,384,384]{3,2,1,0:T(8,128)(2,1)}, bf16[2,2,384,384]{3,2,1,0:T(8,128)(2,1)S(1)}, u32[]{:S(2)}) copy-start(bf16[2,2,384,384]{3,2,1,0:T(8,128)(2,1)S(1)} %near_join.1.refs_6_.near) | copy-start | bytes 3538948
  94.9 35.7 %collective-permute-start.3 = (bf16[3456,128]{1,0:T(8,128)(2,1)S(1)}, bf16[3456,128]{1,0:T(8,128)(2,1)S(1)}, u32[]{:S(2)}, u32[]{:S(2)}) collective-permute-start(bf16[3456,128]{1,0:T(8,128)(2,1)S(1)} %bitcast.14), channel_id=1, source_target_pairs={{0,8},{8,0},{1,9},{9,1},{2,10},{10,2},{3,11},{11,3},{4,12},{12,4},... | collective-permute-start | bytes 2654216 | tf_op jit(solution)/shard_map/ppermute | solution.py:669
  112.4 13.8 %copy-start.3 = (bf16[2,2,384,384]{3,2,1,0:T(8,128)(2,1)}, bf16[2,2,384,384]{3,2,1,0:T(8,128)(2,1)S(1)}, u32[]{:S(2)}) copy-start(bf16[2,2,384,384]{3,2,1,0:T(8,128)(2,1)S(1)} %collective-permute-done.5.refs_7_.far_cross) | copy-start | bytes 3538948
  126.2 4.5 %copy-start.4 = (bf16[768,768]{1,0:T(8,128)(2,1)S(1)}, bf16[768,768]{1,0:T(8,128)(2,1)}, u32[]{:S(2)}) copy-start(bf16[768,768]{1,0:T(8,128)(2,1)} %born_early.1.early) | copy-start | bytes 3538948
  126.2 4.5 %copy-start.5 = (bf16[768,768]{1,0:T(8,128)(2,1)S(1)}, bf16[768,768]{1,0:T(8,128)(2,1)}, u32[]{:S(2)}) copy-start(bf16[768,768]{1,0:T(8,128)(2,1)} %born_late.1.late) | copy-start | bytes 3538948

commit v12 on v9

--- a/solution.py
+++ b/solution.py
@@ -28,6 +28,10 @@
     return pltpu.with_memory_space_constraint(array, pltpu.HBM)
 
 
+def in_vmem(array):
+    return pltpu.with_memory_space_constraint(array, pltpu.VMEM)
+
+
 def first_index(offsets, value):
     return jnp.where(
         offsets[0] == value, 0, jnp.where(offsets[1] == value, 1, jnp.where(offsets[2] == value, 2, 3))
@@ -242,7 +246,7 @@
         compiler_params=pltpu.CompilerParams(vmem_limit_bytes=6 << 20),
         cost_estimate=pl.CostEstimate(flops=20_000_000, bytes_accessed=9_000_000, transcendentals=0),
         name="polar",
-    )(place, offsets, same, cross, chip, turned, partial)
+    )(place, offsets, in_vmem(same), in_vmem(cross), chip, turned, partial)
 
 
 def near_body(place, swapped, cross, out, sems):
@@ -462,15 +466,56 @@
     return value
 
 
+def tables_body(offsets, free, out, plain, table, sems):
+    roles = offset_roles(offsets)
+    loads = [
+        pltpu.make_async_copy(free.at[k], plain.at[role], sems.at[role])
+        for role, k in enumerate(roles)
+    ]
+    for load in loads:
+        load.start()
+    stores = []
+    for role in range(4):
+        loads[role].wait()
+        fr = plain[role, 0]
+        fi = plain[role, 1]
+        table[role, :NB, :NB] = fr
+        table[role, :NB, NB:] = fi
+        table[role, NB:, :NB] = -fi
+        table[role, NB:, NB:] = fr
+        store = pltpu.make_async_copy(table.at[role], out.at[role], sems.at[4 + role])
+        store.start()
+        stores.append(store)
+    for store in stores:
+        store.wait()
+
+
+def tables_call(offsets, free):
+    size = 2 * NB
+    return pl.pallas_call(
+        tables_body,
+        out_shape=pltpu.HBM((4, size, size), BF16),
+        in_specs=[SMEM, ANY],
+        out_specs=ANY,
+        scratch_shapes=[
+            pltpu.VMEM((4, 2, NB, NB), BF16),
+            pltpu.VMEM((4, size, size), BF16),
+            pltpu.SemaphoreType.DMA((8,)),
+        ],
+        compiler_params=pltpu.CompilerParams(vmem_limit_bytes=9 << 20),
+        cost_estimate=pl.CostEstimate(flops=0, bytes_accessed=7_000_000, transcendentals=0),
+        name="tables",
+    )(offsets, in_hbm(free))
+
+
 def start_body(
     place, offsets, mine, free, own, mate,
-    slots, magnon, sums, table, plain, joined, sems,
+    slots, magnon, sums, table, joined, sems,
 ):
     core = place[0]
     roles = offset_roles(offsets)
     tables = [
-        pltpu.make_async_copy(free.at[k], plain.at[role], sems.at[role])
-        for role, k in enumerate(roles)
+        pltpu.make_async_copy(free.at[role], table.at[role], sems.at[role]) for role in range(4)
     ]
     loads = [
         pltpu.make_async_copy(own, slots.at[pl.ds(4, 4)], sems.at[4]),
@@ -481,12 +526,6 @@
     unpack_half(mine, joined)
     for role in range(4):
         tables[role].wait()
-        fr = plain[role, 0]
-        fi = plain[role, 1]
-        table[role, :NB, :NB] = fr
-        table[role, :NB, NB:] = fi
-        table[role, NB:, :NB] = -fi
-        table[role, NB:, NB:] = fr
         if role == 0:
             direct(0, 0, core, joined, table, magnon)
         elif role == 1:
@@ -518,7 +557,6 @@
         in_specs=[SMEM, SMEM, VMEM] + [ANY] * 3,
         out_specs=(VMEM,) * 4,
         scratch_shapes=[
-            pltpu.VMEM((4, 2, NB, NB), BF16),
             pltpu.VMEM((3, HALF, size), BF16),
             pltpu.SemaphoreType.DMA((6,)),
         ],
@@ -631,6 +669,7 @@
     mate = lax.ppermute(own, "core", SWAP)
     inner = cut_call(place, own, 2, -2)
     far = lax.ppermute(inner, ENERGY, across)
+    tables = tables_call(offsets, magnon_free)
     chip, turned, partial = prepare_call(place, offsets, own, mate)
     pair = polar_call(place, offsets, same, cross, chip, turned, partial)
     swapped = lax.ppermute(same, "core", SWAP)
@@ -645,7 +684,7 @@
         place, offsets, occupation, coupling, (own, mate, near, far), vertex
     )
     other = lax.ppermute(mine, "core", SWAP)
-    held = start_call(place, offsets, mine, magnon_free, own, mate)
+    held = start_call(place, offsets, mine, tables, own, mate)
     return final_call(place, offsets, other, near, far, early, late, *held)
 
 

time: 136 us -> 136 us (level)
  Pallas kernels: 54.4 us -> 58.5 us
  waiting for transfers between devices: 29.8 us -> 25.9 us
    pallas_call x0 -> x1, Pallas kernels: none -> 3.91 us  [tables_call(): pl.pallas_call(tables_body, out_shape=pltpu.HBM((4, size, size), BF16), i...]
    all_to_all x1, waiting for transfers between devices: 3.8 us -> 0.01 us  [per_device(): mine = lax.all_to_all(copies, PLANE, 0, 0, tiled=True).reshape(FLAT, 128)]
  transfers between devices with their start and end apart: 7 -> 7, of which waited for: 4 -> 3; matrix products, arithmetic and copies ran while one was open for 0% -> 0% of each run, Pallas kernels for 31% -> 34%
where the time goes in v12:
time: 136 us
  Pallas kernels  58.5 us (43%)
  blocking collectives  30 us (22%)
  waiting for transfers between devices  25.9 us (19%)
  starting transfers between devices  20.9 us (15%)
    pallas_call x2, Pallas kernels, born_call(): pl.pallas_call(lambda *refs: born_body(early, *refs), out_shape=pltpu.HBM...  25.3 us
    all_to_all x1, blocking collectives, per_device(): lax.all_to_all(pair.reshape(BANDS, ROWS, 128), PLANE, 0, 0, tiled=True)  20 us
    ppermute x1, waiting for transfers between devices, per_device(): cross = lax.ppermute(to_cross, ENERGY, across)  12.7 us
    all_to_all x1, blocking collectives, per_device(): bands = lax.all_to_all(copies, ROW, 0, 0, tiled=True)  10 us
    ppermute x1, waiting for transfers between devices, per_device(): far = lax.ppermute(inner, ENERGY, across)  8.67 us
    pallas_call x1, Pallas kernels, final_call(): pl.pallas_call(final_body, out_shape=(jax.ShapeDtypeStruct((4, 1, 2, NB,...  7.56 us
    pallas_call x1, Pallas kernels, prepare_call(): pl.pallas_call(prepare_body, out_shape=(jax.ShapeDtypeStruct((8, 2, NB, N...  7.36 us
    all_to_all x1, starting transfers between devices, per_device(): mine = lax.all_to_all(copies, PLANE, 0, 0, tiled=True).reshape(FLAT, 128)  6.22 us
  transfers between devices with their start and end apart: 7, of which 3 were waited for; matrix products, arithmetic and copies ran while one was open for 0% of the time, Pallas kernels for 34%

profile of v12, /device:TPU:17, one launch (start us, length us, event | category | flops | bytes accessed | tf_op | source)
XLA Modules:
  0.0 135.7 jit_solution(18403374740883254360)
XLA Ops:
  0.0 0.0 copy-start
  0.0 0.0 copy-start.5
  0.0 0.7 collective-permute-start.2
  0.7 1.3 edge.1
  2.0 4.7 %collective-permute-start = (bf16[2,2,192,384]{3,2,1,0:T(8,128)(2,1)S(1)}, bf16[2,2,192,384]{3,2,1,0:T(8,128)(2,1)}, u32[]{:S(2)}, u32[]{:S(2)}) collective-permute-start(bf16[2,2,192,384]{3,2,1,0:T(8,128)(2,1)S(1)} %get-tuple-element.15), channel_id=1, source_target_pairs={{8,24},{24,40},{40,56},{56,72},{72,88},{88,104},{104,120},{16,0},{... | collective-permute-start | bytes 1769480 | tf_op jit(solution)/shard_map/ppermute | solution.py:668
  6.7 2.8 %collective-permute-start.1 = (bf16[2,2,192,384]{3,2,1,0:T(8,128)(2,1)S(1)}, bf16[2,2,192,384]{3,2,1,0:T(8,128)(2,1)S(1)}, u32[]{:S(2)}, u32[]{:S(2)}) collective-permute-start(bf16[2,2,192,384]{3,2,1,0:T(8,128)(2,1)S(1)} %get-tuple-element.16), channel_id=1, source_target_pairs={{8,16},{24,32},{40,48},{56,64},{72,80},{88,96},{104,112},{16,8},{3... | collective-permute-start | bytes 1769480 | tf_op jit(solution)/shard_map/ppermute | solution.py:667
  9.5 0.0 collective-permute-done.2.mate.refs_5_
  9.5 0.0 copy-done
  9.5 0.0 copy-done.5
  9.5 7.4 %prepare.1 = (bf16[8,2,384,384]{3,2,1,0:T(8,128)(2,1)S(1)}, f32[8,2,384,384]{3,2,1,0:T(8,128)S(1)}, f32[3,2,192,384]{3,2,1,0:T(8,128)S(1)}) custom-call(s32[1]{0:T(128)} %bitcast.place.refs_0_, s32[4]{0:T(128)S(1)} %copy-done.5, bf16[4,2,384,384]{3,2,1,0:T(8,128)(2,1)S(1)} %bitcast.10, bf16[4,2,384,384]{3,2,1,0:T(8,128)(2,1)} %collective-permute-done.2.mate.refs_5_), custom_call_target="tpu_custom_call" | custom-call | flops 20000000 | bytes 9000000 | tf_op jit(solution)/shard_map/prepare/pallas_call | solution.py:151
  16.9 4.6 %collective-permute-done.same = bf16[2,2,192,384]{3,2,1,0:T(8,128)(2,1)} collective-permute-done((bf16[2,2,192,384]{3,2,1,0:T(8,128)(2,1)S(1)}, bf16[2,2,192,384]{3,2,1,0:T(8,128)(2,1)}, u32[]{:S(2)}, u32[]{:S(2)}) %collective-permute-start) | collective-permute-done | bytes 589856 | tf_op jit(solution)/shard_map/ppermute | solution.py:668
  21.4 12.7 %collective-permute-done.1.cross = bf16[2,2,192,384]{3,2,1,0:T(8,128)(2,1)S(1)} collective-permute-done((bf16[2,2,192,384]{3,2,1,0:T(8,128)(2,1)S(1)}, bf16[2,2,192,384]{3,2,1,0:T(8,128)(2,1)S(1)}, u32[]{:S(2)}, u32[]{:S(2)}) %collective-permute-start.1) | collective-permute-done | bytes 589856 | tf_op jit(solution)/shard_map/ppermute | solution.py:667
  34.1 0.0 copy-start.2
  34.1 3.7 %polar.1 = bf16[3456,128]{1,0:T(8,128)(2,1)} custom-call(s32[1]{0:T(128)} %bitcast.place.refs_0_, s32[4]{0:T(128)S(1)} %copy-done.5, bf16[2,2,192,384]{3,2,1,0:T(8,128)(2,1)} %collective-permute-done.same, bf16[2,2,192,384]{3,2,1,0:T(8,128)(2,1)S(1)} %collective-permute-done.1.cross, bf16[8,2,384,384]{3,2,1,0:T(8,128)(2,1)S(1)} %get-tuple-element.17.chip, ...), custom_call_target="tpu_custom_call" | custom-call | flops 20000000 | bytes 9000000 | tf_op jit(solution)/shard_map/polar/pallas_call | solution.py:237
  37.8 0.0 copy-done.2
  37.8 20.0 %all_to_all.15.bands = bf16[16,216,128]{2,1,0:T(8,128)(2,1)S(1)} all-to-all(bf16[16,216,128]{2,1,0:T(8,128)(2,1)} %bitcast.13), channel_id=1, replica_groups=mesh['y'=4,'xh'=2,'core'=2,'xl'=2,'z'=4] {'y','z'}, dimensions={0} | all-to-all | bytes 1769472 | tf_op jit(solution)/shard_map/all_to_all | solution.py:677
  57.8 0.1 plane_sum.1
  57.9 10.0 %all_to_all.16.bands = bf16[4,216,128]{2,1,0:T(8,128)(2,1)S(1)} all-to-all(bf16[4,216,128]{2,1,0:T(8,128)(2,1)S(1)} %plane_sum.1), channel_id=1, replica_groups=mesh['y'=4,'xh'=2,'core'=2,'xl'=2,'z'=4] {'xh','xl'}, dimensions={0} | all-to-all | bytes 442368 | tf_op jit(solution)/shard_map/all_to_all | solution.py:680
  68.0 1.2 row_sum.1
  69.1 6.2 %all-to-all-start.2 = ((bf16[16,216,128]{2,1,0:T(8,128)(2,1)}), bf16[16,216,128]{2,1,0:T(8,128)(2,1)S(1)}, u32[]{:S(2)}, u32[]{:S(2)}) async-start(bf16[16,216,128]{2,1,0:T(8,128)(2,1)} %row_sum.1), calls=%async_computation.2 | async-start | bytes 1769472 | tf_op jit(solution)/shard_map/all_to_all | solution.py:682
  75.3 1.6 %collective-permute-start.4 = (bf16[2,2,192,384]{3,2,1,0:T(8,128)(2,1)}, bf16[2,2,192,384]{3,2,1,0:T(8,128)(2,1)S(1)}, u32[]{:S(2)}, u32[]{:S(2)}) collective-permute-start(bf16[2,2,192,384]{3,2,1,0:T(8,128)(2,1)} %collective-permute-done.same), channel_id=1, source_target_pairs={{0,8},{8,0},{1,9},{9,1},{2,10},{10,2},{3,11},{11,3},{4,12},{12,4},... | collective-permute-start | bytes 1769480 | tf_op jit(solution)/shard_map/ppermute | solution.py:675
  76.9 2.3 %shard_map.64 = bf16[2,2,384,384]{3,2,1,0:T(8,128)(2,1)} custom-call(s32[1]{0:T(128)} %bitcast.place.refs_0_, bf16[4,2,384,384]{3,2,1,0:T(8,128)(2,1)} %bitcast.6), custom_call_target="tpu_custom_call" | custom-call | bytes 2400000 | tf_op jit(solution)/shard_map/pallas_call | solution.py:62
  79.2 2.5 %collective-permute-start.5 = (bf16[2,2,384,384]{3,2,1,0:T(8,128)(2,1)}, bf16[2,2,384,384]{3,2,1,0:T(8,128)(2,1)S(1)}, u32[]{:S(2)}, u32[]{:S(2)}) collective-permute-start(bf16[2,2,384,384]{3,2,1,0:T(8,128)(2,1)} %shard_map.64), channel_id=1, source_target_pairs={{8,16},{24,32},{40,48},{56,64},{72,80},{88,96},{104,112},{16,8},{3... | collective-permute-start | bytes 3538952 | tf_op jit(solution)/shard_map/ppermute | solution.py:671
  81.7 3.9 %tables.1.free = bf16[4,768,768]{2,1,0:T(8,128)(2,1)} custom-call(s32[4]{0:T(128)S(1)} %copy-done.5, bf16[4,2,384,384]{3,2,1,0:T(8,128)(2,1)} %free.1), custom_call_target="tpu_custom_call" | custom-call | bytes 7000000 | tf_op jit(solution)/shard_map/tables/pallas_call | solution.py:495
  85.6 0.0 copy-start.6
  85.6 0.0 copy-start.7
  85.6 0.0 collective-permute-done.4.swapped
  85.6 1.5 %near_join.1.refs_6_.near = bf16[2,2,384,384]{3,2,1,0:T(8,128)(2,1)S(1)} custom-call(s32[1]{0:T(128)} %bitcast.place.refs_0_, bf16[2,2,192,384]{3,2,1,0:T(8,128)(2,1)S(1)} %collective-permute-done.4.swapped, bf16[2,2,192,384]{3,2,1,0:T(8,128)(2,1)} %copy-done.2), custom_call_target="tpu_custom_call" | custom-call | bytes 2400000 | tf_op jit(solution)/shard_map/near_join/pallas_call | solution.py:273
  87.1 0.0 copy-start.1
  87.1 0.0 all-to-all-done.2
  87.1 2.4 %collective-permute-start.3 = (bf16[3456,128]{1,0:T(8,128)(2,1)S(1)}, bf16[3456,128]{1,0:T(8,128)(2,1)S(1)}, u32[]{:S(2)}, u32[]{:S(2)}) collective-permute-start(bf16[3456,128]{1,0:T(8,128)(2,1)S(1)} %bitcast.11), channel_id=1, source_target_pairs={{0,8},{8,0},{1,9},{9,1},{2,10},{10,2},{3,11},{11,3},{4,12},{12,4},... | collective-permute-start | bytes 2654216 | tf_op jit(solution)/shard_map/ppermute | solution.py:686
  89.6 0.0 copy-done.6
  89.6 0.0 copy-done.7
  89.6 13.1 %born_early.1.early = bf16[768,768]{1,0:T(8,128)(2,1)} custom-call(s32[1]{0:T(128)} %bitcast.place.refs_0_, s32[4]{0:T(128)S(1)} %copy-done.5, f32[4]{0:T(128)S(1)} %copy-done.6, s32[1,4]{1,0:T(1,128)S(1)} %copy-done.7, bf16[4,2,384,384]{3,2,1,0:T(8,128)(2,1)} %bitcast.7, bf16[4,2,384,384]{3,2,1,0:T(8,128)(2,1)} %collective-permute-done.2.mate.refs_5_, ...), custom_call_target="tpu_custom_call" | custom-call | flops 7247757312 | bytes 12000000 | tf_op jit(solution)/shard_map/born_early/pallas_call | solution.py:367
  102.7 8.7 %collective-permute-done.5.refs_7_.far = bf16[2,2,384,384]{3,2,1,0:T(8,128)(2,1)S(1)} collective-permute-done((bf16[2,2,384,384]{3,2,1,0:T(8,128)(2,1)}, bf16[2,2,384,384]{3,2,1,0:T(8,128)(2,1)S(1)}, u32[]{:S(2)}, u32[]{:S(2)}) %collective-permute-start.5) | collective-permute-done | bytes 1179680 | tf_op jit(solution)/shard_map/ppermute | solution.py:671
  111.3 0.0 copy-done.1
  111.3 0.0 copy-start.3
  111.3 12.2 %born_late.1.late = bf16[768,768]{1,0:T(8,128)(2,1)S(1)} custom-call(s32[1]{0:T(128)} %bitcast.place.refs_0_, s32[4]{0:T(128)S(1)} %copy-done.5, f32[4]{0:T(128)S(1)} %copy-done.6, s32[1,4]{1,0:T(1,128)S(1)} %copy-done.7, bf16[4,2,384,384]{3,2,1,0:T(8,128)(2,1)} %bitcast.8, bf16[4,2,384,384]{3,2,1,0:T(8,128)(2,1)} %collective-permute-done.2.mate.refs_5_, ...), custom_call_target="tpu_custom_call" | custom-call | flops 7247757312 | bytes 12000000 | tf_op jit(solution)/shard_map/born_late/pallas_call | solution.py:367
  123.5 0.0 copy-done.3
  123.5 0.0 copy-start.4
  123.5 4.4 %final_start.1 = (bf16[12,2,384,384]{3,2,1,0:T(8,128)(2,1)S(1)}, f32[3,384,768]{2,1,0:T(8,128)S(1)}, f32[3,384,768]{2,1,0:T(8,128)S(1)}, bf16[4,768,768]{2,1,0:T(8,128)(2,1)S(1)}) custom-call(s32[1]{0:T(128)} %bitcast.place.refs_0_, s32[4]{0:T(128)S(1)} %copy-done.5, bf16[3456,128]{1,0:T(8,128)(2,1)S(1)} %bitcast.12, bf16[4,768,768]{2,1,0:T(8,128)(2,1)} %tables.1.free, ...), custom_call_target="tpu_custom_call" | custom-call | flops 1000000000 | bytes 10000000 | tf_op jit(solution)/shard_map/final_start/pallas_call | solution.py:549
  127.9 0.0 collective-permute-done.3.other
  127.9 0.0 copy-done.4
  127.9 7.6 %final.1 = (bf16[4,1,2,384,384]{4,3,2,1,0:T(8,128)(2,1)}, bf16[12,2,384,384]{3,2,1,0:T(8,128)(2,1)S(1)}, f32[3,384,768]{2,1,0:T(8,128)S(1)}) custom-call(s32[1]{0:T(128)} %bitcast.place.refs_0_, s32[4]{0:T(128)S(1)} %copy-done.5, bf16[3456,128]{1,0:T(8,128)(2,1)S(1)} %collective-permute-done.3.other, ...), custom_call_target="tpu_custom_call", output_to_operand_aliasing={{1}: (7, {}), {2}: (8, {})} | custom-call | flops 1000000000 | bytes 18000000 | tf_op jit(solution)/shard_map/final/pallas_call | solution.py:634
Async XLA Ops:
  0.0 9.5 %copy-start = (bf16[4,1,2,384,384]{4,3,2,1,0:T(8,128)(2,1)S(1)}, bf16[4,1,2,384,384]{4,3,2,1,0:T(8,128)(2,1)}, u32[]{:S(2)}) copy-start(bf16[4,1,2,384,384]{4,3,2,1,0:T(8,128)(2,1)} %param.6) | copy-start | bytes 7077892
  0.0 9.5 %copy-start.5 = (s32[4]{0:T(128)S(1)}, s32[4]{0:T(128)}, u32[]{:S(2)}) copy-start(s32[4]{0:T(128)} %offsets.9) | copy-start | bytes 52
  0.0 9.5 %collective-permute-start.2 = (bf16[4,2,384,384]{3,2,1,0:T(8,128)(2,1)}, bf16[4,2,384,384]{3,2,1,0:T(8,128)(2,1)}, u32[]{:S(2)}, u32[]{:S(2)}) collective-permute-start(bf16[4,2,384,384]{3,2,1,0:T(8,128)(2,1)} %bitcast.4), channel_id=1, source_target_pairs={{0,8},{8,0},{1,9},{9,1},{2,10},{10,2},{3,11},{11,3},{4,12},{12,4},... | collective-permute-start | bytes 7077896 | tf_op jit(solution)/shard_map/ppermute | solution.py:669
  2.0 19.5 %collective-permute-start = (bf16[2,2,192,384]{3,2,1,0:T(8,128)(2,1)S(1)}, bf16[2,2,192,384]{3,2,1,0:T(8,128)(2,1)}, u32[]{:S(2)}, u32[]{:S(2)}) collective-permute-start(bf16[2,2,192,384]{3,2,1,0:T(8,128)(2,1)S(1)} %get-tuple-element.15), channel_id=1, source_target_pairs={{8,24},{24,40},{40,56},{56,72},{72,88},{88,104},{104,120},{16,0},{... | collective-permute-start | bytes 1769480 | tf_op jit(solution)/shard_map/ppermute | solution.py:668
  6.7 27.4 %collective-permute-start.1 = (bf16[2,2,192,384]{3,2,1,0:T(8,128)(2,1)S(1)}, bf16[2,2,192,384]{3,2,1,0:T(8,128)(2,1)S(1)}, u32[]{:S(2)}, u32[]{:S(2)}) collective-permute-start(bf16[2,2,192,384]{3,2,1,0:T(8,128)(2,1)S(1)} %get-tuple-element.16), channel_id=1, source_target_pairs={{8,16},{24,32},{40,48},{56,64},{72,80},{88,96},{104,112},{16,8},{3... | collective-permute-start | bytes 1769480 | tf_op jit(solution)/shard_map/ppermute | solution.py:667
  34.1 3.7 %copy-start.2 = (bf16[2,2,192,384]{3,2,1,0:T(8,128)(2,1)}, bf16[2,2,192,384]{3,2,1,0:T(8,128)(2,1)S(1)}, u32[]{:S(2)}) copy-start(bf16[2,2,192,384]{3,2,1,0:T(8,128)(2,1)S(1)} %collective-permute-done.1.cross) | copy-start | bytes 1769476
  69.1 18.0 %all-to-all-start.2 = ((bf16[16,216,128]{2,1,0:T(8,128)(2,1)}), bf16[16,216,128]{2,1,0:T(8,128)(2,1)S(1)}, u32[]{:S(2)}, u32[]{:S(2)}) async-start(bf16[16,216,128]{2,1,0:T(8,128)(2,1)} %row_sum.1), calls=%async_computation.2 | async-start | bytes 1769472 | tf_op jit(solution)/shard_map/all_to_all | solution.py:682
  75.3 10.3 %collective-permute-start.4 = (bf16[2,2,192,384]{3,2,1,0:T(8,128)(2,1)}, bf16[2,2,192,384]{3,2,1,0:T(8,128)(2,1)S(1)}, u32[]{:S(2)}, u32[]{:S(2)}) collective-permute-start(bf16[2,2,192,384]{3,2,1,0:T(8,128)(2,1)} %collective-permute-done.same), channel_id=1, source_target_pairs={{0,8},{8,0},{1,9},{9,1},{2,10},{10,2},{3,11},{11,3},{4,12},{12,4},... | collective-permute-start | bytes 1769480 | tf_op jit(solution)/shard_map/ppermute | solution.py:675
  79.2 32.1 %collective-permute-start.5 = (bf16[2,2,384,384]{3,2,1,0:T(8,128)(2,1)}, bf16[2,2,384,384]{3,2,1,0:T(8,128)(2,1)S(1)}, u32[]{:S(2)}, u32[]{:S(2)}) collective-permute-start(bf16[2,2,384,384]{3,2,1,0:T(8,128)(2,1)} %shard_map.64), channel_id=1, source_target_pairs={{8,16},{24,32},{40,48},{56,64},{72,80},{88,96},{104,112},{16,8},{3... | collective-permute-start | bytes 3538952 | tf_op jit(solution)/shard_map/ppermute | solution.py:671
  85.6 4.0 %copy-start.6 = (f32[4]{0:T(128)S(1)}, f32[4]{0:T(128)}, u32[]{:S(2)}) copy-start(f32[4]{0:T(128)} %refs_2_.3) | copy-start | bytes 52
  85.6 4.0 %copy-start.7 = (s32[1,4]{1,0:T(1,128)S(1)}, s32[1,4]{1,0:T(1,128)}, u32[]{:S(2)}) copy-start(s32[1,4]{1,0:T(1,128)} %refs_3_.3) | copy-start | bytes 52
  87.1 24.2 %copy-start.1 = (bf16[2,2,384,384]{3,2,1,0:T(8,128)(2,1)}, bf16[2,2,384,384]{3,2,1,0:T(8,128)(2,1)S(1)}, u32[]{:S(2)}) copy-start(bf16[2,2,384,384]{3,2,1,0:T(8,128)(2,1)S(1)} %near_join.1.refs_6_.near) | copy-start | bytes 3538948
  87.1 40.8 %collective-permute-start.3 = (bf16[3456,128]{1,0:T(8,128)(2,1)S(1)}, bf16[3456,128]{1,0:T(8,128)(2,1)S(1)}, u32[]{:S(2)}, u32[]{:S(2)}) collective-permute-start(bf16[3456,128]{1,0:T(8,128)(2,1)S(1)} %bitcast.11), channel_id=1, source_target_pairs={{0,8},{8,0},{1,9},{9,1},{2,10},{10,2},{3,11},{11,3},{4,12},{12,4},... | collective-permute-start | bytes 2654216 | tf_op jit(solution)/shard_map/ppermute | solution.py:686
  111.3 12.2 %copy-start.3 = (bf16[2,2,384,384]{3,2,1,0:T(8,128)(2,1)}, bf16[2,2,384,384]{3,2,1,0:T(8,128)(2,1)S(1)}, u32[]{:S(2)}) copy-start(bf16[2,2,384,384]{3,2,1,0:T(8,128)(2,1)S(1)} %collective-permute-done.5.refs_7_.far) | copy-start | bytes 3538948
  123.5 4.4 %copy-start.4 = (bf16[768,768]{1,0:T(8,128)(2,1)S(1)}, bf16[768,768]{1,0:T(8,128)(2,1)}, u32[]{:S(2)}) copy-start(bf16[768,768]{1,0:T(8,128)(2,1)} %born_early.1.early) | copy-start | bytes 3538948

commit v13 on v12

--- a/solution.py
+++ b/solution.py
@@ -417,12 +417,14 @@
 
 
 def row_body(bands, out, value, sems):
-    for begin in range(0, ROWS, 64):
-        rows = slice(begin, min(begin + 64, ROWS))
+    stores = []
+    for piece, (begin, end) in enumerate(((0, 128), (128, ROWS))):
+        rows = slice(begin, end)
         value[rows, :] = band_total(bands, rows)
-    stores = [pltpu.make_async_copy(value, out.at[i], sems.at[i]) for i in range(BANDS)]
-    for store in stores:
-        store.start()
+        for i in range(BANDS):
+            store = pltpu.make_async_copy(value.at[rows], out.at[i, rows], sems.at[piece, i])
+            store.start()
+            stores.append(store)
     for store in stores:
         store.wait()
 
@@ -433,7 +435,7 @@
         out_shape=pltpu.HBM((BANDS, ROWS, 128), BF16),
         in_specs=[VMEM],
         out_specs=ANY,
-        scratch_shapes=[pltpu.VMEM((ROWS, 128), BF16), pltpu.SemaphoreType.DMA((BANDS,))],
+        scratch_shapes=[pltpu.VMEM((ROWS, 128), BF16), pltpu.SemaphoreType.DMA((2, BANDS))],
         compiler_params=pltpu.CompilerParams(vmem_limit_bytes=4 << 20),
         cost_estimate=pl.CostEstimate(flops=500_000, bytes_accessed=1_200_000, transcendentals=0),
         name="row_sum",

time: 136 us -> 136 us (level)
  no operation moved by 1% of the time
where the time goes in v13:
time: 136 us
  Pallas kernels  58.6 us (43%)
  blocking collectives  30 us (22%)
  waiting for transfers between devices  25.9 us (19%)
  starting transfers between devices  20.9 us (15%)
    pallas_call x2, Pallas kernels, born_call(): pl.pallas_call(lambda *refs: born_body(early, *refs), out_shape=pltpu.HBM...  25.3 us
    all_to_all x1, blocking collectives, per_device(): lax.all_to_all(pair.reshape(BANDS, ROWS, 128), PLANE, 0, 0, tiled=True)  20 us
    ppermute x1, waiting for transfers between devices, per_device(): cross = lax.ppermute(to_cross, ENERGY, across)  12.7 us
    all_to_all x1, blocking collectives, per_device(): bands = lax.all_to_all(copies, ROW, 0, 0, tiled=True)  10 us
    ppermute x1, waiting for transfers between devices, per_device(): far = lax.ppermute(inner, ENERGY, across)  8.66 us
    pallas_call x1, Pallas kernels, final_call(): pl.pallas_call(final_body, out_shape=(jax.ShapeDtypeStruct((4, 1, 2, NB,...  7.56 us
    pallas_call x1, Pallas kernels, prepare_call(): pl.pallas_call(prepare_body, out_shape=(jax.ShapeDtypeStruct((8, 2, NB, N...  7.36 us
    all_to_all x1, starting transfers between devices, per_device(): mine = lax.all_to_all(copies, PLANE, 0, 0, tiled=True).reshape(FLAT, 128)  6.22 us
  transfers between devices with their start and end apart: 7, of which 3 were waited for; matrix products, arithmetic and copies ran while one was open for 0% of the time, Pallas kernels for 34%

profile of v13, /device:TPU:17, one launch (start us, length us, event | category | flops | bytes accessed | tf_op | source)
XLA Modules:
  0.0 135.8 jit_solution(10176386969267636257)
XLA Ops:
  0.0 0.0 copy-start
  0.0 0.0 copy-start.5
  0.0 0.7 collective-permute-start.2
  0.7 1.3 edge.1
  2.0 4.7 %collective-permute-start = (bf16[2,2,192,384]{3,2,1,0:T(8,128)(2,1)S(1)}, bf16[2,2,192,384]{3,2,1,0:T(8,128)(2,1)}, u32[]{:S(2)}, u32[]{:S(2)}) collective-permute-start(bf16[2,2,192,384]{3,2,1,0:T(8,128)(2,1)S(1)} %get-tuple-element.15), channel_id=1, source_target_pairs={{8,24},{24,40},{40,56},{56,72},{72,88},{88,104},{104,120},{16,0},{... | collective-permute-start | bytes 1769480 | tf_op jit(solution)/shard_map/ppermute | solution.py:670
  6.7 2.8 %collective-permute-start.1 = (bf16[2,2,192,384]{3,2,1,0:T(8,128)(2,1)S(1)}, bf16[2,2,192,384]{3,2,1,0:T(8,128)(2,1)S(1)}, u32[]{:S(2)}, u32[]{:S(2)}) collective-permute-start(bf16[2,2,192,384]{3,2,1,0:T(8,128)(2,1)S(1)} %get-tuple-element.16), channel_id=1, source_target_pairs={{8,16},{24,32},{40,48},{56,64},{72,80},{88,96},{104,112},{16,8},{3... | collective-permute-start | bytes 1769480 | tf_op jit(solution)/shard_map/ppermute | solution.py:669
  9.5 0.0 collective-permute-done.2.mate.refs_5_
  9.5 0.0 copy-done
  9.5 0.0 copy-done.5
  9.5 7.4 %prepare.1 = (bf16[8,2,384,384]{3,2,1,0:T(8,128)(2,1)S(1)}, f32[8,2,384,384]{3,2,1,0:T(8,128)S(1)}, f32[3,2,192,384]{3,2,1,0:T(8,128)S(1)}) custom-call(s32[1]{0:T(128)} %bitcast.place.refs_0_, s32[4]{0:T(128)S(1)} %copy-done.5, bf16[4,2,384,384]{3,2,1,0:T(8,128)(2,1)S(1)} %bitcast.10, bf16[4,2,384,384]{3,2,1,0:T(8,128)(2,1)} %collective-permute-done.2.mate.refs_5_), custom_call_target="tpu_custom_call" | custom-call | flops 20000000 | bytes 9000000 | tf_op jit(solution)/shard_map/prepare/pallas_call | solution.py:151
  16.9 4.6 %collective-permute-done.same = bf16[2,2,192,384]{3,2,1,0:T(8,128)(2,1)} collective-permute-done((bf16[2,2,192,384]{3,2,1,0:T(8,128)(2,1)S(1)}, bf16[2,2,192,384]{3,2,1,0:T(8,128)(2,1)}, u32[]{:S(2)}, u32[]{:S(2)}) %collective-permute-start) | collective-permute-done | bytes 589856 | tf_op jit(solution)/shard_map/ppermute | solution.py:670
  21.4 12.7 %collective-permute-done.1.cross = bf16[2,2,192,384]{3,2,1,0:T(8,128)(2,1)S(1)} collective-permute-done((bf16[2,2,192,384]{3,2,1,0:T(8,128)(2,1)S(1)}, bf16[2,2,192,384]{3,2,1,0:T(8,128)(2,1)S(1)}, u32[]{:S(2)}, u32[]{:S(2)}) %collective-permute-start.1) | collective-permute-done | bytes 589856 | tf_op jit(solution)/shard_map/ppermute | solution.py:669
  34.1 0.0 copy-start.2
  34.1 3.7 %polar.1 = bf16[3456,128]{1,0:T(8,128)(2,1)} custom-call(s32[1]{0:T(128)} %bitcast.place.refs_0_, s32[4]{0:T(128)S(1)} %copy-done.5, bf16[2,2,192,384]{3,2,1,0:T(8,128)(2,1)} %collective-permute-done.same, bf16[2,2,192,384]{3,2,1,0:T(8,128)(2,1)S(1)} %collective-permute-done.1.cross, bf16[8,2,384,384]{3,2,1,0:T(8,128)(2,1)S(1)} %get-tuple-element.17.chip, ...), custom_call_target="tpu_custom_call" | custom-call | flops 20000000 | bytes 9000000 | tf_op jit(solution)/shard_map/polar/pallas_call | solution.py:237
  37.8 0.0 copy-done.2
  37.8 20.0 %all_to_all.15.bands = bf16[16,216,128]{2,1,0:T(8,128)(2,1)S(1)} all-to-all(bf16[16,216,128]{2,1,0:T(8,128)(2,1)} %bitcast.13), channel_id=1, replica_groups=mesh['y'=4,'xh'=2,'core'=2,'xl'=2,'z'=4] {'y','z'}, dimensions={0} | all-to-all | bytes 1769472 | tf_op jit(solution)/shard_map/all_to_all | solution.py:679
  57.8 0.1 plane_sum.1
  57.9 10.0 %all_to_all.16.bands = bf16[4,216,128]{2,1,0:T(8,128)(2,1)S(1)} all-to-all(bf16[4,216,128]{2,1,0:T(8,128)(2,1)S(1)} %plane_sum.1), channel_id=1, replica_groups=mesh['y'=4,'xh'=2,'core'=2,'xl'=2,'z'=4] {'xh','xl'}, dimensions={0} | all-to-all | bytes 442368 | tf_op jit(solution)/shard_map/all_to_all | solution.py:682
  68.0 1.3 row_sum.1
  69.3 6.2 %all-to-all-start.2 = ((bf16[16,216,128]{2,1,0:T(8,128)(2,1)}), bf16[16,216,128]{2,1,0:T(8,128)(2,1)S(1)}, u32[]{:S(2)}, u32[]{:S(2)}) async-start(bf16[16,216,128]{2,1,0:T(8,128)(2,1)} %row_sum.1), calls=%async_computation.2 | async-start | bytes 1769472 | tf_op jit(solution)/shard_map/all_to_all | solution.py:684
  75.5 1.6 %collective-permute-start.4 = (bf16[2,2,192,384]{3,2,1,0:T(8,128)(2,1)}, bf16[2,2,192,384]{3,2,1,0:T(8,128)(2,1)S(1)}, u32[]{:S(2)}, u32[]{:S(2)}) collective-permute-start(bf16[2,2,192,384]{3,2,1,0:T(8,128)(2,1)} %collective-permute-done.same), channel_id=1, source_target_pairs={{0,8},{8,0},{1,9},{9,1},{2,10},{10,2},{3,11},{11,3},{4,12},{12,4},... | collective-permute-start | bytes 1769480 | tf_op jit(solution)/shard_map/ppermute | solution.py:677
  77.1 2.3 %shard_map.64 = bf16[2,2,384,384]{3,2,1,0:T(8,128)(2,1)} custom-call(s32[1]{0:T(128)} %bitcast.place.refs_0_, bf16[4,2,384,384]{3,2,1,0:T(8,128)(2,1)} %bitcast.6), custom_call_target="tpu_custom_call" | custom-call | bytes 2400000 | tf_op jit(solution)/shard_map/pallas_call | solution.py:62
  79.4 2.5 %collective-permute-start.5 = (bf16[2,2,384,384]{3,2,1,0:T(8,128)(2,1)}, bf16[2,2,384,384]{3,2,1,0:T(8,128)(2,1)S(1)}, u32[]{:S(2)}, u32[]{:S(2)}) collective-permute-start(bf16[2,2,384,384]{3,2,1,0:T(8,128)(2,1)} %shard_map.64), channel_id=1, source_target_pairs={{8,16},{24,32},{40,48},{56,64},{72,80},{88,96},{104,112},{16,8},{3... | collective-permute-start | bytes 3538952 | tf_op jit(solution)/shard_map/ppermute | solution.py:673
  81.8 3.9 %tables.1.free = bf16[4,768,768]{2,1,0:T(8,128)(2,1)} custom-call(s32[4]{0:T(128)S(1)} %copy-done.5, bf16[4,2,384,384]{3,2,1,0:T(8,128)(2,1)} %free.1), custom_call_target="tpu_custom_call" | custom-call | bytes 7000000 | tf_op jit(solution)/shard_map/tables/pallas_call | solution.py:497
  85.7 0.0 copy-start.6
  85.7 0.0 copy-start.7
  85.8 0.0 collective-permute-done.4.swapped
  85.8 1.5 %near_join.1.refs_6_.near = bf16[2,2,384,384]{3,2,1,0:T(8,128)(2,1)S(1)} custom-call(s32[1]{0:T(128)} %bitcast.place.refs_0_, bf16[2,2,192,384]{3,2,1,0:T(8,128)(2,1)S(1)} %collective-permute-done.4.swapped, bf16[2,2,192,384]{3,2,1,0:T(8,128)(2,1)} %copy-done.2), custom_call_target="tpu_custom_call" | custom-call | bytes 2400000 | tf_op jit(solution)/shard_map/near_join/pallas_call | solution.py:273
  87.2 0.0 copy-start.1
  87.3 0.0 all-to-all-done.2
  87.3 2.4 %collective-permute-start.3 = (bf16[3456,128]{1,0:T(8,128)(2,1)S(1)}, bf16[3456,128]{1,0:T(8,128)(2,1)S(1)}, u32[]{:S(2)}, u32[]{:S(2)}) collective-permute-start(bf16[3456,128]{1,0:T(8,128)(2,1)S(1)} %bitcast.11), channel_id=1, source_target_pairs={{0,8},{8,0},{1,9},{9,1},{2,10},{10,2},{3,11},{11,3},{4,12},{12,4},... | collective-permute-start | bytes 2654216 | tf_op jit(solution)/shard_map/ppermute | solution.py:688
  89.7 0.0 copy-done.6
  89.7 0.0 copy-done.7
  89.7 13.1 %born_early.1.early = bf16[768,768]{1,0:T(8,128)(2,1)} custom-call(s32[1]{0:T(128)} %bitcast.place.refs_0_, s32[4]{0:T(128)S(1)} %copy-done.5, f32[4]{0:T(128)S(1)} %copy-done.6, s32[1,4]{1,0:T(1,128)S(1)} %copy-done.7, bf16[4,2,384,384]{3,2,1,0:T(8,128)(2,1)} %bitcast.7, bf16[4,2,384,384]{3,2,1,0:T(8,128)(2,1)} %collective-permute-done.2.mate.refs_5_, ...), custom_call_target="tpu_custom_call" | custom-call | flops 7247757312 | bytes 12000000 | tf_op jit(solution)/shard_map/born_early/pallas_call | solution.py:367
  102.8 8.7 %collective-permute-done.5.refs_7_.far = bf16[2,2,384,384]{3,2,1,0:T(8,128)(2,1)S(1)} collective-permute-done((bf16[2,2,384,384]{3,2,1,0:T(8,128)(2,1)}, bf16[2,2,384,384]{3,2,1,0:T(8,128)(2,1)S(1)}, u32[]{:S(2)}, u32[]{:S(2)}) %collective-permute-start.5) | collective-permute-done | bytes 1179680 | tf_op jit(solution)/shard_map/ppermute | solution.py:673
  111.5 0.0 copy-done.1
  111.5 0.0 copy-start.3
  111.5 12.2 %born_late.1.late = bf16[768,768]{1,0:T(8,128)(2,1)S(1)} custom-call(s32[1]{0:T(128)} %bitcast.place.refs_0_, s32[4]{0:T(128)S(1)} %copy-done.5, f32[4]{0:T(128)S(1)} %copy-done.6, s32[1,4]{1,0:T(1,128)S(1)} %copy-done.7, bf16[4,2,384,384]{3,2,1,0:T(8,128)(2,1)} %bitcast.8, bf16[4,2,384,384]{3,2,1,0:T(8,128)(2,1)} %collective-permute-done.2.mate.refs_5_, ...), custom_call_target="tpu_custom_call" | custom-call | flops 7247757312 | bytes 12000000 | tf_op jit(solution)/shard_map/born_late/pallas_call | solution.py:367
  123.7 0.0 copy-done.3
  123.7 0.0 copy-start.4
  123.7 4.4 %final_start.1 = (bf16[12,2,384,384]{3,2,1,0:T(8,128)(2,1)S(1)}, f32[3,384,768]{2,1,0:T(8,128)S(1)}, f32[3,384,768]{2,1,0:T(8,128)S(1)}, bf16[4,768,768]{2,1,0:T(8,128)(2,1)S(1)}) custom-call(s32[1]{0:T(128)} %bitcast.place.refs_0_, s32[4]{0:T(128)S(1)} %copy-done.5, bf16[3456,128]{1,0:T(8,128)(2,1)S(1)} %bitcast.12, bf16[4,768,768]{2,1,0:T(8,128)(2,1)} %tables.1.free, ...), custom_call_target="tpu_custom_call" | custom-call | flops 1000000000 | bytes 10000000 | tf_op jit(solution)/shard_map/final_start/pallas_call | solution.py:551
  128.1 0.0 collective-permute-done.3.other
  128.1 0.0 copy-done.4
  128.1 7.6 %final.1 = (bf16[4,1,2,384,384]{4,3,2,1,0:T(8,128)(2,1)}, bf16[12,2,384,384]{3,2,1,0:T(8,128)(2,1)S(1)}, f32[3,384,768]{2,1,0:T(8,128)S(1)}) custom-call(s32[1]{0:T(128)} %bitcast.place.refs_0_, s32[4]{0:T(128)S(1)} %copy-done.5, bf16[3456,128]{1,0:T(8,128)(2,1)S(1)} %collective-permute-done.3.other, ...), custom_call_target="tpu_custom_call", output_to_operand_aliasing={{1}: (7, {}), {2}: (8, {})} | custom-call | flops 1000000000 | bytes 18000000 | tf_op jit(solution)/shard_map/final/pallas_call | solution.py:636
Async XLA Ops:
  0.0 9.5 %copy-start = (bf16[4,1,2,384,384]{4,3,2,1,0:T(8,128)(2,1)S(1)}, bf16[4,1,2,384,384]{4,3,2,1,0:T(8,128)(2,1)}, u32[]{:S(2)}) copy-start(bf16[4,1,2,384,384]{4,3,2,1,0:T(8,128)(2,1)} %param.6) | copy-start | bytes 7077892
  0.0 9.5 %copy-start.5 = (s32[4]{0:T(128)S(1)}, s32[4]{0:T(128)}, u32[]{:S(2)}) copy-start(s32[4]{0:T(128)} %offsets.9) | copy-start | bytes 52
  0.0 9.5 %collective-permute-start.2 = (bf16[4,2,384,384]{3,2,1,0:T(8,128)(2,1)}, bf16[4,2,384,384]{3,2,1,0:T(8,128)(2,1)}, u32[]{:S(2)}, u32[]{:S(2)}) collective-permute-start(bf16[4,2,384,384]{3,2,1,0:T(8,128)(2,1)} %bitcast.4), channel_id=1, source_target_pairs={{0,8},{8,0},{1,9},{9,1},{2,10},{10,2},{3,11},{11,3},{4,12},{12,4},... | collective-permute-start | bytes 7077896 | tf_op jit(solution)/shard_map/ppermute | solution.py:671
  2.0 19.5 %collective-permute-start = (bf16[2,2,192,384]{3,2,1,0:T(8,128)(2,1)S(1)}, bf16[2,2,192,384]{3,2,1,0:T(8,128)(2,1)}, u32[]{:S(2)}, u32[]{:S(2)}) collective-permute-start(bf16[2,2,192,384]{3,2,1,0:T(8,128)(2,1)S(1)} %get-tuple-element.15), channel_id=1, source_target_pairs={{8,24},{24,40},{40,56},{56,72},{72,88},{88,104},{104,120},{16,0},{... | collective-permute-start | bytes 1769480 | tf_op jit(solution)/shard_map/ppermute | solution.py:670
  6.7 27.4 %collective-permute-start.1 = (bf16[2,2,192,384]{3,2,1,0:T(8,128)(2,1)S(1)}, bf16[2,2,192,384]{3,2,1,0:T(8,128)(2,1)S(1)}, u32[]{:S(2)}, u32[]{:S(2)}) collective-permute-start(bf16[2,2,192,384]{3,2,1,0:T(8,128)(2,1)S(1)} %get-tuple-element.16), channel_id=1, source_target_pairs={{8,16},{24,32},{40,48},{56,64},{72,80},{88,96},{104,112},{16,8},{3... | collective-permute-start | bytes 1769480 | tf_op jit(solution)/shard_map/ppermute | solution.py:669
  34.1 3.7 %copy-start.2 = (bf16[2,2,192,384]{3,2,1,0:T(8,128)(2,1)}, bf16[2,2,192,384]{3,2,1,0:T(8,128)(2,1)S(1)}, u32[]{:S(2)}) copy-start(bf16[2,2,192,384]{3,2,1,0:T(8,128)(2,1)S(1)} %collective-permute-done.1.cross) | copy-start | bytes 1769476
  69.3 18.0 %all-to-all-start.2 = ((bf16[16,216,128]{2,1,0:T(8,128)(2,1)}), bf16[16,216,128]{2,1,0:T(8,128)(2,1)S(1)}, u32[]{:S(2)}, u32[]{:S(2)}) async-start(bf16[16,216,128]{2,1,0:T(8,128)(2,1)} %row_sum.1), calls=%async_computation.2 | async-start | bytes 1769472 | tf_op jit(solution)/shard_map/all_to_all | solution.py:684
  75.5 10.3 %collective-permute-start.4 = (bf16[2,2,192,384]{3,2,1,0:T(8,128)(2,1)}, bf16[2,2,192,384]{3,2,1,0:T(8,128)(2,1)S(1)}, u32[]{:S(2)}, u32[]{:S(2)}) collective-permute-start(bf16[2,2,192,384]{3,2,1,0:T(8,128)(2,1)} %collective-permute-done.same), channel_id=1, source_target_pairs={{0,8},{8,0},{1,9},{9,1},{2,10},{10,2},{3,11},{11,3},{4,12},{12,4},... | collective-permute-start | bytes 1769480 | tf_op jit(solution)/shard_map/ppermute | solution.py:677
  79.4 32.1 %collective-permute-start.5 = (bf16[2,2,384,384]{3,2,1,0:T(8,128)(2,1)}, bf16[2,2,384,384]{3,2,1,0:T(8,128)(2,1)S(1)}, u32[]{:S(2)}, u32[]{:S(2)}) collective-permute-start(bf16[2,2,384,384]{3,2,1,0:T(8,128)(2,1)} %shard_map.64), channel_id=1, source_target_pairs={{8,16},{24,32},{40,48},{56,64},{72,80},{88,96},{104,112},{16,8},{3... | collective-permute-start | bytes 3538952 | tf_op jit(solution)/shard_map/ppermute | solution.py:673
  85.7 4.0 %copy-start.6 = (f32[4]{0:T(128)S(1)}, f32[4]{0:T(128)}, u32[]{:S(2)}) copy-start(f32[4]{0:T(128)} %refs_2_.3) | copy-start | bytes 52
  85.7 4.0 %copy-start.7 = (s32[1,4]{1,0:T(1,128)S(1)}, s32[1,4]{1,0:T(1,128)}, u32[]{:S(2)}) copy-start(s32[1,4]{1,0:T(1,128)} %refs_3_.3) | copy-start | bytes 52
  87.2 24.2 %copy-start.1 = (bf16[2,2,384,384]{3,2,1,0:T(8,128)(2,1)}, bf16[2,2,384,384]{3,2,1,0:T(8,128)(2,1)S(1)}, u32[]{:S(2)}) copy-start(bf16[2,2,384,384]{3,2,1,0:T(8,128)(2,1)S(1)} %near_join.1.refs_6_.near) | copy-start | bytes 3538948
  87.3 40.8 %collective-permute-start.3 = (bf16[3456,128]{1,0:T(8,128)(2,1)S(1)}, bf16[3456,128]{1,0:T(8,128)(2,1)S(1)}, u32[]{:S(2)}, u32[]{:S(2)}) collective-permute-start(bf16[3456,128]{1,0:T(8,128)(2,1)S(1)} %bitcast.11), channel_id=1, source_target_pairs={{0,8},{8,0},{1,9},{9,1},{2,10},{10,2},{3,11},{11,3},{4,12},{12,4},... | collective-permute-start | bytes 2654216 | tf_op jit(solution)/shard_map/ppermute | solution.py:688
  111.5 12.2 %copy-start.3 = (bf16[2,2,384,384]{3,2,1,0:T(8,128)(2,1)}, bf16[2,2,384,384]{3,2,1,0:T(8,128)(2,1)S(1)}, u32[]{:S(2)}) copy-start(bf16[2,2,384,384]{3,2,1,0:T(8,128)(2,1)S(1)} %collective-permute-done.5.refs_7_.far) | copy-start | bytes 3538948
  123.7 4.4 %copy-start.4 = (bf16[768,768]{1,0:T(8,128)(2,1)S(1)}, bf16[768,768]{1,0:T(8,128)(2,1)}, u32[]{:S(2)}) copy-start(bf16[768,768]{1,0:T(8,128)(2,1)} %born_early.1.early) | copy-start | bytes 3538948
